TPU v7x, 128 devices: a whole 4x4x4 slice. The times are simulated.
128 devices in a mesh: ctx: 16 (over x, y), tp: 8 (over z, core).
Axes of the slice: x: 4, y: 4, z: 4, core: 2. Of those that a mesh axis runs over, the one named last changes fastest.
Arguments:
- queries: bfloat16 [4096, 8192], P('ctx', 'tp'), may hold values from -160 to 160
- keys: bfloat16 [4096, 1024], P('ctx', 'tp'), may hold values from -4 to 4
- values: bfloat16 [4096, 1024], P('ctx', 'tp'), may hold values from -6 to 6
- positions: int32 [4096], P('ctx'), may hold values from 0 to 4095, as said below
- out_weight: bfloat16 [8192, 8192], P('tp'), may hold values from -0.5 to 0.5
Outputs:
- attn_out: bfloat16 [4096, 8192], P(('ctx', 'tp'))
Inputs may be any that keep to these rules, and one draw needn't show every extreme that they name: positions holds every number of 0 to 4095 once; it is made of 32 runs of 128 rows, each run holding ascending consecutive positions that start at a multiple of 128; the order of the runs is arbitrary.
All inputs are finite; a program needn't handle non-finite values.
Results may differ from a plain program's by a relative error of at most 0.015.
Values may be sent and summed in bfloat16 or wider, within the bound.
No kernel may reach another device: no remote copies, remote signals or barrier semaphores. Data moves between devices by JAX's collectives and lax.ppermute only.
A program may use at most 64 MiB of HBM per device.

v0:
```python
import functools
import math

import jax
import jax.numpy as jnp
from jax import lax
from jax.experimental import pallas as pl
from jax.experimental.pallas import tpu as pltpu
from jax.sharding import PartitionSpec as P


HD = 128
SPAN = 128
QUAD = 4
PACK = 272
LOG_SCALE = HD ** -0.5 * math.log2(math.e)
NEG = -1e30
NX = 4
NZ = 4
NCORE = 2
PIECE = 16
DOUT = 8192
NCOL = 8
GROUP = 4
HEADROOM = 60.0
NW = 4


VMEM = pl.BlockSpec(memory_space=pltpu.VMEM)
SMEM = pl.BlockSpec(memory_space=pltpu.SMEM)
HBM = pl.BlockSpec(memory_space=pltpu.HBM)


def struct(shape, dtype):
    return jax.ShapeDtypeStruct(shape, dtype)


def pack_kernel(pos_hbm, k_hbm, v_hbm, out_ref, pos_ref, k_ref, v_ref, sems):
    copies = [
        pltpu.make_async_copy(src, dst, sems.at[i])
        for i, (src, dst) in enumerate(((v_hbm, v_ref), (k_hbm, k_ref), (pos_hbm, pos_ref)))
    ]
    for copy in copies:
        copy.start()
    for copy in copies:
        copy.wait()
    for s in range(2):
        rows = slice(s * SPAN, (s + 1) * SPAN)
        out_ref[s, 0:128, :] = k_ref[rows, :]
        out_ref[s, 128:256, :] = v_ref[rows, :].T
        span = (pos_ref[s * SPAN] // SPAN).astype(jnp.float32)
        out_ref[s, 256:PACK, :] = jnp.full((16, 128), span, jnp.float32).astype(jnp.bfloat16)


def query_tile(q_ref, chunk, s, quad):
    pieces = []
    for h in range(quad * QUAD, (quad + 1) * QUAD):
        for t in range(4):
            row = s * SPAN + t * 32 + chunk * PIECE
            pieces.append(q_ref[row:row + PIECE, h * HD:(h + 1) * HD])
    return jnp.concatenate(pieces, axis=0)


def scores_of(kt, q):
    return lax.dot_general(kt, q, (((1,), (1,)), ((), ())), preferred_element_type=jnp.float32)


def weighted(vt, probs):
    return jnp.dot(vt, probs, preferred_element_type=jnp.float32)


def store_keys(kv_ref, blocks):
    for i, (ref, j) in enumerate(blocks):
        kv_ref[i, 0:256, :] = ref[j, 0:256, :]
        kv_ref[i, 256:PACK, :] = jnp.ones((16, 128), jnp.bfloat16)
    kv_ref[len(blocks)] = jnp.zeros((PACK, 128), jnp.bfloat16)


def span_id(ref, i):
    return jnp.max(ref[i, 256:PACK, :].astype(jnp.float32)).astype(jnp.int32)


def visible_list(list_ref, ids, limit):
    count = jnp.int32(0)
    for i, span in enumerate(ids):
        list_ref[count] = jnp.int32(i)
        count = count + jnp.where(span < limit, 1, 0)
    for i in range(GROUP):
        list_ref[count + i] = jnp.int32(len(ids))
    return count


def fast_walk(kv_ref, list_ref, count, queries, units, m_ref, peak_ref, acc_ref, probs):
    shifts = [m_ref[u][0:1, :] for u in units]

    def score(g, p_ref):
        slots = [list_ref[g * GROUP + i] for i in range(GROUP)]
        kt = jnp.concatenate([kv_ref[i, 0:128, :] for i in slots], axis=0)
        for n, u in enumerate(units):
            scores = scores_of(kt, queries[n])
            tiles = scores.reshape(GROUP * SPAN // 8, 8, 256)
            peak_ref[u] = jnp.maximum(peak_ref[u], jnp.max(tiles, axis=0))
            p_ref[n] = jnp.exp2((scores - shifts[n]) * LOG_SCALE).astype(jnp.bfloat16)

    def add(g, p_ref):
        slots = [list_ref[g * GROUP + i] for i in range(GROUP)]
        vt = jnp.concatenate([kv_ref[i, 128:PACK, :] for i in slots], axis=1)
        for n, u in enumerate(units):
            acc_ref[u] = acc_ref[u] + weighted(vt, p_ref[n])

    even, odd = probs
    groups = jnp.maximum((count + GROUP - 1) // GROUP, 1)
    score(0, even)

    def pair(i, carry):
        score(2 * i + 1, odd)
        add(2 * i, even)
        score(2 * i + 2, even)
        add(2 * i + 1, odd)
        return carry

    lax.fori_loop(0, (groups - 1) // 2, pair, 0)

    @pl.when(groups % 2 == 1)
    def _():
        add(groups - 1, even)

    @pl.when(groups % 2 == 0)
    def _():
        score(groups - 1, odd)
        add(groups - 2, even)
        add(groups - 1, odd)


def slow_walk(kv_ref, list_ref, count, queries, units, m_ref, acc_ref):
    def step(i, carry):
        slot = list_ref[i]
        for n, u in enumerate(units):
            scores = scores_of(kv_ref[slot, 0:128, :], queries[n])
            m_old = m_ref[u][0:1, :]
            m_new = jnp.maximum(m_old, jnp.max(scores, axis=0, keepdims=True))
            probs = jnp.exp2((scores - m_new) * LOG_SCALE).astype(jnp.bfloat16)
            scale = jnp.exp2((m_old - m_new) * LOG_SCALE)
            acc_ref[u] = acc_ref[u] * scale + weighted(kv_ref[slot, 128:PACK, :], probs)
            m_ref[u] = jnp.broadcast_to(m_new, (8, 256))
        return carry

    lax.fori_loop(0, count, step, 0)


def overshoot(peak_ref, m_ref, units):
    worst = peak_ref[units[0]] - m_ref[units[0]]
    for u in units[1:]:
        worst = jnp.maximum(worst, peak_ref[u] - m_ref[u])
    return jnp.max(worst) * LOG_SCALE > HEADROOM


def first_kernel(q_hbm, w_hbm, own_ref, x1, x2, x3, y1, y2, y3, m_ref, acc_ref, tile_ref, w_ref,
                 q_ref, kv_ref, peak_ref, even_ref, odd_ref, list0, list1, sems):
    fetch_q = pltpu.make_async_copy(q_hbm, q_ref, sems.at[NW])
    fetch_q.start()
    fetch_w = []
    for j in range(NW):
        rows = pl.ds(j * (1024 // NW), 1024 // NW)
        fetch_w.append(pltpu.make_async_copy(w_hbm.at[rows], w_ref.at[rows], sems.at[j]))
        fetch_w[j].start()
    blocks = [(ref, j) for ref in (own_ref, x1, x2, x3, y1, y2, y3) for j in range(2)]
    store_keys(kv_ref, blocks)
    ids = [span_id(ref, j) for ref, j in blocks]
    counts = [visible_list(ref, ids, ids[s]) for s, ref in enumerate((list0, list1))]
    lists = (list0, list1)
    fetch_q.wait()
    for chunk in range(2):
        for s in range(2):
            for quad in range(2):
                tile_ref[chunk * 4 + s * 2 + quad] = query_tile(q_ref, chunk, s, quad)
    units = [[chunk * 4 + s * 2 + quad for chunk in range(2) for quad in range(2)] for s in range(2)]
    queries = [[tile_ref[u] for u in units[s]] for s in range(2)]

    def own_block():
        for s in range(2):
            for n, u in enumerate(units[s]):
                lane = lax.broadcasted_iota(jnp.int32, (SPAN, 256), 1) % 64
                row = (lane // PIECE) * 32 + lane % PIECE + (n // 2) * PIECE
                scores = scores_of(kv_ref[s, 0:128, :], queries[s][n])
                key = lax.broadcasted_iota(jnp.int32, (SPAN, 256), 0)
                scores = jnp.where(key <= row, scores, NEG)
                m_new = jnp.max(scores, axis=0, keepdims=True)
                probs = jnp.exp2((scores - m_new) * LOG_SCALE).astype(jnp.bfloat16)
                acc_ref[u] = weighted(kv_ref[s, 128:PACK, :], probs)
                m_ref[u] = jnp.broadcast_to(m_new, (8, 256))

    own_block()
    peak_ref[...] = m_ref[...]
    for s in range(2):
        fast_walk(kv_ref, lists[s], counts[s], queries[s], units[s], m_ref, peak_ref, acc_ref,
                  (even_ref, odd_ref))

    @pl.when(overshoot(peak_ref, m_ref, units[0] + units[1]))
    def _():
        own_block()
        for s in range(2):
            slow_walk(kv_ref, lists[s], counts[s], queries[s], units[s], m_ref, acc_ref)

    for copy in fetch_w:
        copy.wait()


def rest_of_attention(chunk, spans, tile_ref, own_ref, far, m_in, acc_in, kv_ref, m_ref, peak_ref,
                      acc_ref, even_ref, odd_ref, lists):
    blocks = [(ref, j) for ref in far for j in range(3)]
    store_keys(kv_ref, blocks)
    ids = [span_id(ref, j) for ref, j in blocks]
    counts = [visible_list(lists[n], ids, span_id(own_ref, s)) for n, s in enumerate(spans)]
    queries = [[tile_ref[chunk * 4 + s * 2 + quad] for quad in range(2)] for s in spans]
    units = [(2 * n, 2 * n + 1) for n in range(len(spans))]

    def reset():
        for n, s in enumerate(spans):
            for quad in range(2):
                m_ref[2 * n + quad] = m_in[chunk * 4 + s * 2 + quad]
                acc_ref[2 * n + quad] = acc_in[chunk * 4 + s * 2 + quad]

    reset()
    peak_ref[...] = m_ref[...]
    for n in range(len(spans)):
        fast_walk(kv_ref, lists[n], counts[n], queries[n], units[n], m_ref, peak_ref, acc_ref,
                  (even_ref, odd_ref))

    @pl.when(overshoot(peak_ref, m_ref, range(2 * len(spans))))
    def _():
        reset()
        for n in range(len(spans)):
            slow_walk(kv_ref, lists[n], counts[n], queries[n], units[n], m_ref, acc_ref)


def finish(s, acc_ref, base, place_ref, merged_ref):
    for quad in range(2):
        acc = acc_ref[base + quad]
        o = acc[:128] * (1.0 / acc[128:129])
        for half in range(2):
            rows = o[:, half * 128:(half + 1) * 128].T.astype(jnp.bfloat16)
            for i in range(2):
                h = quad * QUAD + half * 2 + i
                for t in range(4):
                    where = pl.multiple_of(place_ref[s * 4 + t] * PIECE, PIECE)
                    at = i * 64 + t * PIECE
                    merged_ref[pl.ds(where, PIECE), h * HD:(h + 1) * HD] = rows[at:at + PIECE]


def project(merged_ref, w_ref, keep_ref, send_ref):
    cols = DOUT // NCOL
    for j in range(NCOL):
        at = slice(j * cols, (j + 1) * cols)
        part = jnp.dot(merged_ref[...], w_ref[:, at], preferred_element_type=jnp.float32)
        part = part.astype(jnp.bfloat16)
        keep_ref[:, at] = part[:64]
        send_ref[:, at] = part[64:]


def middle_kernel(chunk, spans, tile_ref, own_ref, a1, a2, a3, b1, b2, b3, m_in, acc_in, acc_ref,
                  kv_ref, m_ref, peak_ref, even_ref, odd_ref, list0, list1):
    rest_of_attention(chunk, spans, tile_ref, own_ref, (a1, a2, a3, b1, b2, b3), m_in, acc_in, kv_ref,
                      m_ref, peak_ref, acc_ref, even_ref, odd_ref, (list0, list1))


def last_kernel(chunk, spans, done, place_ref, tile_ref, own_ref, a1, a2, a3, b1, b2, b3, m_in, acc_in,
                w_ref, *refs):
    acc_done = refs[0] if done else None
    (keep_ref, send_ref, acc_ref, merged_ref, kv_ref, m_ref, peak_ref, even_ref, odd_ref,
     list0, list1) = refs[-11:]
    rest_of_attention(chunk, spans, tile_ref, own_ref, (a1, a2, a3, b1, b2, b3), m_in, acc_in, kv_ref,
                      m_ref, peak_ref, acc_ref, even_ref, odd_ref, (list0, list1))
    for n, s in enumerate(spans):
        finish(s, acc_ref, 2 * n, place_ref, merged_ref)
    for n, s in enumerate(done):
        finish(s, acc_done, 2 * n, place_ref, merged_ref)
    project(merged_ref, w_ref, keep_ref, send_ref)


def pair_kernel(keep_ref, got_ref, *out_refs):
    total = keep_ref[...].astype(jnp.float32) + got_ref[...].astype(jnp.float32)
    for d in range(NZ):
        out_refs[d][...] = total[d * PIECE:(d + 1) * PIECE].astype(jnp.bfloat16)


def final_kernel(*refs):
    out_ref = refs[-1]
    for chunk in range(2):
        parts = [r[...].astype(jnp.float32) for r in refs[chunk * NZ:(chunk + 1) * NZ]]
        total = (parts[0] + parts[1]) + (parts[2] + parts[3])
        out_ref[chunk * PIECE:(chunk + 1) * PIECE, :] = total.astype(jnp.bfloat16)


def in_hbm(array):
    return pltpu.with_memory_space_constraint(array, pltpu.HBM)


def params(mib):
    return pltpu.CompilerParams(vmem_limit_bytes=mib << 20)


def estimate(flops, traffic):
    return pl.CostEstimate(flops=flops, bytes_accessed=traffic, transcendentals=0)


def ctx_route(dx, dy):
    return [
        (x * NX + y, ((x + dx) % NX) * NX + (y + dy) % NX)
        for x in range(NX) for y in range(NX)
    ]


def tp_route(dz, swap):
    return [
        (z * NCORE + c, ((z + dz) % NZ) * NCORE + (c ^ swap))
        for z in range(NZ) for c in range(NCORE)
    ]


def on_device(queries, keys, values, positions, out_weight):
    bf16, f32 = jnp.bfloat16, jnp.float32
    t = lax.axis_index("tp")
    z, core = t // NCORE, t % NCORE
    owners = jnp.arange(NZ * NCORE, dtype=jnp.int32)
    places = ((owners % NCORE) ^ core) * NZ + (owners // NCORE - z) % NZ

    own = pl.pallas_call(
        pack_kernel, in_specs=[HBM] * 3, out_specs=VMEM,
        out_shape=struct((2, PACK, 128), bf16), name="pack", compiler_params=params(2),
        scratch_shapes=[
            pltpu.SMEM((2 * SPAN,), jnp.int32), pltpu.VMEM((2 * SPAN, HD), bf16),
            pltpu.VMEM((2 * SPAN, HD), bf16), pltpu.SemaphoreType.DMA((3,)),
        ],
    )(in_hbm(positions), in_hbm(keys), in_hbm(values))

    def shift(block, dx, dy):
        return lax.ppermute(block, "ctx", ctx_route(dx, dy))

    xs = [shift(own, d, 0) for d in (1, 3, 2)]
    ys = [shift(own, 0, d) for d in (1, 3, 2)]
    row = jnp.stack([b[0] for b in xs])
    col = jnp.stack([b[1] for b in ys])
    far = [shift(row, 0, d) for d in (1, 3, 2)] + [shift(col, d, 0) for d in (1, 3, 2)]

    def walk_scratch(slots, units, width):
        return [
            pltpu.VMEM((slots + 1, PACK, 128), bf16),
            pltpu.VMEM((units, 8, 256), f32),
            pltpu.VMEM((units, 8, 256), f32),
            pltpu.VMEM((width, GROUP * SPAN, 256), bf16),
            pltpu.VMEM((width, GROUP * SPAN, 256), bf16),
            pltpu.SMEM((32,), jnp.int32),
            pltpu.SMEM((32,), jnp.int32),
        ]

    scratch = walk_scratch(14, 8, 4)
    maxima, acc, tiles, weight = pl.pallas_call(
        first_kernel, in_specs=[HBM] * 2 + [VMEM] * 7, out_specs=[VMEM] * 4,
        out_shape=[
            struct((8, 8, 256), f32), struct((8, 144, 256), f32),
            struct((8, 256, 128), bf16), struct((1024, DOUT), bf16),
        ],
        scratch_shapes=[pltpu.VMEM((256, 1024), bf16)] + scratch[:1] + scratch[2:]
        + [pltpu.SemaphoreType.DMA((NW + 1,))],
        compiler_params=params(14), name="first",
        cost_estimate=estimate(4 * 10 ** 9, 1 << 20),
    )(in_hbm(queries), in_hbm(out_weight), own, *xs, *ys)

    def middle(chunk, spans, acc):
        n = 2 * len(spans)
        return pl.pallas_call(
            functools.partial(middle_kernel, chunk, spans),
            in_specs=[VMEM] * 10, out_specs=VMEM, out_shape=struct((n, 144, 256), f32),
            scratch_shapes=walk_scratch(18, n, 2),
            compiler_params=params(14), name="middle",
            cost_estimate=estimate(2 * 10 ** 9, 1 << 20),
        )(tiles, own, *far, maxima, acc)

    def last(chunk, spans, acc, done=(), acc_done=()):
        n = 2 * len(spans)
        return pl.pallas_call(
            functools.partial(last_kernel, chunk, spans, done),
            in_specs=[SMEM] + [VMEM] * (11 + len(acc_done)),
            out_specs=[VMEM, VMEM],
            out_shape=[struct((64, DOUT), bf16), struct((64, DOUT), bf16)],
            scratch_shapes=[
                pltpu.VMEM((n, 144, 256), f32), pltpu.VMEM((128, 1024), bf16),
            ] + walk_scratch(18, n, 2),
            compiler_params=params(14),
            cost_estimate=estimate(5 * 10 ** 9, 1 << 20),
        )(places, tiles, own, *far, maxima, acc, weight, *acc_done)

    def pair_sum(keep, got):
        return pl.pallas_call(
            pair_kernel, in_specs=[VMEM, VMEM], out_specs=[VMEM] * NZ,
            out_shape=[struct((PIECE, DOUT), bf16)] * NZ, name="pair",
            compiler_params=params(6),
        )(keep, got)

    def swap(block):
        return lax.ppermute(block, "tp", tp_route(0, 1))

    def exchange(parts):
        return [parts[0]] + [lax.ppermute(parts[d], "tp", tp_route(d, 0)) for d in (1, 3, 2)]

    keep0, send0 = last(0, (0, 1), acc)
    send0, acc1 = lax.optimization_barrier((send0, acc))
    got0 = swap(send0)
    acc_mid = middle(1, (0,), acc1)
    keep0, acc_mid = lax.optimization_barrier((keep0, acc_mid))
    parts0 = pair_sum(keep0, got0)
    *parts0, acc2 = lax.optimization_barrier((*parts0, acc))
    pieces0 = exchange(parts0)
    keep1, send1 = last(1, (1,), acc2, (0,), (acc_mid,))
    pieces1 = exchange(pair_sum(keep1, swap(send1)))
    return pl.pallas_call(
        final_kernel, in_specs=[VMEM] * (2 * NZ), out_specs=VMEM,
        out_shape=struct((2 * PIECE, DOUT), bf16), name="final", compiler_params=params(6),
    )(*pieces0, *pieces1)


def solution(mesh):
    return jax.shard_map(
        on_device,
        mesh=mesh,
        in_specs=(P("ctx", "tp"), P("ctx", "tp"), P("ctx", "tp"), P("ctx"), P("tp", None)),
        out_specs=P(("ctx", "tp"), None),
        check_vma=False,
    )
```

profile of v0, /device:TPU:6, one launch (start us, length us, event | category | flops | bytes accessed | tf_op | source)
XLA Modules:
  0.0 92.3 jit_solution(16540714078480178204)
XLA Ops:
  1.0 1.6 %collective-permute-start.3 = (bf16[2,272,128]{2,1,0:T(8,128)(2,1)S(1)}, bf16[2,272,128]{2,1,0:T(8,128)(2,1)S(1)}, u32[]{:S(2)}, u32[]{:S(2)}) collective-permute-start(bf16[2,272,128]{2,1,0:T(8,128)(2,1)S(1)} %pack.1.own_ref), channel_id=1, source_target_pairs={{0,8},{8,16},{16,24},{24,0},{32,40},{40,48},{48,56},{56,32},{64,72... | collective-permute-start | bytes 417800 | tf_op jit(solution)/shard_map/ppermute | solution.py:338
  2.6 1.7 %collective-permute-start.4 = (bf16[2,272,128]{2,1,0:T(8,128)(2,1)S(1)}, bf16[2,272,128]{2,1,0:T(8,128)(2,1)S(1)}, u32[]{:S(2)}, u32[]{:S(2)}) collective-permute-start(bf16[2,272,128]{2,1,0:T(8,128)(2,1)S(1)} %pack.1.own_ref), channel_id=1, source_target_pairs={{0,24},{8,0},{16,8},{24,16},{32,56},{40,32},{48,40},{56,48},{64,88... | collective-permute-start | bytes 417800 | tf_op jit(solution)/shard_map/ppermute | solution.py:338
  4.3 2.0 %collective-permute-start.5 = (bf16[2,272,128]{2,1,0:T(8,128)(2,1)S(1)}, bf16[2,272,128]{2,1,0:T(8,128)(2,1)S(1)}, u32[]{:S(2)}, u32[]{:S(2)}) collective-permute-start(bf16[2,272,128]{2,1,0:T(8,128)(2,1)S(1)} %pack.1.own_ref), channel_id=1, source_target_pairs={{0,16},{8,24},{16,0},{24,8},{32,48},{40,56},{48,32},{56,40},{64,80... | collective-permute-start | bytes 417800 | tf_op jit(solution)/shard_map/ppermute | solution.py:338
  6.8 1.5 %collective-permute-start.1 = (bf16[2,272,128]{2,1,0:T(8,128)(2,1)S(1)}, bf16[2,272,128]{2,1,0:T(8,128)(2,1)S(1)}, u32[]{:S(2)}, u32[]{:S(2)}) collective-permute-start(bf16[2,272,128]{2,1,0:T(8,128)(2,1)S(1)} %pack.1.own_ref), channel_id=1, source_target_pairs={{0,96},{8,104},{16,112},{24,120},{32,0},{40,8},{48,16},{56,24},{64... | collective-permute-start | bytes 417800 | tf_op jit(solution)/shard_map/ppermute | solution.py:338
  8.3 1.4 %collective-permute-start.2 = (bf16[2,272,128]{2,1,0:T(8,128)(2,1)S(1)}, bf16[2,272,128]{2,1,0:T(8,128)(2,1)S(1)}, u32[]{:S(2)}, u32[]{:S(2)}) collective-permute-start(bf16[2,272,128]{2,1,0:T(8,128)(2,1)S(1)} %pack.1.own_ref), channel_id=1, source_target_pairs={{0,64},{8,72},{16,80},{24,88},{32,96},{40,104},{48,112},{56,120},{... | collective-permute-start | bytes 417800 | tf_op jit(solution)/shard_map/ppermute | solution.py:338
  10.1 1.8 %collective-permute-done.5.y3 = bf16[2,272,128]{2,1,0:T(8,128)(2,1)S(1)} collective-permute-done((bf16[2,272,128]{2,1,0:T(8,128)(2,1)S(1)}, bf16[2,272,128]{2,1,0:T(8,128)(2,1)S(1)}, u32[]{:S(2)}, u32[]{:S(2)}) %collective-permute-start.5) | collective-permute-done | bytes 139296 | tf_op jit(solution)/shard_map/ppermute | solution.py:338
  12.8 1.2 %collective-permute-start.11 = (bf16[3,272,128]{2,1,0:T(8,128)(2,1)S(1)}, bf16[3,272,128]{2,1,0:T(8,128)(2,1)S(1)}, u32[]{:S(2)}, u32[]{:S(2)}) collective-permute-start(bf16[3,272,128]{2,1,0:T(8,128)(2,1)S(1)} %pad_maximum_fusion.1), channel_id=1, source_target_pairs={{0,64},{8,72},{16,80},{24,88},{32,96},{40,104},{48,112},{56,120},{... | collective-permute-start | bytes 626696 | tf_op jit(solution)/shard_map/ppermute | solution.py:338
  14.1 3.1 %collective-permute-done.2.x3 = bf16[2,272,128]{2,1,0:T(8,128)(2,1)S(1)} collective-permute-done((bf16[2,272,128]{2,1,0:T(8,128)(2,1)S(1)}, bf16[2,272,128]{2,1,0:T(8,128)(2,1)S(1)}, u32[]{:S(2)}, u32[]{:S(2)}) %collective-permute-start.2) | collective-permute-done | bytes 139296 | tf_op jit(solution)/shard_map/ppermute | solution.py:338
  17.7 2.8 %collective-permute-start.7 = (bf16[3,272,128]{2,1,0:T(8,128)(2,1)S(1)}, bf16[3,272,128]{2,1,0:T(8,128)(2,1)S(1)}, u32[]{:S(2)}, u32[]{:S(2)}) collective-permute-start(bf16[3,272,128]{2,1,0:T(8,128)(2,1)S(1)} %pad_maximum_fusion), channel_id=1, source_target_pairs={{0,24},{8,0},{16,8},{24,16},{32,56},{40,32},{48,40},{56,48},{64,88... | collective-permute-start | bytes 626696 | tf_op jit(solution)/shard_map/ppermute | solution.py:338
  20.9 4.1 %collective-permute-done.10.b2 = bf16[3,272,128]{2,1,0:T(8,128)(2,1)S(1)} collective-permute-done((bf16[3,272,128]{2,1,0:T(8,128)(2,1)S(1)}, bf16[3,272,128]{2,1,0:T(8,128)(2,1)S(1)}, u32[]{:S(2)}, u32[]{:S(2)}) %collective-permute-start.10) | collective-permute-done | bytes 208928 | tf_op jit(solution)/shard_map/ppermute | solution.py:338
  25.0 22.3 %first.1 = (f32[8,8,256]{2,1,0:T(8,128)S(1)}, f32[8,144,256]{2,1,0:T(8,128)S(1)}, bf16[8,256,128]{2,1,0:T(8,128)(2,1)S(1)}, bf16[1024,8192]{1,0:T(8,128)(2,1)S(1)}) custom-call(bf16[256,1024]{1,0:T(8,128)(2,1)} %q_hbm.1, bf16[1024,8192]{1,0:T(8,128)(2,1)} %w_hbm.1, bf16[2,272,128]{2,1,0:T(8,128)(2,1)S(1)} %pack.1.own_ref, ...), custom_call_target="tpu_custom_call" | custom-call | flops 4000000000 | bytes 1048576 | tf_op jit(solution)/shard_map/first/pallas_call | solution.py:358
  47.3 6.9 %shard_map.55 = (bf16[64,8192]{1,0:T(8,128)(2,1)S(1)}, bf16[64,8192]{1,0:T(8,128)(2,1)S(1)}) custom-call(s32[8]{0:T(128)S(1)} %fusion.place_ref, bf16[8,256,128]{2,1,0:T(8,128)(2,1)S(1)} %get-tuple-element.30.tile_ref, bf16[2,272,128]{2,1,0:T(8,128)(2,1)S(1)} %pack.1.own_ref, bf16[3,272,128]{2,1,0:T(8,128)(2,1)S(1)} %collective-permute-done.6.a1, ...), custom_call_target="tpu_custom_call" | custom-call | flops 5000000000 | bytes 1048576 | tf_op jit(solution)/shard_map/pallas_call | solution.py:382
  54.3 2.1 %middle.1.refs_0_ = f32[2,144,256]{2,1,0:T(8,128)S(1)} custom-call(bf16[8,256,128]{2,1,0:T(8,128)(2,1)S(1)} %get-tuple-element.30.tile_ref, bf16[2,272,128]{2,1,0:T(8,128)(2,1)S(1)} %pack.1.own_ref, bf16[3,272,128]{2,1,0:T(8,128)(2,1)S(1)} %collective-permute-done.6.a1, bf16[3,272,128]{2,1,0:T(8,128)(2,1)S(1)} %collective-permute-done.7.a2, ...), custom_call_target="tpu_custom_call" | custom-call | flops 2000000000 | bytes 1048576 | tf_op jit(solution)/shard_map/middle/pallas_call | solution.py:372
  57.2 4.8 %shard_map.56 = (bf16[64,8192]{1,0:T(8,128)(2,1)S(1)}, bf16[64,8192]{1,0:T(8,128)(2,1)S(1)}) custom-call(s32[8]{0:T(128)S(1)} %fusion.place_ref, bf16[8,256,128]{2,1,0:T(8,128)(2,1)S(1)} %get-tuple-element.30.tile_ref, bf16[2,272,128]{2,1,0:T(8,128)(2,1)S(1)} %pack.1.own_ref, bf16[3,272,128]{2,1,0:T(8,128)(2,1)S(1)} %collective-permute-done.6.a1, ...), custom_call_target="tpu_custom_call" | custom-call | flops 5000000000 | bytes 1048576 | tf_op jit(solution)/shard_map/pallas_call | solution.py:382
  62.2 1.9 %collective-permute-start.13 = (bf16[16,8192]{1,0:T(8,128)(2,1)S(1)}, bf16[16,8192]{1,0:T(8,128)(2,1)S(1)}, u32[]{:S(2)}, u32[]{:S(2)}) collective-permute-start(bf16[16,8192]{1,0:T(8,128)(2,1)S(1)} %get-tuple-element.44), channel_id=1, source_target_pairs={{0,2},{1,3},{2,4},{3,5},{4,6},{5,7},{6,0},{7,1},{8,10},{9,11},{10,... | collective-permute-start | bytes 786440 | tf_op jit(solution)/shard_map/ppermute | solution.py:405
  64.2 2.2 %collective-permute-start.14 = (bf16[16,8192]{1,0:T(8,128)(2,1)S(1)}, bf16[16,8192]{1,0:T(8,128)(2,1)S(1)}, u32[]{:S(2)}, u32[]{:S(2)}) collective-permute-start(bf16[16,8192]{1,0:T(8,128)(2,1)S(1)} %get-tuple-element.45), channel_id=1, source_target_pairs={{0,6},{1,7},{2,0},{3,1},{4,2},{5,3},{6,4},{7,5},{8,14},{9,15},{10,... | collective-permute-start | bytes 786440 | tf_op jit(solution)/shard_map/ppermute | solution.py:405
  66.3 1.8 %collective-permute-start.15 = (bf16[16,8192]{1,0:T(8,128)(2,1)S(1)}, bf16[16,8192]{1,0:T(8,128)(2,1)S(1)}, u32[]{:S(2)}, u32[]{:S(2)}) collective-permute-start(bf16[16,8192]{1,0:T(8,128)(2,1)S(1)} %get-tuple-element.46), channel_id=1, source_target_pairs={{0,4},{1,5},{2,6},{3,7},{4,0},{5,1},{6,2},{7,3},{8,12},{9,13},{10,... | collective-permute-start | bytes 786440 | tf_op jit(solution)/shard_map/ppermute | solution.py:405
  68.4 1.1 %collective-permute-start.17 = (bf16[16,8192]{1,0:T(8,128)(2,1)S(1)}, bf16[16,8192]{1,0:T(8,128)(2,1)S(1)}, u32[]{:S(2)}, u32[]{:S(2)}) collective-permute-start(bf16[16,8192]{1,0:T(8,128)(2,1)S(1)} %get-tuple-element.52), channel_id=1, source_target_pairs={{0,2},{1,3},{2,4},{3,5},{4,6},{5,7},{6,0},{7,1},{8,10},{9,11},{10,... | collective-permute-start | bytes 786440 | tf_op jit(solution)/shard_map/ppermute | solution.py:405
  69.5 2.2 %collective-permute-start.18 = (bf16[16,8192]{1,0:T(8,128)(2,1)S(1)}, bf16[16,8192]{1,0:T(8,128)(2,1)S(1)}, u32[]{:S(2)}, u32[]{:S(2)}) collective-permute-start(bf16[16,8192]{1,0:T(8,128)(2,1)S(1)} %get-tuple-element.53), channel_id=1, source_target_pairs={{0,6},{1,7},{2,0},{3,1},{4,2},{5,3},{6,4},{7,5},{8,14},{9,15},{10,... | collective-permute-start | bytes 786440 | tf_op jit(solution)/shard_map/ppermute | solution.py:405
  71.7 1.7 %collective-permute-done.13.refs_1_ = bf16[16,8192]{1,0:T(8,128)(2,1)S(1)} collective-permute-done((bf16[16,8192]{1,0:T(8,128)(2,1)S(1)}, bf16[16,8192]{1,0:T(8,128)(2,1)S(1)}, u32[]{:S(2)}, u32[]{:S(2)}) %collective-permute-start.13) | collective-permute-done | bytes 262176 | tf_op jit(solution)/shard_map/ppermute | solution.py:405
  73.4 7.5 %collective-permute-start.19 = (bf16[16,8192]{1,0:T(8,128)(2,1)S(1)}, bf16[16,8192]{1,0:T(8,128)(2,1)S(1)}, u32[]{:S(2)}, u32[]{:S(2)}) collective-permute-start(bf16[16,8192]{1,0:T(8,128)(2,1)S(1)} %get-tuple-element.54), channel_id=1, source_target_pairs={{0,4},{1,5},{2,6},{3,7},{4,0},{5,1},{6,2},{7,3},{8,12},{9,13},{10,... | collective-permute-start | bytes 786440 | tf_op jit(solution)/shard_map/ppermute | solution.py:405
  80.9 3.4 %collective-permute-done.17.refs_5_ = bf16[16,8192]{1,0:T(8,128)(2,1)S(1)} collective-permute-done((bf16[16,8192]{1,0:T(8,128)(2,1)S(1)}, bf16[16,8192]{1,0:T(8,128)(2,1)S(1)}, u32[]{:S(2)}, u32[]{:S(2)}) %collective-permute-start.17) | collective-permute-done | bytes 262176 | tf_op jit(solution)/shard_map/ppermute | solution.py:405
  84.4 4.9 %collective-permute-done.18.refs_6_ = bf16[16,8192]{1,0:T(8,128)(2,1)S(1)} collective-permute-done((bf16[16,8192]{1,0:T(8,128)(2,1)S(1)}, bf16[16,8192]{1,0:T(8,128)(2,1)S(1)}, u32[]{:S(2)}, u32[]{:S(2)}) %collective-permute-start.18) | collective-permute-done | bytes 262176 | tf_op jit(solution)/shard_map/ppermute | solution.py:405
  89.3 1.9 %collective-permute-done.19.refs_7_ = bf16[16,8192]{1,0:T(8,128)(2,1)S(1)} collective-permute-done((bf16[16,8192]{1,0:T(8,128)(2,1)S(1)}, bf16[16,8192]{1,0:T(8,128)(2,1)S(1)}, u32[]{:S(2)}, u32[]{:S(2)}) %collective-permute-start.19) | collective-permute-done | bytes 262176 | tf_op jit(solution)/shard_map/ppermute | solution.py:405
  (33 shorter events, 6.1 us)
Async XLA Ops:
  1.0 7.3 %collective-permute-start.3 = (bf16[2,272,128]{2,1,0:T(8,128)(2,1)S(1)}, bf16[2,272,128]{2,1,0:T(8,128)(2,1)S(1)}, u32[]{:S(2)}, u32[]{:S(2)}) collective-permute-start(bf16[2,272,128]{2,1,0:T(8,128)(2,1)S(1)} %pack.1.own_ref), channel_id=1, source_target_pairs={{0,8},{8,16},{16,24},{24,0},{32,40},{40,48},{48,56},{56,32},{64,72... | collective-permute-start | bytes 417800 | tf_op jit(solution)/shard_map/ppermute | solution.py:338
  2.6 7.5 %collective-permute-start.4 = (bf16[2,272,128]{2,1,0:T(8,128)(2,1)S(1)}, bf16[2,272,128]{2,1,0:T(8,128)(2,1)S(1)}, u32[]{:S(2)}, u32[]{:S(2)}) collective-permute-start(bf16[2,272,128]{2,1,0:T(8,128)(2,1)S(1)} %pack.1.own_ref), channel_id=1, source_target_pairs={{0,24},{8,0},{16,8},{24,16},{32,56},{40,32},{48,40},{56,48},{64,88... | collective-permute-start | bytes 417800 | tf_op jit(solution)/shard_map/ppermute | solution.py:338
  4.3 7.6 %collective-permute-start.5 = (bf16[2,272,128]{2,1,0:T(8,128)(2,1)S(1)}, bf16[2,272,128]{2,1,0:T(8,128)(2,1)S(1)}, u32[]{:S(2)}, u32[]{:S(2)}) collective-permute-start(bf16[2,272,128]{2,1,0:T(8,128)(2,1)S(1)} %pack.1.own_ref), channel_id=1, source_target_pairs={{0,16},{8,24},{16,0},{24,8},{32,48},{40,56},{48,32},{56,40},{64,80... | collective-permute-start | bytes 417800 | tf_op jit(solution)/shard_map/ppermute | solution.py:338
  6.3 7.8 %collective-permute-start = (bf16[2,272,128]{2,1,0:T(8,128)(2,1)S(1)}, bf16[2,272,128]{2,1,0:T(8,128)(2,1)S(1)}, u32[]{:S(2)}, u32[]{:S(2)}) collective-permute-start(bf16[2,272,128]{2,1,0:T(8,128)(2,1)S(1)} %pack.1.own_ref), channel_id=1, source_target_pairs={{0,32},{8,40},{16,48},{24,56},{32,64},{40,72},{48,80},{56,88},{64,... | collective-permute-start | bytes 417800 | tf_op jit(solution)/shard_map/ppermute | solution.py:338
  6.8 7.3 %collective-permute-start.1 = (bf16[2,272,128]{2,1,0:T(8,128)(2,1)S(1)}, bf16[2,272,128]{2,1,0:T(8,128)(2,1)S(1)}, u32[]{:S(2)}, u32[]{:S(2)}) collective-permute-start(bf16[2,272,128]{2,1,0:T(8,128)(2,1)S(1)} %pack.1.own_ref), channel_id=1, source_target_pairs={{0,96},{8,104},{16,112},{24,120},{32,0},{40,8},{48,16},{56,24},{64... | collective-permute-start | bytes 417800 | tf_op jit(solution)/shard_map/ppermute | solution.py:338
  8.3 8.9 %collective-permute-start.2 = (bf16[2,272,128]{2,1,0:T(8,128)(2,1)S(1)}, bf16[2,272,128]{2,1,0:T(8,128)(2,1)S(1)}, u32[]{:S(2)}, u32[]{:S(2)}) collective-permute-start(bf16[2,272,128]{2,1,0:T(8,128)(2,1)S(1)} %pack.1.own_ref), channel_id=1, source_target_pairs={{0,64},{8,72},{16,80},{24,88},{32,96},{40,104},{48,112},{56,120},{... | collective-permute-start | bytes 417800 | tf_op jit(solution)/shard_map/ppermute | solution.py:338
  11.9 13.0 %collective-permute-start.10 = (bf16[3,272,128]{2,1,0:T(8,128)(2,1)S(1)}, bf16[3,272,128]{2,1,0:T(8,128)(2,1)S(1)}, u32[]{:S(2)}, u32[]{:S(2)}) collective-permute-start(bf16[3,272,128]{2,1,0:T(8,128)(2,1)S(1)} %pad_maximum_fusion.1), channel_id=1, source_target_pairs={{0,96},{8,104},{16,112},{24,120},{32,0},{40,8},{48,16},{56,24},{64... | collective-permute-start | bytes 626696 | tf_op jit(solution)/shard_map/ppermute | solution.py:338
  12.8 34.4 %collective-permute-start.11 = (bf16[3,272,128]{2,1,0:T(8,128)(2,1)S(1)}, bf16[3,272,128]{2,1,0:T(8,128)(2,1)S(1)}, u32[]{:S(2)}, u32[]{:S(2)}) collective-permute-start(bf16[3,272,128]{2,1,0:T(8,128)(2,1)S(1)} %pad_maximum_fusion.1), channel_id=1, source_target_pairs={{0,64},{8,72},{16,80},{24,88},{32,96},{40,104},{48,112},{56,120},{... | collective-permute-start | bytes 626696 | tf_op jit(solution)/shard_map/ppermute | solution.py:338
  17.2 30.0 %collective-permute-start.6 = (bf16[3,272,128]{2,1,0:T(8,128)(2,1)S(1)}, bf16[3,272,128]{2,1,0:T(8,128)(2,1)S(1)}, u32[]{:S(2)}, u32[]{:S(2)}) collective-permute-start(bf16[3,272,128]{2,1,0:T(8,128)(2,1)S(1)} %pad_maximum_fusion), channel_id=1, source_target_pairs={{0,8},{8,16},{16,24},{24,0},{32,40},{40,48},{48,56},{56,32},{64,72... | collective-permute-start | bytes 626696 | tf_op jit(solution)/shard_map/ppermute | solution.py:338
  17.7 29.5 %collective-permute-start.7 = (bf16[3,272,128]{2,1,0:T(8,128)(2,1)S(1)}, bf16[3,272,128]{2,1,0:T(8,128)(2,1)S(1)}, u32[]{:S(2)}, u32[]{:S(2)}) collective-permute-start(bf16[3,272,128]{2,1,0:T(8,128)(2,1)S(1)} %pad_maximum_fusion), channel_id=1, source_target_pairs={{0,24},{8,0},{16,8},{24,16},{32,56},{40,32},{48,40},{56,48},{64,88... | collective-permute-start | bytes 626696 | tf_op jit(solution)/shard_map/ppermute | solution.py:338
  20.5 26.7 %collective-permute-start.8 = (bf16[3,272,128]{2,1,0:T(8,128)(2,1)S(1)}, bf16[3,272,128]{2,1,0:T(8,128)(2,1)S(1)}, u32[]{:S(2)}, u32[]{:S(2)}) collective-permute-start(bf16[3,272,128]{2,1,0:T(8,128)(2,1)S(1)} %pad_maximum_fusion), channel_id=1, source_target_pairs={{0,16},{8,24},{16,0},{24,8},{32,48},{40,56},{48,32},{56,40},{64,80... | collective-permute-start | bytes 626696 | tf_op jit(solution)/shard_map/ppermute | solution.py:338
  25.0 22.3 %collective-permute-start.9 = (bf16[3,272,128]{2,1,0:T(8,128)(2,1)S(1)}, bf16[3,272,128]{2,1,0:T(8,128)(2,1)S(1)}, u32[]{:S(2)}, u32[]{:S(2)}) collective-permute-start(bf16[3,272,128]{2,1,0:T(8,128)(2,1)S(1)} %pad_maximum_fusion.1), channel_id=1, source_target_pairs={{0,32},{8,40},{16,48},{24,56},{32,64},{40,72},{48,80},{56,88},{64,... | collective-permute-start | bytes 626696 | tf_op jit(solution)/shard_map/ppermute | solution.py:338
  54.2 2.7 %collective-permute-start.12 = (bf16[64,8192]{1,0:T(8,128)(2,1)S(1)}, bf16[64,8192]{1,0:T(8,128)(2,1)S(1)}, u32[]{:S(2)}, u32[]{:S(2)}) collective-permute-start(bf16[64,8192]{1,0:T(8,128)(2,1)S(1)} %get-tuple-element.38), channel_id=1, source_target_pairs={{0,1},{1,0},{2,3},{3,2},{4,5},{5,4},{6,7},{7,6},{8,9},{9,8},{10,11... | collective-permute-start | bytes 3145736 | tf_op jit(solution)/shard_map/ppermute | solution.py:402
  62.0 6.1 %collective-permute-start.16 = (bf16[64,8192]{1,0:T(8,128)(2,1)S(1)}, bf16[64,8192]{1,0:T(8,128)(2,1)S(1)}, u32[]{:S(2)}, u32[]{:S(2)}) collective-permute-start(bf16[64,8192]{1,0:T(8,128)(2,1)S(1)} %get-tuple-element.50), channel_id=1, source_target_pairs={{0,1},{1,0},{2,3},{3,2},{4,5},{5,4},{6,7},{7,6},{8,9},{9,8},{10,11... | collective-permute-start | bytes 3145736 | tf_op jit(solution)/shard_map/ppermute | solution.py:402
  62.2 11.2 %collective-permute-start.13 = (bf16[16,8192]{1,0:T(8,128)(2,1)S(1)}, bf16[16,8192]{1,0:T(8,128)(2,1)S(1)}, u32[]{:S(2)}, u32[]{:S(2)}) collective-permute-start(bf16[16,8192]{1,0:T(8,128)(2,1)S(1)} %get-tuple-element.44), channel_id=1, source_target_pairs={{0,2},{1,3},{2,4},{3,5},{4,6},{5,7},{6,0},{7,1},{8,10},{9,11},{10,... | collective-permute-start | bytes 786440 | tf_op jit(solution)/shard_map/ppermute | solution.py:405
  64.2 16.8 %collective-permute-start.14 = (bf16[16,8192]{1,0:T(8,128)(2,1)S(1)}, bf16[16,8192]{1,0:T(8,128)(2,1)S(1)}, u32[]{:S(2)}, u32[]{:S(2)}) collective-permute-start(bf16[16,8192]{1,0:T(8,128)(2,1)S(1)} %get-tuple-element.45), channel_id=1, source_target_pairs={{0,6},{1,7},{2,0},{3,1},{4,2},{5,3},{6,4},{7,5},{8,14},{9,15},{10,... | collective-permute-start | bytes 786440 | tf_op jit(solution)/shard_map/ppermute | solution.py:405
  66.3 14.6 %collective-permute-start.15 = (bf16[16,8192]{1,0:T(8,128)(2,1)S(1)}, bf16[16,8192]{1,0:T(8,128)(2,1)S(1)}, u32[]{:S(2)}, u32[]{:S(2)}) collective-permute-start(bf16[16,8192]{1,0:T(8,128)(2,1)S(1)} %get-tuple-element.46), channel_id=1, source_target_pairs={{0,4},{1,5},{2,6},{3,7},{4,0},{5,1},{6,2},{7,3},{8,12},{9,13},{10,... | collective-permute-start | bytes 786440 | tf_op jit(solution)/shard_map/ppermute | solution.py:405
  68.4 16.0 %collective-permute-start.17 = (bf16[16,8192]{1,0:T(8,128)(2,1)S(1)}, bf16[16,8192]{1,0:T(8,128)(2,1)S(1)}, u32[]{:S(2)}, u32[]{:S(2)}) collective-permute-start(bf16[16,8192]{1,0:T(8,128)(2,1)S(1)} %get-tuple-element.52), channel_id=1, source_target_pairs={{0,2},{1,3},{2,4},{3,5},{4,6},{5,7},{6,0},{7,1},{8,10},{9,11},{10,... | collective-permute-start | bytes 786440 | tf_op jit(solution)/shard_map/ppermute | solution.py:405
  69.5 19.8 %collective-permute-start.18 = (bf16[16,8192]{1,0:T(8,128)(2,1)S(1)}, bf16[16,8192]{1,0:T(8,128)(2,1)S(1)}, u32[]{:S(2)}, u32[]{:S(2)}) collective-permute-start(bf16[16,8192]{1,0:T(8,128)(2,1)S(1)} %get-tuple-element.53), channel_id=1, source_target_pairs={{0,6},{1,7},{2,0},{3,1},{4,2},{5,3},{6,4},{7,5},{8,14},{9,15},{10,... | collective-permute-start | bytes 786440 | tf_op jit(solution)/shard_map/ppermute | solution.py:405
  73.4 17.8 %collective-permute-start.19 = (bf16[16,8192]{1,0:T(8,128)(2,1)S(1)}, bf16[16,8192]{1,0:T(8,128)(2,1)S(1)}, u32[]{:S(2)}, u32[]{:S(2)}) collective-permute-start(bf16[16,8192]{1,0:T(8,128)(2,1)S(1)} %get-tuple-element.54), channel_id=1, source_target_pairs={{0,4},{1,5},{2,6},{3,7},{4,0},{5,1},{6,2},{7,3},{8,12},{9,13},{10,... | collective-permute-start | bytes 786440 | tf_op jit(solution)/shard_map/ppermute | solution.py:405
where the time goes:
time: 92.4 us; the launch traced here: 92.3 us
  Pallas kernels  38.6 us (42%)
  starting transfers between devices  31.5 us (34%)
  waiting for transfers between devices  22 us (24%)
    pallas_call x1, Pallas kernels, on_device(): pl.pallas_call(first_kernel, in_specs=[HBM] * 2 + [VMEM] * 7, out_specs=[...  22.3 us
    ppermute x6, starting transfers between devices, exchange(): lax.ppermute(parts[d], 'tp', tp_route(d, 0))  16.7 us
    ppermute x12, starting transfers between devices, shift(): return lax.ppermute(block, 'ctx', ctx_route(dx, dy))  14.5 us
    ppermute x6, waiting for transfers between devices, exchange(): lax.ppermute(parts[d], 'tp', tp_route(d, 0))  12 us
    pallas_call x2, Pallas kernels, last(): pl.pallas_call(functools.partial(last_kernel, chunk, spans, done), in_spe...  11.8 us
    ppermute x12, waiting for transfers between devices, shift(): return lax.ppermute(block, 'ctx', ctx_route(dx, dy))  9.38 us
    pallas_call x1, Pallas kernels, middle(): pl.pallas_call(functools.partial(middle_kernel, chunk, spans), in_specs=[...  2.07 us
  transfers between devices with their start and end apart: 20, of which 9 were waited for; matrix products, arithmetic and copies ran while one was open for 0% of the time, Pallas kernels for 27%

commit v1 on v0

--- a/solution.py
+++ b/solution.py
@@ -35,7 +35,10 @@
     return jax.ShapeDtypeStruct(shape, dtype)
 
 
-def pack_kernel(pos_hbm, k_hbm, v_hbm, out_ref, pos_ref, k_ref, v_ref, sems):
+def pack_kernel(index_ref, pos_hbm, k_hbm, v_hbm, out_ref, mine_ref, give_ref, pos_ref, k_ref, v_ref,
+                sems):
+    core = index_ref[0] % NCORE
+
     copies = [
         pltpu.make_async_copy(src, dst, sems.at[i])
         for i, (src, dst) in enumerate(((v_hbm, v_ref), (k_hbm, k_ref), (pos_hbm, pos_ref)))
@@ -46,10 +49,14 @@
         copy.wait()
     for s in range(2):
         rows = slice(s * SPAN, (s + 1) * SPAN)
-        out_ref[s, 0:128, :] = k_ref[rows, :]
-        out_ref[s, 128:256, :] = v_ref[rows, :].T
         span = (pos_ref[s * SPAN] // SPAN).astype(jnp.float32)
-        out_ref[s, 256:PACK, :] = jnp.full((16, 128), span, jnp.float32).astype(jnp.bfloat16)
+        ids = jnp.full((16, 128), span, jnp.float32).astype(jnp.bfloat16)
+        vt = v_ref[rows, :].T
+        for ref, i in ((out_ref, s), (mine_ref, core ^ s), (give_ref, 1 - (core ^ s))):
+            base = pl.multiple_of(i * PACK, 16)
+            ref[pl.ds(base, 128), :] = k_ref[rows, :]
+            ref[pl.ds(base + 128, 128), :] = vt
+            ref[pl.ds(base + 256, 16), :] = ids
 
 
 def query_tile(q_ref, chunk, s, quad):
@@ -71,13 +78,14 @@
 
 def store_keys(kv_ref, blocks):
     for i, (ref, j) in enumerate(blocks):
-        kv_ref[i, 0:256, :] = ref[j, 0:256, :]
+        kv_ref[i, 0:256, :] = ref[j * PACK:j * PACK + 256, :]
         kv_ref[i, 256:PACK, :] = jnp.ones((16, 128), jnp.bfloat16)
     kv_ref[len(blocks)] = jnp.zeros((PACK, 128), jnp.bfloat16)
 
 
 def span_id(ref, i):
-    return jnp.max(ref[i, 256:PACK, :].astype(jnp.float32)).astype(jnp.int32)
+    ids = ref[i * PACK + 256:(i + 1) * PACK, :].astype(jnp.float32)
+    return jnp.max(ids).astype(jnp.int32)
 
 
 def visible_list(list_ref, ids, limit):
@@ -155,7 +163,7 @@
     return jnp.max(worst) * LOG_SCALE > HEADROOM
 
 
-def first_kernel(q_hbm, w_hbm, own_ref, x1, x2, x3, y1, y2, y3, m_ref, acc_ref, tile_ref, w_ref,
+def first_kernel(q_hbm, w_hbm, own_ref, n1, n2, n3, other, m_ref, acc_ref, tile_ref, w_ref,
                  q_ref, kv_ref, peak_ref, even_ref, odd_ref, list0, list1, sems):
     fetch_q = pltpu.make_async_copy(q_hbm, q_ref, sems.at[NW])
     fetch_q.start()
@@ -164,7 +172,9 @@
         rows = pl.ds(j * (1024 // NW), 1024 // NW)
         fetch_w.append(pltpu.make_async_copy(w_hbm.at[rows], w_ref.at[rows], sems.at[j]))
         fetch_w[j].start()
-    blocks = [(ref, j) for ref in (own_ref, x1, x2, x3, y1, y2, y3) for j in range(2)]
+    blocks = [(own_ref, j) for j in range(2)]
+    blocks += [(ref, j) for ref in (n1, n2, n3) for j in (0, 2)]
+    blocks += [(other, j) for j in range(6)]
     store_keys(kv_ref, blocks)
     ids = [span_id(ref, j) for ref, j in blocks]
     counts = [visible_list(ref, ids, ids[s]) for s, ref in enumerate((list0, list1))]
@@ -234,7 +244,8 @@
             slow_walk(kv_ref, lists[n], counts[n], queries[n], units[n], m_ref, acc_ref)
 
 
-def finish(s, acc_ref, base, place_ref, merged_ref):
+def finish(s, acc_ref, base, index_ref, merged_ref):
+    z, core = index_ref[0] // NCORE, index_ref[0] % NCORE
     for quad in range(2):
         acc = acc_ref[base + quad]
         o = acc[:128] * (1.0 / acc[128:129])
@@ -243,7 +254,9 @@
             for i in range(2):
                 h = quad * QUAD + half * 2 + i
                 for t in range(4):
-                    where = pl.multiple_of(place_ref[s * 4 + t] * PIECE, PIECE)
+                    owner = s * 4 + t
+                    place = ((owner % NCORE) ^ core) * NZ + (owner // NCORE - z + NZ) % NZ
+                    where = pl.multiple_of(place * PIECE, PIECE)
                     at = i * 64 + t * PIECE
                     merged_ref[pl.ds(where, PIECE), h * HD:(h + 1) * HD] = rows[at:at + PIECE]
 
@@ -258,23 +271,23 @@
         send_ref[:, at] = part[64:]
 
 
-def middle_kernel(chunk, spans, tile_ref, own_ref, a1, a2, a3, b1, b2, b3, m_in, acc_in, acc_ref,
+def middle_kernel(chunk, spans, tile_ref, own_ref, f1, f2, f3, g1, g2, g3, m_in, acc_in, acc_ref,
                   kv_ref, m_ref, peak_ref, even_ref, odd_ref, list0, list1):
-    rest_of_attention(chunk, spans, tile_ref, own_ref, (a1, a2, a3, b1, b2, b3), m_in, acc_in, kv_ref,
+    rest_of_attention(chunk, spans, tile_ref, own_ref, (f1, f2, f3, g1, g2, g3), m_in, acc_in, kv_ref,
                       m_ref, peak_ref, acc_ref, even_ref, odd_ref, (list0, list1))
 
 
-def last_kernel(chunk, spans, done, place_ref, tile_ref, own_ref, a1, a2, a3, b1, b2, b3, m_in, acc_in,
+def last_kernel(chunk, spans, done, index_ref, tile_ref, own_ref, f1, f2, f3, g1, g2, g3, m_in, acc_in,
                 w_ref, *refs):
     acc_done = refs[0] if done else None
     (keep_ref, send_ref, acc_ref, merged_ref, kv_ref, m_ref, peak_ref, even_ref, odd_ref,
      list0, list1) = refs[-11:]
-    rest_of_attention(chunk, spans, tile_ref, own_ref, (a1, a2, a3, b1, b2, b3), m_in, acc_in, kv_ref,
+    rest_of_attention(chunk, spans, tile_ref, own_ref, (f1, f2, f3, g1, g2, g3), m_in, acc_in, kv_ref,
                       m_ref, peak_ref, acc_ref, even_ref, odd_ref, (list0, list1))
     for n, s in enumerate(spans):
-        finish(s, acc_ref, 2 * n, place_ref, merged_ref)
+        finish(s, acc_ref, 2 * n, index_ref, merged_ref)
     for n, s in enumerate(done):
-        finish(s, acc_done, 2 * n, place_ref, merged_ref)
+        finish(s, acc_done, 2 * n, index_ref, merged_ref)
     project(merged_ref, w_ref, keep_ref, send_ref)
 
 
@@ -292,6 +305,19 @@
         out_ref[chunk * PIECE:(chunk + 1) * PIECE, :] = total.astype(jnp.bfloat16)
 
 
+def assemble(arrays, plans):
+    def kernel(*refs):
+        for out_ref, plan in zip(refs[len(arrays):], plans):
+            for at, (n, i) in enumerate(plan):
+                out_ref[at * PACK:(at + 1) * PACK] = refs[n][i * PACK:(i + 1) * PACK]
+
+    return pl.pallas_call(
+        kernel, in_specs=[VMEM] * len(arrays), out_specs=[VMEM] * len(plans),
+        out_shape=[struct((len(plan) * PACK, HD), jnp.bfloat16) for plan in plans],
+        compiler_params=params(2), name="assemble",
+    )(*arrays)
+
+
 def in_hbm(array):
     return pltpu.with_memory_space_constraint(array, pltpu.HBM)
 
@@ -304,11 +330,16 @@
     return pl.CostEstimate(flops=flops, bytes_accessed=traffic, transcendentals=0)
 
 
-def ctx_route(dx, dy):
-    return [
-        (x * NX + y, ((x + dx) % NX) * NX + (y + dy) % NX)
-        for x in range(NX) for y in range(NX)
-    ]
+def gather_route(distance, phase):
+    route = []
+    for x in range(NX):
+        for y in range(NX):
+            for t in range(NZ * NCORE):
+                along_x = t % NCORE == phase
+                x_to = (x + distance) % NX if along_x else x
+                y_to = y if along_x else (y + distance) % NX
+                route.append(((x * NX + y) * 8 + t, (x_to * NX + y_to) * 8 + t))
+    return route
 
 
 def tp_route(dz, swap):
@@ -320,28 +351,33 @@
 
 def on_device(queries, keys, values, positions, out_weight):
     bf16, f32 = jnp.bfloat16, jnp.float32
-    t = lax.axis_index("tp")
-    z, core = t // NCORE, t % NCORE
-    owners = jnp.arange(NZ * NCORE, dtype=jnp.int32)
-    places = ((owners % NCORE) ^ core) * NZ + (owners // NCORE - z) % NZ
-
-    own = pl.pallas_call(
-        pack_kernel, in_specs=[HBM] * 3, out_specs=VMEM,
-        out_shape=struct((2, PACK, 128), bf16), name="pack", compiler_params=params(2),
+    index = lax.axis_index("tp").reshape(1)
+
+    own, mine, give = pl.pallas_call(
+        pack_kernel, in_specs=[SMEM] + [HBM] * 3, out_specs=[VMEM] * 3,
+        out_shape=[struct((2 * PACK, HD), bf16)] * 3, name="pack", compiler_params=params(4),
         scratch_shapes=[
             pltpu.SMEM((2 * SPAN,), jnp.int32), pltpu.VMEM((2 * SPAN, HD), bf16),
             pltpu.VMEM((2 * SPAN, HD), bf16), pltpu.SemaphoreType.DMA((3,)),
         ],
-    )(in_hbm(positions), in_hbm(keys), in_hbm(values))
-
-    def shift(block, dx, dy):
-        return lax.ppermute(block, "ctx", ctx_route(dx, dy))
-
-    xs = [shift(own, d, 0) for d in (1, 3, 2)]
-    ys = [shift(own, 0, d) for d in (1, 3, 2)]
-    row = jnp.stack([b[0] for b in xs])
-    col = jnp.stack([b[1] for b in ys])
-    far = [shift(row, 0, d) for d in (1, 3, 2)] + [shift(col, d, 0) for d in (1, 3, 2)]
+    )(index, in_hbm(positions), in_hbm(keys), in_hbm(values))
+
+    def swap(block):
+        return lax.ppermute(block, "tp", tp_route(0, 1))
+
+    def shift(block, distance, phase):
+        return lax.ppermute(block, ("ctx", "tp"), gather_route(distance, phase))
+
+    got = swap(give)
+    both, = assemble([mine, got], [[(0, 0), (1, 0), (0, 1), (1, 1)]])
+    near = [shift(both, d, 0) for d in (1, 3, 2)]
+    ahead, mate = assemble(near, [
+        [(n, i) for i in (0, 1) for n in range(3)],
+        [(n, i) for n in range(3) for i in (1, 3)],
+    ])
+    far = [shift(ahead, d, 1) for d in (1, 3, 2)]
+    near_other = swap(mate)
+    far_other = [swap(assemble([b], [[(0, 3), (0, 4), (0, 5)]])[0]) for b in far]
 
     def walk_scratch(slots, units, width):
         return [
@@ -355,8 +391,8 @@
         ]
 
     scratch = walk_scratch(14, 8, 4)
-    maxima, acc, tiles, weight = pl.pallas_call(
-        first_kernel, in_specs=[HBM] * 2 + [VMEM] * 7, out_specs=[VMEM] * 4,
+    first = pl.pallas_call(
+        first_kernel, in_specs=[HBM] * 2 + [VMEM] * 5, out_specs=[VMEM] * 4,
         out_shape=[
             struct((8, 8, 256), f32), struct((8, 144, 256), f32),
             struct((8, 256, 128), bf16), struct((1024, DOUT), bf16),
@@ -365,7 +401,8 @@
         + [pltpu.SemaphoreType.DMA((NW + 1,))],
         compiler_params=params(14), name="first",
         cost_estimate=estimate(4 * 10 ** 9, 1 << 20),
-    )(in_hbm(queries), in_hbm(out_weight), own, *xs, *ys)
+    )
+    maxima, acc, tiles, weight = first(in_hbm(queries), in_hbm(out_weight), own, *near, near_other)
 
     def middle(chunk, spans, acc):
         n = 2 * len(spans)
@@ -375,7 +412,7 @@
             scratch_shapes=walk_scratch(18, n, 2),
             compiler_params=params(14), name="middle",
             cost_estimate=estimate(2 * 10 ** 9, 1 << 20),
-        )(tiles, own, *far, maxima, acc)
+        )(tiles, own, *far, *far_other, maxima, acc)
 
     def last(chunk, spans, acc, done=(), acc_done=()):
         n = 2 * len(spans)
@@ -389,7 +426,7 @@
             ] + walk_scratch(18, n, 2),
             compiler_params=params(14),
             cost_estimate=estimate(5 * 10 ** 9, 1 << 20),
-        )(places, tiles, own, *far, maxima, acc, weight, *acc_done)
+        )(index, tiles, own, *far, *far_other, maxima, acc, weight, *acc_done)
 
     def pair_sum(keep, got):
         return pl.pallas_call(
@@ -397,9 +434,6 @@
             out_shape=[struct((PIECE, DOUT), bf16)] * NZ, name="pair",
             compiler_params=params(6),
         )(keep, got)
-
-    def swap(block):
-        return lax.ppermute(block, "tp", tp_route(0, 1))
 
     def exchange(parts):
         return [parts[0]] + [lax.ppermute(parts[d], "tp", tp_route(d, 0)) for d in (1, 3, 2)]

time: 92.4 us -> 94.9 us (1.027)
  waiting for transfers between devices: 22 us -> 28.9 us
  starting transfers between devices: 31.5 us -> 28.2 us
  Pallas kernels: 38.6 us -> 37.6 us
    ppermute x12 -> x6, waiting for transfers between devices: 9.38 us -> 15.4 us  [shift(): return lax.ppermute(block, ('ctx', 'tp'), gather_route(distance, phase))]
    ppermute x12 -> x6, starting transfers between devices: 14.5 us -> 10.1 us  [shift(): return lax.ppermute(block, ('ctx', 'tp'), gather_route(distance, phase))]
    pallas_call x2, Pallas kernels: 11.8 us -> 10.6 us  [last(): pl.pallas_call(functools.partial(last_kernel, chunk, spans, done), in_spe...]
    ppermute x2 -> x7, waiting for transfers between devices: 0.58 us -> 1.62 us  [swap(): return lax.ppermute(block, 'tp', tp_route(0, 1))]
    ppermute x2 -> x7, starting transfers between devices: 0.28 us -> 1.32 us  [swap(): return lax.ppermute(block, 'tp', tp_route(0, 1))]
    pallas_call x2 -> x7, Pallas kernels: 23.2 us -> 23.4 us  [the longest x1 22.3 us: on_device(): first(in_hbm(queries), in_hbm(out_weight), own, *near, near_other)]
  transfers between devices with their start and end apart: 20 -> 19, of which waited for: 9 -> 11; matrix products, arithmetic and copies ran while one was open for 0% -> 0% of each run, Pallas kernels for 27% -> 26%
where the time goes in v1:
time: 94.9 us; the launch traced here: 94.8 us
  Pallas kernels  37.6 us (40%)
  waiting for transfers between devices  28.9 us (30%)
  starting transfers between devices  28.2 us (30%)
    pallas_call x1, Pallas kernels, on_device(): first(in_hbm(queries), in_hbm(out_weight), own, *near, near_other)  22.3 us
    ppermute x6, starting transfers between devices, exchange(): lax.ppermute(parts[d], 'tp', tp_route(d, 0))  16.7 us
    ppermute x6, waiting for transfers between devices, shift(): return lax.ppermute(block, ('ctx', 'tp'), gather_route(distance, phase))  15.4 us
    ppermute x6, waiting for transfers between devices, exchange(): lax.ppermute(parts[d], 'tp', tp_route(d, 0))  11.9 us
    pallas_call x2, Pallas kernels, last(): pl.pallas_call(functools.partial(last_kernel, chunk, spans, done), in_spe...  10.6 us
    ppermute x6, starting transfers between devices, shift(): return lax.ppermute(block, ('ctx', 'tp'), gather_route(distance, phase))  10.1 us
    pallas_call x1, Pallas kernels, middle(): pl.pallas_call(functools.partial(middle_kernel, chunk, spans), in_specs=[...  2.06 us
  transfers between devices with their start and end apart: 19, of which 11 were waited for; matrix products, arithmetic and copies ran while one was open for 0% of the time, Pallas kernels for 26%

profile of v1, /device:TPU:6, one launch (start us, length us, event | category | flops | bytes accessed | tf_op | source)
XLA Modules:
  0.0 94.8 jit_solution(10912628811985919849)
XLA Ops:
  1.1 1.3 %collective-permute-done.refs_1_ = bf16[544,128]{1,0:T(8,128)(2,1)S(1)} collective-permute-done((bf16[544,128]{1,0:T(8,128)(2,1)S(1)}, bf16[544,128]{1,0:T(8,128)(2,1)S(1)}, u32[]{:S(2)}, u32[]{:S(2)}) %collective-permute-start) | collective-permute-done | bytes 139296 | tf_op jit(solution)/shard_map/ppermute | solution.py:366
  2.9 1.7 %collective-permute-start.2 = (bf16[1088,128]{1,0:T(8,128)(2,1)S(1)}, bf16[1088,128]{1,0:T(8,128)(2,1)S(1)}, u32[]{:S(2)}, u32[]{:S(2)}) collective-permute-start(bf16[1088,128]{1,0:T(8,128)(2,1)S(1)} %assemble.5), channel_id=1, source_target_pairs={{0,96},{1,25},{2,98},{3,27},{4,100},{5,29},{6,102},{7,31},{8,104},... | collective-permute-start | bytes 835592 | tf_op jit(solution)/shard_map/ppermute | solution.py:369
  4.6 1.4 %collective-permute-start.3 = (bf16[1088,128]{1,0:T(8,128)(2,1)S(1)}, bf16[1088,128]{1,0:T(8,128)(2,1)S(1)}, u32[]{:S(2)}, u32[]{:S(2)}) collective-permute-start(bf16[1088,128]{1,0:T(8,128)(2,1)S(1)} %assemble.5), channel_id=1, source_target_pairs={{0,64},{1,17},{2,66},{3,19},{4,68},{5,21},{6,70},{7,23},{8,72},{9,... | collective-permute-start | bytes 835592 | tf_op jit(solution)/shard_map/ppermute | solution.py:369
  6.0 3.1 %collective-permute-done.1.refs_0_.n1 = bf16[1088,128]{1,0:T(8,128)(2,1)S(1)} collective-permute-done((bf16[1088,128]{1,0:T(8,128)(2,1)S(1)}, bf16[1088,128]{1,0:T(8,128)(2,1)S(1)}, u32[]{:S(2)}, u32[]{:S(2)}) %collective-permute-start.1) | collective-permute-done | bytes 278560 | tf_op jit(solution)/shard_map/ppermute | solution.py:369
  9.1 4.6 %collective-permute-done.2.refs_1_.n2 = bf16[1088,128]{1,0:T(8,128)(2,1)S(1)} collective-permute-done((bf16[1088,128]{1,0:T(8,128)(2,1)S(1)}, bf16[1088,128]{1,0:T(8,128)(2,1)S(1)}, u32[]{:S(2)}, u32[]{:S(2)}) %collective-permute-start.2) | collective-permute-done | bytes 278560 | tf_op jit(solution)/shard_map/ppermute | solution.py:369
  13.7 3.4 %collective-permute-start.7 = (bf16[1632,128]{1,0:T(8,128)(2,1)S(1)}, bf16[1632,128]{1,0:T(8,128)(2,1)S(1)}, u32[]{:S(2)}, u32[]{:S(2)}) collective-permute-start(bf16[1632,128]{1,0:T(8,128)(2,1)S(1)} %get-tuple-element.40), channel_id=1, source_target_pairs={{0,16},{1,65},{2,18},{3,67},{4,20},{5,69},{6,22},{7,71},{8,24},{9,... | collective-permute-start | bytes 1253384 | tf_op jit(solution)/shard_map/ppermute | solution.py:369
  17.8 2.6 %collective-permute-start.6 = (bf16[1632,128]{1,0:T(8,128)(2,1)S(1)}, bf16[1632,128]{1,0:T(8,128)(2,1)S(1)}, u32[]{:S(2)}, u32[]{:S(2)}) collective-permute-start(bf16[1632,128]{1,0:T(8,128)(2,1)S(1)} %get-tuple-element.40), channel_id=1, source_target_pairs={{0,24},{1,97},{2,26},{3,99},{4,28},{5,101},{6,30},{7,103},{8,0},{9... | collective-permute-start | bytes 1253384 | tf_op jit(solution)/shard_map/ppermute | solution.py:369
  20.4 3.1 %collective-permute-done.7.refs_0_.f3 = bf16[1632,128]{1,0:T(8,128)(2,1)S(1)} collective-permute-done((bf16[1632,128]{1,0:T(8,128)(2,1)S(1)}, bf16[1632,128]{1,0:T(8,128)(2,1)S(1)}, u32[]{:S(2)}, u32[]{:S(2)}) %collective-permute-start.7) | collective-permute-done | bytes 417824 | tf_op jit(solution)/shard_map/ppermute | solution.py:369
  23.6 4.3 %collective-permute-done.5.refs_0_.f1 = bf16[1632,128]{1,0:T(8,128)(2,1)S(1)} collective-permute-done((bf16[1632,128]{1,0:T(8,128)(2,1)S(1)}, bf16[1632,128]{1,0:T(8,128)(2,1)S(1)}, u32[]{:S(2)}, u32[]{:S(2)}) %collective-permute-start.5) | collective-permute-done | bytes 417824 | tf_op jit(solution)/shard_map/ppermute | solution.py:369
  28.5 22.3 %first.1 = (f32[8,8,256]{2,1,0:T(8,128)S(1)}, f32[8,144,256]{2,1,0:T(8,128)S(1)}, bf16[8,256,128]{2,1,0:T(8,128)(2,1)S(1)}, bf16[1024,8192]{1,0:T(8,128)(2,1)S(1)}) custom-call(bf16[256,1024]{1,0:T(8,128)(2,1)} %q_hbm.1, bf16[1024,8192]{1,0:T(8,128)(2,1)} %w_hbm.1, bf16[544,128]{1,0:T(8,128)(2,1)S(1)} %get-tuple-element.35.own_ref, ...), custom_call_target="tpu_custom_call" | custom-call | flops 4000000000 | bytes 1048576 | tf_op jit(solution)/shard_map/first/pallas_call | solution.py:405
  50.8 6.3 %shard_map.55 = (bf16[64,8192]{1,0:T(8,128)(2,1)S(1)}, bf16[64,8192]{1,0:T(8,128)(2,1)S(1)}) custom-call(s32[1]{0:T(128)} %bitcast.index_ref, bf16[8,256,128]{2,1,0:T(8,128)(2,1)S(1)} %get-tuple-element.39.tile_ref, bf16[544,128]{1,0:T(8,128)(2,1)S(1)} %get-tuple-element.35.own_ref, bf16[1632,128]{1,0:T(8,128)(2,1)S(1)} %collective-permute-done.5.refs_0_.f1, ...), custom_call_target="tpu_custom_call" | custom-call | flops 5000000000 | bytes 1048576 | tf_op jit(solution)/shard_map/pallas_call | solution.py:419
  57.6 2.1 %middle.1.refs_0_ = f32[2,144,256]{2,1,0:T(8,128)S(1)} custom-call(bf16[8,256,128]{2,1,0:T(8,128)(2,1)S(1)} %get-tuple-element.39.tile_ref, bf16[544,128]{1,0:T(8,128)(2,1)S(1)} %get-tuple-element.35.own_ref, bf16[1632,128]{1,0:T(8,128)(2,1)S(1)} %collective-permute-done.5.refs_0_.f1, bf16[1632,128]{1,0:T(8,128)(2,1)S(1)} %collective-permute-done.6.refs_0_.f2, ...), custom_call_target="tpu_custom_call" | custom-call | flops 2000000000 | bytes 1048576 | tf_op jit(solution)/shard_map/middle/pallas_call | solution.py:409
  60.1 4.3 %shard_map.56 = (bf16[64,8192]{1,0:T(8,128)(2,1)S(1)}, bf16[64,8192]{1,0:T(8,128)(2,1)S(1)}) custom-call(s32[1]{0:T(128)} %bitcast.index_ref, bf16[8,256,128]{2,1,0:T(8,128)(2,1)S(1)} %get-tuple-element.39.tile_ref, bf16[544,128]{1,0:T(8,128)(2,1)S(1)} %get-tuple-element.35.own_ref, bf16[1632,128]{1,0:T(8,128)(2,1)S(1)} %collective-permute-done.5.refs_0_.f1, ...), custom_call_target="tpu_custom_call" | custom-call | flops 5000000000 | bytes 1048576 | tf_op jit(solution)/shard_map/pallas_call | solution.py:419
  64.8 1.9 %collective-permute-start.12 = (bf16[16,8192]{1,0:T(8,128)(2,1)S(1)}, bf16[16,8192]{1,0:T(8,128)(2,1)S(1)}, u32[]{:S(2)}, u32[]{:S(2)}) collective-permute-start(bf16[16,8192]{1,0:T(8,128)(2,1)S(1)} %get-tuple-element.54), channel_id=1, source_target_pairs={{0,2},{1,3},{2,4},{3,5},{4,6},{5,7},{6,0},{7,1},{8,10},{9,11},{10,... | collective-permute-start | bytes 786440 | tf_op jit(solution)/shard_map/ppermute | solution.py:439
  66.7 2.1 %collective-permute-start.13 = (bf16[16,8192]{1,0:T(8,128)(2,1)S(1)}, bf16[16,8192]{1,0:T(8,128)(2,1)S(1)}, u32[]{:S(2)}, u32[]{:S(2)}) collective-permute-start(bf16[16,8192]{1,0:T(8,128)(2,1)S(1)} %get-tuple-element.55), channel_id=1, source_target_pairs={{0,6},{1,7},{2,0},{3,1},{4,2},{5,3},{6,4},{7,5},{8,14},{9,15},{10,... | collective-permute-start | bytes 786440 | tf_op jit(solution)/shard_map/ppermute | solution.py:439
  68.9 1.9 %collective-permute-start.14 = (bf16[16,8192]{1,0:T(8,128)(2,1)S(1)}, bf16[16,8192]{1,0:T(8,128)(2,1)S(1)}, u32[]{:S(2)}, u32[]{:S(2)}) collective-permute-start(bf16[16,8192]{1,0:T(8,128)(2,1)S(1)} %get-tuple-element.56), channel_id=1, source_target_pairs={{0,4},{1,5},{2,6},{3,7},{4,0},{5,1},{6,2},{7,3},{8,12},{9,13},{10,... | collective-permute-start | bytes 786440 | tf_op jit(solution)/shard_map/ppermute | solution.py:439
  71.0 1.1 %collective-permute-start.16 = (bf16[16,8192]{1,0:T(8,128)(2,1)S(1)}, bf16[16,8192]{1,0:T(8,128)(2,1)S(1)}, u32[]{:S(2)}, u32[]{:S(2)}) collective-permute-start(bf16[16,8192]{1,0:T(8,128)(2,1)S(1)} %get-tuple-element.62), channel_id=1, source_target_pairs={{0,2},{1,3},{2,4},{3,5},{4,6},{5,7},{6,0},{7,1},{8,10},{9,11},{10,... | collective-permute-start | bytes 786440 | tf_op jit(solution)/shard_map/ppermute | solution.py:439
  72.1 2.2 %collective-permute-start.17 = (bf16[16,8192]{1,0:T(8,128)(2,1)S(1)}, bf16[16,8192]{1,0:T(8,128)(2,1)S(1)}, u32[]{:S(2)}, u32[]{:S(2)}) collective-permute-start(bf16[16,8192]{1,0:T(8,128)(2,1)S(1)} %get-tuple-element.63), channel_id=1, source_target_pairs={{0,6},{1,7},{2,0},{3,1},{4,2},{5,3},{6,4},{7,5},{8,14},{9,15},{10,... | collective-permute-start | bytes 786440 | tf_op jit(solution)/shard_map/ppermute | solution.py:439
  74.3 1.7 %collective-permute-done.12.refs_1_ = bf16[16,8192]{1,0:T(8,128)(2,1)S(1)} collective-permute-done((bf16[16,8192]{1,0:T(8,128)(2,1)S(1)}, bf16[16,8192]{1,0:T(8,128)(2,1)S(1)}, u32[]{:S(2)}, u32[]{:S(2)}) %collective-permute-start.12) | collective-permute-done | bytes 262176 | tf_op jit(solution)/shard_map/ppermute | solution.py:439
  76.0 7.5 %collective-permute-start.18 = (bf16[16,8192]{1,0:T(8,128)(2,1)S(1)}, bf16[16,8192]{1,0:T(8,128)(2,1)S(1)}, u32[]{:S(2)}, u32[]{:S(2)}) collective-permute-start(bf16[16,8192]{1,0:T(8,128)(2,1)S(1)} %get-tuple-element.64), channel_id=1, source_target_pairs={{0,4},{1,5},{2,6},{3,7},{4,0},{5,1},{6,2},{7,3},{8,12},{9,13},{10,... | collective-permute-start | bytes 786440 | tf_op jit(solution)/shard_map/ppermute | solution.py:439
  83.5 3.3 %collective-permute-done.16.refs_5_ = bf16[16,8192]{1,0:T(8,128)(2,1)S(1)} collective-permute-done((bf16[16,8192]{1,0:T(8,128)(2,1)S(1)}, bf16[16,8192]{1,0:T(8,128)(2,1)S(1)}, u32[]{:S(2)}, u32[]{:S(2)}) %collective-permute-start.16) | collective-permute-done | bytes 262176 | tf_op jit(solution)/shard_map/ppermute | solution.py:439
  86.9 4.9 %collective-permute-done.17.refs_6_ = bf16[16,8192]{1,0:T(8,128)(2,1)S(1)} collective-permute-done((bf16[16,8192]{1,0:T(8,128)(2,1)S(1)}, bf16[16,8192]{1,0:T(8,128)(2,1)S(1)}, u32[]{:S(2)}, u32[]{:S(2)}) %collective-permute-start.17) | collective-permute-done | bytes 262176 | tf_op jit(solution)/shard_map/ppermute | solution.py:439
  91.8 1.9 %collective-permute-done.18.refs_7_ = bf16[16,8192]{1,0:T(8,128)(2,1)S(1)} collective-permute-done((bf16[16,8192]{1,0:T(8,128)(2,1)S(1)}, bf16[16,8192]{1,0:T(8,128)(2,1)S(1)}, u32[]{:S(2)}, u32[]{:S(2)}) %collective-permute-start.18) | collective-permute-done | bytes 262176 | tf_op jit(solution)/shard_map/ppermute | solution.py:439
  93.7 1.1 %final.1 = bf16[32,8192]{1,0:T(8,128)(2,1)} custom-call(bf16[16,8192]{1,0:T(8,128)(2,1)S(1)} %get-tuple-element.53.refs_0_, bf16[16,8192]{1,0:T(8,128)(2,1)S(1)} %collective-permute-done.12.refs_1_, bf16[16,8192]{1,0:T(8,128)(2,1)S(1)} %collective-permute-done.13.refs_2_, bf16[16,8192]{1,0:T(8,128)(2,1)S(1)} %collective-permute-done.14.refs_3_, ...), custom_call_target="tpu_custom_call" | custom-call | tf_op jit(solution)/shard_map/final/pallas_call | solution.py:451
  (27 shorter events, 4.7 us)
Async XLA Ops:
  1.0 1.4 %collective-permute-start = (bf16[544,128]{1,0:T(8,128)(2,1)S(1)}, bf16[544,128]{1,0:T(8,128)(2,1)S(1)}, u32[]{:S(2)}, u32[]{:S(2)}) collective-permute-start(bf16[544,128]{1,0:T(8,128)(2,1)S(1)} %get-tuple-element.37), channel_id=1, source_target_pairs={{0,1},{1,0},{2,3},{3,2},{4,5},{5,4},{6,7},{7,6},{8,9},{9,8},{10,11... | collective-permute-start | bytes 417800 | tf_op jit(solution)/shard_map/ppermute | solution.py:366
  2.5 6.6 %collective-permute-start.1 = (bf16[1088,128]{1,0:T(8,128)(2,1)S(1)}, bf16[1088,128]{1,0:T(8,128)(2,1)S(1)}, u32[]{:S(2)}, u32[]{:S(2)}) collective-permute-start(bf16[1088,128]{1,0:T(8,128)(2,1)S(1)} %assemble.5), channel_id=1, source_target_pairs={{0,32},{1,9},{2,34},{3,11},{4,36},{5,13},{6,38},{7,15},{8,40},{9,1... | collective-permute-start | bytes 835592 | tf_op jit(solution)/shard_map/ppermute | solution.py:369
  2.9 10.7 %collective-permute-start.2 = (bf16[1088,128]{1,0:T(8,128)(2,1)S(1)}, bf16[1088,128]{1,0:T(8,128)(2,1)S(1)}, u32[]{:S(2)}, u32[]{:S(2)}) collective-permute-start(bf16[1088,128]{1,0:T(8,128)(2,1)S(1)} %assemble.5), channel_id=1, source_target_pairs={{0,96},{1,25},{2,98},{3,27},{4,100},{5,29},{6,102},{7,31},{8,104},... | collective-permute-start | bytes 835592 | tf_op jit(solution)/shard_map/ppermute | solution.py:369
  4.6 9.1 %collective-permute-start.3 = (bf16[1088,128]{1,0:T(8,128)(2,1)S(1)}, bf16[1088,128]{1,0:T(8,128)(2,1)S(1)}, u32[]{:S(2)}, u32[]{:S(2)}) collective-permute-start(bf16[1088,128]{1,0:T(8,128)(2,1)S(1)} %assemble.5), channel_id=1, source_target_pairs={{0,64},{1,17},{2,66},{3,19},{4,68},{5,21},{6,70},{7,23},{8,72},{9,... | collective-permute-start | bytes 835592 | tf_op jit(solution)/shard_map/ppermute | solution.py:369
  13.7 9.7 %collective-permute-start.7 = (bf16[1632,128]{1,0:T(8,128)(2,1)S(1)}, bf16[1632,128]{1,0:T(8,128)(2,1)S(1)}, u32[]{:S(2)}, u32[]{:S(2)}) collective-permute-start(bf16[1632,128]{1,0:T(8,128)(2,1)S(1)} %get-tuple-element.40), channel_id=1, source_target_pairs={{0,16},{1,65},{2,18},{3,67},{4,20},{5,69},{6,22},{7,71},{8,24},{9,... | collective-permute-start | bytes 1253384 | tf_op jit(solution)/shard_map/ppermute | solution.py:369
  17.1 10.7 %collective-permute-start.5 = (bf16[1632,128]{1,0:T(8,128)(2,1)S(1)}, bf16[1632,128]{1,0:T(8,128)(2,1)S(1)}, u32[]{:S(2)}, u32[]{:S(2)}) collective-permute-start(bf16[1632,128]{1,0:T(8,128)(2,1)S(1)} %get-tuple-element.40), channel_id=1, source_target_pairs={{0,8},{1,33},{2,10},{3,35},{4,12},{5,37},{6,14},{7,39},{8,16},{9,4... | collective-permute-start | bytes 1253384 | tf_op jit(solution)/shard_map/ppermute | solution.py:369
  17.8 10.5 %collective-permute-start.6 = (bf16[1632,128]{1,0:T(8,128)(2,1)S(1)}, bf16[1632,128]{1,0:T(8,128)(2,1)S(1)}, u32[]{:S(2)}, u32[]{:S(2)}) collective-permute-start(bf16[1632,128]{1,0:T(8,128)(2,1)S(1)} %get-tuple-element.40), channel_id=1, source_target_pairs={{0,24},{1,97},{2,26},{3,99},{4,28},{5,101},{6,30},{7,103},{8,0},{9... | collective-permute-start | bytes 1253384 | tf_op jit(solution)/shard_map/ppermute | solution.py:369
  20.4 8.2 %collective-permute-start.4 = (bf16[1632,128]{1,0:T(8,128)(2,1)S(1)}, bf16[1632,128]{1,0:T(8,128)(2,1)S(1)}, u32[]{:S(2)}, u32[]{:S(2)}) collective-permute-start(bf16[1632,128]{1,0:T(8,128)(2,1)S(1)} %get-tuple-element.38), channel_id=1, source_target_pairs={{0,1},{1,0},{2,3},{3,2},{4,5},{5,4},{6,7},{7,6},{8,9},{9,8},{10,11... | collective-permute-start | bytes 1253384 | tf_op jit(solution)/shard_map/ppermute | solution.py:366
  23.5 27.3 %collective-permute-start.10 = (bf16[816,128]{1,0:T(8,128)(2,1)S(1)}, bf16[816,128]{1,0:T(8,128)(2,1)S(1)}, u32[]{:S(2)}, u32[]{:S(2)}) collective-permute-start(bf16[816,128]{1,0:T(8,128)(2,1)S(1)} %assemble.9), channel_id=1, source_target_pairs={{0,1},{1,0},{2,3},{3,2},{4,5},{5,4},{6,7},{7,6},{8,9},{9,8},{10,11... | collective-permute-start | bytes 626696 | tf_op jit(solution)/shard_map/ppermute | solution.py:366
  27.9 23.0 %collective-permute-start.8 = (bf16[816,128]{1,0:T(8,128)(2,1)S(1)}, bf16[816,128]{1,0:T(8,128)(2,1)S(1)}, u32[]{:S(2)}, u32[]{:S(2)}) collective-permute-start(bf16[816,128]{1,0:T(8,128)(2,1)S(1)} %assemble.7), channel_id=1, source_target_pairs={{0,1},{1,0},{2,3},{3,2},{4,5},{5,4},{6,7},{7,6},{8,9},{9,8},{10,11... | collective-permute-start | bytes 626696 | tf_op jit(solution)/shard_map/ppermute | solution.py:366
  28.3 22.5 %collective-permute-start.9 = (bf16[816,128]{1,0:T(8,128)(2,1)S(1)}, bf16[816,128]{1,0:T(8,128)(2,1)S(1)}, u32[]{:S(2)}, u32[]{:S(2)}) collective-permute-start(bf16[816,128]{1,0:T(8,128)(2,1)S(1)} %assemble.8), channel_id=1, source_target_pairs={{0,1},{1,0},{2,3},{3,2},{4,5},{5,4},{6,7},{7,6},{8,9},{9,8},{10,11... | collective-permute-start | bytes 626696 | tf_op jit(solution)/shard_map/ppermute | solution.py:366
  57.2 2.7 %collective-permute-start.11 = (bf16[64,8192]{1,0:T(8,128)(2,1)S(1)}, bf16[64,8192]{1,0:T(8,128)(2,1)S(1)}, u32[]{:S(2)}, u32[]{:S(2)}) collective-permute-start(bf16[64,8192]{1,0:T(8,128)(2,1)S(1)} %get-tuple-element.48), channel_id=1, source_target_pairs={{0,1},{1,0},{2,3},{3,2},{4,5},{5,4},{6,7},{7,6},{8,9},{9,8},{10,11... | collective-permute-start | bytes 3145736 | tf_op jit(solution)/shard_map/ppermute | solution.py:366
  64.4 6.3 %collective-permute-start.15 = (bf16[64,8192]{1,0:T(8,128)(2,1)S(1)}, bf16[64,8192]{1,0:T(8,128)(2,1)S(1)}, u32[]{:S(2)}, u32[]{:S(2)}) collective-permute-start(bf16[64,8192]{1,0:T(8,128)(2,1)S(1)} %get-tuple-element.60), channel_id=1, source_target_pairs={{0,1},{1,0},{2,3},{3,2},{4,5},{5,4},{6,7},{7,6},{8,9},{9,8},{10,11... | collective-permute-start | bytes 3145736 | tf_op jit(solution)/shard_map/ppermute | solution.py:366
  64.8 11.2 %collective-permute-start.12 = (bf16[16,8192]{1,0:T(8,128)(2,1)S(1)}, bf16[16,8192]{1,0:T(8,128)(2,1)S(1)}, u32[]{:S(2)}, u32[]{:S(2)}) collective-permute-start(bf16[16,8192]{1,0:T(8,128)(2,1)S(1)} %get-tuple-element.54), channel_id=1, source_target_pairs={{0,2},{1,3},{2,4},{3,5},{4,6},{5,7},{6,0},{7,1},{8,10},{9,11},{10,... | collective-permute-start | bytes 786440 | tf_op jit(solution)/shard_map/ppermute | solution.py:439
  66.7 16.8 %collective-permute-start.13 = (bf16[16,8192]{1,0:T(8,128)(2,1)S(1)}, bf16[16,8192]{1,0:T(8,128)(2,1)S(1)}, u32[]{:S(2)}, u32[]{:S(2)}) collective-permute-start(bf16[16,8192]{1,0:T(8,128)(2,1)S(1)} %get-tuple-element.55), channel_id=1, source_target_pairs={{0,6},{1,7},{2,0},{3,1},{4,2},{5,3},{6,4},{7,5},{8,14},{9,15},{10,... | collective-permute-start | bytes 786440 | tf_op jit(solution)/shard_map/ppermute | solution.py:439
  68.9 14.7 %collective-permute-start.14 = (bf16[16,8192]{1,0:T(8,128)(2,1)S(1)}, bf16[16,8192]{1,0:T(8,128)(2,1)S(1)}, u32[]{:S(2)}, u32[]{:S(2)}) collective-permute-start(bf16[16,8192]{1,0:T(8,128)(2,1)S(1)} %get-tuple-element.56), channel_id=1, source_target_pairs={{0,4},{1,5},{2,6},{3,7},{4,0},{5,1},{6,2},{7,3},{8,12},{9,13},{10,... | collective-permute-start | bytes 786440 | tf_op jit(solution)/shard_map/ppermute | solution.py:439
  71.0 15.9 %collective-permute-start.16 = (bf16[16,8192]{1,0:T(8,128)(2,1)S(1)}, bf16[16,8192]{1,0:T(8,128)(2,1)S(1)}, u32[]{:S(2)}, u32[]{:S(2)}) collective-permute-start(bf16[16,8192]{1,0:T(8,128)(2,1)S(1)} %get-tuple-element.62), channel_id=1, source_target_pairs={{0,2},{1,3},{2,4},{3,5},{4,6},{5,7},{6,0},{7,1},{8,10},{9,11},{10,... | collective-permute-start | bytes 786440 | tf_op jit(solution)/shard_map/ppermute | solution.py:439
  72.1 19.7 %collective-permute-start.17 = (bf16[16,8192]{1,0:T(8,128)(2,1)S(1)}, bf16[16,8192]{1,0:T(8,128)(2,1)S(1)}, u32[]{:S(2)}, u32[]{:S(2)}) collective-permute-start(bf16[16,8192]{1,0:T(8,128)(2,1)S(1)} %get-tuple-element.63), channel_id=1, source_target_pairs={{0,6},{1,7},{2,0},{3,1},{4,2},{5,3},{6,4},{7,5},{8,14},{9,15},{10,... | collective-permute-start | bytes 786440 | tf_op jit(solution)/shard_map/ppermute | solution.py:439
  76.0 17.7 %collective-permute-start.18 = (bf16[16,8192]{1,0:T(8,128)(2,1)S(1)}, bf16[16,8192]{1,0:T(8,128)(2,1)S(1)}, u32[]{:S(2)}, u32[]{:S(2)}) collective-permute-start(bf16[16,8192]{1,0:T(8,128)(2,1)S(1)} %get-tuple-element.64), channel_id=1, source_target_pairs={{0,4},{1,5},{2,6},{3,7},{4,0},{5,1},{6,2},{7,3},{8,12},{9,13},{10,... | collective-permute-start | bytes 786440 | tf_op jit(solution)/shard_map/ppermute | solution.py:439

commit v2 on v0

--- a/solution.py
+++ b/solution.py
@@ -24,6 +24,7 @@
 GROUP = 4
 HEADROOM = 60.0
 NW = 4
+HOPS = (2, 1, 3)
 
 
 VMEM = pl.BlockSpec(memory_space=pltpu.VMEM)
@@ -35,7 +36,7 @@
     return jax.ShapeDtypeStruct(shape, dtype)
 
 
-def pack_kernel(pos_hbm, k_hbm, v_hbm, out_ref, pos_ref, k_ref, v_ref, sems):
+def pack_kernel(pos_hbm, k_hbm, v_hbm, out_ref, half_ref, pos_ref, k_ref, v_ref, sems):
     copies = [
         pltpu.make_async_copy(src, dst, sems.at[i])
         for i, (src, dst) in enumerate(((v_hbm, v_ref), (k_hbm, k_ref), (pos_hbm, pos_ref)))
@@ -46,10 +47,20 @@
         copy.wait()
     for s in range(2):
         rows = slice(s * SPAN, (s + 1) * SPAN)
-        out_ref[s, 0:128, :] = k_ref[rows, :]
-        out_ref[s, 128:256, :] = v_ref[rows, :].T
         span = (pos_ref[s * SPAN] // SPAN).astype(jnp.float32)
-        out_ref[s, 256:PACK, :] = jnp.full((16, 128), span, jnp.float32).astype(jnp.bfloat16)
+        base = s * PACK
+        out_ref[base:base + 128] = k_ref[rows, :]
+        out_ref[base + 128:base + 256] = v_ref[rows, :].T
+        ids = jnp.full((16, 128), span, jnp.float32).astype(jnp.bfloat16)
+        out_ref[base + 256:base + PACK] = ids
+    half_ref[...] = out_ref[0:PACK]
+
+
+def join_kernel(*refs):
+    out_ref = refs[-1]
+    for i, ref in enumerate(refs[:-1]):
+        rows = ref.shape[0]
+        out_ref[i * PACK:(i + 1) * PACK] = ref[rows - PACK:rows]
 
 
 def query_tile(q_ref, chunk, s, quad):
@@ -71,13 +82,14 @@
 
 def store_keys(kv_ref, blocks):
     for i, (ref, j) in enumerate(blocks):
-        kv_ref[i, 0:256, :] = ref[j, 0:256, :]
+        kv_ref[i, 0:256, :] = ref[j * PACK:j * PACK + 256, :]
         kv_ref[i, 256:PACK, :] = jnp.ones((16, 128), jnp.bfloat16)
     kv_ref[len(blocks)] = jnp.zeros((PACK, 128), jnp.bfloat16)
 
 
 def span_id(ref, i):
-    return jnp.max(ref[i, 256:PACK, :].astype(jnp.float32)).astype(jnp.int32)
+    ids = ref[i * PACK + 256:(i + 1) * PACK, :].astype(jnp.float32)
+    return jnp.max(ids).astype(jnp.int32)
 
 
 def visible_list(list_ref, ids, limit):
@@ -155,16 +167,23 @@
     return jnp.max(worst) * LOG_SCALE > HEADROOM
 
 
+def fetch_half(half, w_hbm, w_ref, sems):
+    copies = []
+    for j in range(NW):
+        rows = pl.ds(j * (1024 // NW), 1024 // NW)
+        columns = pl.ds(half * DOUT // 2, DOUT // 2)
+        copies.append(pltpu.make_async_copy(w_hbm.at[rows, columns], w_ref.at[rows], sems.at[j]))
+        copies[j].start()
+    return copies
+
+
 def first_kernel(q_hbm, w_hbm, own_ref, x1, x2, x3, y1, y2, y3, m_ref, acc_ref, tile_ref, w_ref,
                  q_ref, kv_ref, peak_ref, even_ref, odd_ref, list0, list1, sems):
     fetch_q = pltpu.make_async_copy(q_hbm, q_ref, sems.at[NW])
     fetch_q.start()
-    fetch_w = []
-    for j in range(NW):
-        rows = pl.ds(j * (1024 // NW), 1024 // NW)
-        fetch_w.append(pltpu.make_async_copy(w_hbm.at[rows], w_ref.at[rows], sems.at[j]))
-        fetch_w[j].start()
-    blocks = [(ref, j) for ref in (own_ref, x1, x2, x3, y1, y2, y3) for j in range(2)]
+    fetch_w = fetch_half(0, w_hbm, w_ref, sems)
+    blocks = [(ref, j) for ref in (own_ref, y1, y2, y3) for j in range(2)]
+    blocks += [(ref, 0) for ref in (x1, x2, x3)]
     store_keys(kv_ref, blocks)
     ids = [span_id(ref, j) for ref, j in blocks]
     counts = [visible_list(ref, ids, ids[s]) for s, ref in enumerate((list0, list1))]
@@ -206,6 +225,37 @@
         copy.wait()
 
 
+def second_kernel(w_hbm, tile_ref, own_ref, b1, b2, b3, m_in, acc_in, m_ref, acc_ref, w_ref,
+                  kv_ref, peak_ref, even_ref, odd_ref, list0, list1, sems):
+    fetch_w = fetch_half(1, w_hbm, w_ref, sems)
+    blocks = [(ref, j) for ref in (b1, b2, b3) for j in range(4)]
+    store_keys(kv_ref, blocks)
+    ids = [span_id(ref, j) for ref, j in blocks]
+    lists = (list0, list1)
+    counts = [visible_list(lists[s], ids, span_id(own_ref, s)) for s in range(2)]
+    units = [[chunk * 4 + s * 2 + quad for chunk in range(2) for quad in range(2)] for s in range(2)]
+    queries = [[tile_ref[u] for u in units[s]] for s in range(2)]
+
+    def reset():
+        m_ref[...] = m_in[...]
+        acc_ref[...] = acc_in[...]
+
+    reset()
+    peak_ref[...] = m_in[...]
+    for s in range(2):
+        fast_walk(kv_ref, lists[s], counts[s], queries[s], units[s], m_ref, peak_ref, acc_ref,
+                  (even_ref, odd_ref))
+
+    @pl.when(overshoot(peak_ref, m_ref, units[0] + units[1]))
+    def _():
+        reset()
+        for s in range(2):
+            slow_walk(kv_ref, lists[s], counts[s], queries[s], units[s], m_ref, acc_ref)
+
+    for copy in fetch_w:
+        copy.wait()
+
+
 def rest_of_attention(chunk, spans, tile_ref, own_ref, far, m_in, acc_in, kv_ref, m_ref, peak_ref,
                       acc_ref, even_ref, odd_ref, lists):
     blocks = [(ref, j) for ref in far for j in range(3)]
@@ -234,7 +284,8 @@
             slow_walk(kv_ref, lists[n], counts[n], queries[n], units[n], m_ref, acc_ref)
 
 
-def finish(s, acc_ref, base, place_ref, merged_ref):
+def finish(s, acc_ref, base, index_ref, merged_ref):
+    z, core = index_ref[0] // NCORE, index_ref[0] % NCORE
     for quad in range(2):
         acc = acc_ref[base + quad]
         o = acc[:128] * (1.0 / acc[128:129])
@@ -243,14 +294,16 @@
             for i in range(2):
                 h = quad * QUAD + half * 2 + i
                 for t in range(4):
-                    where = pl.multiple_of(place_ref[s * 4 + t] * PIECE, PIECE)
+                    owner = s * 4 + t
+                    place = ((owner % NCORE) ^ core) * NZ + (owner // NCORE - z + NZ) % NZ
+                    where = pl.multiple_of(place * PIECE, PIECE)
                     at = i * 64 + t * PIECE
                     merged_ref[pl.ds(where, PIECE), h * HD:(h + 1) * HD] = rows[at:at + PIECE]
 
 
 def project(merged_ref, w_ref, keep_ref, send_ref):
     cols = DOUT // NCOL
-    for j in range(NCOL):
+    for j in range(NCOL // 2):
         at = slice(j * cols, (j + 1) * cols)
         part = jnp.dot(merged_ref[...], w_ref[:, at], preferred_element_type=jnp.float32)
         part = part.astype(jnp.bfloat16)
@@ -258,30 +311,32 @@
         send_ref[:, at] = part[64:]
 
 
-def middle_kernel(chunk, spans, tile_ref, own_ref, a1, a2, a3, b1, b2, b3, m_in, acc_in, acc_ref,
+def middle_kernel(chunk, spans, tile_ref, own_ref, a1, a2, a3, m_in, acc_in, acc_ref,
                   kv_ref, m_ref, peak_ref, even_ref, odd_ref, list0, list1):
-    rest_of_attention(chunk, spans, tile_ref, own_ref, (a1, a2, a3, b1, b2, b3), m_in, acc_in, kv_ref,
+    rest_of_attention(chunk, spans, tile_ref, own_ref, (a1, a2, a3), m_in, acc_in, kv_ref,
                       m_ref, peak_ref, acc_ref, even_ref, odd_ref, (list0, list1))
 
 
-def last_kernel(chunk, spans, done, place_ref, tile_ref, own_ref, a1, a2, a3, b1, b2, b3, m_in, acc_in,
+def last_kernel(chunk, spans, done, index_ref, tile_ref, own_ref, a1, a2, a3, m_in, acc_in,
                 w_ref, *refs):
     acc_done = refs[0] if done else None
-    (keep_ref, send_ref, acc_ref, merged_ref, kv_ref, m_ref, peak_ref, even_ref, odd_ref,
+    (keep_ref, send_ref, merged_ref, acc_ref, kv_ref, m_ref, peak_ref, even_ref, odd_ref,
      list0, list1) = refs[-11:]
-    rest_of_attention(chunk, spans, tile_ref, own_ref, (a1, a2, a3, b1, b2, b3), m_in, acc_in, kv_ref,
+    rest_of_attention(chunk, spans, tile_ref, own_ref, (a1, a2, a3), m_in, acc_in, kv_ref,
                       m_ref, peak_ref, acc_ref, even_ref, odd_ref, (list0, list1))
     for n, s in enumerate(spans):
-        finish(s, acc_ref, 2 * n, place_ref, merged_ref)
+        finish(s, acc_ref, 2 * n, index_ref, merged_ref)
     for n, s in enumerate(done):
-        finish(s, acc_done, 2 * n, place_ref, merged_ref)
+        finish(s, acc_done, 2 * n, index_ref, merged_ref)
     project(merged_ref, w_ref, keep_ref, send_ref)
 
 
-def pair_kernel(keep_ref, got_ref, *out_refs):
-    total = keep_ref[...].astype(jnp.float32) + got_ref[...].astype(jnp.float32)
-    for d in range(NZ):
-        out_refs[d][...] = total[d * PIECE:(d + 1) * PIECE].astype(jnp.bfloat16)
+def pair_kernel(keep_a, got_a, keep_b, got_b, *out_refs):
+    for half, keep_ref, got_ref in ((0, keep_a, got_a), (1, keep_b, got_b)):
+        total = keep_ref[...].astype(jnp.float32) + got_ref[...].astype(jnp.float32)
+        columns = slice(half * DOUT // 2, (half + 1) * DOUT // 2)
+        for d in range(NZ):
+            out_refs[d][:, columns] = total[d * PIECE:(d + 1) * PIECE].astype(jnp.bfloat16)
 
 
 def final_kernel(*refs):
@@ -320,28 +375,36 @@
 
 def on_device(queries, keys, values, positions, out_weight):
     bf16, f32 = jnp.bfloat16, jnp.float32
-    t = lax.axis_index("tp")
-    z, core = t // NCORE, t % NCORE
-    owners = jnp.arange(NZ * NCORE, dtype=jnp.int32)
-    places = ((owners % NCORE) ^ core) * NZ + (owners // NCORE - z) % NZ
-
-    own = pl.pallas_call(
-        pack_kernel, in_specs=[HBM] * 3, out_specs=VMEM,
-        out_shape=struct((2, PACK, 128), bf16), name="pack", compiler_params=params(2),
+    index = lax.axis_index("tp").reshape(1)
+
+    own, half = pl.pallas_call(
+        pack_kernel, in_specs=[HBM] * 3, out_specs=[VMEM] * 2,
+        out_shape=[struct((2 * PACK, HD), bf16), struct((PACK, HD), bf16)],
+        name="pack", compiler_params=params(2),
         scratch_shapes=[
             pltpu.SMEM((2 * SPAN,), jnp.int32), pltpu.VMEM((2 * SPAN, HD), bf16),
             pltpu.VMEM((2 * SPAN, HD), bf16), pltpu.SemaphoreType.DMA((3,)),
         ],
     )(in_hbm(positions), in_hbm(keys), in_hbm(values))
 
-    def shift(block, dx, dy):
-        return lax.ppermute(block, "ctx", ctx_route(dx, dy))
-
-    xs = [shift(own, d, 0) for d in (1, 3, 2)]
-    ys = [shift(own, 0, d) for d in (1, 3, 2)]
-    row = jnp.stack([b[0] for b in xs])
-    col = jnp.stack([b[1] for b in ys])
-    far = [shift(row, 0, d) for d in (1, 3, 2)] + [shift(col, d, 0) for d in (1, 3, 2)]
+    def shifts(block, dx, dy):
+        moved = []
+        for d in HOPS:
+            moved.append(lax.ppermute(block, "ctx", ctx_route(dx * d, dy * d)))
+        return moved
+
+    def join(*blocks):
+        return pl.pallas_call(
+            join_kernel, in_specs=[VMEM] * len(blocks), out_specs=VMEM,
+            out_shape=struct((len(blocks) * PACK, HD), bf16), name="join",
+            compiler_params=params(2),
+        )(*blocks)
+
+    ys = shifts(own, 0, 1)
+    xs = shifts(half, 1, 0)
+    column = join(own, *ys)
+    fb = shifts(column, 1, 0)
+    fa = shifts(join(*xs), 0, 1)
 
     def walk_scratch(slots, units, width):
         return [
@@ -354,66 +417,91 @@
             pltpu.SMEM((32,), jnp.int32),
         ]
 
-    scratch = walk_scratch(14, 8, 4)
-    maxima, acc, tiles, weight = pl.pallas_call(
+    scratch = walk_scratch(11, 8, 4)
+    first = pl.pallas_call(
         first_kernel, in_specs=[HBM] * 2 + [VMEM] * 7, out_specs=[VMEM] * 4,
         out_shape=[
             struct((8, 8, 256), f32), struct((8, 144, 256), f32),
-            struct((8, 256, 128), bf16), struct((1024, DOUT), bf16),
+            struct((8, 256, 128), bf16), struct((1024, DOUT // 2), bf16),
         ],
         scratch_shapes=[pltpu.VMEM((256, 1024), bf16)] + scratch[:1] + scratch[2:]
         + [pltpu.SemaphoreType.DMA((NW + 1,))],
         compiler_params=params(14), name="first",
         cost_estimate=estimate(4 * 10 ** 9, 1 << 20),
-    )(in_hbm(queries), in_hbm(out_weight), own, *xs, *ys)
+    )
+    maxima, acc, tiles, weight_a = first(
+        in_hbm(queries), in_hbm(out_weight), own, *xs, *ys
+    )
+
+    scratch = walk_scratch(12, 8, 4)
+    second = pl.pallas_call(
+        second_kernel, in_specs=[HBM] + [VMEM] * 7, out_specs=[VMEM] * 3,
+        out_shape=[
+            struct((8, 8, 256), f32), struct((8, 144, 256), f32), struct((1024, DOUT // 2), bf16),
+        ],
+        scratch_shapes=scratch[:1] + scratch[2:] + [pltpu.SemaphoreType.DMA((NW,))],
+        compiler_params=params(14), name="second",
+        cost_estimate=estimate(4 * 10 ** 9, 1 << 20),
+    )
+    maxima, acc, weight_b = second(in_hbm(out_weight), tiles, own, *fb, maxima, acc)
 
     def middle(chunk, spans, acc):
         n = 2 * len(spans)
         return pl.pallas_call(
             functools.partial(middle_kernel, chunk, spans),
-            in_specs=[VMEM] * 10, out_specs=VMEM, out_shape=struct((n, 144, 256), f32),
-            scratch_shapes=walk_scratch(18, n, 2),
+            in_specs=[VMEM] * 7, out_specs=VMEM, out_shape=struct((n, 144, 256), f32),
+            scratch_shapes=walk_scratch(9, n, 2),
             compiler_params=params(14), name="middle",
             cost_estimate=estimate(2 * 10 ** 9, 1 << 20),
-        )(tiles, own, *far, maxima, acc)
+        )(tiles, own, *fa, maxima, acc)
+
+    halves = [struct((64, DOUT // 2), bf16)] * 2
 
     def last(chunk, spans, acc, done=(), acc_done=()):
         n = 2 * len(spans)
         return pl.pallas_call(
             functools.partial(last_kernel, chunk, spans, done),
-            in_specs=[SMEM] + [VMEM] * (11 + len(acc_done)),
-            out_specs=[VMEM, VMEM],
-            out_shape=[struct((64, DOUT), bf16), struct((64, DOUT), bf16)],
-            scratch_shapes=[
-                pltpu.VMEM((n, 144, 256), f32), pltpu.VMEM((128, 1024), bf16),
-            ] + walk_scratch(18, n, 2),
+            in_specs=[SMEM] + [VMEM] * (8 + len(acc_done)),
+            out_specs=[VMEM] * 3,
+            out_shape=halves + [struct((128, 1024), bf16)],
+            scratch_shapes=[pltpu.VMEM((n, 144, 256), f32)] + walk_scratch(9, n, 2),
             compiler_params=params(14),
             cost_estimate=estimate(5 * 10 ** 9, 1 << 20),
-        )(places, tiles, own, *far, maxima, acc, weight, *acc_done)
-
-    def pair_sum(keep, got):
+        )(index, tiles, own, *fa, maxima, acc, weight_a, *acc_done)
+
+    def rest(merged):
         return pl.pallas_call(
-            pair_kernel, in_specs=[VMEM, VMEM], out_specs=[VMEM] * NZ,
+            project, in_specs=[VMEM] * 2, out_specs=[VMEM] * 2, out_shape=halves,
+            compiler_params=params(6), name="rest", cost_estimate=estimate(10 ** 9, 1 << 20),
+        )(merged, weight_b)
+
+    def pair_sum(*blocks):
+        return pl.pallas_call(
+            pair_kernel, in_specs=[VMEM] * 4, out_specs=[VMEM] * NZ,
             out_shape=[struct((PIECE, DOUT), bf16)] * NZ, name="pair",
             compiler_params=params(6),
-        )(keep, got)
+        )(*blocks)
 
     def swap(block):
         return lax.ppermute(block, "tp", tp_route(0, 1))
 
     def exchange(parts):
-        return [parts[0]] + [lax.ppermute(parts[d], "tp", tp_route(d, 0)) for d in (1, 3, 2)]
-
-    keep0, send0 = last(0, (0, 1), acc)
-    send0, acc1 = lax.optimization_barrier((send0, acc))
-    got0 = swap(send0)
+        return [parts[0]] + [lax.ppermute(parts[d], "tp", tp_route(d, 0)) for d in HOPS]
+
+    keep0a, send0a, merged0 = last(0, (0, 1), acc)
+    got0a = swap(send0a)
+    keep0b, send0b = rest(merged0)
+    send0b, acc1 = lax.optimization_barrier((send0b, acc))
+    got0b = swap(send0b)
     acc_mid = middle(1, (0,), acc1)
-    keep0, acc_mid = lax.optimization_barrier((keep0, acc_mid))
-    parts0 = pair_sum(keep0, got0)
+    keep0b, acc_mid = lax.optimization_barrier((keep0b, acc_mid))
+    parts0 = pair_sum(keep0a, got0a, keep0b, got0b)
     *parts0, acc2 = lax.optimization_barrier((*parts0, acc))
     pieces0 = exchange(parts0)
-    keep1, send1 = last(1, (1,), acc2, (0,), (acc_mid,))
-    pieces1 = exchange(pair_sum(keep1, swap(send1)))
+    keep1a, send1a, merged1 = last(1, (1,), acc2, (0,), (acc_mid,))
+    got1a = swap(send1a)
+    keep1b, send1b = rest(merged1)
+    pieces1 = exchange(pair_sum(keep1a, got1a, keep1b, swap(send1b)))
     return pl.pallas_call(
         final_kernel, in_specs=[VMEM] * (2 * NZ), out_specs=VMEM,
         out_shape=struct((2 * PIECE, DOUT), bf16), name="final", compiler_params=params(6),

time: 92.4 us -> 86.8 us (0.939)
  starting transfers between devices: 31.5 us -> 27.2 us
  Pallas kernels: 38.6 us -> 34.4 us
  waiting for transfers between devices: 22 us -> 24.9 us
    pallas_call x2, Pallas kernels: 11.8 us -> 6.17 us  [last(): pl.pallas_call(functools.partial(last_kernel, chunk, spans, done), in_spe...]
    ppermute x6, starting transfers between devices: 16.7 us -> 11.7 us  [exchange(): lax.ppermute(parts[d], 'tp', tp_route(d, 0))]
    ppermute x6, waiting for transfers between devices: 12 us -> 16.2 us  [exchange(): lax.ppermute(parts[d], 'tp', tp_route(d, 0))]
    pallas_call x4 -> x9, Pallas kernels: 23.7 us -> 25.5 us  [the longest x1 17.2 us: on_device(): first(in_hbm(queries), in_hbm(out_weight), own, *xs, *ys)]
    ppermute x2 -> x4, starting transfers between devices: 0.28 us -> 1.25 us  [swap(): return lax.ppermute(block, 'tp', tp_route(0, 1))]
  transfers between devices with their start and end apart: 20 -> 22, of which waited for: 9 -> 9; matrix products, arithmetic and copies ran while one was open for 0% -> 0% of each run, Pallas kernels for 27% -> 28%
where the time goes in v2:
time: 86.8 us; the launch traced here: 86.6 us
  Pallas kernels  34.4 us (40%)
  starting transfers between devices  27.2 us (31%)
  waiting for transfers between devices  24.9 us (29%)
    pallas_call x1, Pallas kernels, on_device(): first(in_hbm(queries), in_hbm(out_weight), own, *xs, *ys)  17.2 us
    ppermute x6, waiting for transfers between devices, exchange(): lax.ppermute(parts[d], 'tp', tp_route(d, 0))  16.2 us
    ppermute x12, starting transfers between devices, shifts(): moved.append(lax.ppermute(block, 'ctx', ctx_route(dx * d, dy * d)))  14.2 us
    ppermute x6, starting transfers between devices, exchange(): lax.ppermute(parts[d], 'tp', tp_route(d, 0))  11.7 us
    ppermute x12, waiting for transfers between devices, shifts(): moved.append(lax.ppermute(block, 'ctx', ctx_route(dx * d, dy * d)))  8.64 us
    pallas_call x2, Pallas kernels, last(): pl.pallas_call(functools.partial(last_kernel, chunk, spans, done), in_spe...  6.17 us
    pallas_call x1, Pallas kernels, on_device(): second(in_hbm(out_weight), tiles, own, *fb, maxima, acc)  4.24 us
    pallas_call x2, Pallas kernels, rest(): pl.pallas_call(project, in_specs=[VMEM] * 2, out_specs=[VMEM] * 2, out_sh...  2.53 us
  transfers between devices with their start and end apart: 22, of which 9 were waited for; matrix products, arithmetic and copies ran while one was open for 0% of the time, Pallas kernels for 28%

profile of v2, /device:TPU:6, one launch (start us, length us, event | category | flops | bytes accessed | tf_op | source)
XLA Modules:
  0.0 86.6 jit_solution(7208103424051839974)
XLA Ops:
  1.9 3.0 %collective-permute-start.5 = (bf16[544,128]{1,0:T(8,128)(2,1)S(1)}, bf16[544,128]{1,0:T(8,128)(2,1)S(1)}, u32[]{:S(2)}, u32[]{:S(2)}) collective-permute-start(bf16[544,128]{1,0:T(8,128)(2,1)S(1)} %get-tuple-element.41.own_ref.refs_0_), channel_id=1, source_target_pairs={{0,24},{8,0},{16,8},{24,16},{32,56},{40,32},{48,40},{56,48},{64,88... | collective-permute-start | bytes 417800 | tf_op jit(solution)/shard_map/ppermute | solution.py:393
  4.9 2.2 %collective-permute-start.3 = (bf16[544,128]{1,0:T(8,128)(2,1)S(1)}, bf16[544,128]{1,0:T(8,128)(2,1)S(1)}, u32[]{:S(2)}, u32[]{:S(2)}) collective-permute-start(bf16[544,128]{1,0:T(8,128)(2,1)S(1)} %get-tuple-element.41.own_ref.refs_0_), channel_id=1, source_target_pairs={{0,16},{8,24},{16,0},{24,8},{32,48},{40,56},{48,32},{56,40},{64,80... | collective-permute-start | bytes 417800 | tf_op jit(solution)/shard_map/ppermute | solution.py:393
  7.1 2.4 %collective-permute-start.1 = (bf16[272,128]{1,0:T(8,128)(2,1)S(1)}, bf16[272,128]{1,0:T(8,128)(2,1)S(1)}, u32[]{:S(2)}, u32[]{:S(2)}) collective-permute-start(bf16[272,128]{1,0:T(8,128)(2,1)S(1)} %get-tuple-element.42), channel_id=1, source_target_pairs={{0,32},{8,40},{16,48},{24,56},{32,64},{40,72},{48,80},{56,88},{64,... | collective-permute-start | bytes 208904 | tf_op jit(solution)/shard_map/ppermute | solution.py:393
  9.7 2.4 %collective-permute-done.1.x2.refs_1_ = bf16[272,128]{1,0:T(8,128)(2,1)S(1)} collective-permute-done((bf16[272,128]{1,0:T(8,128)(2,1)S(1)}, bf16[272,128]{1,0:T(8,128)(2,1)S(1)}, u32[]{:S(2)}, u32[]{:S(2)}) %collective-permute-start.1) | collective-permute-done | bytes 69664 | tf_op jit(solution)/shard_map/ppermute | solution.py:393
  12.1 3.2 %collective-permute-done.x1.refs_0_ = bf16[272,128]{1,0:T(8,128)(2,1)S(1)} collective-permute-done((bf16[272,128]{1,0:T(8,128)(2,1)S(1)}, bf16[272,128]{1,0:T(8,128)(2,1)S(1)}, u32[]{:S(2)}, u32[]{:S(2)}) %collective-permute-start) | collective-permute-done | bytes 69664 | tf_op jit(solution)/shard_map/ppermute | solution.py:393
  15.4 1.1 %collective-permute-start.8 = (bf16[816,128]{1,0:T(8,128)(2,1)S(1)}, bf16[816,128]{1,0:T(8,128)(2,1)S(1)}, u32[]{:S(2)}, u32[]{:S(2)}) collective-permute-start(bf16[816,128]{1,0:T(8,128)(2,1)S(1)} %join.2), channel_id=1, source_target_pairs={{0,24},{8,0},{16,8},{24,16},{32,56},{40,32},{48,40},{56,48},{64,88... | collective-permute-start | bytes 626696 | tf_op jit(solution)/shard_map/ppermute | solution.py:393
  17.6 3.2 %collective-permute-start.10 = (bf16[1088,128]{1,0:T(8,128)(2,1)S(1)}, bf16[1088,128]{1,0:T(8,128)(2,1)S(1)}, u32[]{:S(2)}, u32[]{:S(2)}) collective-permute-start(bf16[1088,128]{1,0:T(8,128)(2,1)S(1)} %join.3), channel_id=1, source_target_pairs={{0,32},{8,40},{16,48},{24,56},{32,64},{40,72},{48,80},{56,88},{64,... | collective-permute-start | bytes 835592 | tf_op jit(solution)/shard_map/ppermute | solution.py:393
  20.8 17.2 %first.1 = (f32[8,8,256]{2,1,0:T(8,128)S(1)}, f32[8,144,256]{2,1,0:T(8,128)S(1)}, bf16[8,256,128]{2,1,0:T(8,128)(2,1)S(1)}, bf16[1024,4096]{1,0:T(8,128)(2,1)S(1)}) custom-call(bf16[256,1024]{1,0:T(8,128)(2,1)} %q_hbm.1, bf16[1024,8192]{1,0:T(8,128)(2,1)} %w_hbm.3, bf16[544,128]{1,0:T(8,128)(2,1)S(1)} %get-tuple-element.41.own_ref.refs_0_, ...), custom_call_target="tpu_custom_call" | custom-call | flops 4000000000 | bytes 1048576 | tf_op jit(solution)/shard_map/first/pallas_call | solution.py:432
  38.2 4.2 %second.1 = (f32[8,8,256]{2,1,0:T(8,128)S(1)}, f32[8,144,256]{2,1,0:T(8,128)S(1)}, bf16[1024,4096]{1,0:T(8,128)(2,1)S(1)}) custom-call(bf16[1024,8192]{1,0:T(8,128)(2,1)} %w_hbm.3, bf16[8,256,128]{2,1,0:T(8,128)(2,1)S(1)} %get-tuple-element.43.tile_ref, bf16[544,128]{1,0:T(8,128)(2,1)S(1)} %get-tuple-element.41.own_ref.refs_0_, ...), custom_call_target="tpu_custom_call" | custom-call | flops 4000000000 | bytes 1048576 | tf_op jit(solution)/shard_map/second/pallas_call | solution.py:446
  42.4 3.0 %collective-permute-done.6.a1 = bf16[816,128]{1,0:T(8,128)(2,1)S(1)} collective-permute-done((bf16[816,128]{1,0:T(8,128)(2,1)S(1)}, bf16[816,128]{1,0:T(8,128)(2,1)S(1)}, u32[]{:S(2)}, u32[]{:S(2)}) %collective-permute-start.6) | collective-permute-done | bytes 208928 | tf_op jit(solution)/shard_map/ppermute | solution.py:393
  45.4 3.7 %shard_map.55 = (bf16[64,4096]{1,0:T(8,128)(2,1)S(1)}, bf16[64,4096]{1,0:T(8,128)(2,1)S(1)}, bf16[128,1024]{1,0:T(8,128)(2,1)S(1)}) custom-call(s32[1]{0:T(128)} %bitcast.index_ref, bf16[8,256,128]{2,1,0:T(8,128)(2,1)S(1)} %get-tuple-element.43.tile_ref, bf16[544,128]{1,0:T(8,128)(2,1)S(1)} %get-tuple-element.41.own_ref.refs_0_, ...), custom_call_target="tpu_custom_call" | custom-call | flops 5000000000 | bytes 1048576 | tf_op jit(solution)/shard_map/pallas_call | solution.py:462
  49.2 1.3 %rest.2 = (bf16[64,4096]{1,0:T(8,128)(2,1)S(1)}, bf16[64,4096]{1,0:T(8,128)(2,1)S(1)}) custom-call(bf16[128,1024]{1,0:T(8,128)(2,1)S(1)} %get-tuple-element.51.merged_ref, bf16[1024,4096]{1,0:T(8,128)(2,1)S(1)} %get-tuple-element.52.w_ref), custom_call_target="tpu_custom_call" | custom-call | flops 1000000000 | bytes 1048576 | tf_op jit(solution)/shard_map/rest/pallas_call | solution.py:473
  51.1 1.7 %middle.1.refs_0_ = f32[2,144,256]{2,1,0:T(8,128)S(1)} custom-call(bf16[8,256,128]{2,1,0:T(8,128)(2,1)S(1)} %get-tuple-element.43.tile_ref, bf16[544,128]{1,0:T(8,128)(2,1)S(1)} %get-tuple-element.41.own_ref.refs_0_, bf16[816,128]{1,0:T(8,128)(2,1)S(1)} %collective-permute-done.6.a1, bf16[816,128]{1,0:T(8,128)(2,1)S(1)} %collective-permute-done.7.a2, ...), custom_call_target="tpu_custom_call" | custom-call | flops 2000000000 | bytes 1048576 | tf_op jit(solution)/shard_map/middle/pallas_call | solution.py:450
  53.0 2.5 %shard_map.56 = (bf16[64,4096]{1,0:T(8,128)(2,1)S(1)}, bf16[64,4096]{1,0:T(8,128)(2,1)S(1)}, bf16[128,1024]{1,0:T(8,128)(2,1)S(1)}) custom-call(s32[1]{0:T(128)} %bitcast.index_ref, bf16[8,256,128]{2,1,0:T(8,128)(2,1)S(1)} %get-tuple-element.43.tile_ref, bf16[544,128]{1,0:T(8,128)(2,1)S(1)} %get-tuple-element.41.own_ref.refs_0_, ...), custom_call_target="tpu_custom_call" | custom-call | flops 5000000000 | bytes 1048576 | tf_op jit(solution)/shard_map/pallas_call | solution.py:462
  55.5 1.3 %rest.3 = (bf16[64,4096]{1,0:T(8,128)(2,1)S(1)}, bf16[64,4096]{1,0:T(8,128)(2,1)S(1)}) custom-call(bf16[128,1024]{1,0:T(8,128)(2,1)S(1)} %get-tuple-element.70.merged_ref, bf16[1024,4096]{1,0:T(8,128)(2,1)S(1)} %get-tuple-element.52.w_ref), custom_call_target="tpu_custom_call" | custom-call | flops 1000000000 | bytes 1048576 | tf_op jit(solution)/shard_map/rest/pallas_call | solution.py:473
  57.4 3.9 %collective-permute-start.14 = (bf16[16,8192]{1,0:T(8,128)(2,1)S(1)}, bf16[16,8192]{1,0:T(8,128)(2,1)S(1)}, u32[]{:S(2)}, u32[]{:S(2)}) collective-permute-start(bf16[16,8192]{1,0:T(8,128)(2,1)S(1)} %get-tuple-element.63), channel_id=1, source_target_pairs={{0,4},{1,5},{2,6},{3,7},{4,0},{5,1},{6,2},{7,3},{8,12},{9,13},{10,... | collective-permute-start | bytes 786440 | tf_op jit(solution)/shard_map/ppermute | solution.py:489
  61.2 1.0 %collective-permute-start.15 = (bf16[16,8192]{1,0:T(8,128)(2,1)S(1)}, bf16[16,8192]{1,0:T(8,128)(2,1)S(1)}, u32[]{:S(2)}, u32[]{:S(2)}) collective-permute-start(bf16[16,8192]{1,0:T(8,128)(2,1)S(1)} %get-tuple-element.64), channel_id=1, source_target_pairs={{0,2},{1,3},{2,4},{3,5},{4,6},{5,7},{6,0},{7,1},{8,10},{9,11},{10,... | collective-permute-start | bytes 786440 | tf_op jit(solution)/shard_map/ppermute | solution.py:489
  62.3 2.2 %collective-permute-start.16 = (bf16[16,8192]{1,0:T(8,128)(2,1)S(1)}, bf16[16,8192]{1,0:T(8,128)(2,1)S(1)}, u32[]{:S(2)}, u32[]{:S(2)}) collective-permute-start(bf16[16,8192]{1,0:T(8,128)(2,1)S(1)} %get-tuple-element.65), channel_id=1, source_target_pairs={{0,6},{1,7},{2,0},{3,1},{4,2},{5,3},{6,4},{7,5},{8,14},{9,15},{10,... | collective-permute-start | bytes 786440 | tf_op jit(solution)/shard_map/ppermute | solution.py:489
  65.7 2.8 %collective-permute-done.14.refs_1_ = bf16[16,8192]{1,0:T(8,128)(2,1)S(1)} collective-permute-done((bf16[16,8192]{1,0:T(8,128)(2,1)S(1)}, bf16[16,8192]{1,0:T(8,128)(2,1)S(1)}, u32[]{:S(2)}, u32[]{:S(2)}) %collective-permute-start.14) | collective-permute-done | bytes 262176 | tf_op jit(solution)/shard_map/ppermute | solution.py:489
  68.4 3.7 %collective-permute-start.21 = (bf16[16,8192]{1,0:T(8,128)(2,1)S(1)}, bf16[16,8192]{1,0:T(8,128)(2,1)S(1)}, u32[]{:S(2)}, u32[]{:S(2)}) collective-permute-start(bf16[16,8192]{1,0:T(8,128)(2,1)S(1)} %get-tuple-element.76), channel_id=1, source_target_pairs={{0,6},{1,7},{2,0},{3,1},{4,2},{5,3},{6,4},{7,5},{8,14},{9,15},{10,... | collective-permute-start | bytes 786440 | tf_op jit(solution)/shard_map/ppermute | solution.py:489
  72.1 2.0 %collective-permute-done.15.refs_2_ = bf16[16,8192]{1,0:T(8,128)(2,1)S(1)} collective-permute-done((bf16[16,8192]{1,0:T(8,128)(2,1)S(1)}, bf16[16,8192]{1,0:T(8,128)(2,1)S(1)}, u32[]{:S(2)}, u32[]{:S(2)}) %collective-permute-start.15) | collective-permute-done | bytes 262176 | tf_op jit(solution)/shard_map/ppermute | solution.py:489
  75.1 4.6 %collective-permute-done.19.refs_5_ = bf16[16,8192]{1,0:T(8,128)(2,1)S(1)} collective-permute-done((bf16[16,8192]{1,0:T(8,128)(2,1)S(1)}, bf16[16,8192]{1,0:T(8,128)(2,1)S(1)}, u32[]{:S(2)}, u32[]{:S(2)}) %collective-permute-start.19) | collective-permute-done | bytes 262176 | tf_op jit(solution)/shard_map/ppermute | solution.py:489
  79.7 5.1 %collective-permute-done.20.refs_6_ = bf16[16,8192]{1,0:T(8,128)(2,1)S(1)} collective-permute-done((bf16[16,8192]{1,0:T(8,128)(2,1)S(1)}, bf16[16,8192]{1,0:T(8,128)(2,1)S(1)}, u32[]{:S(2)}, u32[]{:S(2)}) %collective-permute-start.20) | collective-permute-done | bytes 262176 | tf_op jit(solution)/shard_map/ppermute | solution.py:489
  85.6 1.0 %final.1 = bf16[32,8192]{1,0:T(8,128)(2,1)} custom-call(bf16[16,8192]{1,0:T(8,128)(2,1)S(1)} %get-tuple-element.62.refs_0_, bf16[16,8192]{1,0:T(8,128)(2,1)S(1)} %collective-permute-done.14.refs_1_, bf16[16,8192]{1,0:T(8,128)(2,1)S(1)} %collective-permute-done.15.refs_2_, bf16[16,8192]{1,0:T(8,128)(2,1)S(1)} %collective-permute-done.16.refs_3_, ...), custom_call_target="tpu_custom_call" | custom-call | tf_op jit(solution)/shard_map/final/pallas_call | solution.py:505
  (33 shorter events, 7.7 us)
Async XLA Ops:
  1.0 8.5 %collective-permute-start.2 = (bf16[272,128]{1,0:T(8,128)(2,1)S(1)}, bf16[272,128]{1,0:T(8,128)(2,1)S(1)}, u32[]{:S(2)}, u32[]{:S(2)}) collective-permute-start(bf16[272,128]{1,0:T(8,128)(2,1)S(1)} %get-tuple-element.42), channel_id=1, source_target_pairs={{0,96},{8,104},{16,112},{24,120},{32,0},{40,8},{48,16},{56,24},{64... | collective-permute-start | bytes 208904 | tf_op jit(solution)/shard_map/ppermute | solution.py:393
  1.9 15.6 %collective-permute-start.5 = (bf16[544,128]{1,0:T(8,128)(2,1)S(1)}, bf16[544,128]{1,0:T(8,128)(2,1)S(1)}, u32[]{:S(2)}, u32[]{:S(2)}) collective-permute-start(bf16[544,128]{1,0:T(8,128)(2,1)S(1)} %get-tuple-element.41.own_ref.refs_0_), channel_id=1, source_target_pairs={{0,24},{8,0},{16,8},{24,16},{32,56},{40,32},{48,40},{56,48},{64,88... | collective-permute-start | bytes 417800 | tf_op jit(solution)/shard_map/ppermute | solution.py:393
  4.9 12.6 %collective-permute-start.4 = (bf16[544,128]{1,0:T(8,128)(2,1)S(1)}, bf16[544,128]{1,0:T(8,128)(2,1)S(1)}, u32[]{:S(2)}, u32[]{:S(2)}) collective-permute-start(bf16[544,128]{1,0:T(8,128)(2,1)S(1)} %get-tuple-element.41.own_ref.refs_0_), channel_id=1, source_target_pairs={{0,8},{8,16},{16,24},{24,0},{32,40},{40,48},{48,56},{56,32},{64,72... | collective-permute-start | bytes 417800 | tf_op jit(solution)/shard_map/ppermute | solution.py:393
  4.9 12.6 %collective-permute-start.3 = (bf16[544,128]{1,0:T(8,128)(2,1)S(1)}, bf16[544,128]{1,0:T(8,128)(2,1)S(1)}, u32[]{:S(2)}, u32[]{:S(2)}) collective-permute-start(bf16[544,128]{1,0:T(8,128)(2,1)S(1)} %get-tuple-element.41.own_ref.refs_0_), channel_id=1, source_target_pairs={{0,16},{8,24},{16,0},{24,8},{32,48},{40,56},{48,32},{56,40},{64,80... | collective-permute-start | bytes 417800 | tf_op jit(solution)/shard_map/ppermute | solution.py:393
  7.1 5.0 %collective-permute-start.1 = (bf16[272,128]{1,0:T(8,128)(2,1)S(1)}, bf16[272,128]{1,0:T(8,128)(2,1)S(1)}, u32[]{:S(2)}, u32[]{:S(2)}) collective-permute-start(bf16[272,128]{1,0:T(8,128)(2,1)S(1)} %get-tuple-element.42), channel_id=1, source_target_pairs={{0,32},{8,40},{16,48},{24,56},{32,64},{40,72},{48,80},{56,88},{64,... | collective-permute-start | bytes 208904 | tf_op jit(solution)/shard_map/ppermute | solution.py:393
  9.5 5.8 %collective-permute-start = (bf16[272,128]{1,0:T(8,128)(2,1)S(1)}, bf16[272,128]{1,0:T(8,128)(2,1)S(1)}, u32[]{:S(2)}, u32[]{:S(2)}) collective-permute-start(bf16[272,128]{1,0:T(8,128)(2,1)S(1)} %get-tuple-element.42), channel_id=1, source_target_pairs={{0,64},{8,72},{16,80},{24,88},{32,96},{40,104},{48,112},{56,120},{... | collective-permute-start | bytes 208904 | tf_op jit(solution)/shard_map/ppermute | solution.py:393
  15.4 27.1 %collective-permute-start.8 = (bf16[816,128]{1,0:T(8,128)(2,1)S(1)}, bf16[816,128]{1,0:T(8,128)(2,1)S(1)}, u32[]{:S(2)}, u32[]{:S(2)}) collective-permute-start(bf16[816,128]{1,0:T(8,128)(2,1)S(1)} %join.2), channel_id=1, source_target_pairs={{0,24},{8,0},{16,8},{24,16},{32,56},{40,32},{48,40},{56,48},{64,88... | collective-permute-start | bytes 626696 | tf_op jit(solution)/shard_map/ppermute | solution.py:393
  16.5 25.9 %collective-permute-start.7 = (bf16[816,128]{1,0:T(8,128)(2,1)S(1)}, bf16[816,128]{1,0:T(8,128)(2,1)S(1)}, u32[]{:S(2)}, u32[]{:S(2)}) collective-permute-start(bf16[816,128]{1,0:T(8,128)(2,1)S(1)} %join.2), channel_id=1, source_target_pairs={{0,8},{8,16},{16,24},{24,0},{32,40},{40,48},{48,56},{56,32},{64,72... | collective-permute-start | bytes 626696 | tf_op jit(solution)/shard_map/ppermute | solution.py:393
  17.5 20.5 %collective-permute-start.11 = (bf16[1088,128]{1,0:T(8,128)(2,1)S(1)}, bf16[1088,128]{1,0:T(8,128)(2,1)S(1)}, u32[]{:S(2)}, u32[]{:S(2)}) collective-permute-start(bf16[1088,128]{1,0:T(8,128)(2,1)S(1)} %join.3), channel_id=1, source_target_pairs={{0,96},{8,104},{16,112},{24,120},{32,0},{40,8},{48,16},{56,24},{64... | collective-permute-start | bytes 835592 | tf_op jit(solution)/shard_map/ppermute | solution.py:393
  17.6 20.6 %collective-permute-start.10 = (bf16[1088,128]{1,0:T(8,128)(2,1)S(1)}, bf16[1088,128]{1,0:T(8,128)(2,1)S(1)}, u32[]{:S(2)}, u32[]{:S(2)}) collective-permute-start(bf16[1088,128]{1,0:T(8,128)(2,1)S(1)} %join.3), channel_id=1, source_target_pairs={{0,32},{8,40},{16,48},{24,56},{32,64},{40,72},{48,80},{56,88},{64,... | collective-permute-start | bytes 835592 | tf_op jit(solution)/shard_map/ppermute | solution.py:393
  20.8 17.4 %collective-permute-start.9 = (bf16[1088,128]{1,0:T(8,128)(2,1)S(1)}, bf16[1088,128]{1,0:T(8,128)(2,1)S(1)}, u32[]{:S(2)}, u32[]{:S(2)}) collective-permute-start(bf16[1088,128]{1,0:T(8,128)(2,1)S(1)} %join.3), channel_id=1, source_target_pairs={{0,64},{8,72},{16,80},{24,88},{32,96},{40,104},{48,112},{56,120},{... | collective-permute-start | bytes 835592 | tf_op jit(solution)/shard_map/ppermute | solution.py:393
  38.1 7.4 %collective-permute-start.6 = (bf16[816,128]{1,0:T(8,128)(2,1)S(1)}, bf16[816,128]{1,0:T(8,128)(2,1)S(1)}, u32[]{:S(2)}, u32[]{:S(2)}) collective-permute-start(bf16[816,128]{1,0:T(8,128)(2,1)S(1)} %join.2), channel_id=1, source_target_pairs={{0,16},{8,24},{16,0},{24,8},{32,48},{40,56},{48,32},{56,40},{64,80... | collective-permute-start | bytes 626696 | tf_op jit(solution)/shard_map/ppermute | solution.py:393
  49.1 3.6 %collective-permute-start.12 = (bf16[64,4096]{1,0:T(8,128)(2,1)S(1)}, bf16[64,4096]{1,0:T(8,128)(2,1)S(1)}, u32[]{:S(2)}, u32[]{:S(2)}) collective-permute-start(bf16[64,4096]{1,0:T(8,128)(2,1)S(1)} %get-tuple-element.50), channel_id=1, source_target_pairs={{0,1},{1,0},{2,3},{3,2},{4,5},{5,4},{6,7},{7,6},{8,9},{9,8},{10,11... | collective-permute-start | bytes 1572872 | tf_op jit(solution)/shard_map/ppermute | solution.py:486
  50.5 2.3 %collective-permute-start.13 = (bf16[64,4096]{1,0:T(8,128)(2,1)S(1)}, bf16[64,4096]{1,0:T(8,128)(2,1)S(1)}, u32[]{:S(2)}, u32[]{:S(2)}) collective-permute-start(bf16[64,4096]{1,0:T(8,128)(2,1)S(1)} %get-tuple-element.57), channel_id=1, source_target_pairs={{0,1},{1,0},{2,3},{3,2},{4,5},{5,4},{6,7},{7,6},{8,9},{9,8},{10,11... | collective-permute-start | bytes 1572872 | tf_op jit(solution)/shard_map/ppermute | solution.py:486
  56.8 7.7 %collective-permute-start.17 = (bf16[64,4096]{1,0:T(8,128)(2,1)S(1)}, bf16[64,4096]{1,0:T(8,128)(2,1)S(1)}, u32[]{:S(2)}, u32[]{:S(2)}) collective-permute-start(bf16[64,4096]{1,0:T(8,128)(2,1)S(1)} %get-tuple-element.69), channel_id=1, source_target_pairs={{0,1},{1,0},{2,3},{3,2},{4,5},{5,4},{6,7},{7,6},{8,9},{9,8},{10,11... | collective-permute-start | bytes 1572872 | tf_op jit(solution)/shard_map/ppermute | solution.py:486
  57.1 7.4 %collective-permute-start.18 = (bf16[64,4096]{1,0:T(8,128)(2,1)S(1)}, bf16[64,4096]{1,0:T(8,128)(2,1)S(1)}, u32[]{:S(2)}, u32[]{:S(2)}) collective-permute-start(bf16[64,4096]{1,0:T(8,128)(2,1)S(1)} %get-tuple-element.72), channel_id=1, source_target_pairs={{0,1},{1,0},{2,3},{3,2},{4,5},{5,4},{6,7},{7,6},{8,9},{9,8},{10,11... | collective-permute-start | bytes 1572872 | tf_op jit(solution)/shard_map/ppermute | solution.py:486
  57.4 11.1 %collective-permute-start.14 = (bf16[16,8192]{1,0:T(8,128)(2,1)S(1)}, bf16[16,8192]{1,0:T(8,128)(2,1)S(1)}, u32[]{:S(2)}, u32[]{:S(2)}) collective-permute-start(bf16[16,8192]{1,0:T(8,128)(2,1)S(1)} %get-tuple-element.63), channel_id=1, source_target_pairs={{0,4},{1,5},{2,6},{3,7},{4,0},{5,1},{6,2},{7,3},{8,12},{9,13},{10,... | collective-permute-start | bytes 786440 | tf_op jit(solution)/shard_map/ppermute | solution.py:489
  61.2 12.9 %collective-permute-start.15 = (bf16[16,8192]{1,0:T(8,128)(2,1)S(1)}, bf16[16,8192]{1,0:T(8,128)(2,1)S(1)}, u32[]{:S(2)}, u32[]{:S(2)}) collective-permute-start(bf16[16,8192]{1,0:T(8,128)(2,1)S(1)} %get-tuple-element.64), channel_id=1, source_target_pairs={{0,2},{1,3},{2,4},{3,5},{4,6},{5,7},{6,0},{7,1},{8,10},{9,11},{10,... | collective-permute-start | bytes 786440 | tf_op jit(solution)/shard_map/ppermute | solution.py:489
  62.3 12.8 %collective-permute-start.16 = (bf16[16,8192]{1,0:T(8,128)(2,1)S(1)}, bf16[16,8192]{1,0:T(8,128)(2,1)S(1)}, u32[]{:S(2)}, u32[]{:S(2)}) collective-permute-start(bf16[16,8192]{1,0:T(8,128)(2,1)S(1)} %get-tuple-element.65), channel_id=1, source_target_pairs={{0,6},{1,7},{2,0},{3,1},{4,2},{5,3},{6,4},{7,5},{8,14},{9,15},{10,... | collective-permute-start | bytes 786440 | tf_op jit(solution)/shard_map/ppermute | solution.py:489
  64.7 15.0 %collective-permute-start.19 = (bf16[16,8192]{1,0:T(8,128)(2,1)S(1)}, bf16[16,8192]{1,0:T(8,128)(2,1)S(1)}, u32[]{:S(2)}, u32[]{:S(2)}) collective-permute-start(bf16[16,8192]{1,0:T(8,128)(2,1)S(1)} %get-tuple-element.74), channel_id=1, source_target_pairs={{0,4},{1,5},{2,6},{3,7},{4,0},{5,1},{6,2},{7,3},{8,12},{9,13},{10,... | collective-permute-start | bytes 786440 | tf_op jit(solution)/shard_map/ppermute | solution.py:489
  64.8 20.0 %collective-permute-start.20 = (bf16[16,8192]{1,0:T(8,128)(2,1)S(1)}, bf16[16,8192]{1,0:T(8,128)(2,1)S(1)}, u32[]{:S(2)}, u32[]{:S(2)}) collective-permute-start(bf16[16,8192]{1,0:T(8,128)(2,1)S(1)} %get-tuple-element.75), channel_id=1, source_target_pairs={{0,2},{1,3},{2,4},{3,5},{4,6},{5,7},{6,0},{7,1},{8,10},{9,11},{10,... | collective-permute-start | bytes 786440 | tf_op jit(solution)/shard_map/ppermute | solution.py:489
  68.4 17.2 %collective-permute-start.21 = (bf16[16,8192]{1,0:T(8,128)(2,1)S(1)}, bf16[16,8192]{1,0:T(8,128)(2,1)S(1)}, u32[]{:S(2)}, u32[]{:S(2)}) collective-permute-start(bf16[16,8192]{1,0:T(8,128)(2,1)S(1)} %get-tuple-element.76), channel_id=1, source_target_pairs={{0,6},{1,7},{2,0},{3,1},{4,2},{5,3},{6,4},{7,5},{8,14},{9,15},{10,... | collective-permute-start | bytes 786440 | tf_op jit(solution)/shard_map/ppermute | solution.py:489

commit v3 on v2

--- a/solution.py
+++ b/solution.py
@@ -24,7 +24,7 @@
 GROUP = 4
 HEADROOM = 60.0
 NW = 4
-HOPS = (2, 1, 3)
+HOPS = (1, 3, 2)
 
 
 VMEM = pl.BlockSpec(memory_space=pltpu.VMEM)
@@ -36,7 +36,7 @@
     return jax.ShapeDtypeStruct(shape, dtype)
 
 
-def pack_kernel(pos_hbm, k_hbm, v_hbm, out_ref, half_ref, pos_ref, k_ref, v_ref, sems):
+def pack_kernel(pos_hbm, k_hbm, v_hbm, out_ref, pos_ref, k_ref, v_ref, sems):
     copies = [
         pltpu.make_async_copy(src, dst, sems.at[i])
         for i, (src, dst) in enumerate(((v_hbm, v_ref), (k_hbm, k_ref), (pos_hbm, pos_ref)))
@@ -53,14 +53,12 @@
         out_ref[base + 128:base + 256] = v_ref[rows, :].T
         ids = jnp.full((16, 128), span, jnp.float32).astype(jnp.bfloat16)
         out_ref[base + 256:base + PACK] = ids
-    half_ref[...] = out_ref[0:PACK]
-
-
-def join_kernel(*refs):
+
+
+def join_kernel(part, *refs):
     out_ref = refs[-1]
     for i, ref in enumerate(refs[:-1]):
-        rows = ref.shape[0]
-        out_ref[i * PACK:(i + 1) * PACK] = ref[rows - PACK:rows]
+        out_ref[i * PACK:(i + 1) * PACK] = ref[part * PACK:(part + 1) * PACK]
 
 
 def query_tile(q_ref, chunk, s, quad):
@@ -182,8 +180,7 @@
     fetch_q = pltpu.make_async_copy(q_hbm, q_ref, sems.at[NW])
     fetch_q.start()
     fetch_w = fetch_half(0, w_hbm, w_ref, sems)
-    blocks = [(ref, j) for ref in (own_ref, y1, y2, y3) for j in range(2)]
-    blocks += [(ref, 0) for ref in (x1, x2, x3)]
+    blocks = [(ref, j) for ref in (own_ref, x1, x2, x3, y1, y2, y3) for j in range(2)]
     store_keys(kv_ref, blocks)
     ids = [span_id(ref, j) for ref, j in blocks]
     counts = [visible_list(ref, ids, ids[s]) for s, ref in enumerate((list0, list1))]
@@ -225,37 +222,6 @@
         copy.wait()
 
 
-def second_kernel(w_hbm, tile_ref, own_ref, b1, b2, b3, m_in, acc_in, m_ref, acc_ref, w_ref,
-                  kv_ref, peak_ref, even_ref, odd_ref, list0, list1, sems):
-    fetch_w = fetch_half(1, w_hbm, w_ref, sems)
-    blocks = [(ref, j) for ref in (b1, b2, b3) for j in range(4)]
-    store_keys(kv_ref, blocks)
-    ids = [span_id(ref, j) for ref, j in blocks]
-    lists = (list0, list1)
-    counts = [visible_list(lists[s], ids, span_id(own_ref, s)) for s in range(2)]
-    units = [[chunk * 4 + s * 2 + quad for chunk in range(2) for quad in range(2)] for s in range(2)]
-    queries = [[tile_ref[u] for u in units[s]] for s in range(2)]
-
-    def reset():
-        m_ref[...] = m_in[...]
-        acc_ref[...] = acc_in[...]
-
-    reset()
-    peak_ref[...] = m_in[...]
-    for s in range(2):
-        fast_walk(kv_ref, lists[s], counts[s], queries[s], units[s], m_ref, peak_ref, acc_ref,
-                  (even_ref, odd_ref))
-
-    @pl.when(overshoot(peak_ref, m_ref, units[0] + units[1]))
-    def _():
-        reset()
-        for s in range(2):
-            slow_walk(kv_ref, lists[s], counts[s], queries[s], units[s], m_ref, acc_ref)
-
-    for copy in fetch_w:
-        copy.wait()
-
-
 def rest_of_attention(chunk, spans, tile_ref, own_ref, far, m_in, acc_in, kv_ref, m_ref, peak_ref,
                       acc_ref, even_ref, odd_ref, lists):
     blocks = [(ref, j) for ref in far for j in range(3)]
@@ -282,6 +248,16 @@
         reset()
         for n in range(len(spans)):
             slow_walk(kv_ref, lists[n], counts[n], queries[n], units[n], m_ref, acc_ref)
+
+
+def first_partner(z, core):
+    return (((z + core) ^ 1) - core + NZ) % NZ
+
+
+def place_of(z_to, core_to, z, core):
+    near = jnp.where(first_partner(z, core_to) == z_to, 2, 1)
+    slot = jnp.where(z_to == z, 0, jnp.where((z_to + 2) % NZ == z, 3, near))
+    return (core_to ^ core) * NZ + slot
 
 
 def finish(s, acc_ref, base, index_ref, merged_ref):
@@ -295,7 +271,7 @@
                 h = quad * QUAD + half * 2 + i
                 for t in range(4):
                     owner = s * 4 + t
-                    place = ((owner % NCORE) ^ core) * NZ + (owner // NCORE - z + NZ) % NZ
+                    place = place_of(owner // NCORE, owner % NCORE, z, core)
                     where = pl.multiple_of(place * PIECE, PIECE)
                     at = i * 64 + t * PIECE
                     merged_ref[pl.ds(where, PIECE), h * HD:(h + 1) * HD] = rows[at:at + PIECE]
@@ -311,39 +287,51 @@
         send_ref[:, at] = part[64:]
 
 
-def middle_kernel(chunk, spans, tile_ref, own_ref, a1, a2, a3, m_in, acc_in, acc_ref,
+def middle_kernel(chunk, spans, tile_ref, own_ref, a1, a2, a3, b1, b2, b3, m_in, acc_in, acc_ref,
                   kv_ref, m_ref, peak_ref, even_ref, odd_ref, list0, list1):
-    rest_of_attention(chunk, spans, tile_ref, own_ref, (a1, a2, a3), m_in, acc_in, kv_ref,
+    rest_of_attention(chunk, spans, tile_ref, own_ref, (a1, a2, a3, b1, b2, b3), m_in, acc_in, kv_ref,
                       m_ref, peak_ref, acc_ref, even_ref, odd_ref, (list0, list1))
 
 
-def last_kernel(chunk, spans, done, index_ref, tile_ref, own_ref, a1, a2, a3, m_in, acc_in,
+def last_kernel(chunk, spans, done, index_ref, tile_ref, own_ref, a1, a2, a3, b1, b2, b3, m_in, acc_in,
                 w_ref, *refs):
-    acc_done = refs[0] if done else None
+    if done:
+        acc_done = refs[0]
+    else:
+        w_hbm, w_next, sems = refs[0], refs[4], refs[-1]
+        refs = refs[:4] + refs[5:-1]
+        fetch_w = fetch_half(1, w_hbm, w_next, sems)
     (keep_ref, send_ref, merged_ref, acc_ref, kv_ref, m_ref, peak_ref, even_ref, odd_ref,
      list0, list1) = refs[-11:]
-    rest_of_attention(chunk, spans, tile_ref, own_ref, (a1, a2, a3), m_in, acc_in, kv_ref,
+    rest_of_attention(chunk, spans, tile_ref, own_ref, (a1, a2, a3, b1, b2, b3), m_in, acc_in, kv_ref,
                       m_ref, peak_ref, acc_ref, even_ref, odd_ref, (list0, list1))
     for n, s in enumerate(spans):
         finish(s, acc_ref, 2 * n, index_ref, merged_ref)
     for n, s in enumerate(done):
         finish(s, acc_done, 2 * n, index_ref, merged_ref)
     project(merged_ref, w_ref, keep_ref, send_ref)
-
-
-def pair_kernel(keep_a, got_a, keep_b, got_b, *out_refs):
+    if not done:
+        for copy in fetch_w:
+            copy.wait()
+
+
+def pair_kernel(keep_a, got_a, keep_b, got_b, stay_ref, send_ref):
     for half, keep_ref, got_ref in ((0, keep_a, got_a), (1, keep_b, got_b)):
-        total = keep_ref[...].astype(jnp.float32) + got_ref[...].astype(jnp.float32)
+        total = (keep_ref[...].astype(jnp.float32) + got_ref[...]).astype(jnp.bfloat16)
         columns = slice(half * DOUT // 2, (half + 1) * DOUT // 2)
-        for d in range(NZ):
-            out_refs[d][:, columns] = total[d * PIECE:(d + 1) * PIECE].astype(jnp.bfloat16)
-
-
-def final_kernel(*refs):
-    out_ref = refs[-1]
-    for chunk in range(2):
-        parts = [r[...].astype(jnp.float32) for r in refs[chunk * NZ:(chunk + 1) * NZ]]
-        total = (parts[0] + parts[1]) + (parts[2] + parts[3])
+        stay_ref[:, columns] = total[:2 * PIECE]
+        send_ref[:, columns] = total[2 * PIECE:]
+
+
+def fold_kernel(stay_ref, got_ref, mine_ref, send_ref):
+    total = (stay_ref[...].astype(jnp.float32) + got_ref[...]).astype(jnp.bfloat16)
+    mine_ref[...] = total[:PIECE]
+    send_ref[...] = total[PIECE:]
+
+
+def final_kernel(mine0, got0, mine1, got1, out_ref):
+    for chunk, mine_ref, got_ref in ((0, mine0, got0), (1, mine1, got1)):
+        total = mine_ref[...].astype(jnp.float32) + got_ref[...]
         out_ref[chunk * PIECE:(chunk + 1) * PIECE, :] = total.astype(jnp.bfloat16)
 
 
@@ -366,9 +354,13 @@
     ]
 
 
-def tp_route(dz, swap):
+def swap_route():
+    return [(t, t ^ 1) for t in range(NZ * NCORE)]
+
+
+def step_route(step):
     return [
-        (z * NCORE + c, ((z + dz) % NZ) * NCORE + (c ^ swap))
+        (z * NCORE + c, first_partner(z, c ^ step) * NCORE + c)
         for z in range(NZ) for c in range(NCORE)
     ]
 
@@ -377,9 +369,8 @@
     bf16, f32 = jnp.bfloat16, jnp.float32
     index = lax.axis_index("tp").reshape(1)
 
-    own, half = pl.pallas_call(
-        pack_kernel, in_specs=[HBM] * 3, out_specs=[VMEM] * 2,
-        out_shape=[struct((2 * PACK, HD), bf16), struct((PACK, HD), bf16)],
+    own = pl.pallas_call(
+        pack_kernel, in_specs=[HBM] * 3, out_specs=VMEM, out_shape=struct((2 * PACK, HD), bf16),
         name="pack", compiler_params=params(2),
         scratch_shapes=[
             pltpu.SMEM((2 * SPAN,), jnp.int32), pltpu.VMEM((2 * SPAN, HD), bf16),
@@ -393,18 +384,18 @@
             moved.append(lax.ppermute(block, "ctx", ctx_route(dx * d, dy * d)))
         return moved
 
-    def join(*blocks):
+    def join(part, *blocks):
         return pl.pallas_call(
-            join_kernel, in_specs=[VMEM] * len(blocks), out_specs=VMEM,
+            functools.partial(join_kernel, part), in_specs=[VMEM] * len(blocks), out_specs=VMEM,
             out_shape=struct((len(blocks) * PACK, HD), bf16), name="join",
             compiler_params=params(2),
         )(*blocks)
 
     ys = shifts(own, 0, 1)
-    xs = shifts(half, 1, 0)
-    column = join(own, *ys)
+    xs = shifts(own, 1, 0)
+    column = join(1, *ys)
     fb = shifts(column, 1, 0)
-    fa = shifts(join(*xs), 0, 1)
+    fa = shifts(join(0, *xs), 0, 1)
 
     def walk_scratch(slots, units, width):
         return [
@@ -417,7 +408,7 @@
             pltpu.SMEM((32,), jnp.int32),
         ]
 
-    scratch = walk_scratch(11, 8, 4)
+    scratch = walk_scratch(14, 8, 4)
     first = pl.pallas_call(
         first_kernel, in_specs=[HBM] * 2 + [VMEM] * 7, out_specs=[VMEM] * 4,
         out_shape=[
@@ -433,41 +424,32 @@
         in_hbm(queries), in_hbm(out_weight), own, *xs, *ys
     )
 
-    scratch = walk_scratch(12, 8, 4)
-    second = pl.pallas_call(
-        second_kernel, in_specs=[HBM] + [VMEM] * 7, out_specs=[VMEM] * 3,
-        out_shape=[
-            struct((8, 8, 256), f32), struct((8, 144, 256), f32), struct((1024, DOUT // 2), bf16),
-        ],
-        scratch_shapes=scratch[:1] + scratch[2:] + [pltpu.SemaphoreType.DMA((NW,))],
-        compiler_params=params(14), name="second",
-        cost_estimate=estimate(4 * 10 ** 9, 1 << 20),
-    )
-    maxima, acc, weight_b = second(in_hbm(out_weight), tiles, own, *fb, maxima, acc)
-
     def middle(chunk, spans, acc):
         n = 2 * len(spans)
         return pl.pallas_call(
             functools.partial(middle_kernel, chunk, spans),
-            in_specs=[VMEM] * 7, out_specs=VMEM, out_shape=struct((n, 144, 256), f32),
-            scratch_shapes=walk_scratch(9, n, 2),
+            in_specs=[VMEM] * 10, out_specs=VMEM, out_shape=struct((n, 144, 256), f32),
+            scratch_shapes=walk_scratch(18, n, 2),
             compiler_params=params(14), name="middle",
             cost_estimate=estimate(2 * 10 ** 9, 1 << 20),
-        )(tiles, own, *fa, maxima, acc)
+        )(tiles, own, *fa, *fb, maxima, acc)
 
     halves = [struct((64, DOUT // 2), bf16)] * 2
 
-    def last(chunk, spans, acc, done=(), acc_done=()):
+    def last(chunk, spans, acc, done, extra):
         n = 2 * len(spans)
+        outs = halves + [struct((128, 1024), bf16)]
+        scratch = [pltpu.VMEM((n, 144, 256), f32)] + walk_scratch(18, n, 2)
+        if not done:
+            outs = outs + [struct((1024, DOUT // 2), bf16)]
+            scratch = scratch + [pltpu.SemaphoreType.DMA((NW,))]
         return pl.pallas_call(
             functools.partial(last_kernel, chunk, spans, done),
-            in_specs=[SMEM] + [VMEM] * (8 + len(acc_done)),
-            out_specs=[VMEM] * 3,
-            out_shape=halves + [struct((128, 1024), bf16)],
-            scratch_shapes=[pltpu.VMEM((n, 144, 256), f32)] + walk_scratch(9, n, 2),
+            in_specs=[SMEM] + [VMEM] * 11 + [VMEM if done else HBM],
+            out_specs=[VMEM] * len(outs), out_shape=outs, scratch_shapes=scratch,
             compiler_params=params(14),
             cost_estimate=estimate(5 * 10 ** 9, 1 << 20),
-        )(index, tiles, own, *fa, maxima, acc, weight_a, *acc_done)
+        )(index, tiles, own, *fa, *fb, maxima, acc, weight_a, extra)
 
     def rest(merged):
         return pl.pallas_call(
@@ -475,37 +457,41 @@
             compiler_params=params(6), name="rest", cost_estimate=estimate(10 ** 9, 1 << 20),
         )(merged, weight_b)
 
-    def pair_sum(*blocks):
+    def call(kernel, rows, blocks):
         return pl.pallas_call(
-            pair_kernel, in_specs=[VMEM] * 4, out_specs=[VMEM] * NZ,
-            out_shape=[struct((PIECE, DOUT), bf16)] * NZ, name="pair",
-            compiler_params=params(6),
+            kernel, in_specs=[VMEM] * len(blocks), out_specs=[VMEM] * len(rows),
+            out_shape=[struct((r, DOUT), bf16) for r in rows],
+            compiler_params=params(6), cost_estimate=estimate(10 ** 6, 1 << 20),
         )(*blocks)
 
     def swap(block):
-        return lax.ppermute(block, "tp", tp_route(0, 1))
-
-    def exchange(parts):
-        return [parts[0]] + [lax.ppermute(parts[d], "tp", tp_route(d, 0)) for d in HOPS]
-
-    keep0a, send0a, merged0 = last(0, (0, 1), acc)
+        return lax.ppermute(block, "tp", swap_route())
+
+    def step(number, block):
+        return lax.ppermute(block, "tp", step_route(number))
+
+    keep0a, send0a, merged0, weight_b = last(0, (0, 1), acc, (), in_hbm(out_weight))
     got0a = swap(send0a)
     keep0b, send0b = rest(merged0)
     send0b, acc1 = lax.optimization_barrier((send0b, acc))
     got0b = swap(send0b)
     acc_mid = middle(1, (0,), acc1)
     keep0b, acc_mid = lax.optimization_barrier((keep0b, acc_mid))
-    parts0 = pair_sum(keep0a, got0a, keep0b, got0b)
-    *parts0, acc2 = lax.optimization_barrier((*parts0, acc))
-    pieces0 = exchange(parts0)
-    keep1a, send1a, merged1 = last(1, (1,), acc2, (0,), (acc_mid,))
+    stay0, out0 = call(pair_kernel, (32, 32), (keep0a, got0a, keep0b, got0b))
+    stay0, out0, acc2 = lax.optimization_barrier((stay0, out0, acc))
+    in0 = step(0, out0)
+    keep1a, send1a, merged1 = last(1, (1,), acc2, (0,), acc_mid)
     got1a = swap(send1a)
     keep1b, send1b = rest(merged1)
-    pieces1 = exchange(pair_sum(keep1a, got1a, keep1b, swap(send1b)))
-    return pl.pallas_call(
-        final_kernel, in_specs=[VMEM] * (2 * NZ), out_specs=VMEM,
-        out_shape=struct((2 * PIECE, DOUT), bf16), name="final", compiler_params=params(6),
-    )(*pieces0, *pieces1)
+    in0, send1b = lax.optimization_barrier((in0, send1b))
+    got1b = swap(send1b)
+    mine0, out0 = call(fold_kernel, (16, 16), (stay0, in0))
+    in0 = step(1, out0)
+    stay1, out1 = call(pair_kernel, (32, 32), (keep1a, got1a, keep1b, got1b))
+    in1 = step(0, out1)
+    mine1, out1 = call(fold_kernel, (16, 16), (stay1, in1))
+    in1 = step(1, out1)
+    return call(final_kernel, (32,), (mine0, in0, mine1, in1))[0]
 
 
 def solution(mesh):

time: 86.8 us -> 95.9 us (1.10)
  Pallas kernels: 34.4 us -> 37.9 us
  starting transfers between devices: 27.2 us -> 30.2 us
  waiting for transfers between devices: 24.9 us -> 27.5 us
    pallas_call x1, Pallas kernels: 17.2 us -> 22.3 us  [on_device(): first(in_hbm(queries), in_hbm(out_weight), own, *xs, *ys)]
    pallas_call x7 -> x8, Pallas kernels: 6.8 us -> 2.66 us  [the longest x5 1.65 us: call(): pl.pallas_call(kernel, in_specs=[VMEM] * len(blocks), out_specs=[VMEM] *...]
    ppermute x12, starting transfers between devices: 14.2 us -> 17.9 us  [shifts(): moved.append(lax.ppermute(block, 'ctx', ctx_route(dx * d, dy * d)))]
    ppermute x12, waiting for transfers between devices: 8.64 us -> 12 us  [shifts(): moved.append(lax.ppermute(block, 'ctx', ctx_route(dx * d, dy * d)))]
    pallas_call x2, Pallas kernels: 6.17 us -> 8.39 us  [last(): pl.pallas_call(functools.partial(last_kernel, chunk, spans, done), in_spe...]
    ppermute x10 -> x8, waiting for transfers between devices: 16.2 us -> 15.5 us  [the longest x4 14 us: step(): return lax.ppermute(block, 'tp', step_route(number))]
    ppermute x10 -> x8, starting transfers between devices: 13 us -> 12.3 us  [the longest x4 8.54 us: step(): return lax.ppermute(block, 'tp', step_route(number))]
  transfers between devices with their start and end apart: 22 -> 20, of which waited for: 9 -> 9; matrix products, arithmetic and copies ran while one was open for 0% -> 0% of each run, Pallas kernels for 28% -> 32%
where the time goes in v3:
time: 95.9 us; the launch traced here: 95.7 us
  Pallas kernels  37.9 us (40%)
  starting transfers between devices  30.2 us (31%)
  waiting for transfers between devices  27.5 us (29%)
    pallas_call x1, Pallas kernels, on_device(): first(in_hbm(queries), in_hbm(out_weight), own, *xs, *ys)  22.3 us
    ppermute x12, starting transfers between devices, shifts(): moved.append(lax.ppermute(block, 'ctx', ctx_route(dx * d, dy * d)))  17.9 us
    ppermute x4, waiting for transfers between devices, step(): return lax.ppermute(block, 'tp', step_route(number))  14 us
    ppermute x12, waiting for transfers between devices, shifts(): moved.append(lax.ppermute(block, 'ctx', ctx_route(dx * d, dy * d)))  12 us
    ppermute x4, starting transfers between devices, step(): return lax.ppermute(block, 'tp', step_route(number))  8.54 us
    pallas_call x2, Pallas kernels, last(): pl.pallas_call(functools.partial(last_kernel, chunk, spans, done), in_spe...  8.39 us
    ppermute x4, starting transfers between devices, swap(): return lax.ppermute(block, 'tp', swap_route())  3.75 us
    pallas_call x2, Pallas kernels, rest(): pl.pallas_call(project, in_specs=[VMEM] * 2, out_specs=[VMEM] * 2, out_sh...  2.56 us
  transfers between devices with their start and end apart: 20, of which 9 were waited for; matrix products, arithmetic and copies ran while one was open for 0% of the time, Pallas kernels for 32%

profile of v3, /device:TPU:6, one launch (start us, length us, event | category | flops | bytes accessed | tf_op | source)
XLA Modules:
  0.0 95.7 jit_solution(17138077917390849865)
XLA Ops:
  1.0 3.3 %collective-permute-start.5 = (bf16[544,128]{1,0:T(8,128)(2,1)S(1)}, bf16[544,128]{1,0:T(8,128)(2,1)S(1)}, u32[]{:S(2)}, u32[]{:S(2)}) collective-permute-start(bf16[544,128]{1,0:T(8,128)(2,1)S(1)} %pack.1.own_ref), channel_id=1, source_target_pairs={{0,16},{8,24},{16,0},{24,8},{32,48},{40,56},{48,32},{56,40},{64,80... | collective-permute-start | bytes 417800 | tf_op jit(solution)/shard_map/ppermute | solution.py:384
  6.3 2.5 %collective-permute-done.5.y3.refs_2_ = bf16[544,128]{1,0:T(8,128)(2,1)S(1)} collective-permute-done((bf16[544,128]{1,0:T(8,128)(2,1)S(1)}, bf16[544,128]{1,0:T(8,128)(2,1)S(1)}, u32[]{:S(2)}, u32[]{:S(2)}) %collective-permute-start.5) | collective-permute-done | bytes 139296 | tf_op jit(solution)/shard_map/ppermute | solution.py:384
  8.8 2.5 %collective-permute-done.4.y2.refs_1_ = bf16[544,128]{1,0:T(8,128)(2,1)S(1)} collective-permute-done((bf16[544,128]{1,0:T(8,128)(2,1)S(1)}, bf16[544,128]{1,0:T(8,128)(2,1)S(1)}, u32[]{:S(2)}, u32[]{:S(2)}) %collective-permute-start.4) | collective-permute-done | bytes 139296 | tf_op jit(solution)/shard_map/ppermute | solution.py:384
  11.6 1.5 %collective-permute-start.11 = (bf16[816,128]{1,0:T(8,128)(2,1)S(1)}, bf16[816,128]{1,0:T(8,128)(2,1)S(1)}, u32[]{:S(2)}, u32[]{:S(2)}) collective-permute-start(bf16[816,128]{1,0:T(8,128)(2,1)S(1)} %join.3), channel_id=1, source_target_pairs={{0,64},{8,72},{16,80},{24,88},{32,96},{40,104},{48,112},{56,120},{... | collective-permute-start | bytes 626696 | tf_op jit(solution)/shard_map/ppermute | solution.py:384
  13.1 2.1 %collective-permute-start.2 = (bf16[544,128]{1,0:T(8,128)(2,1)S(1)}, bf16[544,128]{1,0:T(8,128)(2,1)S(1)}, u32[]{:S(2)}, u32[]{:S(2)}) collective-permute-start(bf16[544,128]{1,0:T(8,128)(2,1)S(1)} %pack.1.own_ref), channel_id=1, source_target_pairs={{0,64},{8,72},{16,80},{24,88},{32,96},{40,104},{48,112},{56,120},{... | collective-permute-start | bytes 417800 | tf_op jit(solution)/shard_map/ppermute | solution.py:384
  16.1 2.4 %collective-permute-start = (bf16[544,128]{1,0:T(8,128)(2,1)S(1)}, bf16[544,128]{1,0:T(8,128)(2,1)S(1)}, u32[]{:S(2)}, u32[]{:S(2)}) collective-permute-start(bf16[544,128]{1,0:T(8,128)(2,1)S(1)} %pack.1.own_ref), channel_id=1, source_target_pairs={{0,32},{8,40},{16,48},{24,56},{32,64},{40,72},{48,80},{56,88},{64,... | collective-permute-start | bytes 417800 | tf_op jit(solution)/shard_map/ppermute | solution.py:384
  18.5 5.8 %collective-permute-done.2.x3.refs_2_ = bf16[544,128]{1,0:T(8,128)(2,1)S(1)} collective-permute-done((bf16[544,128]{1,0:T(8,128)(2,1)S(1)}, bf16[544,128]{1,0:T(8,128)(2,1)S(1)}, u32[]{:S(2)}, u32[]{:S(2)}) %collective-permute-start.2) | collective-permute-done | bytes 139296 | tf_op jit(solution)/shard_map/ppermute | solution.py:384
  25.1 3.7 %collective-permute-start.8 = (bf16[816,128]{1,0:T(8,128)(2,1)S(1)}, bf16[816,128]{1,0:T(8,128)(2,1)S(1)}, u32[]{:S(2)}, u32[]{:S(2)}) collective-permute-start(bf16[816,128]{1,0:T(8,128)(2,1)S(1)} %join.2), channel_id=1, source_target_pairs={{0,16},{8,24},{16,0},{24,8},{32,48},{40,56},{48,32},{56,40},{64,80... | collective-permute-start | bytes 626696 | tf_op jit(solution)/shard_map/ppermute | solution.py:384
  28.8 1.2 %collective-permute-start.7 = (bf16[816,128]{1,0:T(8,128)(2,1)S(1)}, bf16[816,128]{1,0:T(8,128)(2,1)S(1)}, u32[]{:S(2)}, u32[]{:S(2)}) collective-permute-start(bf16[816,128]{1,0:T(8,128)(2,1)S(1)} %join.2), channel_id=1, source_target_pairs={{0,24},{8,0},{16,8},{24,16},{32,56},{40,32},{48,40},{56,48},{64,88... | collective-permute-start | bytes 626696 | tf_op jit(solution)/shard_map/ppermute | solution.py:384
  30.9 22.3 %first.1 = (f32[8,8,256]{2,1,0:T(8,128)S(1)}, f32[8,144,256]{2,1,0:T(8,128)S(1)}, bf16[8,256,128]{2,1,0:T(8,128)(2,1)S(1)}, bf16[1024,4096]{1,0:T(8,128)(2,1)S(1)}) custom-call(bf16[256,1024]{1,0:T(8,128)(2,1)} %q_hbm.1, bf16[1024,8192]{1,0:T(8,128)(2,1)} %refs_0_.1, bf16[544,128]{1,0:T(8,128)(2,1)S(1)} %pack.1.own_ref, ...), custom_call_target="tpu_custom_call" | custom-call | flops 4000000000 | bytes 1048576 | tf_op jit(solution)/shard_map/first/pallas_call | solution.py:423
  53.2 5.3 %shard_map.55 = (bf16[64,4096]{1,0:T(8,128)(2,1)S(1)}, bf16[64,4096]{1,0:T(8,128)(2,1)S(1)}, bf16[128,1024]{1,0:T(8,128)(2,1)S(1)}, bf16[1024,4096]{1,0:T(8,128)(2,1)S(1)}) custom-call(s32[1]{0:T(128)} %bitcast.index_ref, bf16[8,256,128]{2,1,0:T(8,128)(2,1)S(1)} %get-tuple-element.37.tile_ref, bf16[544,128]{1,0:T(8,128)(2,1)S(1)} %pack.1.own_ref, ...), custom_call_target="tpu_custom_call" | custom-call | flops 5000000000 | bytes 1048576 | tf_op jit(solution)/shard_map/pallas_call | solution.py:446
  58.6 1.3 %rest.2 = (bf16[64,4096]{1,0:T(8,128)(2,1)S(1)}, bf16[64,4096]{1,0:T(8,128)(2,1)S(1)}) custom-call(bf16[128,1024]{1,0:T(8,128)(2,1)S(1)} %get-tuple-element.43.merged_ref, bf16[1024,4096]{1,0:T(8,128)(2,1)S(1)} %get-tuple-element.44.w_ref), custom_call_target="tpu_custom_call" | custom-call | flops 1000000000 | bytes 1048576 | tf_op jit(solution)/shard_map/rest/pallas_call | solution.py:455
  60.4 2.1 %middle.1.refs_0_ = f32[2,144,256]{2,1,0:T(8,128)S(1)} custom-call(bf16[8,256,128]{2,1,0:T(8,128)(2,1)S(1)} %get-tuple-element.37.tile_ref, bf16[544,128]{1,0:T(8,128)(2,1)S(1)} %pack.1.own_ref, bf16[816,128]{1,0:T(8,128)(2,1)S(1)} %collective-permute-done.6.a1, bf16[816,128]{1,0:T(8,128)(2,1)S(1)} %collective-permute-done.7.a2, ...), custom_call_target="tpu_custom_call" | custom-call | flops 2000000000 | bytes 1048576 | tf_op jit(solution)/shard_map/middle/pallas_call | solution.py:429
  62.8 2.0 %collective-permute-start.14 = (bf16[32,8192]{1,0:T(8,128)(2,1)S(1)}, bf16[32,8192]{1,0:T(8,128)(2,1)S(1)}, u32[]{:S(2)}, u32[]{:S(2)}) collective-permute-start(bf16[32,8192]{1,0:T(8,128)(2,1)S(1)} %get-tuple-element.53), channel_id=1, source_target_pairs={{0,2},{1,7},{2,0},{3,5},{4,6},{5,3},{6,4},{7,1},{8,10},{9,15},{10,... | collective-permute-start | bytes 1572872 | tf_op jit(solution)/shard_map/ppermute | solution.py:471
  64.8 3.1 %shard_map.57 = (bf16[64,4096]{1,0:T(8,128)(2,1)S(1)}, bf16[64,4096]{1,0:T(8,128)(2,1)S(1)}, bf16[128,1024]{1,0:T(8,128)(2,1)S(1)}) custom-call(s32[1]{0:T(128)} %bitcast.index_ref, bf16[8,256,128]{2,1,0:T(8,128)(2,1)S(1)} %get-tuple-element.37.tile_ref, bf16[544,128]{1,0:T(8,128)(2,1)S(1)} %pack.1.own_ref, bf16[816,128]{1,0:T(8,128)(2,1)S(1)} %collective-permute-done.6.a1, ...), custom_call_target="tpu_custom_call" | custom-call | flops 5000000000 | bytes 1048576 | tf_op jit(solution)/shard_map/pallas_call | solution.py:446
  67.9 1.9 %collective-permute-start.16 = (bf16[64,4096]{1,0:T(8,128)(2,1)S(1)}, bf16[64,4096]{1,0:T(8,128)(2,1)S(1)}, u32[]{:S(2)}, u32[]{:S(2)}) collective-permute-start(bf16[64,4096]{1,0:T(8,128)(2,1)S(1)} %get-tuple-element.62), channel_id=1, source_target_pairs={{0,1},{1,0},{2,3},{3,2},{4,5},{5,4},{6,7},{7,6},{8,9},{9,8},{10,11... | collective-permute-start | bytes 1572872 | tf_op jit(solution)/shard_map/ppermute | solution.py:468
  69.8 1.3 %rest.3 = (bf16[64,4096]{1,0:T(8,128)(2,1)S(1)}, bf16[64,4096]{1,0:T(8,128)(2,1)S(1)}) custom-call(bf16[128,1024]{1,0:T(8,128)(2,1)S(1)} %get-tuple-element.56.merged_ref, bf16[1024,4096]{1,0:T(8,128)(2,1)S(1)} %get-tuple-element.44.w_ref), custom_call_target="tpu_custom_call" | custom-call | flops 1000000000 | bytes 1048576 | tf_op jit(solution)/shard_map/rest/pallas_call | solution.py:455
  72.0 1.2 %collective-permute-start.17 = (bf16[64,4096]{1,0:T(8,128)(2,1)S(1)}, bf16[64,4096]{1,0:T(8,128)(2,1)S(1)}, u32[]{:S(2)}, u32[]{:S(2)}) collective-permute-start(bf16[64,4096]{1,0:T(8,128)(2,1)S(1)} %get-tuple-element.64), channel_id=1, source_target_pairs={{0,1},{1,0},{2,3},{3,2},{4,5},{5,4},{6,7},{7,6},{8,9},{9,8},{10,11... | collective-permute-start | bytes 1572872 | tf_op jit(solution)/shard_map/ppermute | solution.py:468
  73.2 1.5 %collective-permute-done.17.got_b = bf16[64,4096]{1,0:T(8,128)(2,1)S(1)} collective-permute-done((bf16[64,4096]{1,0:T(8,128)(2,1)S(1)}, bf16[64,4096]{1,0:T(8,128)(2,1)S(1)}, u32[]{:S(2)}, u32[]{:S(2)}) %collective-permute-start.17) | collective-permute-done | bytes 524320 | tf_op jit(solution)/shard_map/ppermute | solution.py:468
  75.0 1.2 %collective-permute-start.18 = (bf16[32,8192]{1,0:T(8,128)(2,1)S(1)}, bf16[32,8192]{1,0:T(8,128)(2,1)S(1)}, u32[]{:S(2)}, u32[]{:S(2)}) collective-permute-start(bf16[32,8192]{1,0:T(8,128)(2,1)S(1)} %get-tuple-element.66), channel_id=1, source_target_pairs={{0,2},{1,7},{2,0},{3,5},{4,6},{5,3},{6,4},{7,1},{8,10},{9,15},{10,... | collective-permute-start | bytes 1572872 | tf_op jit(solution)/shard_map/ppermute | solution.py:471
  76.3 2.6 %collective-permute-start.15 = (bf16[16,8192]{1,0:T(8,128)(2,1)S(1)}, bf16[16,8192]{1,0:T(8,128)(2,1)S(1)}, u32[]{:S(2)}, u32[]{:S(2)}) collective-permute-start(bf16[16,8192]{1,0:T(8,128)(2,1)S(1)} %get-tuple-element.60), channel_id=1, source_target_pairs={{0,6},{1,3},{2,4},{3,1},{4,2},{5,7},{6,0},{7,5},{8,14},{9,11},{10,... | collective-permute-start | bytes 786440 | tf_op jit(solution)/shard_map/ppermute | solution.py:471
  78.9 8.1 %collective-permute-done.18.got_ref = bf16[32,8192]{1,0:T(8,128)(2,1)S(1)} collective-permute-done((bf16[32,8192]{1,0:T(8,128)(2,1)S(1)}, bf16[32,8192]{1,0:T(8,128)(2,1)S(1)}, u32[]{:S(2)}, u32[]{:S(2)}) %collective-permute-start.18) | collective-permute-done | bytes 524320 | tf_op jit(solution)/shard_map/ppermute | solution.py:471
  87.2 2.7 %collective-permute-start.19 = (bf16[16,8192]{1,0:T(8,128)(2,1)S(1)}, bf16[16,8192]{1,0:T(8,128)(2,1)S(1)}, u32[]{:S(2)}, u32[]{:S(2)}) collective-permute-start(bf16[16,8192]{1,0:T(8,128)(2,1)S(1)} %get-tuple-element.68), channel_id=1, source_target_pairs={{0,6},{1,3},{2,4},{3,1},{4,2},{5,7},{6,0},{7,5},{8,14},{9,11},{10,... | collective-permute-start | bytes 786440 | tf_op jit(solution)/shard_map/ppermute | solution.py:471
  89.9 4.9 %collective-permute-done.19.got1 = bf16[16,8192]{1,0:T(8,128)(2,1)S(1)} collective-permute-done((bf16[16,8192]{1,0:T(8,128)(2,1)S(1)}, bf16[16,8192]{1,0:T(8,128)(2,1)S(1)}, u32[]{:S(2)}, u32[]{:S(2)}) %collective-permute-start.19) | collective-permute-done | bytes 262176 | tf_op jit(solution)/shard_map/ppermute | solution.py:471
  (30 shorter events, 9.1 us)
Async XLA Ops:
  1.0 7.8 %collective-permute-start.5 = (bf16[544,128]{1,0:T(8,128)(2,1)S(1)}, bf16[544,128]{1,0:T(8,128)(2,1)S(1)}, u32[]{:S(2)}, u32[]{:S(2)}) collective-permute-start(bf16[544,128]{1,0:T(8,128)(2,1)S(1)} %pack.1.own_ref), channel_id=1, source_target_pairs={{0,16},{8,24},{16,0},{24,8},{32,48},{40,56},{48,32},{56,40},{64,80... | collective-permute-start | bytes 417800 | tf_op jit(solution)/shard_map/ppermute | solution.py:384
  4.3 7.0 %collective-permute-start.4 = (bf16[544,128]{1,0:T(8,128)(2,1)S(1)}, bf16[544,128]{1,0:T(8,128)(2,1)S(1)}, u32[]{:S(2)}, u32[]{:S(2)}) collective-permute-start(bf16[544,128]{1,0:T(8,128)(2,1)S(1)} %pack.1.own_ref), channel_id=1, source_target_pairs={{0,24},{8,0},{16,8},{24,16},{32,56},{40,32},{48,40},{56,48},{64,88... | collective-permute-start | bytes 417800 | tf_op jit(solution)/shard_map/ppermute | solution.py:384
  5.3 6.3 %collective-permute-start.3 = (bf16[544,128]{1,0:T(8,128)(2,1)S(1)}, bf16[544,128]{1,0:T(8,128)(2,1)S(1)}, u32[]{:S(2)}, u32[]{:S(2)}) collective-permute-start(bf16[544,128]{1,0:T(8,128)(2,1)S(1)} %pack.1.own_ref), channel_id=1, source_target_pairs={{0,8},{8,16},{16,24},{24,0},{32,40},{40,48},{48,56},{56,32},{64,72... | collective-permute-start | bytes 417800 | tf_op jit(solution)/shard_map/ppermute | solution.py:384
  11.6 18.5 %collective-permute-start.11 = (bf16[816,128]{1,0:T(8,128)(2,1)S(1)}, bf16[816,128]{1,0:T(8,128)(2,1)S(1)}, u32[]{:S(2)}, u32[]{:S(2)}) collective-permute-start(bf16[816,128]{1,0:T(8,128)(2,1)S(1)} %join.3), channel_id=1, source_target_pairs={{0,64},{8,72},{16,80},{24,88},{32,96},{40,104},{48,112},{56,120},{... | collective-permute-start | bytes 626696 | tf_op jit(solution)/shard_map/ppermute | solution.py:384
  13.1 11.2 %collective-permute-start.2 = (bf16[544,128]{1,0:T(8,128)(2,1)S(1)}, bf16[544,128]{1,0:T(8,128)(2,1)S(1)}, u32[]{:S(2)}, u32[]{:S(2)}) collective-permute-start(bf16[544,128]{1,0:T(8,128)(2,1)S(1)} %pack.1.own_ref), channel_id=1, source_target_pairs={{0,64},{8,72},{16,80},{24,88},{32,96},{40,104},{48,112},{56,120},{... | collective-permute-start | bytes 417800 | tf_op jit(solution)/shard_map/ppermute | solution.py:384
  15.2 9.9 %collective-permute-start.1 = (bf16[544,128]{1,0:T(8,128)(2,1)S(1)}, bf16[544,128]{1,0:T(8,128)(2,1)S(1)}, u32[]{:S(2)}, u32[]{:S(2)}) collective-permute-start(bf16[544,128]{1,0:T(8,128)(2,1)S(1)} %pack.1.own_ref), channel_id=1, source_target_pairs={{0,96},{8,104},{16,112},{24,120},{32,0},{40,8},{48,16},{56,24},{64... | collective-permute-start | bytes 417800 | tf_op jit(solution)/shard_map/ppermute | solution.py:384
  16.1 9.1 %collective-permute-start = (bf16[544,128]{1,0:T(8,128)(2,1)S(1)}, bf16[544,128]{1,0:T(8,128)(2,1)S(1)}, u32[]{:S(2)}, u32[]{:S(2)}) collective-permute-start(bf16[544,128]{1,0:T(8,128)(2,1)S(1)} %pack.1.own_ref), channel_id=1, source_target_pairs={{0,32},{8,40},{16,48},{24,56},{32,64},{40,72},{48,80},{56,88},{64,... | collective-permute-start | bytes 417800 | tf_op jit(solution)/shard_map/ppermute | solution.py:384
  18.5 34.7 %collective-permute-start.10 = (bf16[816,128]{1,0:T(8,128)(2,1)S(1)}, bf16[816,128]{1,0:T(8,128)(2,1)S(1)}, u32[]{:S(2)}, u32[]{:S(2)}) collective-permute-start(bf16[816,128]{1,0:T(8,128)(2,1)S(1)} %join.3), channel_id=1, source_target_pairs={{0,96},{8,104},{16,112},{24,120},{32,0},{40,8},{48,16},{56,24},{64... | collective-permute-start | bytes 626696 | tf_op jit(solution)/shard_map/ppermute | solution.py:384
  24.3 28.9 %collective-permute-start.9 = (bf16[816,128]{1,0:T(8,128)(2,1)S(1)}, bf16[816,128]{1,0:T(8,128)(2,1)S(1)}, u32[]{:S(2)}, u32[]{:S(2)}) collective-permute-start(bf16[816,128]{1,0:T(8,128)(2,1)S(1)} %join.3), channel_id=1, source_target_pairs={{0,32},{8,40},{16,48},{24,56},{32,64},{40,72},{48,80},{56,88},{64,... | collective-permute-start | bytes 626696 | tf_op jit(solution)/shard_map/ppermute | solution.py:384
  25.1 28.0 %collective-permute-start.8 = (bf16[816,128]{1,0:T(8,128)(2,1)S(1)}, bf16[816,128]{1,0:T(8,128)(2,1)S(1)}, u32[]{:S(2)}, u32[]{:S(2)}) collective-permute-start(bf16[816,128]{1,0:T(8,128)(2,1)S(1)} %join.2), channel_id=1, source_target_pairs={{0,16},{8,24},{16,0},{24,8},{32,48},{40,56},{48,32},{56,40},{64,80... | collective-permute-start | bytes 626696 | tf_op jit(solution)/shard_map/ppermute | solution.py:384
  28.8 24.3 %collective-permute-start.7 = (bf16[816,128]{1,0:T(8,128)(2,1)S(1)}, bf16[816,128]{1,0:T(8,128)(2,1)S(1)}, u32[]{:S(2)}, u32[]{:S(2)}) collective-permute-start(bf16[816,128]{1,0:T(8,128)(2,1)S(1)} %join.2), channel_id=1, source_target_pairs={{0,24},{8,0},{16,8},{24,16},{32,56},{40,32},{48,40},{56,48},{64,88... | collective-permute-start | bytes 626696 | tf_op jit(solution)/shard_map/ppermute | solution.py:384
  30.1 23.1 %collective-permute-start.6 = (bf16[816,128]{1,0:T(8,128)(2,1)S(1)}, bf16[816,128]{1,0:T(8,128)(2,1)S(1)}, u32[]{:S(2)}, u32[]{:S(2)}) collective-permute-start(bf16[816,128]{1,0:T(8,128)(2,1)S(1)} %join.2), channel_id=1, source_target_pairs={{0,8},{8,16},{16,24},{24,0},{32,40},{40,48},{48,56},{56,32},{64,72... | collective-permute-start | bytes 626696 | tf_op jit(solution)/shard_map/ppermute | solution.py:384
  58.5 4.0 %collective-permute-start.12 = (bf16[64,4096]{1,0:T(8,128)(2,1)S(1)}, bf16[64,4096]{1,0:T(8,128)(2,1)S(1)}, u32[]{:S(2)}, u32[]{:S(2)}) collective-permute-start(bf16[64,4096]{1,0:T(8,128)(2,1)S(1)} %get-tuple-element.42), channel_id=1, source_target_pairs={{0,1},{1,0},{2,3},{3,2},{4,5},{5,4},{6,7},{7,6},{8,9},{9,8},{10,11... | collective-permute-start | bytes 1572872 | tf_op jit(solution)/shard_map/ppermute | solution.py:468
  59.9 2.7 %collective-permute-start.13 = (bf16[64,4096]{1,0:T(8,128)(2,1)S(1)}, bf16[64,4096]{1,0:T(8,128)(2,1)S(1)}, u32[]{:S(2)}, u32[]{:S(2)}) collective-permute-start(bf16[64,4096]{1,0:T(8,128)(2,1)S(1)} %get-tuple-element.49), channel_id=1, source_target_pairs={{0,1},{1,0},{2,3},{3,2},{4,5},{5,4},{6,7},{7,6},{8,9},{9,8},{10,11... | collective-permute-start | bytes 1572872 | tf_op jit(solution)/shard_map/ppermute | solution.py:468
  62.8 9.3 %collective-permute-start.14 = (bf16[32,8192]{1,0:T(8,128)(2,1)S(1)}, bf16[32,8192]{1,0:T(8,128)(2,1)S(1)}, u32[]{:S(2)}, u32[]{:S(2)}) collective-permute-start(bf16[32,8192]{1,0:T(8,128)(2,1)S(1)} %get-tuple-element.53), channel_id=1, source_target_pairs={{0,2},{1,7},{2,0},{3,5},{4,6},{5,3},{6,4},{7,1},{8,10},{9,15},{10,... | collective-permute-start | bytes 1572872 | tf_op jit(solution)/shard_map/ppermute | solution.py:471
  67.9 5.3 %collective-permute-start.16 = (bf16[64,4096]{1,0:T(8,128)(2,1)S(1)}, bf16[64,4096]{1,0:T(8,128)(2,1)S(1)}, u32[]{:S(2)}, u32[]{:S(2)}) collective-permute-start(bf16[64,4096]{1,0:T(8,128)(2,1)S(1)} %get-tuple-element.62), channel_id=1, source_target_pairs={{0,1},{1,0},{2,3},{3,2},{4,5},{5,4},{6,7},{7,6},{8,9},{9,8},{10,11... | collective-permute-start | bytes 1572872 | tf_op jit(solution)/shard_map/ppermute | solution.py:468
  72.0 2.7 %collective-permute-start.17 = (bf16[64,4096]{1,0:T(8,128)(2,1)S(1)}, bf16[64,4096]{1,0:T(8,128)(2,1)S(1)}, u32[]{:S(2)}, u32[]{:S(2)}) collective-permute-start(bf16[64,4096]{1,0:T(8,128)(2,1)S(1)} %get-tuple-element.64), channel_id=1, source_target_pairs={{0,1},{1,0},{2,3},{3,2},{4,5},{5,4},{6,7},{7,6},{8,9},{9,8},{10,11... | collective-permute-start | bytes 1572872 | tf_op jit(solution)/shard_map/ppermute | solution.py:468
  75.0 12.1 %collective-permute-start.18 = (bf16[32,8192]{1,0:T(8,128)(2,1)S(1)}, bf16[32,8192]{1,0:T(8,128)(2,1)S(1)}, u32[]{:S(2)}, u32[]{:S(2)}) collective-permute-start(bf16[32,8192]{1,0:T(8,128)(2,1)S(1)} %get-tuple-element.66), channel_id=1, source_target_pairs={{0,2},{1,7},{2,0},{3,5},{4,6},{5,3},{6,4},{7,1},{8,10},{9,15},{10,... | collective-permute-start | bytes 1572872 | tf_op jit(solution)/shard_map/ppermute | solution.py:471
  76.3 13.6 %collective-permute-start.15 = (bf16[16,8192]{1,0:T(8,128)(2,1)S(1)}, bf16[16,8192]{1,0:T(8,128)(2,1)S(1)}, u32[]{:S(2)}, u32[]{:S(2)}) collective-permute-start(bf16[16,8192]{1,0:T(8,128)(2,1)S(1)} %get-tuple-element.60), channel_id=1, source_target_pairs={{0,6},{1,3},{2,4},{3,1},{4,2},{5,7},{6,0},{7,5},{8,14},{9,11},{10,... | collective-permute-start | bytes 786440 | tf_op jit(solution)/shard_map/ppermute | solution.py:471
  87.2 7.7 %collective-permute-start.19 = (bf16[16,8192]{1,0:T(8,128)(2,1)S(1)}, bf16[16,8192]{1,0:T(8,128)(2,1)S(1)}, u32[]{:S(2)}, u32[]{:S(2)}) collective-permute-start(bf16[16,8192]{1,0:T(8,128)(2,1)S(1)} %get-tuple-element.68), channel_id=1, source_target_pairs={{0,6},{1,3},{2,4},{3,1},{4,2},{5,7},{6,0},{7,5},{8,14},{9,11},{10,... | collective-permute-start | bytes 786440 | tf_op jit(solution)/shard_map/ppermute | solution.py:471

commit v4 on v3

--- a/solution.py
+++ b/solution.py
@@ -250,13 +250,9 @@
             slow_walk(kv_ref, lists[n], counts[n], queries[n], units[n], m_ref, acc_ref)
 
 
-def first_partner(z, core):
-    return (((z + core) ^ 1) - core + NZ) % NZ
-
-
 def place_of(z_to, core_to, z, core):
-    near = jnp.where(first_partner(z, core_to) == z_to, 2, 1)
-    slot = jnp.where(z_to == z, 0, jnp.where((z_to + 2) % NZ == z, 3, near))
+    slot = jnp.where((z ^ 1) == z_to, 2, 1)
+    slot = jnp.where(z_to == z, 0, jnp.where((z_to + 2) % NZ == z, 3, slot))
     return (core_to ^ core) * NZ + slot
 
 
@@ -287,40 +283,32 @@
         send_ref[:, at] = part[64:]
 
 
-def middle_kernel(chunk, spans, tile_ref, own_ref, a1, a2, a3, b1, b2, b3, m_in, acc_in, acc_ref,
-                  kv_ref, m_ref, peak_ref, even_ref, odd_ref, list0, list1):
-    rest_of_attention(chunk, spans, tile_ref, own_ref, (a1, a2, a3, b1, b2, b3), m_in, acc_in, kv_ref,
-                      m_ref, peak_ref, acc_ref, even_ref, odd_ref, (list0, list1))
-
-
-def last_kernel(chunk, spans, done, index_ref, tile_ref, own_ref, a1, a2, a3, b1, b2, b3, m_in, acc_in,
-                w_ref, *refs):
-    if done:
-        acc_done = refs[0]
-    else:
+def last_kernel(chunk, index_ref, tile_ref, own_ref, f1, f2, f3, f4, f5, f6, m_in, acc_in, w_ref,
+                *refs):
+    if chunk == 0:
         w_hbm, w_next, sems = refs[0], refs[4], refs[-1]
-        refs = refs[:4] + refs[5:-1]
+        refs = refs[1:4] + refs[5:-1]
         fetch_w = fetch_half(1, w_hbm, w_next, sems)
     (keep_ref, send_ref, merged_ref, acc_ref, kv_ref, m_ref, peak_ref, even_ref, odd_ref,
-     list0, list1) = refs[-11:]
-    rest_of_attention(chunk, spans, tile_ref, own_ref, (a1, a2, a3, b1, b2, b3), m_in, acc_in, kv_ref,
-                      m_ref, peak_ref, acc_ref, even_ref, odd_ref, (list0, list1))
-    for n, s in enumerate(spans):
-        finish(s, acc_ref, 2 * n, index_ref, merged_ref)
-    for n, s in enumerate(done):
-        finish(s, acc_done, 2 * n, index_ref, merged_ref)
+     list0, list1) = refs
+    spans = (0, 1)
+    rest_of_attention(chunk, spans, tile_ref, own_ref, (f1, f2, f3, f4, f5, f6), m_in, acc_in,
+                      kv_ref, m_ref, peak_ref, acc_ref, even_ref, odd_ref, (list0, list1))
+    for s in spans:
+        finish(s, acc_ref, 2 * s, index_ref, merged_ref)
     project(merged_ref, w_ref, keep_ref, send_ref)
-    if not done:
+    if chunk == 0:
         for copy in fetch_w:
             copy.wait()
 
 
-def pair_kernel(keep_a, got_a, keep_b, got_b, stay_ref, send_ref):
-    for half, keep_ref, got_ref in ((0, keep_a, got_a), (1, keep_b, got_b)):
-        total = (keep_ref[...].astype(jnp.float32) + got_ref[...]).astype(jnp.bfloat16)
-        columns = slice(half * DOUT // 2, (half + 1) * DOUT // 2)
-        stay_ref[:, columns] = total[:2 * PIECE]
-        send_ref[:, columns] = total[2 * PIECE:]
+def pair_kernel(half, keep_ref, got_ref, stay_ref, send_ref):
+    stay, send = ((0, 1), (2, 3)) if half == 0 else ((0, 2), (1, 3))
+    for out_ref, slots in ((stay_ref, stay), (send_ref, send)):
+        for i, slot in enumerate(slots):
+            rows = slice(slot * PIECE, (slot + 1) * PIECE)
+            total = keep_ref[rows].astype(jnp.float32) + got_ref[rows]
+            out_ref[i * PIECE:(i + 1) * PIECE] = total.astype(jnp.bfloat16)
 
 
 def fold_kernel(stay_ref, got_ref, mine_ref, send_ref):
@@ -329,10 +317,13 @@
     send_ref[...] = total[PIECE:]
 
 
-def final_kernel(mine0, got0, mine1, got1, out_ref):
-    for chunk, mine_ref, got_ref in ((0, mine0, got0), (1, mine1, got1)):
-        total = mine_ref[...].astype(jnp.float32) + got_ref[...]
-        out_ref[chunk * PIECE:(chunk + 1) * PIECE, :] = total.astype(jnp.bfloat16)
+def final_kernel(*refs):
+    out_ref = refs[-1]
+    for i in range(4):
+        chunk, half = i // 2, i % 2
+        total = refs[2 * i][...].astype(jnp.float32) + refs[2 * i + 1][...]
+        columns = slice(half * DOUT // 2, (half + 1) * DOUT // 2)
+        out_ref[chunk * PIECE:(chunk + 1) * PIECE, columns] = total.astype(jnp.bfloat16)
 
 
 def in_hbm(array):
@@ -358,9 +349,9 @@
     return [(t, t ^ 1) for t in range(NZ * NCORE)]
 
 
-def step_route(step):
+def step_route(pairing):
     return [
-        (z * NCORE + c, first_partner(z, c ^ step) * NCORE + c)
+        (z * NCORE + c, ((((z + pairing) ^ 1) - pairing) % NZ) * NCORE + c)
         for z in range(NZ) for c in range(NCORE)
     ]
 
@@ -424,74 +415,70 @@
         in_hbm(queries), in_hbm(out_weight), own, *xs, *ys
     )
 
-    def middle(chunk, spans, acc):
-        n = 2 * len(spans)
-        return pl.pallas_call(
-            functools.partial(middle_kernel, chunk, spans),
-            in_specs=[VMEM] * 10, out_specs=VMEM, out_shape=struct((n, 144, 256), f32),
-            scratch_shapes=walk_scratch(18, n, 2),
-            compiler_params=params(14), name="middle",
-            cost_estimate=estimate(2 * 10 ** 9, 1 << 20),
-        )(tiles, own, *fa, *fb, maxima, acc)
-
     halves = [struct((64, DOUT // 2), bf16)] * 2
 
-    def last(chunk, spans, acc, done, extra):
-        n = 2 * len(spans)
+    def last(chunk, acc, *w_hbm):
         outs = halves + [struct((128, 1024), bf16)]
-        scratch = [pltpu.VMEM((n, 144, 256), f32)] + walk_scratch(18, n, 2)
-        if not done:
+        scratch = [pltpu.VMEM((4, 144, 256), f32)] + walk_scratch(18, 4, 2)
+        if w_hbm:
             outs = outs + [struct((1024, DOUT // 2), bf16)]
             scratch = scratch + [pltpu.SemaphoreType.DMA((NW,))]
         return pl.pallas_call(
-            functools.partial(last_kernel, chunk, spans, done),
-            in_specs=[SMEM] + [VMEM] * 11 + [VMEM if done else HBM],
+            functools.partial(last_kernel, chunk),
+            in_specs=[SMEM] + [VMEM] * 11 + [HBM] * len(w_hbm),
             out_specs=[VMEM] * len(outs), out_shape=outs, scratch_shapes=scratch,
             compiler_params=params(14),
             cost_estimate=estimate(5 * 10 ** 9, 1 << 20),
-        )(index, tiles, own, *fa, *fb, maxima, acc, weight_a, extra)
-
-    def rest(merged):
+        )(index, tiles, own, *fa, *fb, maxima, acc, weight_a, *w_hbm)
+
+    def rest(merged, weight):
         return pl.pallas_call(
             project, in_specs=[VMEM] * 2, out_specs=[VMEM] * 2, out_shape=halves,
             compiler_params=params(6), name="rest", cost_estimate=estimate(10 ** 9, 1 << 20),
-        )(merged, weight_b)
-
-    def call(kernel, rows, blocks):
+        )(merged, weight)
+
+    def call(kernel, rows, columns, *blocks):
         return pl.pallas_call(
             kernel, in_specs=[VMEM] * len(blocks), out_specs=[VMEM] * len(rows),
-            out_shape=[struct((r, DOUT), bf16) for r in rows],
+            out_shape=[struct((r, columns), bf16) for r in rows],
             compiler_params=params(6), cost_estimate=estimate(10 ** 6, 1 << 20),
         )(*blocks)
 
     def swap(block):
         return lax.ppermute(block, "tp", swap_route())
 
-    def step(number, block):
-        return lax.ppermute(block, "tp", step_route(number))
-
-    keep0a, send0a, merged0, weight_b = last(0, (0, 1), acc, (), in_hbm(out_weight))
-    got0a = swap(send0a)
-    keep0b, send0b = rest(merged0)
-    send0b, acc1 = lax.optimization_barrier((send0b, acc))
-    got0b = swap(send0b)
-    acc_mid = middle(1, (0,), acc1)
-    keep0b, acc_mid = lax.optimization_barrier((keep0b, acc_mid))
-    stay0, out0 = call(pair_kernel, (32, 32), (keep0a, got0a, keep0b, got0b))
-    stay0, out0, acc2 = lax.optimization_barrier((stay0, out0, acc))
-    in0 = step(0, out0)
-    keep1a, send1a, merged1 = last(1, (1,), acc2, (0,), acc_mid)
-    got1a = swap(send1a)
-    keep1b, send1b = rest(merged1)
-    in0, send1b = lax.optimization_barrier((in0, send1b))
-    got1b = swap(send1b)
-    mine0, out0 = call(fold_kernel, (16, 16), (stay0, in0))
-    in0 = step(1, out0)
-    stay1, out1 = call(pair_kernel, (32, 32), (keep1a, got1a, keep1b, got1b))
-    in1 = step(0, out1)
-    mine1, out1 = call(fold_kernel, (16, 16), (stay1, in1))
-    in1 = step(1, out1)
-    return call(final_kernel, (32,), (mine0, in0, mine1, in1))[0]
+    def step(pairing, block):
+        return lax.ppermute(block, "tp", step_route(pairing))
+
+    def pair(half, keep, got):
+        kernel = functools.partial(pair_kernel, half)
+        return call(kernel, (32, 32), DOUT // 2, keep, got)
+
+    def chunk_parts(chunk, acc, *w_hbm):
+        keep_a, send_a, merged, *w_next = last(chunk, acc, *w_hbm)
+        got_a = swap(send_a)
+        w_half = w_next[0] if w_next else weight_b
+        keep_b, send_b = rest(merged, w_half)
+        got_b = swap(send_b)
+        stay_a, out_a = pair(0, keep_a, got_a)
+        in_a = step(0, out_a)
+        stay_b, out_b = pair(1, keep_b, got_b)
+        in_b = step(1, out_b)
+        return stay_a, in_a, stay_b, in_b, out_b, w_half
+
+    def second_step(half, stay, got):
+        mine, out = call(fold_kernel, (16, 16), DOUT // 2, stay, got)
+        return mine, step(1 - half, out)
+
+    *early, out_b0, weight_b = chunk_parts(0, acc, in_hbm(out_weight))
+    out_b0, acc = lax.optimization_barrier((out_b0, acc))
+    *late, out_b1, _ = chunk_parts(1, acc)
+    *early, out_b1 = lax.optimization_barrier((*early, out_b1))
+    blocks = []
+    for stay_a, in_a, stay_b, in_b in (early, late):
+        blocks += second_step(0, stay_a, in_a)
+        blocks += second_step(1, stay_b, in_b)
+    return call(final_kernel, (32,), DOUT, *blocks)[0]
 
 
 def solution(mesh):

time: 95.9 us -> 94.7 us (0.987)
  waiting for transfers between devices: 27.5 us -> 26.1 us
    ppermute x4 -> x8, starting transfers between devices: 8.54 us -> 11.5 us  [step(): return lax.ppermute(block, 'tp', step_route(pairing))]
    ppermute x4, starting transfers between devices: 3.75 us -> 1.17 us  [swap(): return lax.ppermute(block, 'tp', swap_route())]
    ppermute x4 -> x8, waiting for transfers between devices: 14 us -> 12.7 us  [step(): return lax.ppermute(block, 'tp', step_route(pairing))]
    pallas_call x3 -> x2, Pallas kernels: 10.4 us -> 10.3 us  [last(): pl.pallas_call(functools.partial(last_kernel, chunk), in_specs=[SMEM] + [...]
  transfers between devices with their start and end apart: 20 -> 24, of which waited for: 9 -> 12; matrix products, arithmetic and copies ran while one was open for 0% -> 0% of each run, Pallas kernels for 32% -> 31%
where the time goes in v4:
time: 94.7 us; the launch traced here: 94.6 us
  Pallas kernels  37.7 us (40%)
  starting transfers between devices  30.6 us (32%)
  waiting for transfers between devices  26.1 us (28%)
    pallas_call x1, Pallas kernels, on_device(): first(in_hbm(queries), in_hbm(out_weight), own, *xs, *ys)  22.3 us
    ppermute x12, starting transfers between devices, shifts(): moved.append(lax.ppermute(block, 'ctx', ctx_route(dx * d, dy * d)))  17.9 us
    ppermute x8, waiting for transfers between devices, step(): return lax.ppermute(block, 'tp', step_route(pairing))  12.7 us
    ppermute x12, waiting for transfers between devices, shifts(): moved.append(lax.ppermute(block, 'ctx', ctx_route(dx * d, dy * d)))  12 us
    ppermute x8, starting transfers between devices, step(): return lax.ppermute(block, 'tp', step_route(pairing))  11.5 us
    pallas_call x2, Pallas kernels, last(): pl.pallas_call(functools.partial(last_kernel, chunk), in_specs=[SMEM] + [...  10.3 us
    pallas_call x2, Pallas kernels, rest(): pl.pallas_call(project, in_specs=[VMEM] * 2, out_specs=[VMEM] * 2, out_sh...  2.54 us
  transfers between devices with their start and end apart: 24, of which 12 were waited for; matrix products, arithmetic and copies ran while one was open for 0% of the time, Pallas kernels for 31%

profile of v4, /device:TPU:6, one launch (start us, length us, event | category | flops | bytes accessed | tf_op | source)
XLA Modules:
  0.0 94.6 jit_solution(5408660312210030248)
XLA Ops:
  1.0 3.3 %collective-permute-start.5 = (bf16[544,128]{1,0:T(8,128)(2,1)S(1)}, bf16[544,128]{1,0:T(8,128)(2,1)S(1)}, u32[]{:S(2)}, u32[]{:S(2)}) collective-permute-start(bf16[544,128]{1,0:T(8,128)(2,1)S(1)} %pack.1.own_ref), channel_id=1, source_target_pairs={{0,16},{8,24},{16,0},{24,8},{32,48},{40,56},{48,32},{56,40},{64,80... | collective-permute-start | bytes 417800 | tf_op jit(solution)/shard_map/ppermute | solution.py:375
  6.3 2.5 %collective-permute-done.5.y3.refs_2_ = bf16[544,128]{1,0:T(8,128)(2,1)S(1)} collective-permute-done((bf16[544,128]{1,0:T(8,128)(2,1)S(1)}, bf16[544,128]{1,0:T(8,128)(2,1)S(1)}, u32[]{:S(2)}, u32[]{:S(2)}) %collective-permute-start.5) | collective-permute-done | bytes 139296 | tf_op jit(solution)/shard_map/ppermute | solution.py:375
  8.8 2.5 %collective-permute-done.4.y2.refs_1_ = bf16[544,128]{1,0:T(8,128)(2,1)S(1)} collective-permute-done((bf16[544,128]{1,0:T(8,128)(2,1)S(1)}, bf16[544,128]{1,0:T(8,128)(2,1)S(1)}, u32[]{:S(2)}, u32[]{:S(2)}) %collective-permute-start.4) | collective-permute-done | bytes 139296 | tf_op jit(solution)/shard_map/ppermute | solution.py:375
  11.6 1.5 %collective-permute-start.11 = (bf16[816,128]{1,0:T(8,128)(2,1)S(1)}, bf16[816,128]{1,0:T(8,128)(2,1)S(1)}, u32[]{:S(2)}, u32[]{:S(2)}) collective-permute-start(bf16[816,128]{1,0:T(8,128)(2,1)S(1)} %join.3), channel_id=1, source_target_pairs={{0,64},{8,72},{16,80},{24,88},{32,96},{40,104},{48,112},{56,120},{... | collective-permute-start | bytes 626696 | tf_op jit(solution)/shard_map/ppermute | solution.py:375
  13.1 2.1 %collective-permute-start.2 = (bf16[544,128]{1,0:T(8,128)(2,1)S(1)}, bf16[544,128]{1,0:T(8,128)(2,1)S(1)}, u32[]{:S(2)}, u32[]{:S(2)}) collective-permute-start(bf16[544,128]{1,0:T(8,128)(2,1)S(1)} %pack.1.own_ref), channel_id=1, source_target_pairs={{0,64},{8,72},{16,80},{24,88},{32,96},{40,104},{48,112},{56,120},{... | collective-permute-start | bytes 417800 | tf_op jit(solution)/shard_map/ppermute | solution.py:375
  16.1 2.4 %collective-permute-start = (bf16[544,128]{1,0:T(8,128)(2,1)S(1)}, bf16[544,128]{1,0:T(8,128)(2,1)S(1)}, u32[]{:S(2)}, u32[]{:S(2)}) collective-permute-start(bf16[544,128]{1,0:T(8,128)(2,1)S(1)} %pack.1.own_ref), channel_id=1, source_target_pairs={{0,32},{8,40},{16,48},{24,56},{32,64},{40,72},{48,80},{56,88},{64,... | collective-permute-start | bytes 417800 | tf_op jit(solution)/shard_map/ppermute | solution.py:375
  18.5 5.8 %collective-permute-done.2.x3.refs_2_ = bf16[544,128]{1,0:T(8,128)(2,1)S(1)} collective-permute-done((bf16[544,128]{1,0:T(8,128)(2,1)S(1)}, bf16[544,128]{1,0:T(8,128)(2,1)S(1)}, u32[]{:S(2)}, u32[]{:S(2)}) %collective-permute-start.2) | collective-permute-done | bytes 139296 | tf_op jit(solution)/shard_map/ppermute | solution.py:375
  25.1 3.7 %collective-permute-start.8 = (bf16[816,128]{1,0:T(8,128)(2,1)S(1)}, bf16[816,128]{1,0:T(8,128)(2,1)S(1)}, u32[]{:S(2)}, u32[]{:S(2)}) collective-permute-start(bf16[816,128]{1,0:T(8,128)(2,1)S(1)} %join.2), channel_id=1, source_target_pairs={{0,16},{8,24},{16,0},{24,8},{32,48},{40,56},{48,32},{56,40},{64,80... | collective-permute-start | bytes 626696 | tf_op jit(solution)/shard_map/ppermute | solution.py:375
  28.8 1.2 %collective-permute-start.7 = (bf16[816,128]{1,0:T(8,128)(2,1)S(1)}, bf16[816,128]{1,0:T(8,128)(2,1)S(1)}, u32[]{:S(2)}, u32[]{:S(2)}) collective-permute-start(bf16[816,128]{1,0:T(8,128)(2,1)S(1)} %join.2), channel_id=1, source_target_pairs={{0,24},{8,0},{16,8},{24,16},{32,56},{40,32},{48,40},{56,48},{64,88... | collective-permute-start | bytes 626696 | tf_op jit(solution)/shard_map/ppermute | solution.py:375
  30.9 22.3 %first.1 = (f32[8,8,256]{2,1,0:T(8,128)S(1)}, f32[8,144,256]{2,1,0:T(8,128)S(1)}, bf16[8,256,128]{2,1,0:T(8,128)(2,1)S(1)}, bf16[1024,4096]{1,0:T(8,128)(2,1)S(1)}) custom-call(bf16[256,1024]{1,0:T(8,128)(2,1)} %q_hbm.1, bf16[1024,8192]{1,0:T(8,128)(2,1)} %refs_0_.1, bf16[544,128]{1,0:T(8,128)(2,1)S(1)} %pack.1.own_ref, ...), custom_call_target="tpu_custom_call" | custom-call | flops 4000000000 | bytes 1048576 | tf_op jit(solution)/shard_map/first/pallas_call | solution.py:414
  53.2 5.2 %shard_map.55 = (bf16[64,4096]{1,0:T(8,128)(2,1)S(1)}, bf16[64,4096]{1,0:T(8,128)(2,1)S(1)}, bf16[128,1024]{1,0:T(8,128)(2,1)S(1)}, bf16[1024,4096]{1,0:T(8,128)(2,1)S(1)}) custom-call(s32[1]{0:T(128)} %bitcast.index_ref, bf16[8,256,128]{2,1,0:T(8,128)(2,1)S(1)} %get-tuple-element.41.tile_ref, bf16[544,128]{1,0:T(8,128)(2,1)S(1)} %pack.1.own_ref, ...), custom_call_target="tpu_custom_call" | custom-call | flops 5000000000 | bytes 1048576 | tf_op jit(solution)/shard_map/pallas_call | solution.py:426
  58.5 1.3 %rest.2 = (bf16[64,4096]{1,0:T(8,128)(2,1)S(1)}, bf16[64,4096]{1,0:T(8,128)(2,1)S(1)}) custom-call(bf16[128,1024]{1,0:T(8,128)(2,1)S(1)} %get-tuple-element.49.merged_ref, bf16[1024,4096]{1,0:T(8,128)(2,1)S(1)} %get-tuple-element.50.w_ref), custom_call_target="tpu_custom_call" | custom-call | flops 1000000000 | bytes 1048576 | tf_op jit(solution)/shard_map/rest/pallas_call | solution.py:435
  60.3 1.4 %collective-permute-done.14.got_ref = bf16[64,4096]{1,0:T(8,128)(2,1)S(1)} collective-permute-done((bf16[64,4096]{1,0:T(8,128)(2,1)S(1)}, bf16[64,4096]{1,0:T(8,128)(2,1)S(1)}, u32[]{:S(2)}, u32[]{:S(2)}) %collective-permute-start.14) | collective-permute-done | bytes 524320 | tf_op jit(solution)/shard_map/ppermute | solution.py:448
  61.9 5.0 %shard_map.58 = (bf16[64,4096]{1,0:T(8,128)(2,1)S(1)}, bf16[64,4096]{1,0:T(8,128)(2,1)S(1)}, bf16[128,1024]{1,0:T(8,128)(2,1)S(1)}) custom-call(s32[1]{0:T(128)} %bitcast.index_ref, bf16[8,256,128]{2,1,0:T(8,128)(2,1)S(1)} %get-tuple-element.41.tile_ref, bf16[544,128]{1,0:T(8,128)(2,1)S(1)} %pack.1.own_ref, bf16[816,128]{1,0:T(8,128)(2,1)S(1)} %collective-permute-done.6.f1, ...), custom_call_target="tpu_custom_call" | custom-call | flops 5000000000 | bytes 1048576 | tf_op jit(solution)/shard_map/pallas_call | solution.py:426
  66.9 1.3 %rest.3 = (bf16[64,4096]{1,0:T(8,128)(2,1)S(1)}, bf16[64,4096]{1,0:T(8,128)(2,1)S(1)}) custom-call(bf16[128,1024]{1,0:T(8,128)(2,1)S(1)} %get-tuple-element.56.merged_ref, bf16[1024,4096]{1,0:T(8,128)(2,1)S(1)} %get-tuple-element.50.w_ref), custom_call_target="tpu_custom_call" | custom-call | flops 1000000000 | bytes 1048576 | tf_op jit(solution)/shard_map/rest/pallas_call | solution.py:435
  68.9 2.0 %collective-permute-start.13 = (bf16[32,4096]{1,0:T(8,128)(2,1)S(1)}, bf16[32,4096]{1,0:T(8,128)(2,1)S(1)}, u32[]{:S(2)}, u32[]{:S(2)}) collective-permute-start(bf16[32,4096]{1,0:T(8,128)(2,1)S(1)} %get-tuple-element.48), channel_id=1, source_target_pairs={{0,2},{1,3},{2,0},{3,1},{4,6},{5,7},{6,4},{7,5},{8,10},{9,11},{10,... | collective-permute-start | bytes 786440 | tf_op jit(solution)/shard_map/ppermute | solution.py:451
  70.9 2.5 %collective-permute-start.15 = (bf16[32,4096]{1,0:T(8,128)(2,1)S(1)}, bf16[32,4096]{1,0:T(8,128)(2,1)S(1)}, u32[]{:S(2)}, u32[]{:S(2)}) collective-permute-start(bf16[32,4096]{1,0:T(8,128)(2,1)S(1)} %get-tuple-element.54), channel_id=1, source_target_pairs={{0,6},{1,7},{2,4},{3,5},{4,2},{5,3},{6,0},{7,1},{8,14},{9,15},{10,... | collective-permute-start | bytes 786440 | tf_op jit(solution)/shard_map/ppermute | solution.py:451
  74.9 3.0 %collective-permute-done.13.got_ref = bf16[32,4096]{1,0:T(8,128)(2,1)S(1)} collective-permute-done((bf16[32,4096]{1,0:T(8,128)(2,1)S(1)}, bf16[32,4096]{1,0:T(8,128)(2,1)S(1)}, u32[]{:S(2)}, u32[]{:S(2)}) %collective-permute-start.13) | collective-permute-done | bytes 262176 | tf_op jit(solution)/shard_map/ppermute | solution.py:451
  77.9 3.4 %collective-permute-done.15.got_ref = bf16[32,4096]{1,0:T(8,128)(2,1)S(1)} collective-permute-done((bf16[32,4096]{1,0:T(8,128)(2,1)S(1)}, bf16[32,4096]{1,0:T(8,128)(2,1)S(1)}, u32[]{:S(2)}, u32[]{:S(2)}) %collective-permute-start.15) | collective-permute-done | bytes 262176 | tf_op jit(solution)/shard_map/ppermute | solution.py:451
  81.3 2.6 %collective-permute-start.17 = (bf16[16,4096]{1,0:T(8,128)(2,1)S(1)}, bf16[16,4096]{1,0:T(8,128)(2,1)S(1)}, u32[]{:S(2)}, u32[]{:S(2)}) collective-permute-start(bf16[16,4096]{1,0:T(8,128)(2,1)S(1)} %get-tuple-element.63), channel_id=1, source_target_pairs={{0,6},{1,7},{2,4},{3,5},{4,2},{5,3},{6,0},{7,1},{8,14},{9,15},{10,... | collective-permute-start | bytes 393224 | tf_op jit(solution)/shard_map/ppermute | solution.py:451
  84.1 2.8 %collective-permute-done.22.got_ref = bf16[32,4096]{1,0:T(8,128)(2,1)S(1)} collective-permute-done((bf16[32,4096]{1,0:T(8,128)(2,1)S(1)}, bf16[32,4096]{1,0:T(8,128)(2,1)S(1)}, u32[]{:S(2)}, u32[]{:S(2)}) %collective-permute-start.22) | collective-permute-done | bytes 262176 | tf_op jit(solution)/shard_map/ppermute | solution.py:451
  87.4 2.7 %collective-permute-start.21 = (bf16[16,4096]{1,0:T(8,128)(2,1)S(1)}, bf16[16,4096]{1,0:T(8,128)(2,1)S(1)}, u32[]{:S(2)}, u32[]{:S(2)}) collective-permute-start(bf16[16,4096]{1,0:T(8,128)(2,1)S(1)} %get-tuple-element.73), channel_id=1, source_target_pairs={{0,6},{1,7},{2,4},{3,5},{4,2},{5,3},{6,0},{7,1},{8,14},{9,15},{10,... | collective-permute-start | bytes 393224 | tf_op jit(solution)/shard_map/ppermute | solution.py:451
  90.3 1.7 %collective-permute-done.23.refs_7_ = bf16[16,4096]{1,0:T(8,128)(2,1)S(1)} collective-permute-done((bf16[16,4096]{1,0:T(8,128)(2,1)S(1)}, bf16[16,4096]{1,0:T(8,128)(2,1)S(1)}, u32[]{:S(2)}, u32[]{:S(2)}) %collective-permute-start.23) | collective-permute-done | bytes 131104 | tf_op jit(solution)/shard_map/ppermute | solution.py:451
  92.0 1.7 %collective-permute-done.21.refs_5_ = bf16[16,4096]{1,0:T(8,128)(2,1)S(1)} collective-permute-done((bf16[16,4096]{1,0:T(8,128)(2,1)S(1)}, bf16[16,4096]{1,0:T(8,128)(2,1)S(1)}, u32[]{:S(2)}, u32[]{:S(2)}) %collective-permute-start.21) | collective-permute-done | bytes 131104 | tf_op jit(solution)/shard_map/ppermute | solution.py:451
  (41 shorter events, 10.5 us)
Async XLA Ops:
  1.0 7.8 %collective-permute-start.5 = (bf16[544,128]{1,0:T(8,128)(2,1)S(1)}, bf16[544,128]{1,0:T(8,128)(2,1)S(1)}, u32[]{:S(2)}, u32[]{:S(2)}) collective-permute-start(bf16[544,128]{1,0:T(8,128)(2,1)S(1)} %pack.1.own_ref), channel_id=1, source_target_pairs={{0,16},{8,24},{16,0},{24,8},{32,48},{40,56},{48,32},{56,40},{64,80... | collective-permute-start | bytes 417800 | tf_op jit(solution)/shard_map/ppermute | solution.py:375
  4.3 7.0 %collective-permute-start.4 = (bf16[544,128]{1,0:T(8,128)(2,1)S(1)}, bf16[544,128]{1,0:T(8,128)(2,1)S(1)}, u32[]{:S(2)}, u32[]{:S(2)}) collective-permute-start(bf16[544,128]{1,0:T(8,128)(2,1)S(1)} %pack.1.own_ref), channel_id=1, source_target_pairs={{0,24},{8,0},{16,8},{24,16},{32,56},{40,32},{48,40},{56,48},{64,88... | collective-permute-start | bytes 417800 | tf_op jit(solution)/shard_map/ppermute | solution.py:375
  5.3 6.3 %collective-permute-start.3 = (bf16[544,128]{1,0:T(8,128)(2,1)S(1)}, bf16[544,128]{1,0:T(8,128)(2,1)S(1)}, u32[]{:S(2)}, u32[]{:S(2)}) collective-permute-start(bf16[544,128]{1,0:T(8,128)(2,1)S(1)} %pack.1.own_ref), channel_id=1, source_target_pairs={{0,8},{8,16},{16,24},{24,0},{32,40},{40,48},{48,56},{56,32},{64,72... | collective-permute-start | bytes 417800 | tf_op jit(solution)/shard_map/ppermute | solution.py:375
  11.6 18.5 %collective-permute-start.11 = (bf16[816,128]{1,0:T(8,128)(2,1)S(1)}, bf16[816,128]{1,0:T(8,128)(2,1)S(1)}, u32[]{:S(2)}, u32[]{:S(2)}) collective-permute-start(bf16[816,128]{1,0:T(8,128)(2,1)S(1)} %join.3), channel_id=1, source_target_pairs={{0,64},{8,72},{16,80},{24,88},{32,96},{40,104},{48,112},{56,120},{... | collective-permute-start | bytes 626696 | tf_op jit(solution)/shard_map/ppermute | solution.py:375
  13.1 11.2 %collective-permute-start.2 = (bf16[544,128]{1,0:T(8,128)(2,1)S(1)}, bf16[544,128]{1,0:T(8,128)(2,1)S(1)}, u32[]{:S(2)}, u32[]{:S(2)}) collective-permute-start(bf16[544,128]{1,0:T(8,128)(2,1)S(1)} %pack.1.own_ref), channel_id=1, source_target_pairs={{0,64},{8,72},{16,80},{24,88},{32,96},{40,104},{48,112},{56,120},{... | collective-permute-start | bytes 417800 | tf_op jit(solution)/shard_map/ppermute | solution.py:375
  15.2 9.9 %collective-permute-start.1 = (bf16[544,128]{1,0:T(8,128)(2,1)S(1)}, bf16[544,128]{1,0:T(8,128)(2,1)S(1)}, u32[]{:S(2)}, u32[]{:S(2)}) collective-permute-start(bf16[544,128]{1,0:T(8,128)(2,1)S(1)} %pack.1.own_ref), channel_id=1, source_target_pairs={{0,96},{8,104},{16,112},{24,120},{32,0},{40,8},{48,16},{56,24},{64... | collective-permute-start | bytes 417800 | tf_op jit(solution)/shard_map/ppermute | solution.py:375
  16.1 9.1 %collective-permute-start = (bf16[544,128]{1,0:T(8,128)(2,1)S(1)}, bf16[544,128]{1,0:T(8,128)(2,1)S(1)}, u32[]{:S(2)}, u32[]{:S(2)}) collective-permute-start(bf16[544,128]{1,0:T(8,128)(2,1)S(1)} %pack.1.own_ref), channel_id=1, source_target_pairs={{0,32},{8,40},{16,48},{24,56},{32,64},{40,72},{48,80},{56,88},{64,... | collective-permute-start | bytes 417800 | tf_op jit(solution)/shard_map/ppermute | solution.py:375
  18.5 34.7 %collective-permute-start.10 = (bf16[816,128]{1,0:T(8,128)(2,1)S(1)}, bf16[816,128]{1,0:T(8,128)(2,1)S(1)}, u32[]{:S(2)}, u32[]{:S(2)}) collective-permute-start(bf16[816,128]{1,0:T(8,128)(2,1)S(1)} %join.3), channel_id=1, source_target_pairs={{0,96},{8,104},{16,112},{24,120},{32,0},{40,8},{48,16},{56,24},{64... | collective-permute-start | bytes 626696 | tf_op jit(solution)/shard_map/ppermute | solution.py:375
  24.3 28.9 %collective-permute-start.9 = (bf16[816,128]{1,0:T(8,128)(2,1)S(1)}, bf16[816,128]{1,0:T(8,128)(2,1)S(1)}, u32[]{:S(2)}, u32[]{:S(2)}) collective-permute-start(bf16[816,128]{1,0:T(8,128)(2,1)S(1)} %join.3), channel_id=1, source_target_pairs={{0,32},{8,40},{16,48},{24,56},{32,64},{40,72},{48,80},{56,88},{64,... | collective-permute-start | bytes 626696 | tf_op jit(solution)/shard_map/ppermute | solution.py:375
  25.1 28.0 %collective-permute-start.8 = (bf16[816,128]{1,0:T(8,128)(2,1)S(1)}, bf16[816,128]{1,0:T(8,128)(2,1)S(1)}, u32[]{:S(2)}, u32[]{:S(2)}) collective-permute-start(bf16[816,128]{1,0:T(8,128)(2,1)S(1)} %join.2), channel_id=1, source_target_pairs={{0,16},{8,24},{16,0},{24,8},{32,48},{40,56},{48,32},{56,40},{64,80... | collective-permute-start | bytes 626696 | tf_op jit(solution)/shard_map/ppermute | solution.py:375
  28.8 24.3 %collective-permute-start.7 = (bf16[816,128]{1,0:T(8,128)(2,1)S(1)}, bf16[816,128]{1,0:T(8,128)(2,1)S(1)}, u32[]{:S(2)}, u32[]{:S(2)}) collective-permute-start(bf16[816,128]{1,0:T(8,128)(2,1)S(1)} %join.2), channel_id=1, source_target_pairs={{0,24},{8,0},{16,8},{24,16},{32,56},{40,32},{48,40},{56,48},{64,88... | collective-permute-start | bytes 626696 | tf_op jit(solution)/shard_map/ppermute | solution.py:375
  30.1 23.1 %collective-permute-start.6 = (bf16[816,128]{1,0:T(8,128)(2,1)S(1)}, bf16[816,128]{1,0:T(8,128)(2,1)S(1)}, u32[]{:S(2)}, u32[]{:S(2)}) collective-permute-start(bf16[816,128]{1,0:T(8,128)(2,1)S(1)} %join.2), channel_id=1, source_target_pairs={{0,8},{8,16},{16,24},{24,0},{32,40},{40,48},{48,56},{56,32},{64,72... | collective-permute-start | bytes 626696 | tf_op jit(solution)/shard_map/ppermute | solution.py:375
  59.7 2.0 %collective-permute-start.14 = (bf16[64,4096]{1,0:T(8,128)(2,1)S(1)}, bf16[64,4096]{1,0:T(8,128)(2,1)S(1)}, u32[]{:S(2)}, u32[]{:S(2)}) collective-permute-start(bf16[64,4096]{1,0:T(8,128)(2,1)S(1)} %get-tuple-element.52), channel_id=1, source_target_pairs={{0,1},{1,0},{2,3},{3,2},{4,5},{5,4},{6,7},{7,6},{8,9},{9,8},{10,11... | collective-permute-start | bytes 1572872 | tf_op jit(solution)/shard_map/ppermute | solution.py:448
  59.8 8.9 %collective-permute-start.12 = (bf16[64,4096]{1,0:T(8,128)(2,1)S(1)}, bf16[64,4096]{1,0:T(8,128)(2,1)S(1)}, u32[]{:S(2)}, u32[]{:S(2)}) collective-permute-start(bf16[64,4096]{1,0:T(8,128)(2,1)S(1)} %get-tuple-element.46), channel_id=1, source_target_pairs={{0,1},{1,0},{2,3},{3,2},{4,5},{5,4},{6,7},{7,6},{8,9},{9,8},{10,11... | collective-permute-start | bytes 1572872 | tf_op jit(solution)/shard_map/ppermute | solution.py:448
  68.2 5.3 %collective-permute-start.16 = (bf16[64,4096]{1,0:T(8,128)(2,1)S(1)}, bf16[64,4096]{1,0:T(8,128)(2,1)S(1)}, u32[]{:S(2)}, u32[]{:S(2)}) collective-permute-start(bf16[64,4096]{1,0:T(8,128)(2,1)S(1)} %get-tuple-element.58), channel_id=1, source_target_pairs={{0,1},{1,0},{2,3},{3,2},{4,5},{5,4},{6,7},{7,6},{8,9},{9,8},{10,11... | collective-permute-start | bytes 1572872 | tf_op jit(solution)/shard_map/ppermute | solution.py:448
  68.4 6.0 %collective-permute-start.19 = (bf16[64,4096]{1,0:T(8,128)(2,1)S(1)}, bf16[64,4096]{1,0:T(8,128)(2,1)S(1)}, u32[]{:S(2)}, u32[]{:S(2)}) collective-permute-start(bf16[64,4096]{1,0:T(8,128)(2,1)S(1)} %get-tuple-element.69), channel_id=1, source_target_pairs={{0,1},{1,0},{2,3},{3,2},{4,5},{5,4},{6,7},{7,6},{8,9},{9,8},{10,11... | collective-permute-start | bytes 1572872 | tf_op jit(solution)/shard_map/ppermute | solution.py:448
  68.9 9.0 %collective-permute-start.13 = (bf16[32,4096]{1,0:T(8,128)(2,1)S(1)}, bf16[32,4096]{1,0:T(8,128)(2,1)S(1)}, u32[]{:S(2)}, u32[]{:S(2)}) collective-permute-start(bf16[32,4096]{1,0:T(8,128)(2,1)S(1)} %get-tuple-element.48), channel_id=1, source_target_pairs={{0,2},{1,3},{2,0},{3,1},{4,6},{5,7},{6,4},{7,5},{8,10},{9,11},{10,... | collective-permute-start | bytes 786440 | tf_op jit(solution)/shard_map/ppermute | solution.py:451
  70.9 10.4 %collective-permute-start.15 = (bf16[32,4096]{1,0:T(8,128)(2,1)S(1)}, bf16[32,4096]{1,0:T(8,128)(2,1)S(1)}, u32[]{:S(2)}, u32[]{:S(2)}) collective-permute-start(bf16[32,4096]{1,0:T(8,128)(2,1)S(1)} %get-tuple-element.54), channel_id=1, source_target_pairs={{0,6},{1,7},{2,4},{3,5},{4,2},{5,3},{6,0},{7,1},{8,14},{9,15},{10,... | collective-permute-start | bytes 786440 | tf_op jit(solution)/shard_map/ppermute | solution.py:451
  73.5 13.3 %collective-permute-start.22 = (bf16[32,4096]{1,0:T(8,128)(2,1)S(1)}, bf16[32,4096]{1,0:T(8,128)(2,1)S(1)}, u32[]{:S(2)}, u32[]{:S(2)}) collective-permute-start(bf16[32,4096]{1,0:T(8,128)(2,1)S(1)} %get-tuple-element.59), channel_id=1, source_target_pairs={{0,6},{1,7},{2,4},{3,5},{4,2},{5,3},{6,0},{7,1},{8,14},{9,15},{10,... | collective-permute-start | bytes 786440 | tf_op jit(solution)/shard_map/ppermute | solution.py:451
  74.5 12.8 %collective-permute-start.20 = (bf16[32,4096]{1,0:T(8,128)(2,1)S(1)}, bf16[32,4096]{1,0:T(8,128)(2,1)S(1)}, u32[]{:S(2)}, u32[]{:S(2)}) collective-permute-start(bf16[32,4096]{1,0:T(8,128)(2,1)S(1)} %get-tuple-element.71), channel_id=1, source_target_pairs={{0,2},{1,3},{2,0},{3,1},{4,6},{5,7},{6,4},{7,5},{8,10},{9,11},{10,... | collective-permute-start | bytes 786440 | tf_op jit(solution)/shard_map/ppermute | solution.py:451
  81.3 8.8 %collective-permute-start.17 = (bf16[16,4096]{1,0:T(8,128)(2,1)S(1)}, bf16[16,4096]{1,0:T(8,128)(2,1)S(1)}, u32[]{:S(2)}, u32[]{:S(2)}) collective-permute-start(bf16[16,4096]{1,0:T(8,128)(2,1)S(1)} %get-tuple-element.63), channel_id=1, source_target_pairs={{0,6},{1,7},{2,4},{3,5},{4,2},{5,3},{6,0},{7,1},{8,14},{9,15},{10,... | collective-permute-start | bytes 393224 | tf_op jit(solution)/shard_map/ppermute | solution.py:451
  84.0 6.3 %collective-permute-start.18 = (bf16[16,4096]{1,0:T(8,128)(2,1)S(1)}, bf16[16,4096]{1,0:T(8,128)(2,1)S(1)}, u32[]{:S(2)}, u32[]{:S(2)}) collective-permute-start(bf16[16,4096]{1,0:T(8,128)(2,1)S(1)} %get-tuple-element.67), channel_id=1, source_target_pairs={{0,2},{1,3},{2,0},{3,1},{4,6},{5,7},{6,4},{7,5},{8,10},{9,11},{10,... | collective-permute-start | bytes 393224 | tf_op jit(solution)/shard_map/ppermute | solution.py:451
  86.9 5.0 %collective-permute-start.23 = (bf16[16,4096]{1,0:T(8,128)(2,1)S(1)}, bf16[16,4096]{1,0:T(8,128)(2,1)S(1)}, u32[]{:S(2)}, u32[]{:S(2)}) collective-permute-start(bf16[16,4096]{1,0:T(8,128)(2,1)S(1)} %get-tuple-element.76), channel_id=1, source_target_pairs={{0,2},{1,3},{2,0},{3,1},{4,6},{5,7},{6,4},{7,5},{8,10},{9,11},{10,... | collective-permute-start | bytes 393224 | tf_op jit(solution)/shard_map/ppermute | solution.py:451
  87.4 6.3 %collective-permute-start.21 = (bf16[16,4096]{1,0:T(8,128)(2,1)S(1)}, bf16[16,4096]{1,0:T(8,128)(2,1)S(1)}, u32[]{:S(2)}, u32[]{:S(2)}) collective-permute-start(bf16[16,4096]{1,0:T(8,128)(2,1)S(1)} %get-tuple-element.73), channel_id=1, source_target_pairs={{0,6},{1,7},{2,4},{3,5},{4,2},{5,3},{6,0},{7,1},{8,14},{9,15},{10,... | collective-permute-start | bytes 393224 | tf_op jit(solution)/shard_map/ppermute | solution.py:451

commit v5 on v4

--- a/solution.py
+++ b/solution.py
@@ -11,14 +11,15 @@
 
 HD = 128
 SPAN = 128
-QUAD = 4
+HEADS = 8
+SLICE = 8
+CHUNKS = ((0, 1, 2), (3,))
 PACK = 272
 LOG_SCALE = HD ** -0.5 * math.log2(math.e)
 NEG = -1e30
 NX = 4
 NZ = 4
 NCORE = 2
-PIECE = 16
 DOUT = 8192
 NCOL = 8
 GROUP = 4
@@ -61,12 +62,12 @@
         out_ref[i * PACK:(i + 1) * PACK] = ref[part * PACK:(part + 1) * PACK]
 
 
-def query_tile(q_ref, chunk, s, quad):
+def query_tile(q_ref, s, j):
     pieces = []
-    for h in range(quad * QUAD, (quad + 1) * QUAD):
+    for h in range(HEADS):
         for t in range(4):
-            row = s * SPAN + t * 32 + chunk * PIECE
-            pieces.append(q_ref[row:row + PIECE, h * HD:(h + 1) * HD])
+            row = s * SPAN + t * 32 + j * SLICE
+            pieces.append(q_ref[row:row + SLICE, h * HD:(h + 1) * HD])
     return jnp.concatenate(pieces, axis=0)
 
 
@@ -186,18 +187,17 @@
     counts = [visible_list(ref, ids, ids[s]) for s, ref in enumerate((list0, list1))]
     lists = (list0, list1)
     fetch_q.wait()
-    for chunk in range(2):
-        for s in range(2):
-            for quad in range(2):
-                tile_ref[chunk * 4 + s * 2 + quad] = query_tile(q_ref, chunk, s, quad)
-    units = [[chunk * 4 + s * 2 + quad for chunk in range(2) for quad in range(2)] for s in range(2)]
+    for s in range(2):
+        for j in range(4):
+            tile_ref[s * 4 + j] = query_tile(q_ref, s, j)
+    units = [[s * 4 + j for j in range(4)] for s in range(2)]
     queries = [[tile_ref[u] for u in units[s]] for s in range(2)]
 
     def own_block():
         for s in range(2):
             for n, u in enumerate(units[s]):
-                lane = lax.broadcasted_iota(jnp.int32, (SPAN, 256), 1) % 64
-                row = (lane // PIECE) * 32 + lane % PIECE + (n // 2) * PIECE
+                lane = lax.broadcasted_iota(jnp.int32, (SPAN, 256), 1) % 32
+                row = (lane // SLICE) * 32 + lane % SLICE + n * SLICE
                 scores = scores_of(kv_ref[s, 0:128, :], queries[s][n])
                 key = lax.broadcasted_iota(jnp.int32, (SPAN, 256), 0)
                 scores = jnp.where(key <= row, scores, NEG)
@@ -222,32 +222,34 @@
         copy.wait()
 
 
-def rest_of_attention(chunk, spans, tile_ref, own_ref, far, m_in, acc_in, kv_ref, m_ref, peak_ref,
+def rest_of_attention(chunk, tile_ref, own_ref, far, m_in, acc_in, kv_ref, m_ref, peak_ref,
                       acc_ref, even_ref, odd_ref, lists):
     blocks = [(ref, j) for ref in far for j in range(3)]
     store_keys(kv_ref, blocks)
     ids = [span_id(ref, j) for ref, j in blocks]
-    counts = [visible_list(lists[n], ids, span_id(own_ref, s)) for n, s in enumerate(spans)]
-    queries = [[tile_ref[chunk * 4 + s * 2 + quad] for quad in range(2)] for s in spans]
-    units = [(2 * n, 2 * n + 1) for n in range(len(spans))]
+    counts = [visible_list(lists[s], ids, span_id(own_ref, s)) for s in range(2)]
+    slices = CHUNKS[chunk]
+    width = len(slices)
+    queries = [[tile_ref[s * 4 + j] for j in slices] for s in range(2)]
+    units = [[s * width + n for n in range(width)] for s in range(2)]
 
     def reset():
-        for n, s in enumerate(spans):
-            for quad in range(2):
-                m_ref[2 * n + quad] = m_in[chunk * 4 + s * 2 + quad]
-                acc_ref[2 * n + quad] = acc_in[chunk * 4 + s * 2 + quad]
+        for s in range(2):
+            for n, j in enumerate(slices):
+                m_ref[s * width + n] = m_in[s * 4 + j]
+                acc_ref[s * width + n] = acc_in[s * 4 + j]
 
     reset()
     peak_ref[...] = m_ref[...]
-    for n in range(len(spans)):
-        fast_walk(kv_ref, lists[n], counts[n], queries[n], units[n], m_ref, peak_ref, acc_ref,
+    for s in range(2):
+        fast_walk(kv_ref, lists[s], counts[s], queries[s], units[s], m_ref, peak_ref, acc_ref,
                   (even_ref, odd_ref))
 
-    @pl.when(overshoot(peak_ref, m_ref, range(2 * len(spans))))
+    @pl.when(overshoot(peak_ref, m_ref, range(2 * width)))
     def _():
         reset()
-        for n in range(len(spans)):
-            slow_walk(kv_ref, lists[n], counts[n], queries[n], units[n], m_ref, acc_ref)
+        for s in range(2):
+            slow_walk(kv_ref, lists[s], counts[s], queries[s], units[s], m_ref, acc_ref)
 
 
 def place_of(z_to, core_to, z, core):
@@ -256,21 +258,25 @@
     return (core_to ^ core) * NZ + slot
 
 
-def finish(s, acc_ref, base, index_ref, merged_ref):
+def finish(acc_ref, width, index_ref, merged_ref):
     z, core = index_ref[0] // NCORE, index_ref[0] % NCORE
-    for quad in range(2):
-        acc = acc_ref[base + quad]
-        o = acc[:128] * (1.0 / acc[128:129])
-        for half in range(2):
-            rows = o[:, half * 128:(half + 1) * 128].T.astype(jnp.bfloat16)
-            for i in range(2):
-                h = quad * QUAD + half * 2 + i
-                for t in range(4):
-                    owner = s * 4 + t
-                    place = place_of(owner // NCORE, owner % NCORE, z, core)
-                    where = pl.multiple_of(place * PIECE, PIECE)
-                    at = i * 64 + t * PIECE
-                    merged_ref[pl.ds(where, PIECE), h * HD:(h + 1) * HD] = rows[at:at + PIECE]
+    for s in range(2):
+        starts = []
+        for t in range(4):
+            owner = s * 4 + t
+            place = place_of(owner // NCORE, owner % NCORE, z, core)
+            starts.append(pl.multiple_of(place * (width * SLICE), SLICE))
+        for n in range(width):
+            acc = acc_ref[s * width + n]
+            o = acc[:128] * (1.0 / acc[128:129])
+            for half in range(2):
+                rows = o[:, half * 128:(half + 1) * 128].T.astype(jnp.bfloat16)
+                for i in range(4):
+                    columns = slice((half * 4 + i) * HD, (half * 4 + i + 1) * HD)
+                    for t in range(4):
+                        at = i * 32 + t * SLICE
+                        where = pl.ds(starts[t] + n * SLICE, SLICE)
+                        merged_ref[where, columns] = rows[at:at + SLICE]
 
 
 def project(merged_ref, w_ref, keep_ref, send_ref):
@@ -279,8 +285,9 @@
         at = slice(j * cols, (j + 1) * cols)
         part = jnp.dot(merged_ref[...], w_ref[:, at], preferred_element_type=jnp.float32)
         part = part.astype(jnp.bfloat16)
-        keep_ref[:, at] = part[:64]
-        send_ref[:, at] = part[64:]
+        rows = part.shape[0] // 2
+        keep_ref[:, at] = part[:rows]
+        send_ref[:, at] = part[rows:]
 
 
 def last_kernel(chunk, index_ref, tile_ref, own_ref, f1, f2, f3, f4, f5, f6, m_in, acc_in, w_ref,
@@ -291,11 +298,9 @@
         fetch_w = fetch_half(1, w_hbm, w_next, sems)
     (keep_ref, send_ref, merged_ref, acc_ref, kv_ref, m_ref, peak_ref, even_ref, odd_ref,
      list0, list1) = refs
-    spans = (0, 1)
-    rest_of_attention(chunk, spans, tile_ref, own_ref, (f1, f2, f3, f4, f5, f6), m_in, acc_in,
+    rest_of_attention(chunk, tile_ref, own_ref, (f1, f2, f3, f4, f5, f6), m_in, acc_in,
                       kv_ref, m_ref, peak_ref, acc_ref, even_ref, odd_ref, (list0, list1))
-    for s in spans:
-        finish(s, acc_ref, 2 * s, index_ref, merged_ref)
+    finish(acc_ref, len(CHUNKS[chunk]), index_ref, merged_ref)
     project(merged_ref, w_ref, keep_ref, send_ref)
     if chunk == 0:
         for copy in fetch_w:
@@ -304,17 +309,19 @@
 
 def pair_kernel(half, keep_ref, got_ref, stay_ref, send_ref):
     stay, send = ((0, 1), (2, 3)) if half == 0 else ((0, 2), (1, 3))
+    size = keep_ref.shape[0] // NZ
     for out_ref, slots in ((stay_ref, stay), (send_ref, send)):
         for i, slot in enumerate(slots):
-            rows = slice(slot * PIECE, (slot + 1) * PIECE)
+            rows = slice(slot * size, (slot + 1) * size)
             total = keep_ref[rows].astype(jnp.float32) + got_ref[rows]
-            out_ref[i * PIECE:(i + 1) * PIECE] = total.astype(jnp.bfloat16)
+            out_ref[i * size:(i + 1) * size] = total.astype(jnp.bfloat16)
 
 
 def fold_kernel(stay_ref, got_ref, mine_ref, send_ref):
     total = (stay_ref[...].astype(jnp.float32) + got_ref[...]).astype(jnp.bfloat16)
-    mine_ref[...] = total[:PIECE]
-    send_ref[...] = total[PIECE:]
+    size = total.shape[0] // 2
+    mine_ref[...] = total[:size]
+    send_ref[...] = total[size:]
 
 
 def final_kernel(*refs):
@@ -323,7 +330,8 @@
         chunk, half = i // 2, i % 2
         total = refs[2 * i][...].astype(jnp.float32) + refs[2 * i + 1][...]
         columns = slice(half * DOUT // 2, (half + 1) * DOUT // 2)
-        out_ref[chunk * PIECE:(chunk + 1) * PIECE, columns] = total.astype(jnp.bfloat16)
+        rows = slice(CHUNKS[chunk][0] * SLICE, (CHUNKS[chunk][-1] + 1) * SLICE)
+        out_ref[rows, columns] = total.astype(jnp.bfloat16)
 
 
 def in_hbm(array):
@@ -415,11 +423,14 @@
         in_hbm(queries), in_hbm(out_weight), own, *xs, *ys
     )
 
-    halves = [struct((64, DOUT // 2), bf16)] * 2
+    def halves(chunk):
+        return [struct((NZ * SLICE * len(CHUNKS[chunk]), DOUT // 2), bf16)] * 2
 
     def last(chunk, acc, *w_hbm):
-        outs = halves + [struct((128, 1024), bf16)]
-        scratch = [pltpu.VMEM((4, 144, 256), f32)] + walk_scratch(18, 4, 2)
+        width = len(CHUNKS[chunk])
+        rows = 2 * NZ * SLICE * width
+        outs = halves(chunk) + [struct((rows, 1024), bf16)]
+        scratch = [pltpu.VMEM((2 * width, 144, 256), f32)] + walk_scratch(18, 2 * width, width)
         if w_hbm:
             outs = outs + [struct((1024, DOUT // 2), bf16)]
             scratch = scratch + [pltpu.SemaphoreType.DMA((NW,))]
@@ -431,10 +442,10 @@
             cost_estimate=estimate(5 * 10 ** 9, 1 << 20),
         )(index, tiles, own, *fa, *fb, maxima, acc, weight_a, *w_hbm)
 
-    def rest(merged, weight):
+    def rest(chunk, merged, weight):
         return pl.pallas_call(
-            project, in_specs=[VMEM] * 2, out_specs=[VMEM] * 2, out_shape=halves,
-            compiler_params=params(6), name="rest", cost_estimate=estimate(10 ** 9, 1 << 20),
+            project, in_specs=[VMEM] * 2, out_specs=[VMEM] * 2, out_shape=halves(chunk),
+            compiler_params=params(8), cost_estimate=estimate(10 ** 9, 1 << 20),
         )(merged, weight)
 
     def call(kernel, rows, columns, *blocks):
@@ -452,13 +463,14 @@
 
     def pair(half, keep, got):
         kernel = functools.partial(pair_kernel, half)
-        return call(kernel, (32, 32), DOUT // 2, keep, got)
+        rows = keep.shape[0] // 2
+        return call(kernel, (rows, rows), DOUT // 2, keep, got)
 
     def chunk_parts(chunk, acc, *w_hbm):
         keep_a, send_a, merged, *w_next = last(chunk, acc, *w_hbm)
         got_a = swap(send_a)
         w_half = w_next[0] if w_next else weight_b
-        keep_b, send_b = rest(merged, w_half)
+        keep_b, send_b = rest(chunk, merged, w_half)
         got_b = swap(send_b)
         stay_a, out_a = pair(0, keep_a, got_a)
         in_a = step(0, out_a)
@@ -467,7 +479,8 @@
         return stay_a, in_a, stay_b, in_b, out_b, w_half
 
     def second_step(half, stay, got):
-        mine, out = call(fold_kernel, (16, 16), DOUT // 2, stay, got)
+        rows = stay.shape[0] // 2
+        mine, out = call(fold_kernel, (rows, rows), DOUT // 2, stay, got)
         return mine, step(1 - half, out)
 
     *early, out_b0, weight_b = chunk_parts(0, acc, in_hbm(out_weight))

time: 94.7 us -> 92.3 us (0.975)
  waiting for transfers between devices: 26.1 us -> 21.9 us
  Pallas kernels: 37.7 us -> 40.1 us
    ppermute x8, waiting for transfers between devices: 12.7 us -> 7.1 us  [step(): return lax.ppermute(block, 'tp', step_route(pairing))]
    pallas_call x2, Pallas kernels: 10.3 us -> 11.7 us  [last(): pl.pallas_call(functools.partial(last_kernel, chunk), in_specs=[SMEM] + [...]
    ppermute x4, waiting for transfers between devices: 1.41 us -> 2.8 us  [swap(): return lax.ppermute(block, 'tp', swap_route())]
  transfers between devices with their start and end apart: 24 -> 24, of which waited for: 12 -> 11; matrix products, arithmetic and copies ran while one was open for 0% -> 0% of each run, Pallas kernels for 31% -> 32%
where the time goes in v5:
time: 92.3 us; the launch traced here: 92.1 us
  Pallas kernels  40.1 us (43%)
  starting transfers between devices  30 us (33%)
  waiting for transfers between devices  21.9 us (24%)
    pallas_call x1, Pallas kernels, on_device(): first(in_hbm(queries), in_hbm(out_weight), own, *xs, *ys)  22.3 us
    ppermute x12, starting transfers between devices, shifts(): moved.append(lax.ppermute(block, 'ctx', ctx_route(dx * d, dy * d)))  17.9 us
    ppermute x12, waiting for transfers between devices, shifts(): moved.append(lax.ppermute(block, 'ctx', ctx_route(dx * d, dy * d)))  12 us
    pallas_call x2, Pallas kernels, last(): pl.pallas_call(functools.partial(last_kernel, chunk), in_specs=[SMEM] + [...  11.7 us
    ppermute x8, starting transfers between devices, step(): return lax.ppermute(block, 'tp', step_route(pairing))  10.9 us
    ppermute x8, waiting for transfers between devices, step(): return lax.ppermute(block, 'tp', step_route(pairing))  7.1 us
    pallas_call x2, Pallas kernels, rest(): pl.pallas_call(project, in_specs=[VMEM] * 2, out_specs=[VMEM] * 2, out_sh...  3.4 us
    ppermute x4, waiting for transfers between devices, swap(): return lax.ppermute(block, 'tp', swap_route())  2.8 us
  transfers between devices with their start and end apart: 24, of which 11 were waited for; matrix products, arithmetic and copies ran while one was open for 0% of the time, Pallas kernels for 32%

profile of v5, /device:TPU:6, one launch (start us, length us, event | category | flops | bytes accessed | tf_op | source)
XLA Modules:
  0.0 92.1 jit_solution(13585200788715593532)
XLA Ops:
  1.0 3.3 %collective-permute-start.5 = (bf16[544,128]{1,0:T(8,128)(2,1)S(1)}, bf16[544,128]{1,0:T(8,128)(2,1)S(1)}, u32[]{:S(2)}, u32[]{:S(2)}) collective-permute-start(bf16[544,128]{1,0:T(8,128)(2,1)S(1)} %pack.1.own_ref), channel_id=1, source_target_pairs={{0,16},{8,24},{16,0},{24,8},{32,48},{40,56},{48,32},{56,40},{64,80... | collective-permute-start | bytes 417800 | tf_op jit(solution)/shard_map/ppermute | solution.py:383
  4.3 1.1 %collective-permute-start.4 = (bf16[544,128]{1,0:T(8,128)(2,1)S(1)}, bf16[544,128]{1,0:T(8,128)(2,1)S(1)}, u32[]{:S(2)}, u32[]{:S(2)}) collective-permute-start(bf16[544,128]{1,0:T(8,128)(2,1)S(1)} %pack.1.own_ref), channel_id=1, source_target_pairs={{0,24},{8,0},{16,8},{24,16},{32,56},{40,32},{48,40},{56,48},{64,88... | collective-permute-start | bytes 417800 | tf_op jit(solution)/shard_map/ppermute | solution.py:383
  6.3 2.5 %collective-permute-done.5.y3.refs_2_ = bf16[544,128]{1,0:T(8,128)(2,1)S(1)} collective-permute-done((bf16[544,128]{1,0:T(8,128)(2,1)S(1)}, bf16[544,128]{1,0:T(8,128)(2,1)S(1)}, u32[]{:S(2)}, u32[]{:S(2)}) %collective-permute-start.5) | collective-permute-done | bytes 139296 | tf_op jit(solution)/shard_map/ppermute | solution.py:383
  8.8 2.5 %collective-permute-done.4.y2.refs_1_ = bf16[544,128]{1,0:T(8,128)(2,1)S(1)} collective-permute-done((bf16[544,128]{1,0:T(8,128)(2,1)S(1)}, bf16[544,128]{1,0:T(8,128)(2,1)S(1)}, u32[]{:S(2)}, u32[]{:S(2)}) %collective-permute-start.4) | collective-permute-done | bytes 139296 | tf_op jit(solution)/shard_map/ppermute | solution.py:383
  11.6 1.5 %collective-permute-start.11 = (bf16[816,128]{1,0:T(8,128)(2,1)S(1)}, bf16[816,128]{1,0:T(8,128)(2,1)S(1)}, u32[]{:S(2)}, u32[]{:S(2)}) collective-permute-start(bf16[816,128]{1,0:T(8,128)(2,1)S(1)} %join.3), channel_id=1, source_target_pairs={{0,64},{8,72},{16,80},{24,88},{32,96},{40,104},{48,112},{56,120},{... | collective-permute-start | bytes 626696 | tf_op jit(solution)/shard_map/ppermute | solution.py:383
  13.1 2.1 %collective-permute-start.2 = (bf16[544,128]{1,0:T(8,128)(2,1)S(1)}, bf16[544,128]{1,0:T(8,128)(2,1)S(1)}, u32[]{:S(2)}, u32[]{:S(2)}) collective-permute-start(bf16[544,128]{1,0:T(8,128)(2,1)S(1)} %pack.1.own_ref), channel_id=1, source_target_pairs={{0,64},{8,72},{16,80},{24,88},{32,96},{40,104},{48,112},{56,120},{... | collective-permute-start | bytes 417800 | tf_op jit(solution)/shard_map/ppermute | solution.py:383
  16.1 2.4 %collective-permute-start = (bf16[544,128]{1,0:T(8,128)(2,1)S(1)}, bf16[544,128]{1,0:T(8,128)(2,1)S(1)}, u32[]{:S(2)}, u32[]{:S(2)}) collective-permute-start(bf16[544,128]{1,0:T(8,128)(2,1)S(1)} %pack.1.own_ref), channel_id=1, source_target_pairs={{0,32},{8,40},{16,48},{24,56},{32,64},{40,72},{48,80},{56,88},{64,... | collective-permute-start | bytes 417800 | tf_op jit(solution)/shard_map/ppermute | solution.py:383
  18.5 5.8 %collective-permute-done.2.x3.refs_2_ = bf16[544,128]{1,0:T(8,128)(2,1)S(1)} collective-permute-done((bf16[544,128]{1,0:T(8,128)(2,1)S(1)}, bf16[544,128]{1,0:T(8,128)(2,1)S(1)}, u32[]{:S(2)}, u32[]{:S(2)}) %collective-permute-start.2) | collective-permute-done | bytes 139296 | tf_op jit(solution)/shard_map/ppermute | solution.py:383
  25.1 3.7 %collective-permute-start.8 = (bf16[816,128]{1,0:T(8,128)(2,1)S(1)}, bf16[816,128]{1,0:T(8,128)(2,1)S(1)}, u32[]{:S(2)}, u32[]{:S(2)}) collective-permute-start(bf16[816,128]{1,0:T(8,128)(2,1)S(1)} %join.2), channel_id=1, source_target_pairs={{0,16},{8,24},{16,0},{24,8},{32,48},{40,56},{48,32},{56,40},{64,80... | collective-permute-start | bytes 626696 | tf_op jit(solution)/shard_map/ppermute | solution.py:383
  28.8 1.2 %collective-permute-start.7 = (bf16[816,128]{1,0:T(8,128)(2,1)S(1)}, bf16[816,128]{1,0:T(8,128)(2,1)S(1)}, u32[]{:S(2)}, u32[]{:S(2)}) collective-permute-start(bf16[816,128]{1,0:T(8,128)(2,1)S(1)} %join.2), channel_id=1, source_target_pairs={{0,24},{8,0},{16,8},{24,16},{32,56},{40,32},{48,40},{56,48},{64,88... | collective-permute-start | bytes 626696 | tf_op jit(solution)/shard_map/ppermute | solution.py:383
  30.9 22.3 %first.1 = (f32[8,8,256]{2,1,0:T(8,128)S(1)}, f32[8,144,256]{2,1,0:T(8,128)S(1)}, bf16[8,256,128]{2,1,0:T(8,128)(2,1)S(1)}, bf16[1024,4096]{1,0:T(8,128)(2,1)S(1)}) custom-call(bf16[256,1024]{1,0:T(8,128)(2,1)} %q_hbm.1, bf16[1024,8192]{1,0:T(8,128)(2,1)} %refs_0_.1, bf16[544,128]{1,0:T(8,128)(2,1)S(1)} %pack.1.own_ref, ...), custom_call_target="tpu_custom_call" | custom-call | flops 4000000000 | bytes 1048576 | tf_op jit(solution)/shard_map/first/pallas_call | solution.py:422
  53.2 6.9 %shard_map.55 = (bf16[96,4096]{1,0:T(8,128)(2,1)S(1)}, bf16[96,4096]{1,0:T(8,128)(2,1)S(1)}, bf16[192,1024]{1,0:T(8,128)(2,1)S(1)}, bf16[1024,4096]{1,0:T(8,128)(2,1)S(1)}) custom-call(s32[1]{0:T(128)} %bitcast.index_ref, bf16[8,256,128]{2,1,0:T(8,128)(2,1)S(1)} %get-tuple-element.41.tile_ref, bf16[544,128]{1,0:T(8,128)(2,1)S(1)} %pack.1.own_ref, ...), custom_call_target="tpu_custom_call" | custom-call | flops 5000000000 | bytes 1048576 | tf_op jit(solution)/shard_map/pallas_call | solution.py:437
  60.1 1.8 %shard_map.57 = (bf16[96,4096]{1,0:T(8,128)(2,1)S(1)}, bf16[96,4096]{1,0:T(8,128)(2,1)S(1)}) custom-call(bf16[192,1024]{1,0:T(8,128)(2,1)S(1)} %get-tuple-element.49.merged_ref, bf16[1024,4096]{1,0:T(8,128)(2,1)S(1)} %get-tuple-element.50.w_ref), custom_call_target="tpu_custom_call" | custom-call | flops 1000000000 | bytes 1048576 | tf_op jit(solution)/shard_map/pallas_call | solution.py:446
  62.5 1.8 %collective-permute-done.14.got_ref = bf16[96,4096]{1,0:T(8,128)(2,1)S(1)} collective-permute-done((bf16[96,4096]{1,0:T(8,128)(2,1)S(1)}, bf16[96,4096]{1,0:T(8,128)(2,1)S(1)}, u32[]{:S(2)}, u32[]{:S(2)}) %collective-permute-start.14) | collective-permute-done | bytes 786464 | tf_op jit(solution)/shard_map/ppermute | solution.py:459
  64.5 4.1 %collective-permute-start.15 = (bf16[48,4096]{1,0:T(8,128)(2,1)S(1)}, bf16[48,4096]{1,0:T(8,128)(2,1)S(1)}, u32[]{:S(2)}, u32[]{:S(2)}) collective-permute-start(bf16[48,4096]{1,0:T(8,128)(2,1)S(1)} %get-tuple-element.54), channel_id=1, source_target_pairs={{0,6},{1,7},{2,4},{3,5},{4,2},{5,3},{6,0},{7,1},{8,14},{9,15},{10,... | collective-permute-start | bytes 1179656 | tf_op jit(solution)/shard_map/ppermute | solution.py:462
  68.9 4.9 %shard_map.59 = (bf16[32,4096]{1,0:T(8,128)(2,1)S(1)}, bf16[32,4096]{1,0:T(8,128)(2,1)S(1)}, bf16[64,1024]{1,0:T(8,128)(2,1)S(1)}) custom-call(s32[1]{0:T(128)} %bitcast.index_ref, bf16[8,256,128]{2,1,0:T(8,128)(2,1)S(1)} %get-tuple-element.41.tile_ref, bf16[544,128]{1,0:T(8,128)(2,1)S(1)} %pack.1.own_ref, bf16[816,128]{1,0:T(8,128)(2,1)S(1)} %collective-permute-done.6.f1, ...), custom_call_target="tpu_custom_call" | custom-call | flops 5000000000 | bytes 1048576 | tf_op jit(solution)/shard_map/pallas_call | solution.py:437
  73.7 1.6 %shard_map.60 = (bf16[32,4096]{1,0:T(8,128)(2,1)S(1)}, bf16[32,4096]{1,0:T(8,128)(2,1)S(1)}) custom-call(bf16[64,1024]{1,0:T(8,128)(2,1)S(1)} %get-tuple-element.56.merged_ref, bf16[1024,4096]{1,0:T(8,128)(2,1)S(1)} %get-tuple-element.50.w_ref), custom_call_target="tpu_custom_call" | custom-call | flops 1000000000 | bytes 1048576 | tf_op jit(solution)/shard_map/pallas_call | solution.py:446
  77.0 1.3 %collective-permute-start.22 = (bf16[16,4096]{1,0:T(8,128)(2,1)S(1)}, bf16[16,4096]{1,0:T(8,128)(2,1)S(1)}, u32[]{:S(2)}, u32[]{:S(2)}) collective-permute-start(bf16[16,4096]{1,0:T(8,128)(2,1)S(1)} %get-tuple-element.59), channel_id=1, source_target_pairs={{0,6},{1,7},{2,4},{3,5},{4,2},{5,3},{6,0},{7,1},{8,14},{9,15},{10,... | collective-permute-start | bytes 393224 | tf_op jit(solution)/shard_map/ppermute | solution.py:462
  78.4 1.1 %collective-permute-start.20 = (bf16[16,4096]{1,0:T(8,128)(2,1)S(1)}, bf16[16,4096]{1,0:T(8,128)(2,1)S(1)}, u32[]{:S(2)}, u32[]{:S(2)}) collective-permute-start(bf16[16,4096]{1,0:T(8,128)(2,1)S(1)} %get-tuple-element.71), channel_id=1, source_target_pairs={{0,2},{1,3},{2,0},{3,1},{4,6},{5,7},{6,4},{7,5},{8,10},{9,11},{10,... | collective-permute-start | bytes 393224 | tf_op jit(solution)/shard_map/ppermute | solution.py:462
  79.8 2.2 %collective-permute-start.17 = (bf16[24,4096]{1,0:T(8,128)(2,1)S(1)}, bf16[24,4096]{1,0:T(8,128)(2,1)S(1)}, u32[]{:S(2)}, u32[]{:S(2)}) collective-permute-start(bf16[24,4096]{1,0:T(8,128)(2,1)S(1)} %get-tuple-element.63), channel_id=1, source_target_pairs={{0,6},{1,7},{2,4},{3,5},{4,2},{5,3},{6,0},{7,1},{8,14},{9,15},{10,... | collective-permute-start | bytes 589832 | tf_op jit(solution)/shard_map/ppermute | solution.py:462
  82.3 2.1 %collective-permute-done.22.got_ref = bf16[16,4096]{1,0:T(8,128)(2,1)S(1)} collective-permute-done((bf16[16,4096]{1,0:T(8,128)(2,1)S(1)}, bf16[16,4096]{1,0:T(8,128)(2,1)S(1)}, u32[]{:S(2)}, u32[]{:S(2)}) %collective-permute-start.22) | collective-permute-done | bytes 131104 | tf_op jit(solution)/shard_map/ppermute | solution.py:462
  84.4 1.2 %collective-permute-start.23 = (bf16[8,4096]{1,0:T(8,128)(2,1)S(1)}, bf16[8,4096]{1,0:T(8,128)(2,1)S(1)}, u32[]{:S(2)}, u32[]{:S(2)}) collective-permute-start(bf16[8,4096]{1,0:T(8,128)(2,1)S(1)} %get-tuple-element.76), channel_id=1, source_target_pairs={{0,2},{1,3},{2,0},{3,1},{4,6},{5,7},{6,4},{7,5},{8,10},{9,11},{10,... | collective-permute-start | bytes 196616 | tf_op jit(solution)/shard_map/ppermute | solution.py:462
  86.4 3.3 %collective-permute-done.23.refs_7_ = bf16[8,4096]{1,0:T(8,128)(2,1)S(1)} collective-permute-done((bf16[8,4096]{1,0:T(8,128)(2,1)S(1)}, bf16[8,4096]{1,0:T(8,128)(2,1)S(1)}, u32[]{:S(2)}, u32[]{:S(2)}) %collective-permute-start.23) | collective-permute-done | bytes 65568 | tf_op jit(solution)/shard_map/ppermute | solution.py:462
  89.7 1.4 %collective-permute-done.21.refs_5_ = bf16[8,4096]{1,0:T(8,128)(2,1)S(1)} collective-permute-done((bf16[8,4096]{1,0:T(8,128)(2,1)S(1)}, bf16[8,4096]{1,0:T(8,128)(2,1)S(1)}, u32[]{:S(2)}, u32[]{:S(2)}) %collective-permute-start.21) | collective-permute-done | bytes 65568 | tf_op jit(solution)/shard_map/ppermute | solution.py:462
  (41 shorter events, 9.9 us)
Async XLA Ops:
  1.0 7.8 %collective-permute-start.5 = (bf16[544,128]{1,0:T(8,128)(2,1)S(1)}, bf16[544,128]{1,0:T(8,128)(2,1)S(1)}, u32[]{:S(2)}, u32[]{:S(2)}) collective-permute-start(bf16[544,128]{1,0:T(8,128)(2,1)S(1)} %pack.1.own_ref), channel_id=1, source_target_pairs={{0,16},{8,24},{16,0},{24,8},{32,48},{40,56},{48,32},{56,40},{64,80... | collective-permute-start | bytes 417800 | tf_op jit(solution)/shard_map/ppermute | solution.py:383
  4.3 7.0 %collective-permute-start.4 = (bf16[544,128]{1,0:T(8,128)(2,1)S(1)}, bf16[544,128]{1,0:T(8,128)(2,1)S(1)}, u32[]{:S(2)}, u32[]{:S(2)}) collective-permute-start(bf16[544,128]{1,0:T(8,128)(2,1)S(1)} %pack.1.own_ref), channel_id=1, source_target_pairs={{0,24},{8,0},{16,8},{24,16},{32,56},{40,32},{48,40},{56,48},{64,88... | collective-permute-start | bytes 417800 | tf_op jit(solution)/shard_map/ppermute | solution.py:383
  5.3 6.3 %collective-permute-start.3 = (bf16[544,128]{1,0:T(8,128)(2,1)S(1)}, bf16[544,128]{1,0:T(8,128)(2,1)S(1)}, u32[]{:S(2)}, u32[]{:S(2)}) collective-permute-start(bf16[544,128]{1,0:T(8,128)(2,1)S(1)} %pack.1.own_ref), channel_id=1, source_target_pairs={{0,8},{8,16},{16,24},{24,0},{32,40},{40,48},{48,56},{56,32},{64,72... | collective-permute-start | bytes 417800 | tf_op jit(solution)/shard_map/ppermute | solution.py:383
  11.6 18.5 %collective-permute-start.11 = (bf16[816,128]{1,0:T(8,128)(2,1)S(1)}, bf16[816,128]{1,0:T(8,128)(2,1)S(1)}, u32[]{:S(2)}, u32[]{:S(2)}) collective-permute-start(bf16[816,128]{1,0:T(8,128)(2,1)S(1)} %join.3), channel_id=1, source_target_pairs={{0,64},{8,72},{16,80},{24,88},{32,96},{40,104},{48,112},{56,120},{... | collective-permute-start | bytes 626696 | tf_op jit(solution)/shard_map/ppermute | solution.py:383
  13.1 11.2 %collective-permute-start.2 = (bf16[544,128]{1,0:T(8,128)(2,1)S(1)}, bf16[544,128]{1,0:T(8,128)(2,1)S(1)}, u32[]{:S(2)}, u32[]{:S(2)}) collective-permute-start(bf16[544,128]{1,0:T(8,128)(2,1)S(1)} %pack.1.own_ref), channel_id=1, source_target_pairs={{0,64},{8,72},{16,80},{24,88},{32,96},{40,104},{48,112},{56,120},{... | collective-permute-start | bytes 417800 | tf_op jit(solution)/shard_map/ppermute | solution.py:383
  15.2 9.9 %collective-permute-start.1 = (bf16[544,128]{1,0:T(8,128)(2,1)S(1)}, bf16[544,128]{1,0:T(8,128)(2,1)S(1)}, u32[]{:S(2)}, u32[]{:S(2)}) collective-permute-start(bf16[544,128]{1,0:T(8,128)(2,1)S(1)} %pack.1.own_ref), channel_id=1, source_target_pairs={{0,96},{8,104},{16,112},{24,120},{32,0},{40,8},{48,16},{56,24},{64... | collective-permute-start | bytes 417800 | tf_op jit(solution)/shard_map/ppermute | solution.py:383
  16.1 9.1 %collective-permute-start = (bf16[544,128]{1,0:T(8,128)(2,1)S(1)}, bf16[544,128]{1,0:T(8,128)(2,1)S(1)}, u32[]{:S(2)}, u32[]{:S(2)}) collective-permute-start(bf16[544,128]{1,0:T(8,128)(2,1)S(1)} %pack.1.own_ref), channel_id=1, source_target_pairs={{0,32},{8,40},{16,48},{24,56},{32,64},{40,72},{48,80},{56,88},{64,... | collective-permute-start | bytes 417800 | tf_op jit(solution)/shard_map/ppermute | solution.py:383
  18.5 34.7 %collective-permute-start.10 = (bf16[816,128]{1,0:T(8,128)(2,1)S(1)}, bf16[816,128]{1,0:T(8,128)(2,1)S(1)}, u32[]{:S(2)}, u32[]{:S(2)}) collective-permute-start(bf16[816,128]{1,0:T(8,128)(2,1)S(1)} %join.3), channel_id=1, source_target_pairs={{0,96},{8,104},{16,112},{24,120},{32,0},{40,8},{48,16},{56,24},{64... | collective-permute-start | bytes 626696 | tf_op jit(solution)/shard_map/ppermute | solution.py:383
  24.3 28.9 %collective-permute-start.9 = (bf16[816,128]{1,0:T(8,128)(2,1)S(1)}, bf16[816,128]{1,0:T(8,128)(2,1)S(1)}, u32[]{:S(2)}, u32[]{:S(2)}) collective-permute-start(bf16[816,128]{1,0:T(8,128)(2,1)S(1)} %join.3), channel_id=1, source_target_pairs={{0,32},{8,40},{16,48},{24,56},{32,64},{40,72},{48,80},{56,88},{64,... | collective-permute-start | bytes 626696 | tf_op jit(solution)/shard_map/ppermute | solution.py:383
  25.1 28.1 %collective-permute-start.8 = (bf16[816,128]{1,0:T(8,128)(2,1)S(1)}, bf16[816,128]{1,0:T(8,128)(2,1)S(1)}, u32[]{:S(2)}, u32[]{:S(2)}) collective-permute-start(bf16[816,128]{1,0:T(8,128)(2,1)S(1)} %join.2), channel_id=1, source_target_pairs={{0,16},{8,24},{16,0},{24,8},{32,48},{40,56},{48,32},{56,40},{64,80... | collective-permute-start | bytes 626696 | tf_op jit(solution)/shard_map/ppermute | solution.py:383
  28.8 24.4 %collective-permute-start.7 = (bf16[816,128]{1,0:T(8,128)(2,1)S(1)}, bf16[816,128]{1,0:T(8,128)(2,1)S(1)}, u32[]{:S(2)}, u32[]{:S(2)}) collective-permute-start(bf16[816,128]{1,0:T(8,128)(2,1)S(1)} %join.2), channel_id=1, source_target_pairs={{0,24},{8,0},{16,8},{24,16},{32,56},{40,32},{48,40},{56,48},{64,88... | collective-permute-start | bytes 626696 | tf_op jit(solution)/shard_map/ppermute | solution.py:383
  30.1 23.1 %collective-permute-start.6 = (bf16[816,128]{1,0:T(8,128)(2,1)S(1)}, bf16[816,128]{1,0:T(8,128)(2,1)S(1)}, u32[]{:S(2)}, u32[]{:S(2)}) collective-permute-start(bf16[816,128]{1,0:T(8,128)(2,1)S(1)} %join.2), channel_id=1, source_target_pairs={{0,8},{8,16},{16,24},{24,0},{32,40},{40,48},{48,56},{56,32},{64,72... | collective-permute-start | bytes 626696 | tf_op jit(solution)/shard_map/ppermute | solution.py:383
  61.9 2.4 %collective-permute-start.14 = (bf16[96,4096]{1,0:T(8,128)(2,1)S(1)}, bf16[96,4096]{1,0:T(8,128)(2,1)S(1)}, u32[]{:S(2)}, u32[]{:S(2)}) collective-permute-start(bf16[96,4096]{1,0:T(8,128)(2,1)S(1)} %get-tuple-element.52), channel_id=1, source_target_pairs={{0,1},{1,0},{2,3},{3,2},{4,5},{5,4},{6,7},{7,6},{8,9},{9,8},{10,11... | collective-permute-start | bytes 2359304 | tf_op jit(solution)/shard_map/ppermute | solution.py:459
  62.0 6.6 %collective-permute-start.12 = (bf16[96,4096]{1,0:T(8,128)(2,1)S(1)}, bf16[96,4096]{1,0:T(8,128)(2,1)S(1)}, u32[]{:S(2)}, u32[]{:S(2)}) collective-permute-start(bf16[96,4096]{1,0:T(8,128)(2,1)S(1)} %get-tuple-element.46), channel_id=1, source_target_pairs={{0,1},{1,0},{2,3},{3,2},{4,5},{5,4},{6,7},{7,6},{8,9},{9,8},{10,11... | collective-permute-start | bytes 2359304 | tf_op jit(solution)/shard_map/ppermute | solution.py:459
  64.5 15.3 %collective-permute-start.15 = (bf16[48,4096]{1,0:T(8,128)(2,1)S(1)}, bf16[48,4096]{1,0:T(8,128)(2,1)S(1)}, u32[]{:S(2)}, u32[]{:S(2)}) collective-permute-start(bf16[48,4096]{1,0:T(8,128)(2,1)S(1)} %get-tuple-element.54), channel_id=1, source_target_pairs={{0,6},{1,7},{2,4},{3,5},{4,2},{5,3},{6,0},{7,1},{8,14},{9,15},{10,... | collective-permute-start | bytes 1179656 | tf_op jit(solution)/shard_map/ppermute | solution.py:462
  68.8 11.0 %collective-permute-start.13 = (bf16[48,4096]{1,0:T(8,128)(2,1)S(1)}, bf16[48,4096]{1,0:T(8,128)(2,1)S(1)}, u32[]{:S(2)}, u32[]{:S(2)}) collective-permute-start(bf16[48,4096]{1,0:T(8,128)(2,1)S(1)} %get-tuple-element.48), channel_id=1, source_target_pairs={{0,2},{1,3},{2,0},{3,1},{4,6},{5,7},{6,4},{7,5},{8,10},{9,11},{10,... | collective-permute-start | bytes 1179656 | tf_op jit(solution)/shard_map/ppermute | solution.py:462
  75.3 1.6 %collective-permute-start.16 = (bf16[32,4096]{1,0:T(8,128)(2,1)S(1)}, bf16[32,4096]{1,0:T(8,128)(2,1)S(1)}, u32[]{:S(2)}, u32[]{:S(2)}) collective-permute-start(bf16[32,4096]{1,0:T(8,128)(2,1)S(1)} %get-tuple-element.58), channel_id=1, source_target_pairs={{0,1},{1,0},{2,3},{3,2},{4,5},{5,4},{6,7},{7,6},{8,9},{9,8},{10,11... | collective-permute-start | bytes 786440 | tf_op jit(solution)/shard_map/ppermute | solution.py:459
  75.4 2.9 %collective-permute-start.19 = (bf16[32,4096]{1,0:T(8,128)(2,1)S(1)}, bf16[32,4096]{1,0:T(8,128)(2,1)S(1)}, u32[]{:S(2)}, u32[]{:S(2)}) collective-permute-start(bf16[32,4096]{1,0:T(8,128)(2,1)S(1)} %get-tuple-element.69), channel_id=1, source_target_pairs={{0,1},{1,0},{2,3},{3,2},{4,5},{5,4},{6,7},{7,6},{8,9},{9,8},{10,11... | collective-permute-start | bytes 786440 | tf_op jit(solution)/shard_map/ppermute | solution.py:459
  77.0 7.4 %collective-permute-start.22 = (bf16[16,4096]{1,0:T(8,128)(2,1)S(1)}, bf16[16,4096]{1,0:T(8,128)(2,1)S(1)}, u32[]{:S(2)}, u32[]{:S(2)}) collective-permute-start(bf16[16,4096]{1,0:T(8,128)(2,1)S(1)} %get-tuple-element.59), channel_id=1, source_target_pairs={{0,6},{1,7},{2,4},{3,5},{4,2},{5,3},{6,0},{7,1},{8,14},{9,15},{10,... | collective-permute-start | bytes 393224 | tf_op jit(solution)/shard_map/ppermute | solution.py:462
  78.4 7.2 %collective-permute-start.20 = (bf16[16,4096]{1,0:T(8,128)(2,1)S(1)}, bf16[16,4096]{1,0:T(8,128)(2,1)S(1)}, u32[]{:S(2)}, u32[]{:S(2)}) collective-permute-start(bf16[16,4096]{1,0:T(8,128)(2,1)S(1)} %get-tuple-element.71), channel_id=1, source_target_pairs={{0,2},{1,3},{2,0},{3,1},{4,6},{5,7},{6,4},{7,5},{8,10},{9,11},{10,... | collective-permute-start | bytes 393224 | tf_op jit(solution)/shard_map/ppermute | solution.py:462
  79.8 11.3 %collective-permute-start.17 = (bf16[24,4096]{1,0:T(8,128)(2,1)S(1)}, bf16[24,4096]{1,0:T(8,128)(2,1)S(1)}, u32[]{:S(2)}, u32[]{:S(2)}) collective-permute-start(bf16[24,4096]{1,0:T(8,128)(2,1)S(1)} %get-tuple-element.63), channel_id=1, source_target_pairs={{0,6},{1,7},{2,4},{3,5},{4,2},{5,3},{6,0},{7,1},{8,14},{9,15},{10,... | collective-permute-start | bytes 589832 | tf_op jit(solution)/shard_map/ppermute | solution.py:462
  82.2 9.0 %collective-permute-start.18 = (bf16[24,4096]{1,0:T(8,128)(2,1)S(1)}, bf16[24,4096]{1,0:T(8,128)(2,1)S(1)}, u32[]{:S(2)}, u32[]{:S(2)}) collective-permute-start(bf16[24,4096]{1,0:T(8,128)(2,1)S(1)} %get-tuple-element.67), channel_id=1, source_target_pairs={{0,2},{1,3},{2,0},{3,1},{4,6},{5,7},{6,4},{7,5},{8,10},{9,11},{10,... | collective-permute-start | bytes 589832 | tf_op jit(solution)/shard_map/ppermute | solution.py:462
  84.4 5.3 %collective-permute-start.23 = (bf16[8,4096]{1,0:T(8,128)(2,1)S(1)}, bf16[8,4096]{1,0:T(8,128)(2,1)S(1)}, u32[]{:S(2)}, u32[]{:S(2)}) collective-permute-start(bf16[8,4096]{1,0:T(8,128)(2,1)S(1)} %get-tuple-element.76), channel_id=1, source_target_pairs={{0,2},{1,3},{2,0},{3,1},{4,6},{5,7},{6,4},{7,5},{8,10},{9,11},{10,... | collective-permute-start | bytes 196616 | tf_op jit(solution)/shard_map/ppermute | solution.py:462
  85.6 5.6 %collective-permute-start.21 = (bf16[8,4096]{1,0:T(8,128)(2,1)S(1)}, bf16[8,4096]{1,0:T(8,128)(2,1)S(1)}, u32[]{:S(2)}, u32[]{:S(2)}) collective-permute-start(bf16[8,4096]{1,0:T(8,128)(2,1)S(1)} %get-tuple-element.73), channel_id=1, source_target_pairs={{0,6},{1,7},{2,4},{3,5},{4,2},{5,3},{6,0},{7,1},{8,14},{9,15},{10,... | collective-permute-start | bytes 196616 | tf_op jit(solution)/shard_map/ppermute | solution.py:462

commit v6 on v5

--- a/solution.py
+++ b/solution.py
@@ -13,7 +13,8 @@
 SPAN = 128
 HEADS = 8
 SLICE = 8
-CHUNKS = ((0, 1, 2), (3,))
+WIDTH = 4
+QUARTERS = 4
 PACK = 272
 LOG_SCALE = HD ** -0.5 * math.log2(math.e)
 NEG = -1e30
@@ -21,9 +22,10 @@
 NZ = 4
 NCORE = 2
 DOUT = 8192
-NCOL = 8
+QCOLS = DOUT // QUARTERS
 GROUP = 4
 HEADROOM = 60.0
+TILE = 1024
 NW = 4
 HOPS = (1, 3, 2)
 
@@ -222,22 +224,18 @@
         copy.wait()
 
 
-def rest_of_attention(chunk, tile_ref, own_ref, far, m_in, acc_in, kv_ref, m_ref, peak_ref,
+def rest_of_attention(tile_ref, own_ref, far, m_in, acc_in, kv_ref, m_ref, peak_ref,
                       acc_ref, even_ref, odd_ref, lists):
     blocks = [(ref, j) for ref in far for j in range(3)]
     store_keys(kv_ref, blocks)
     ids = [span_id(ref, j) for ref, j in blocks]
     counts = [visible_list(lists[s], ids, span_id(own_ref, s)) for s in range(2)]
-    slices = CHUNKS[chunk]
-    width = len(slices)
-    queries = [[tile_ref[s * 4 + j] for j in slices] for s in range(2)]
-    units = [[s * width + n for n in range(width)] for s in range(2)]
+    units = [[s * WIDTH + n for n in range(WIDTH)] for s in range(2)]
+    queries = [[tile_ref[u] for u in units[s]] for s in range(2)]
 
     def reset():
-        for s in range(2):
-            for n, j in enumerate(slices):
-                m_ref[s * width + n] = m_in[s * 4 + j]
-                acc_ref[s * width + n] = acc_in[s * 4 + j]
+        m_ref[...] = m_in[...]
+        acc_ref[...] = acc_in[...]
 
     reset()
     peak_ref[...] = m_ref[...]
@@ -245,7 +243,7 @@
         fast_walk(kv_ref, lists[s], counts[s], queries[s], units[s], m_ref, peak_ref, acc_ref,
                   (even_ref, odd_ref))
 
-    @pl.when(overshoot(peak_ref, m_ref, range(2 * width)))
+    @pl.when(overshoot(peak_ref, m_ref, range(2 * WIDTH)))
     def _():
         reset()
         for s in range(2):
@@ -258,16 +256,16 @@
     return (core_to ^ core) * NZ + slot
 
 
-def finish(acc_ref, width, index_ref, merged_ref):
+def finish(acc_ref, index_ref, merged_ref):
     z, core = index_ref[0] // NCORE, index_ref[0] % NCORE
     for s in range(2):
         starts = []
         for t in range(4):
             owner = s * 4 + t
             place = place_of(owner // NCORE, owner % NCORE, z, core)
-            starts.append(pl.multiple_of(place * (width * SLICE), SLICE))
-        for n in range(width):
-            acc = acc_ref[s * width + n]
+            starts.append(pl.multiple_of(place * (WIDTH * SLICE), SLICE))
+        for n in range(WIDTH):
+            acc = acc_ref[s * WIDTH + n]
             o = acc[:128] * (1.0 / acc[128:129])
             for half in range(2):
                 rows = o[:, half * 128:(half + 1) * 128].T.astype(jnp.bfloat16)
@@ -279,36 +277,32 @@
                         merged_ref[where, columns] = rows[at:at + SLICE]
 
 
-def project(merged_ref, w_ref, keep_ref, send_ref):
-    cols = DOUT // NCOL
-    for j in range(NCOL // 2):
-        at = slice(j * cols, (j + 1) * cols)
-        part = jnp.dot(merged_ref[...], w_ref[:, at], preferred_element_type=jnp.float32)
-        part = part.astype(jnp.bfloat16)
-        rows = part.shape[0] // 2
+def project(quarter, merged_ref, w_ref, keep_ref, send_ref):
+    rows = keep_ref.shape[0]
+    for j in range(QCOLS // TILE):
+        at = slice(j * TILE, (j + 1) * TILE)
+        start = quarter % 2 * QCOLS + j * TILE
+        part = jnp.dot(
+            merged_ref[...], w_ref[:, start:start + TILE], preferred_element_type=jnp.float32
+        ).astype(jnp.bfloat16)
         keep_ref[:, at] = part[:rows]
         send_ref[:, at] = part[rows:]
 
 
-def last_kernel(chunk, index_ref, tile_ref, own_ref, f1, f2, f3, f4, f5, f6, m_in, acc_in, w_ref,
-                *refs):
-    if chunk == 0:
-        w_hbm, w_next, sems = refs[0], refs[4], refs[-1]
-        refs = refs[1:4] + refs[5:-1]
-        fetch_w = fetch_half(1, w_hbm, w_next, sems)
-    (keep_ref, send_ref, merged_ref, acc_ref, kv_ref, m_ref, peak_ref, even_ref, odd_ref,
-     list0, list1) = refs
-    rest_of_attention(chunk, tile_ref, own_ref, (f1, f2, f3, f4, f5, f6), m_in, acc_in,
-                      kv_ref, m_ref, peak_ref, acc_ref, even_ref, odd_ref, (list0, list1))
-    finish(acc_ref, len(CHUNKS[chunk]), index_ref, merged_ref)
-    project(merged_ref, w_ref, keep_ref, send_ref)
-    if chunk == 0:
-        for copy in fetch_w:
-            copy.wait()
-
-
-def pair_kernel(half, keep_ref, got_ref, stay_ref, send_ref):
-    stay, send = ((0, 1), (2, 3)) if half == 0 else ((0, 2), (1, 3))
+def last_kernel(index_ref, tile_ref, own_ref, f1, f2, f3, f4, f5, f6, m_in, acc_in, w_ref, w_hbm,
+                keep_ref, send_ref, merged_ref, w_next, acc_ref, kv_ref, m_ref, peak_ref, even_ref,
+                odd_ref, list0, list1, sems):
+    fetch_w = fetch_half(1, w_hbm, w_next, sems)
+    rest_of_attention(tile_ref, own_ref, (f1, f2, f3, f4, f5, f6), m_in, acc_in, kv_ref, m_ref,
+                      peak_ref, acc_ref, even_ref, odd_ref, (list0, list1))
+    finish(acc_ref, index_ref, merged_ref)
+    project(0, merged_ref, w_ref, keep_ref, send_ref)
+    for copy in fetch_w:
+        copy.wait()
+
+
+def pair_kernel(pairing, keep_ref, got_ref, stay_ref, send_ref):
+    stay, send = ((0, 1), (2, 3)) if pairing == 0 else ((0, 2), (1, 3))
     size = keep_ref.shape[0] // NZ
     for out_ref, slots in ((stay_ref, stay), (send_ref, send)):
         for i, slot in enumerate(slots):
@@ -326,12 +320,9 @@
 
 def final_kernel(*refs):
     out_ref = refs[-1]
-    for i in range(4):
-        chunk, half = i // 2, i % 2
-        total = refs[2 * i][...].astype(jnp.float32) + refs[2 * i + 1][...]
-        columns = slice(half * DOUT // 2, (half + 1) * DOUT // 2)
-        rows = slice(CHUNKS[chunk][0] * SLICE, (CHUNKS[chunk][-1] + 1) * SLICE)
-        out_ref[rows, columns] = total.astype(jnp.bfloat16)
+    for q in range(QUARTERS):
+        total = refs[2 * q][...].astype(jnp.float32) + refs[2 * q + 1][...]
+        out_ref[:, q * QCOLS:(q + 1) * QCOLS] = total.astype(jnp.bfloat16)
 
 
 def in_hbm(array):
@@ -423,29 +414,22 @@
         in_hbm(queries), in_hbm(out_weight), own, *xs, *ys
     )
 
-    def halves(chunk):
-        return [struct((NZ * SLICE * len(CHUNKS[chunk]), DOUT // 2), bf16)] * 2
-
-    def last(chunk, acc, *w_hbm):
-        width = len(CHUNKS[chunk])
-        rows = 2 * NZ * SLICE * width
-        outs = halves(chunk) + [struct((rows, 1024), bf16)]
-        scratch = [pltpu.VMEM((2 * width, 144, 256), f32)] + walk_scratch(18, 2 * width, width)
-        if w_hbm:
-            outs = outs + [struct((1024, DOUT // 2), bf16)]
-            scratch = scratch + [pltpu.SemaphoreType.DMA((NW,))]
+    rows = NZ * WIDTH * SLICE
+    piece = [struct((rows, QCOLS), bf16)] * 2
+    scratch = walk_scratch(18, 2 * WIDTH, WIDTH)
+    last = pl.pallas_call(
+        last_kernel, in_specs=[SMEM] + [VMEM] * 11 + [HBM], out_specs=[VMEM] * 4,
+        out_shape=piece + [struct((2 * rows, 1024), bf16), struct((1024, DOUT // 2), bf16)],
+        scratch_shapes=[pltpu.VMEM((2 * WIDTH, 144, 256), f32)] + scratch
+        + [pltpu.SemaphoreType.DMA((NW,))],
+        compiler_params=params(16), name="last", cost_estimate=estimate(5 * 10 ** 9, 1 << 20),
+    )
+
+    def rest(quarter, merged, weight):
         return pl.pallas_call(
-            functools.partial(last_kernel, chunk),
-            in_specs=[SMEM] + [VMEM] * 11 + [HBM] * len(w_hbm),
-            out_specs=[VMEM] * len(outs), out_shape=outs, scratch_shapes=scratch,
-            compiler_params=params(14),
-            cost_estimate=estimate(5 * 10 ** 9, 1 << 20),
-        )(index, tiles, own, *fa, *fb, maxima, acc, weight_a, *w_hbm)
-
-    def rest(chunk, merged, weight):
-        return pl.pallas_call(
-            project, in_specs=[VMEM] * 2, out_specs=[VMEM] * 2, out_shape=halves(chunk),
-            compiler_params=params(8), cost_estimate=estimate(10 ** 9, 1 << 20),
+            functools.partial(project, quarter), in_specs=[VMEM] * 2, out_specs=[VMEM] * 2,
+            out_shape=piece, compiler_params=params(8),
+            cost_estimate=estimate(10 ** 9, 1 << 20),
         )(merged, weight)
 
     def call(kernel, rows, columns, *blocks):
@@ -455,43 +439,24 @@
             compiler_params=params(6), cost_estimate=estimate(10 ** 6, 1 << 20),
         )(*blocks)
 
-    def swap(block):
-        return lax.ppermute(block, "tp", swap_route())
-
-    def step(pairing, block):
-        return lax.ppermute(block, "tp", step_route(pairing))
-
-    def pair(half, keep, got):
-        kernel = functools.partial(pair_kernel, half)
-        rows = keep.shape[0] // 2
-        return call(kernel, (rows, rows), DOUT // 2, keep, got)
-
-    def chunk_parts(chunk, acc, *w_hbm):
-        keep_a, send_a, merged, *w_next = last(chunk, acc, *w_hbm)
-        got_a = swap(send_a)
-        w_half = w_next[0] if w_next else weight_b
-        keep_b, send_b = rest(chunk, merged, w_half)
-        got_b = swap(send_b)
-        stay_a, out_a = pair(0, keep_a, got_a)
-        in_a = step(0, out_a)
-        stay_b, out_b = pair(1, keep_b, got_b)
-        in_b = step(1, out_b)
-        return stay_a, in_a, stay_b, in_b, out_b, w_half
-
-    def second_step(half, stay, got):
-        rows = stay.shape[0] // 2
-        mine, out = call(fold_kernel, (rows, rows), DOUT // 2, stay, got)
-        return mine, step(1 - half, out)
-
-    *early, out_b0, weight_b = chunk_parts(0, acc, in_hbm(out_weight))
-    out_b0, acc = lax.optimization_barrier((out_b0, acc))
-    *late, out_b1, _ = chunk_parts(1, acc)
-    *early, out_b1 = lax.optimization_barrier((*early, out_b1))
-    blocks = []
-    for stay_a, in_a, stay_b, in_b in (early, late):
-        blocks += second_step(0, stay_a, in_a)
-        blocks += second_step(1, stay_b, in_b)
-    return call(final_kernel, (32,), DOUT, *blocks)[0]
+    def move(block, route):
+        return lax.ppermute(block, "tp", route)
+
+    keep, send, merged, weight_b = last(
+        index, tiles, own, *fa, *fb, maxima, acc, weight_a, in_hbm(out_weight)
+    )
+    stays, blocks = [], []
+    for q in range(QUARTERS):
+        if q > 0:
+            keep, send = rest(q, merged, weight_a if q < 2 else weight_b)
+        got = move(send, swap_route())
+        kernel = functools.partial(pair_kernel, q % 2)
+        stay, out = call(kernel, (rows // 2,) * 2, QCOLS, keep, got)
+        stays.append((stay, move(out, step_route(q % 2))))
+    for q, (stay, got) in enumerate(stays):
+        mine, out = call(fold_kernel, (rows // 4,) * 2, QCOLS, stay, got)
+        blocks += [mine, move(out, step_route(1 - q % 2))]
+    return call(final_kernel, (rows // 4,), DOUT, *blocks)[0]
 
 
 def solution(mesh):

time: 92.3 us -> 91.9 us (level)
  Pallas kernels: 40.1 us -> 36.2 us
  starting transfers between devices: 30 us -> 32.2 us
  waiting for transfers between devices: 21.9 us -> 23.2 us
    pallas_call x4, Pallas kernels: 15.1 us -> 11.2 us  [the longest x1 7.42 us: on_device(): last(index, tiles, own, *fa, *fb, maxima, acc, weight_a, in_hbm(out_weight))]
    ppermute x12, starting transfers between devices: 12.1 us -> 14.3 us  [move(): return lax.ppermute(block, 'tp', route)]
    ppermute x12, waiting for transfers between devices: 9.91 us -> 11.2 us  [move(): return lax.ppermute(block, 'tp', route)]
  transfers between devices with their start and end apart: 24 -> 24, of which waited for: 11 -> 9; matrix products, arithmetic and copies ran while one was open for 0% -> 0% of each run, Pallas kernels for 32% -> 28%
where the time goes in v6:
time: 91.9 us; the launch traced here: 91.8 us
  Pallas kernels  36.2 us (39%)
  starting transfers between devices  32.2 us (35%)
  waiting for transfers between devices  23.2 us (25%)
    pallas_call x1, Pallas kernels, on_device(): first(in_hbm(queries), in_hbm(out_weight), own, *xs, *ys)  22.3 us
    ppermute x12, starting transfers between devices, shifts(): moved.append(lax.ppermute(block, 'ctx', ctx_route(dx * d, dy * d)))  17.9 us
    ppermute x12, starting transfers between devices, move(): return lax.ppermute(block, 'tp', route)  14.3 us
    ppermute x12, waiting for transfers between devices, shifts(): moved.append(lax.ppermute(block, 'ctx', ctx_route(dx * d, dy * d)))  12 us
    ppermute x12, waiting for transfers between devices, move(): return lax.ppermute(block, 'tp', route)  11.2 us
    pallas_call x1, Pallas kernels, on_device(): last(index, tiles, own, *fa, *fb, maxima, acc, weight_a, in_hbm(out_weight))  7.42 us
    pallas_call x3, Pallas kernels, rest(): pl.pallas_call(functools.partial(project, quarter), in_specs=[VMEM] * 2,...  3.8 us
  transfers between devices with their start and end apart: 24, of which 9 were waited for; matrix products, arithmetic and copies ran while one was open for 0% of the time, Pallas kernels for 28%

profile of v6, /device:TPU:6, one launch (start us, length us, event | category | flops | bytes accessed | tf_op | source)
XLA Modules:
  0.0 91.8 jit_solution(9846956662242519337)
XLA Ops:
  0.0 1.0 %pack.1.own_ref = bf16[544,128]{1,0:T(8,128)(2,1)S(1)} custom-call(s32[256]{0:T(256)} %pos_hbm.1, bf16[256,128]{1,0:T(8,128)(2,1)} %k_hbm.1, bf16[256,128]{1,0:T(8,128)(2,1)} %v_hbm.1), custom_call_target="tpu_custom_call" | custom-call | tf_op jit(solution)/shard_map/pack/pallas_call | solution.py:362
  1.0 3.3 %collective-permute-start.5 = (bf16[544,128]{1,0:T(8,128)(2,1)S(1)}, bf16[544,128]{1,0:T(8,128)(2,1)S(1)}, u32[]{:S(2)}, u32[]{:S(2)}) collective-permute-start(bf16[544,128]{1,0:T(8,128)(2,1)S(1)} %pack.1.own_ref), channel_id=1, source_target_pairs={{0,16},{8,24},{16,0},{24,8},{32,48},{40,56},{48,32},{56,40},{64,80... | collective-permute-start | bytes 417800 | tf_op jit(solution)/shard_map/ppermute | solution.py:374
  4.3 1.1 %collective-permute-start.4 = (bf16[544,128]{1,0:T(8,128)(2,1)S(1)}, bf16[544,128]{1,0:T(8,128)(2,1)S(1)}, u32[]{:S(2)}, u32[]{:S(2)}) collective-permute-start(bf16[544,128]{1,0:T(8,128)(2,1)S(1)} %pack.1.own_ref), channel_id=1, source_target_pairs={{0,24},{8,0},{16,8},{24,16},{32,56},{40,32},{48,40},{56,48},{64,88... | collective-permute-start | bytes 417800 | tf_op jit(solution)/shard_map/ppermute | solution.py:374
  6.3 2.5 %collective-permute-done.5.y3.refs_2_ = bf16[544,128]{1,0:T(8,128)(2,1)S(1)} collective-permute-done((bf16[544,128]{1,0:T(8,128)(2,1)S(1)}, bf16[544,128]{1,0:T(8,128)(2,1)S(1)}, u32[]{:S(2)}, u32[]{:S(2)}) %collective-permute-start.5) | collective-permute-done | bytes 139296 | tf_op jit(solution)/shard_map/ppermute | solution.py:374
  8.8 2.5 %collective-permute-done.4.y2.refs_1_ = bf16[544,128]{1,0:T(8,128)(2,1)S(1)} collective-permute-done((bf16[544,128]{1,0:T(8,128)(2,1)S(1)}, bf16[544,128]{1,0:T(8,128)(2,1)S(1)}, u32[]{:S(2)}, u32[]{:S(2)}) %collective-permute-start.4) | collective-permute-done | bytes 139296 | tf_op jit(solution)/shard_map/ppermute | solution.py:374
  11.6 1.5 %collective-permute-start.11 = (bf16[816,128]{1,0:T(8,128)(2,1)S(1)}, bf16[816,128]{1,0:T(8,128)(2,1)S(1)}, u32[]{:S(2)}, u32[]{:S(2)}) collective-permute-start(bf16[816,128]{1,0:T(8,128)(2,1)S(1)} %join.3), channel_id=1, source_target_pairs={{0,64},{8,72},{16,80},{24,88},{32,96},{40,104},{48,112},{56,120},{... | collective-permute-start | bytes 626696 | tf_op jit(solution)/shard_map/ppermute | solution.py:374
  13.1 2.1 %collective-permute-start.2 = (bf16[544,128]{1,0:T(8,128)(2,1)S(1)}, bf16[544,128]{1,0:T(8,128)(2,1)S(1)}, u32[]{:S(2)}, u32[]{:S(2)}) collective-permute-start(bf16[544,128]{1,0:T(8,128)(2,1)S(1)} %pack.1.own_ref), channel_id=1, source_target_pairs={{0,64},{8,72},{16,80},{24,88},{32,96},{40,104},{48,112},{56,120},{... | collective-permute-start | bytes 417800 | tf_op jit(solution)/shard_map/ppermute | solution.py:374
  16.1 2.4 %collective-permute-start = (bf16[544,128]{1,0:T(8,128)(2,1)S(1)}, bf16[544,128]{1,0:T(8,128)(2,1)S(1)}, u32[]{:S(2)}, u32[]{:S(2)}) collective-permute-start(bf16[544,128]{1,0:T(8,128)(2,1)S(1)} %pack.1.own_ref), channel_id=1, source_target_pairs={{0,32},{8,40},{16,48},{24,56},{32,64},{40,72},{48,80},{56,88},{64,... | collective-permute-start | bytes 417800 | tf_op jit(solution)/shard_map/ppermute | solution.py:374
  18.5 5.8 %collective-permute-done.2.x3.refs_2_ = bf16[544,128]{1,0:T(8,128)(2,1)S(1)} collective-permute-done((bf16[544,128]{1,0:T(8,128)(2,1)S(1)}, bf16[544,128]{1,0:T(8,128)(2,1)S(1)}, u32[]{:S(2)}, u32[]{:S(2)}) %collective-permute-start.2) | collective-permute-done | bytes 139296 | tf_op jit(solution)/shard_map/ppermute | solution.py:374
  25.1 3.7 %collective-permute-start.8 = (bf16[816,128]{1,0:T(8,128)(2,1)S(1)}, bf16[816,128]{1,0:T(8,128)(2,1)S(1)}, u32[]{:S(2)}, u32[]{:S(2)}) collective-permute-start(bf16[816,128]{1,0:T(8,128)(2,1)S(1)} %join.2), channel_id=1, source_target_pairs={{0,16},{8,24},{16,0},{24,8},{32,48},{40,56},{48,32},{56,40},{64,80... | collective-permute-start | bytes 626696 | tf_op jit(solution)/shard_map/ppermute | solution.py:374
  28.8 1.2 %collective-permute-start.7 = (bf16[816,128]{1,0:T(8,128)(2,1)S(1)}, bf16[816,128]{1,0:T(8,128)(2,1)S(1)}, u32[]{:S(2)}, u32[]{:S(2)}) collective-permute-start(bf16[816,128]{1,0:T(8,128)(2,1)S(1)} %join.2), channel_id=1, source_target_pairs={{0,24},{8,0},{16,8},{24,16},{32,56},{40,32},{48,40},{56,48},{64,88... | collective-permute-start | bytes 626696 | tf_op jit(solution)/shard_map/ppermute | solution.py:374
  30.9 22.3 %first.1 = (f32[8,8,256]{2,1,0:T(8,128)S(1)}, f32[8,144,256]{2,1,0:T(8,128)S(1)}, bf16[8,256,128]{2,1,0:T(8,128)(2,1)S(1)}, bf16[1024,4096]{1,0:T(8,128)(2,1)S(1)}) custom-call(bf16[256,1024]{1,0:T(8,128)(2,1)} %q_hbm.1, bf16[1024,8192]{1,0:T(8,128)(2,1)} %w_hbm.3, bf16[544,128]{1,0:T(8,128)(2,1)S(1)} %pack.1.own_ref, ...), custom_call_target="tpu_custom_call" | custom-call | flops 4000000000 | bytes 1048576 | tf_op jit(solution)/shard_map/first/pallas_call | solution.py:413
  53.2 7.4 %last.1 = (bf16[128,2048]{1,0:T(8,128)(2,1)S(1)}, bf16[128,2048]{1,0:T(8,128)(2,1)S(1)}, bf16[256,1024]{1,0:T(8,128)(2,1)S(1)}, bf16[1024,4096]{1,0:T(8,128)(2,1)S(1)}) custom-call(s32[1]{0:T(128)} %bitcast.index_ref, bf16[8,256,128]{2,1,0:T(8,128)(2,1)S(1)} %get-tuple-element.35.tile_ref, bf16[544,128]{1,0:T(8,128)(2,1)S(1)} %pack.1.own_ref, ...), custom_call_target="tpu_custom_call" | custom-call | flops 5000000000 | bytes 1048576 | tf_op jit(solution)/shard_map/last/pallas_call | solution.py:445
  60.7 1.3 %shard_map.57 = (bf16[128,2048]{1,0:T(8,128)(2,1)S(1)}, bf16[128,2048]{1,0:T(8,128)(2,1)S(1)}) custom-call(bf16[256,1024]{1,0:T(8,128)(2,1)S(1)} %get-tuple-element.45.merged_ref, bf16[1024,4096]{1,0:T(8,128)(2,1)S(1)} %get-tuple-element.38.w_ref), custom_call_target="tpu_custom_call" | custom-call | flops 1000000000 | bytes 1048576 | tf_op jit(solution)/shard_map/pallas_call | solution.py:429
  62.5 1.3 %shard_map.63 = (bf16[128,2048]{1,0:T(8,128)(2,1)S(1)}, bf16[128,2048]{1,0:T(8,128)(2,1)S(1)}) custom-call(bf16[256,1024]{1,0:T(8,128)(2,1)S(1)} %get-tuple-element.45.merged_ref, bf16[1024,4096]{1,0:T(8,128)(2,1)S(1)} %get-tuple-element.52.w_ref), custom_call_target="tpu_custom_call" | custom-call | flops 1000000000 | bytes 1048576 | tf_op jit(solution)/shard_map/pallas_call | solution.py:429
  64.0 1.3 %shard_map.60 = (bf16[128,2048]{1,0:T(8,128)(2,1)S(1)}, bf16[128,2048]{1,0:T(8,128)(2,1)S(1)}) custom-call(bf16[256,1024]{1,0:T(8,128)(2,1)S(1)} %get-tuple-element.45.merged_ref, bf16[1024,4096]{1,0:T(8,128)(2,1)S(1)} %get-tuple-element.52.w_ref), custom_call_target="tpu_custom_call" | custom-call | flops 1000000000 | bytes 1048576 | tf_op jit(solution)/shard_map/pallas_call | solution.py:429
  65.9 2.0 %collective-permute-start.13 = (bf16[64,2048]{1,0:T(8,128)(2,1)S(1)}, bf16[64,2048]{1,0:T(8,128)(2,1)S(1)}, u32[]{:S(2)}, u32[]{:S(2)}) collective-permute-start(bf16[64,2048]{1,0:T(8,128)(2,1)S(1)} %get-tuple-element.42), channel_id=1, source_target_pairs={{0,2},{1,3},{2,0},{3,1},{4,6},{5,7},{6,4},{7,5},{8,10},{9,11},{10,... | collective-permute-start | bytes 786440 | tf_op jit(solution)/shard_map/ppermute | solution.py:443
  68.0 2.6 %collective-permute-start.16 = (bf16[64,2048]{1,0:T(8,128)(2,1)S(1)}, bf16[64,2048]{1,0:T(8,128)(2,1)S(1)}, u32[]{:S(2)}, u32[]{:S(2)}) collective-permute-start(bf16[64,2048]{1,0:T(8,128)(2,1)S(1)} %get-tuple-element.49), channel_id=1, source_target_pairs={{0,6},{1,7},{2,4},{3,5},{4,2},{5,3},{6,0},{7,1},{8,14},{9,15},{10,... | collective-permute-start | bytes 786440 | tf_op jit(solution)/shard_map/ppermute | solution.py:443
  72.1 3.1 %collective-permute-done.13.got_ref = bf16[64,2048]{1,0:T(8,128)(2,1)S(1)} collective-permute-done((bf16[64,2048]{1,0:T(8,128)(2,1)S(1)}, bf16[64,2048]{1,0:T(8,128)(2,1)S(1)}, u32[]{:S(2)}, u32[]{:S(2)}) %collective-permute-start.13) | collective-permute-done | bytes 262176 | tf_op jit(solution)/shard_map/ppermute | solution.py:443
  75.2 4.1 %collective-permute-start.14 = (bf16[32,2048]{1,0:T(8,128)(2,1)S(1)}, bf16[32,2048]{1,0:T(8,128)(2,1)S(1)}, u32[]{:S(2)}, u32[]{:S(2)}) collective-permute-start(bf16[32,2048]{1,0:T(8,128)(2,1)S(1)} %get-tuple-element.44), channel_id=1, source_target_pairs={{0,6},{1,7},{2,4},{3,5},{4,2},{5,3},{6,0},{7,1},{8,14},{9,15},{10,... | collective-permute-start | bytes 393224 | tf_op jit(solution)/shard_map/ppermute | solution.py:443
  79.5 4.6 %collective-permute-done.22.got_ref = bf16[64,2048]{1,0:T(8,128)(2,1)S(1)} collective-permute-done((bf16[64,2048]{1,0:T(8,128)(2,1)S(1)}, bf16[64,2048]{1,0:T(8,128)(2,1)S(1)}, u32[]{:S(2)}, u32[]{:S(2)}) %collective-permute-start.22) | collective-permute-done | bytes 262176 | tf_op jit(solution)/shard_map/ppermute | solution.py:443
  84.6 2.7 %collective-permute-start.20 = (bf16[32,2048]{1,0:T(8,128)(2,1)S(1)}, bf16[32,2048]{1,0:T(8,128)(2,1)S(1)}, u32[]{:S(2)}, u32[]{:S(2)}) collective-permute-start(bf16[32,2048]{1,0:T(8,128)(2,1)S(1)} %get-tuple-element.58), channel_id=1, source_target_pairs={{0,6},{1,7},{2,4},{3,5},{4,2},{5,3},{6,0},{7,1},{8,14},{9,15},{10,... | collective-permute-start | bytes 393224 | tf_op jit(solution)/shard_map/ppermute | solution.py:443
  87.3 1.9 %collective-permute-done.23.refs_7_ = bf16[32,2048]{1,0:T(8,128)(2,1)S(1)} collective-permute-done((bf16[32,2048]{1,0:T(8,128)(2,1)S(1)}, bf16[32,2048]{1,0:T(8,128)(2,1)S(1)}, u32[]{:S(2)}, u32[]{:S(2)}) %collective-permute-start.23) | collective-permute-done | bytes 131104 | tf_op jit(solution)/shard_map/ppermute | solution.py:443
  89.2 1.7 %collective-permute-done.20.refs_5_ = bf16[32,2048]{1,0:T(8,128)(2,1)S(1)} collective-permute-done((bf16[32,2048]{1,0:T(8,128)(2,1)S(1)}, bf16[32,2048]{1,0:T(8,128)(2,1)S(1)}, u32[]{:S(2)}, u32[]{:S(2)}) %collective-permute-start.20) | collective-permute-done | bytes 131104 | tf_op jit(solution)/shard_map/ppermute | solution.py:443
  (41 shorter events, 8.4 us)
Async XLA Ops:
  1.0 7.8 %collective-permute-start.5 = (bf16[544,128]{1,0:T(8,128)(2,1)S(1)}, bf16[544,128]{1,0:T(8,128)(2,1)S(1)}, u32[]{:S(2)}, u32[]{:S(2)}) collective-permute-start(bf16[544,128]{1,0:T(8,128)(2,1)S(1)} %pack.1.own_ref), channel_id=1, source_target_pairs={{0,16},{8,24},{16,0},{24,8},{32,48},{40,56},{48,32},{56,40},{64,80... | collective-permute-start | bytes 417800 | tf_op jit(solution)/shard_map/ppermute | solution.py:374
  4.3 7.0 %collective-permute-start.4 = (bf16[544,128]{1,0:T(8,128)(2,1)S(1)}, bf16[544,128]{1,0:T(8,128)(2,1)S(1)}, u32[]{:S(2)}, u32[]{:S(2)}) collective-permute-start(bf16[544,128]{1,0:T(8,128)(2,1)S(1)} %pack.1.own_ref), channel_id=1, source_target_pairs={{0,24},{8,0},{16,8},{24,16},{32,56},{40,32},{48,40},{56,48},{64,88... | collective-permute-start | bytes 417800 | tf_op jit(solution)/shard_map/ppermute | solution.py:374
  5.3 6.3 %collective-permute-start.3 = (bf16[544,128]{1,0:T(8,128)(2,1)S(1)}, bf16[544,128]{1,0:T(8,128)(2,1)S(1)}, u32[]{:S(2)}, u32[]{:S(2)}) collective-permute-start(bf16[544,128]{1,0:T(8,128)(2,1)S(1)} %pack.1.own_ref), channel_id=1, source_target_pairs={{0,8},{8,16},{16,24},{24,0},{32,40},{40,48},{48,56},{56,32},{64,72... | collective-permute-start | bytes 417800 | tf_op jit(solution)/shard_map/ppermute | solution.py:374
  11.6 18.5 %collective-permute-start.11 = (bf16[816,128]{1,0:T(8,128)(2,1)S(1)}, bf16[816,128]{1,0:T(8,128)(2,1)S(1)}, u32[]{:S(2)}, u32[]{:S(2)}) collective-permute-start(bf16[816,128]{1,0:T(8,128)(2,1)S(1)} %join.3), channel_id=1, source_target_pairs={{0,64},{8,72},{16,80},{24,88},{32,96},{40,104},{48,112},{56,120},{... | collective-permute-start | bytes 626696 | tf_op jit(solution)/shard_map/ppermute | solution.py:374
  13.1 11.2 %collective-permute-start.2 = (bf16[544,128]{1,0:T(8,128)(2,1)S(1)}, bf16[544,128]{1,0:T(8,128)(2,1)S(1)}, u32[]{:S(2)}, u32[]{:S(2)}) collective-permute-start(bf16[544,128]{1,0:T(8,128)(2,1)S(1)} %pack.1.own_ref), channel_id=1, source_target_pairs={{0,64},{8,72},{16,80},{24,88},{32,96},{40,104},{48,112},{56,120},{... | collective-permute-start | bytes 417800 | tf_op jit(solution)/shard_map/ppermute | solution.py:374
  15.2 9.9 %collective-permute-start.1 = (bf16[544,128]{1,0:T(8,128)(2,1)S(1)}, bf16[544,128]{1,0:T(8,128)(2,1)S(1)}, u32[]{:S(2)}, u32[]{:S(2)}) collective-permute-start(bf16[544,128]{1,0:T(8,128)(2,1)S(1)} %pack.1.own_ref), channel_id=1, source_target_pairs={{0,96},{8,104},{16,112},{24,120},{32,0},{40,8},{48,16},{56,24},{64... | collective-permute-start | bytes 417800 | tf_op jit(solution)/shard_map/ppermute | solution.py:374
  16.1 9.1 %collective-permute-start = (bf16[544,128]{1,0:T(8,128)(2,1)S(1)}, bf16[544,128]{1,0:T(8,128)(2,1)S(1)}, u32[]{:S(2)}, u32[]{:S(2)}) collective-permute-start(bf16[544,128]{1,0:T(8,128)(2,1)S(1)} %pack.1.own_ref), channel_id=1, source_target_pairs={{0,32},{8,40},{16,48},{24,56},{32,64},{40,72},{48,80},{56,88},{64,... | collective-permute-start | bytes 417800 | tf_op jit(solution)/shard_map/ppermute | solution.py:374
  18.5 34.7 %collective-permute-start.10 = (bf16[816,128]{1,0:T(8,128)(2,1)S(1)}, bf16[816,128]{1,0:T(8,128)(2,1)S(1)}, u32[]{:S(2)}, u32[]{:S(2)}) collective-permute-start(bf16[816,128]{1,0:T(8,128)(2,1)S(1)} %join.3), channel_id=1, source_target_pairs={{0,96},{8,104},{16,112},{24,120},{32,0},{40,8},{48,16},{56,24},{64... | collective-permute-start | bytes 626696 | tf_op jit(solution)/shard_map/ppermute | solution.py:374
  24.3 28.9 %collective-permute-start.9 = (bf16[816,128]{1,0:T(8,128)(2,1)S(1)}, bf16[816,128]{1,0:T(8,128)(2,1)S(1)}, u32[]{:S(2)}, u32[]{:S(2)}) collective-permute-start(bf16[816,128]{1,0:T(8,128)(2,1)S(1)} %join.3), channel_id=1, source_target_pairs={{0,32},{8,40},{16,48},{24,56},{32,64},{40,72},{48,80},{56,88},{64,... | collective-permute-start | bytes 626696 | tf_op jit(solution)/shard_map/ppermute | solution.py:374
  25.1 28.1 %collective-permute-start.8 = (bf16[816,128]{1,0:T(8,128)(2,1)S(1)}, bf16[816,128]{1,0:T(8,128)(2,1)S(1)}, u32[]{:S(2)}, u32[]{:S(2)}) collective-permute-start(bf16[816,128]{1,0:T(8,128)(2,1)S(1)} %join.2), channel_id=1, source_target_pairs={{0,16},{8,24},{16,0},{24,8},{32,48},{40,56},{48,32},{56,40},{64,80... | collective-permute-start | bytes 626696 | tf_op jit(solution)/shard_map/ppermute | solution.py:374
  28.8 24.4 %collective-permute-start.7 = (bf16[816,128]{1,0:T(8,128)(2,1)S(1)}, bf16[816,128]{1,0:T(8,128)(2,1)S(1)}, u32[]{:S(2)}, u32[]{:S(2)}) collective-permute-start(bf16[816,128]{1,0:T(8,128)(2,1)S(1)} %join.2), channel_id=1, source_target_pairs={{0,24},{8,0},{16,8},{24,16},{32,56},{40,32},{48,40},{56,48},{64,88... | collective-permute-start | bytes 626696 | tf_op jit(solution)/shard_map/ppermute | solution.py:374
  30.1 23.1 %collective-permute-start.6 = (bf16[816,128]{1,0:T(8,128)(2,1)S(1)}, bf16[816,128]{1,0:T(8,128)(2,1)S(1)}, u32[]{:S(2)}, u32[]{:S(2)}) collective-permute-start(bf16[816,128]{1,0:T(8,128)(2,1)S(1)} %join.2), channel_id=1, source_target_pairs={{0,8},{8,16},{16,24},{24,0},{32,40},{40,48},{48,56},{56,32},{64,72... | collective-permute-start | bytes 626696 | tf_op jit(solution)/shard_map/ppermute | solution.py:374
  62.0 3.8 %collective-permute-start.12 = (bf16[128,2048]{1,0:T(8,128)(2,1)S(1)}, bf16[128,2048]{1,0:T(8,128)(2,1)S(1)}, u32[]{:S(2)}, u32[]{:S(2)}) collective-permute-start(bf16[128,2048]{1,0:T(8,128)(2,1)S(1)} %get-tuple-element.40), channel_id=1, source_target_pairs={{0,1},{1,0},{2,3},{3,2},{4,5},{5,4},{6,7},{7,6},{8,9},{9,8},{10,11... | collective-permute-start | bytes 1572872 | tf_op jit(solution)/shard_map/ppermute | solution.py:443
  62.1 5.8 %collective-permute-start.15 = (bf16[128,2048]{1,0:T(8,128)(2,1)S(1)}, bf16[128,2048]{1,0:T(8,128)(2,1)S(1)}, u32[]{:S(2)}, u32[]{:S(2)}) collective-permute-start(bf16[128,2048]{1,0:T(8,128)(2,1)S(1)} %get-tuple-element.47), channel_id=1, source_target_pairs={{0,1},{1,0},{2,3},{3,2},{4,5},{5,4},{6,7},{7,6},{8,9},{9,8},{10,11... | collective-permute-start | bytes 1572872 | tf_op jit(solution)/shard_map/ppermute | solution.py:443
  63.8 6.8 %collective-permute-start.21 = (bf16[128,2048]{1,0:T(8,128)(2,1)S(1)}, bf16[128,2048]{1,0:T(8,128)(2,1)S(1)}, u32[]{:S(2)}, u32[]{:S(2)}) collective-permute-start(bf16[128,2048]{1,0:T(8,128)(2,1)S(1)} %get-tuple-element.60), channel_id=1, source_target_pairs={{0,1},{1,0},{2,3},{3,2},{4,5},{5,4},{6,7},{7,6},{8,9},{9,8},{10,11... | collective-permute-start | bytes 1572872 | tf_op jit(solution)/shard_map/ppermute | solution.py:443
  65.2 6.3 %collective-permute-start.18 = (bf16[128,2048]{1,0:T(8,128)(2,1)S(1)}, bf16[128,2048]{1,0:T(8,128)(2,1)S(1)}, u32[]{:S(2)}, u32[]{:S(2)}) collective-permute-start(bf16[128,2048]{1,0:T(8,128)(2,1)S(1)} %get-tuple-element.54), channel_id=1, source_target_pairs={{0,1},{1,0},{2,3},{3,2},{4,5},{5,4},{6,7},{7,6},{8,9},{9,8},{10,11... | collective-permute-start | bytes 1572872 | tf_op jit(solution)/shard_map/ppermute | solution.py:443
  65.9 9.3 %collective-permute-start.13 = (bf16[64,2048]{1,0:T(8,128)(2,1)S(1)}, bf16[64,2048]{1,0:T(8,128)(2,1)S(1)}, u32[]{:S(2)}, u32[]{:S(2)}) collective-permute-start(bf16[64,2048]{1,0:T(8,128)(2,1)S(1)} %get-tuple-element.42), channel_id=1, source_target_pairs={{0,2},{1,3},{2,0},{3,1},{4,6},{5,7},{6,4},{7,5},{8,10},{9,11},{10,... | collective-permute-start | bytes 786440 | tf_op jit(solution)/shard_map/ppermute | solution.py:443
  68.0 11.3 %collective-permute-start.16 = (bf16[64,2048]{1,0:T(8,128)(2,1)S(1)}, bf16[64,2048]{1,0:T(8,128)(2,1)S(1)}, u32[]{:S(2)}, u32[]{:S(2)}) collective-permute-start(bf16[64,2048]{1,0:T(8,128)(2,1)S(1)} %get-tuple-element.49), channel_id=1, source_target_pairs={{0,6},{1,7},{2,4},{3,5},{4,2},{5,3},{6,0},{7,1},{8,14},{9,15},{10,... | collective-permute-start | bytes 786440 | tf_op jit(solution)/shard_map/ppermute | solution.py:443
  70.7 13.3 %collective-permute-start.22 = (bf16[64,2048]{1,0:T(8,128)(2,1)S(1)}, bf16[64,2048]{1,0:T(8,128)(2,1)S(1)}, u32[]{:S(2)}, u32[]{:S(2)}) collective-permute-start(bf16[64,2048]{1,0:T(8,128)(2,1)S(1)} %get-tuple-element.62), channel_id=1, source_target_pairs={{0,6},{1,7},{2,4},{3,5},{4,2},{5,3},{6,0},{7,1},{8,14},{9,15},{10,... | collective-permute-start | bytes 786440 | tf_op jit(solution)/shard_map/ppermute | solution.py:443
  71.6 12.9 %collective-permute-start.19 = (bf16[64,2048]{1,0:T(8,128)(2,1)S(1)}, bf16[64,2048]{1,0:T(8,128)(2,1)S(1)}, u32[]{:S(2)}, u32[]{:S(2)}) collective-permute-start(bf16[64,2048]{1,0:T(8,128)(2,1)S(1)} %get-tuple-element.56), channel_id=1, source_target_pairs={{0,2},{1,3},{2,0},{3,1},{4,6},{5,7},{6,4},{7,5},{8,10},{9,11},{10,... | collective-permute-start | bytes 786440 | tf_op jit(solution)/shard_map/ppermute | solution.py:443
  75.2 12.1 %collective-permute-start.14 = (bf16[32,2048]{1,0:T(8,128)(2,1)S(1)}, bf16[32,2048]{1,0:T(8,128)(2,1)S(1)}, u32[]{:S(2)}, u32[]{:S(2)}) collective-permute-start(bf16[32,2048]{1,0:T(8,128)(2,1)S(1)} %get-tuple-element.44), channel_id=1, source_target_pairs={{0,6},{1,7},{2,4},{3,5},{4,2},{5,3},{6,0},{7,1},{8,14},{9,15},{10,... | collective-permute-start | bytes 393224 | tf_op jit(solution)/shard_map/ppermute | solution.py:443
  79.4 7.9 %collective-permute-start.17 = (bf16[32,2048]{1,0:T(8,128)(2,1)S(1)}, bf16[32,2048]{1,0:T(8,128)(2,1)S(1)}, u32[]{:S(2)}, u32[]{:S(2)}) collective-permute-start(bf16[32,2048]{1,0:T(8,128)(2,1)S(1)} %get-tuple-element.51), channel_id=1, source_target_pairs={{0,2},{1,3},{2,0},{3,1},{4,6},{5,7},{6,4},{7,5},{8,10},{9,11},{10,... | collective-permute-start | bytes 393224 | tf_op jit(solution)/shard_map/ppermute | solution.py:443
  84.1 5.0 %collective-permute-start.23 = (bf16[32,2048]{1,0:T(8,128)(2,1)S(1)}, bf16[32,2048]{1,0:T(8,128)(2,1)S(1)}, u32[]{:S(2)}, u32[]{:S(2)}) collective-permute-start(bf16[32,2048]{1,0:T(8,128)(2,1)S(1)} %get-tuple-element.64), channel_id=1, source_target_pairs={{0,2},{1,3},{2,0},{3,1},{4,6},{5,7},{6,4},{7,5},{8,10},{9,11},{10,... | collective-permute-start | bytes 393224 | tf_op jit(solution)/shard_map/ppermute | solution.py:443
  84.6 6.3 %collective-permute-start.20 = (bf16[32,2048]{1,0:T(8,128)(2,1)S(1)}, bf16[32,2048]{1,0:T(8,128)(2,1)S(1)}, u32[]{:S(2)}, u32[]{:S(2)}) collective-permute-start(bf16[32,2048]{1,0:T(8,128)(2,1)S(1)} %get-tuple-element.58), channel_id=1, source_target_pairs={{0,6},{1,7},{2,4},{3,5},{4,2},{5,3},{6,0},{7,1},{8,14},{9,15},{10,... | collective-permute-start | bytes 393224 | tf_op jit(solution)/shard_map/ppermute | solution.py:443

commit v7 on v6

--- a/solution.py
+++ b/solution.py
@@ -14,18 +14,19 @@
 HEADS = 8
 SLICE = 8
 WIDTH = 4
-QUARTERS = 4
-PACK = 272
+COLUMNS = (2048, 2048, 2560, 1536)
+PACK = 264
+SLOT = 272
 LOG_SCALE = HD ** -0.5 * math.log2(math.e)
 NEG = -1e30
 NX = 4
 NZ = 4
 NCORE = 2
 DOUT = 8192
-QCOLS = DOUT // QUARTERS
+STARTS_AT = (0, 2048, 4096, 6656)
 GROUP = 4
 HEADROOM = 60.0
-TILE = 1024
+TILE = 512
 NW = 4
 HOPS = (1, 3, 2)
 
@@ -54,7 +55,7 @@
         base = s * PACK
         out_ref[base:base + 128] = k_ref[rows, :]
         out_ref[base + 128:base + 256] = v_ref[rows, :].T
-        ids = jnp.full((16, 128), span, jnp.float32).astype(jnp.bfloat16)
+        ids = jnp.full((PACK - 256, 128), span, jnp.float32).astype(jnp.bfloat16)
         out_ref[base + 256:base + PACK] = ids
 
 
@@ -84,8 +85,8 @@
 def store_keys(kv_ref, blocks):
     for i, (ref, j) in enumerate(blocks):
         kv_ref[i, 0:256, :] = ref[j * PACK:j * PACK + 256, :]
-        kv_ref[i, 256:PACK, :] = jnp.ones((16, 128), jnp.bfloat16)
-    kv_ref[len(blocks)] = jnp.zeros((PACK, 128), jnp.bfloat16)
+        kv_ref[i, 256:SLOT, :] = jnp.ones((16, 128), jnp.bfloat16)
+    kv_ref[len(blocks)] = jnp.zeros((SLOT, 128), jnp.bfloat16)
 
 
 def span_id(ref, i):
@@ -117,7 +118,7 @@
 
     def add(g, p_ref):
         slots = [list_ref[g * GROUP + i] for i in range(GROUP)]
-        vt = jnp.concatenate([kv_ref[i, 128:PACK, :] for i in slots], axis=1)
+        vt = jnp.concatenate([kv_ref[i, 128:SLOT, :] for i in slots], axis=1)
         for n, u in enumerate(units):
             acc_ref[u] = acc_ref[u] + weighted(vt, p_ref[n])
 
@@ -154,7 +155,7 @@
             m_new = jnp.maximum(m_old, jnp.max(scores, axis=0, keepdims=True))
             probs = jnp.exp2((scores - m_new) * LOG_SCALE).astype(jnp.bfloat16)
             scale = jnp.exp2((m_old - m_new) * LOG_SCALE)
-            acc_ref[u] = acc_ref[u] * scale + weighted(kv_ref[slot, 128:PACK, :], probs)
+            acc_ref[u] = acc_ref[u] * scale + weighted(kv_ref[slot, 128:SLOT, :], probs)
             m_ref[u] = jnp.broadcast_to(m_new, (8, 256))
         return carry
 
@@ -205,7 +206,7 @@
                 scores = jnp.where(key <= row, scores, NEG)
                 m_new = jnp.max(scores, axis=0, keepdims=True)
                 probs = jnp.exp2((scores - m_new) * LOG_SCALE).astype(jnp.bfloat16)
-                acc_ref[u] = weighted(kv_ref[s, 128:PACK, :], probs)
+                acc_ref[u] = weighted(kv_ref[s, 128:SLOT, :], probs)
                 m_ref[u] = jnp.broadcast_to(m_new, (8, 256))
 
     own_block()
@@ -279,12 +280,12 @@
 
 def project(quarter, merged_ref, w_ref, keep_ref, send_ref):
     rows = keep_ref.shape[0]
-    for j in range(QCOLS // TILE):
+    first = STARTS_AT[quarter] - quarter // 2 * (DOUT // 2)
+    for j in range(COLUMNS[quarter] // TILE):
         at = slice(j * TILE, (j + 1) * TILE)
-        start = quarter % 2 * QCOLS + j * TILE
-        part = jnp.dot(
-            merged_ref[...], w_ref[:, start:start + TILE], preferred_element_type=jnp.float32
-        ).astype(jnp.bfloat16)
+        w = w_ref[:, first + j * TILE:first + (j + 1) * TILE]
+        part = jnp.dot(merged_ref[...], w, preferred_element_type=jnp.float32)
+        part = part.astype(jnp.bfloat16)
         keep_ref[:, at] = part[:rows]
         send_ref[:, at] = part[rows:]
 
@@ -320,9 +321,9 @@
 
 def final_kernel(*refs):
     out_ref = refs[-1]
-    for q in range(QUARTERS):
+    for q, (start, width) in enumerate(zip(STARTS_AT, COLUMNS)):
         total = refs[2 * q][...].astype(jnp.float32) + refs[2 * q + 1][...]
-        out_ref[:, q * QCOLS:(q + 1) * QCOLS] = total.astype(jnp.bfloat16)
+        out_ref[:, start:start + width] = total.astype(jnp.bfloat16)
 
 
 def in_hbm(array):
@@ -389,7 +390,7 @@
 
     def walk_scratch(slots, units, width):
         return [
-            pltpu.VMEM((slots + 1, PACK, 128), bf16),
+            pltpu.VMEM((slots + 1, SLOT, 128), bf16),
             pltpu.VMEM((units, 8, 256), f32),
             pltpu.VMEM((units, 8, 256), f32),
             pltpu.VMEM((width, GROUP * SPAN, 256), bf16),
@@ -415,11 +416,14 @@
     )
 
     rows = NZ * WIDTH * SLICE
-    piece = [struct((rows, QCOLS), bf16)] * 2
+
+    def piece(quarter):
+        return [struct((rows, COLUMNS[quarter]), bf16)] * 2
+
     scratch = walk_scratch(18, 2 * WIDTH, WIDTH)
     last = pl.pallas_call(
         last_kernel, in_specs=[SMEM] + [VMEM] * 11 + [HBM], out_specs=[VMEM] * 4,
-        out_shape=piece + [struct((2 * rows, 1024), bf16), struct((1024, DOUT // 2), bf16)],
+        out_shape=piece(0) + [struct((2 * rows, 1024), bf16), struct((1024, DOUT // 2), bf16)],
         scratch_shapes=[pltpu.VMEM((2 * WIDTH, 144, 256), f32)] + scratch
         + [pltpu.SemaphoreType.DMA((NW,))],
         compiler_params=params(16), name="last", cost_estimate=estimate(5 * 10 ** 9, 1 << 20),
@@ -428,7 +432,7 @@
     def rest(quarter, merged, weight):
         return pl.pallas_call(
             functools.partial(project, quarter), in_specs=[VMEM] * 2, out_specs=[VMEM] * 2,
-            out_shape=piece, compiler_params=params(8),
+            out_shape=piece(quarter), compiler_params=params(8),
             cost_estimate=estimate(10 ** 9, 1 << 20),
         )(merged, weight)
 
@@ -446,15 +450,15 @@
         index, tiles, own, *fa, *fb, maxima, acc, weight_a, in_hbm(out_weight)
     )
     stays, blocks = [], []
-    for q in range(QUARTERS):
+    for q in range(4):
         if q > 0:
             keep, send = rest(q, merged, weight_a if q < 2 else weight_b)
         got = move(send, swap_route())
         kernel = functools.partial(pair_kernel, q % 2)
-        stay, out = call(kernel, (rows // 2,) * 2, QCOLS, keep, got)
+        stay, out = call(kernel, (rows // 2,) * 2, COLUMNS[q], keep, got)
         stays.append((stay, move(out, step_route(q % 2))))
     for q, (stay, got) in enumerate(stays):
-        mine, out = call(fold_kernel, (rows // 4,) * 2, QCOLS, stay, got)
+        mine, out = call(fold_kernel, (rows // 4,) * 2, COLUMNS[q], stay, got)
         blocks += [mine, move(out, step_route(1 - q % 2))]
     return call(final_kernel, (rows // 4,), DOUT, *blocks)[0]
 

time: 91.9 us -> 92.6 us (level)
  starting transfers between devices: 32.2 us -> 35.5 us
  waiting for transfers between devices: 23.2 us -> 20.6 us
    ppermute x12, starting transfers between devices: 14.3 us -> 17.9 us  [move(): return lax.ppermute(block, 'tp', route)]
    ppermute x12, waiting for transfers between devices: 11.2 us -> 8.93 us  [move(): return lax.ppermute(block, 'tp', route)]
  transfers between devices with their start and end apart: 24 -> 24, of which waited for: 9 -> 8; matrix products, arithmetic and copies ran while one was open for 0% -> 0% of each run, Pallas kernels for 28% -> 27%
where the time goes in v7:
time: 92.6 us; the launch traced here: 92.4 us
  Pallas kernels  36.1 us (39%)
  starting transfers between devices  35.5 us (38%)
  waiting for transfers between devices  20.6 us (22%)
    pallas_call x1, Pallas kernels, on_device(): first(in_hbm(queries), in_hbm(out_weight), own, *xs, *ys)  22.3 us
    ppermute x12, starting transfers between devices, move(): return lax.ppermute(block, 'tp', route)  17.9 us
    ppermute x12, starting transfers between devices, shifts(): moved.append(lax.ppermute(block, 'ctx', ctx_route(dx * d, dy * d)))  17.6 us
    ppermute x12, waiting for transfers between devices, shifts(): moved.append(lax.ppermute(block, 'ctx', ctx_route(dx * d, dy * d)))  11.7 us
    ppermute x12, waiting for transfers between devices, move(): return lax.ppermute(block, 'tp', route)  8.93 us
    pallas_call x1, Pallas kernels, on_device(): last(index, tiles, own, *fa, *fb, maxima, acc, weight_a, in_hbm(out_weight))  7.41 us
    pallas_call x3, Pallas kernels, rest(): pl.pallas_call(functools.partial(project, quarter), in_specs=[VMEM] * 2,...  3.77 us
  transfers between devices with their start and end apart: 24, of which 8 were waited for; matrix products, arithmetic and copies ran while one was open for 0% of the time, Pallas kernels for 27%

profile of v7, /device:TPU:6, one launch (start us, length us, event | category | flops | bytes accessed | tf_op | source)
XLA Modules:
  0.0 92.4 jit_solution(12469211312815649648)
XLA Ops:
  0.0 1.0 %pack.1.own_ref = bf16[528,128]{1,0:T(8,128)(2,1)S(1)} custom-call(s32[256]{0:T(256)} %pos_hbm.1, bf16[256,128]{1,0:T(8,128)(2,1)} %k_hbm.1, bf16[256,128]{1,0:T(8,128)(2,1)} %v_hbm.1), custom_call_target="tpu_custom_call" | custom-call | tf_op jit(solution)/shard_map/pack/pallas_call | solution.py:363
  1.0 3.3 %collective-permute-start.5 = (bf16[528,128]{1,0:T(8,128)(2,1)S(1)}, bf16[528,128]{1,0:T(8,128)(2,1)S(1)}, u32[]{:S(2)}, u32[]{:S(2)}) collective-permute-start(bf16[528,128]{1,0:T(8,128)(2,1)S(1)} %pack.1.own_ref), channel_id=1, source_target_pairs={{0,16},{8,24},{16,0},{24,8},{32,48},{40,56},{48,32},{56,40},{64,80... | collective-permute-start | bytes 405512 | tf_op jit(solution)/shard_map/ppermute | solution.py:375
  4.3 1.1 %collective-permute-start.4 = (bf16[528,128]{1,0:T(8,128)(2,1)S(1)}, bf16[528,128]{1,0:T(8,128)(2,1)S(1)}, u32[]{:S(2)}, u32[]{:S(2)}) collective-permute-start(bf16[528,128]{1,0:T(8,128)(2,1)S(1)} %pack.1.own_ref), channel_id=1, source_target_pairs={{0,24},{8,0},{16,8},{24,16},{32,56},{40,32},{48,40},{56,48},{64,88... | collective-permute-start | bytes 405512 | tf_op jit(solution)/shard_map/ppermute | solution.py:375
  5.3 1.0 %collective-permute-start.3 = (bf16[528,128]{1,0:T(8,128)(2,1)S(1)}, bf16[528,128]{1,0:T(8,128)(2,1)S(1)}, u32[]{:S(2)}, u32[]{:S(2)}) collective-permute-start(bf16[528,128]{1,0:T(8,128)(2,1)S(1)} %pack.1.own_ref), channel_id=1, source_target_pairs={{0,8},{8,16},{16,24},{24,0},{32,40},{40,48},{48,56},{56,32},{64,72... | collective-permute-start | bytes 405512 | tf_op jit(solution)/shard_map/ppermute | solution.py:375
  6.3 2.4 %collective-permute-done.5.y3.refs_2_ = bf16[528,128]{1,0:T(8,128)(2,1)S(1)} collective-permute-done((bf16[528,128]{1,0:T(8,128)(2,1)S(1)}, bf16[528,128]{1,0:T(8,128)(2,1)S(1)}, u32[]{:S(2)}, u32[]{:S(2)}) %collective-permute-start.5) | collective-permute-done | bytes 135200 | tf_op jit(solution)/shard_map/ppermute | solution.py:375
  8.7 2.5 %collective-permute-done.4.y2.refs_1_ = bf16[528,128]{1,0:T(8,128)(2,1)S(1)} collective-permute-done((bf16[528,128]{1,0:T(8,128)(2,1)S(1)}, bf16[528,128]{1,0:T(8,128)(2,1)S(1)}, u32[]{:S(2)}, u32[]{:S(2)}) %collective-permute-start.4) | collective-permute-done | bytes 135200 | tf_op jit(solution)/shard_map/ppermute | solution.py:375
  11.6 1.5 %collective-permute-start.11 = (bf16[792,128]{1,0:T(8,128)(2,1)S(1)}, bf16[792,128]{1,0:T(8,128)(2,1)S(1)}, u32[]{:S(2)}, u32[]{:S(2)}) collective-permute-start(bf16[792,128]{1,0:T(8,128)(2,1)S(1)} %join.3), channel_id=1, source_target_pairs={{0,64},{8,72},{16,80},{24,88},{32,96},{40,104},{48,112},{56,120},{... | collective-permute-start | bytes 608264 | tf_op jit(solution)/shard_map/ppermute | solution.py:375
  13.0 2.1 %collective-permute-start.2 = (bf16[528,128]{1,0:T(8,128)(2,1)S(1)}, bf16[528,128]{1,0:T(8,128)(2,1)S(1)}, u32[]{:S(2)}, u32[]{:S(2)}) collective-permute-start(bf16[528,128]{1,0:T(8,128)(2,1)S(1)} %pack.1.own_ref), channel_id=1, source_target_pairs={{0,64},{8,72},{16,80},{24,88},{32,96},{40,104},{48,112},{56,120},{... | collective-permute-start | bytes 405512 | tf_op jit(solution)/shard_map/ppermute | solution.py:375
  16.0 2.4 %collective-permute-start = (bf16[528,128]{1,0:T(8,128)(2,1)S(1)}, bf16[528,128]{1,0:T(8,128)(2,1)S(1)}, u32[]{:S(2)}, u32[]{:S(2)}) collective-permute-start(bf16[528,128]{1,0:T(8,128)(2,1)S(1)} %pack.1.own_ref), channel_id=1, source_target_pairs={{0,32},{8,40},{16,48},{24,56},{32,64},{40,72},{48,80},{56,88},{64,... | collective-permute-start | bytes 405512 | tf_op jit(solution)/shard_map/ppermute | solution.py:375
  18.4 5.6 %collective-permute-done.2.x3.refs_2_ = bf16[528,128]{1,0:T(8,128)(2,1)S(1)} collective-permute-done((bf16[528,128]{1,0:T(8,128)(2,1)S(1)}, bf16[528,128]{1,0:T(8,128)(2,1)S(1)}, u32[]{:S(2)}, u32[]{:S(2)}) %collective-permute-start.2) | collective-permute-done | bytes 135200 | tf_op jit(solution)/shard_map/ppermute | solution.py:375
  24.9 3.4 %collective-permute-start.8 = (bf16[792,128]{1,0:T(8,128)(2,1)S(1)}, bf16[792,128]{1,0:T(8,128)(2,1)S(1)}, u32[]{:S(2)}, u32[]{:S(2)}) collective-permute-start(bf16[792,128]{1,0:T(8,128)(2,1)S(1)} %join.2), channel_id=1, source_target_pairs={{0,16},{8,24},{16,0},{24,8},{32,48},{40,56},{48,32},{56,40},{64,80... | collective-permute-start | bytes 608264 | tf_op jit(solution)/shard_map/ppermute | solution.py:375
  28.3 1.3 %collective-permute-start.7 = (bf16[792,128]{1,0:T(8,128)(2,1)S(1)}, bf16[792,128]{1,0:T(8,128)(2,1)S(1)}, u32[]{:S(2)}, u32[]{:S(2)}) collective-permute-start(bf16[792,128]{1,0:T(8,128)(2,1)S(1)} %join.2), channel_id=1, source_target_pairs={{0,24},{8,0},{16,8},{24,16},{32,56},{40,32},{48,40},{56,48},{64,88... | collective-permute-start | bytes 608264 | tf_op jit(solution)/shard_map/ppermute | solution.py:375
  30.4 22.3 %first.1 = (f32[8,8,256]{2,1,0:T(8,128)S(1)}, f32[8,144,256]{2,1,0:T(8,128)S(1)}, bf16[8,256,128]{2,1,0:T(8,128)(2,1)S(1)}, bf16[1024,4096]{1,0:T(8,128)(2,1)S(1)}) custom-call(bf16[256,1024]{1,0:T(8,128)(2,1)} %q_hbm.1, bf16[1024,8192]{1,0:T(8,128)(2,1)} %w_hbm.3, bf16[528,128]{1,0:T(8,128)(2,1)S(1)} %pack.1.own_ref, ...), custom_call_target="tpu_custom_call" | custom-call | flops 4000000000 | bytes 1048576 | tf_op jit(solution)/shard_map/first/pallas_call | solution.py:414
  52.7 7.4 %last.1 = (bf16[128,2048]{1,0:T(8,128)(2,1)S(1)}, bf16[128,2048]{1,0:T(8,128)(2,1)S(1)}, bf16[256,1024]{1,0:T(8,128)(2,1)S(1)}, bf16[1024,4096]{1,0:T(8,128)(2,1)S(1)}) custom-call(s32[1]{0:T(128)} %bitcast.index_ref, bf16[8,256,128]{2,1,0:T(8,128)(2,1)S(1)} %get-tuple-element.35.tile_ref, bf16[528,128]{1,0:T(8,128)(2,1)S(1)} %pack.1.own_ref, ...), custom_call_target="tpu_custom_call" | custom-call | flops 5000000000 | bytes 1048576 | tf_op jit(solution)/shard_map/last/pallas_call | solution.py:449
  60.1 1.5 %shard_map.60 = (bf16[128,2560]{1,0:T(8,128)(2,1)S(1)}, bf16[128,2560]{1,0:T(8,128)(2,1)S(1)}) custom-call(bf16[256,1024]{1,0:T(8,128)(2,1)S(1)} %get-tuple-element.45.merged_ref, bf16[1024,4096]{1,0:T(8,128)(2,1)S(1)} %get-tuple-element.52.w_ref), custom_call_target="tpu_custom_call" | custom-call | flops 1000000000 | bytes 1048576 | tf_op jit(solution)/shard_map/pallas_call | solution.py:433
  62.2 1.3 %shard_map.57 = (bf16[128,2048]{1,0:T(8,128)(2,1)S(1)}, bf16[128,2048]{1,0:T(8,128)(2,1)S(1)}) custom-call(bf16[256,1024]{1,0:T(8,128)(2,1)S(1)} %get-tuple-element.45.merged_ref, bf16[1024,4096]{1,0:T(8,128)(2,1)S(1)} %get-tuple-element.38.w_ref), custom_call_target="tpu_custom_call" | custom-call | flops 1000000000 | bytes 1048576 | tf_op jit(solution)/shard_map/pallas_call | solution.py:433
  63.7 1.0 %shard_map.63 = (bf16[128,1536]{1,0:T(8,128)(2,1)S(1)}, bf16[128,1536]{1,0:T(8,128)(2,1)S(1)}) custom-call(bf16[256,1024]{1,0:T(8,128)(2,1)S(1)} %get-tuple-element.45.merged_ref, bf16[1024,4096]{1,0:T(8,128)(2,1)S(1)} %get-tuple-element.52.w_ref), custom_call_target="tpu_custom_call" | custom-call | flops 1000000000 | bytes 1048576 | tf_op jit(solution)/shard_map/pallas_call | solution.py:433
  65.3 2.0 %collective-permute-start.19 = (bf16[64,2560]{1,0:T(8,128)(2,1)S(1)}, bf16[64,2560]{1,0:T(8,128)(2,1)S(1)}, u32[]{:S(2)}, u32[]{:S(2)}) collective-permute-start(bf16[64,2560]{1,0:T(8,128)(2,1)S(1)} %get-tuple-element.56), channel_id=1, source_target_pairs={{0,2},{1,3},{2,0},{3,1},{4,6},{5,7},{6,4},{7,5},{8,10},{9,11},{10,... | collective-permute-start | bytes 983048 | tf_op jit(solution)/shard_map/ppermute | solution.py:447
  67.8 4.1 %collective-permute-start.16 = (bf16[64,2048]{1,0:T(8,128)(2,1)S(1)}, bf16[64,2048]{1,0:T(8,128)(2,1)S(1)}, u32[]{:S(2)}, u32[]{:S(2)}) collective-permute-start(bf16[64,2048]{1,0:T(8,128)(2,1)S(1)} %get-tuple-element.49), channel_id=1, source_target_pairs={{0,6},{1,7},{2,4},{3,5},{4,2},{5,3},{6,0},{7,1},{8,14},{9,15},{10,... | collective-permute-start | bytes 786440 | tf_op jit(solution)/shard_map/ppermute | solution.py:447
  72.1 3.9 %collective-permute-done.19.got_ref = bf16[64,2560]{1,0:T(8,128)(2,1)S(1)} collective-permute-done((bf16[64,2560]{1,0:T(8,128)(2,1)S(1)}, bf16[64,2560]{1,0:T(8,128)(2,1)S(1)}, u32[]{:S(2)}, u32[]{:S(2)}) %collective-permute-start.19) | collective-permute-done | bytes 327712 | tf_op jit(solution)/shard_map/ppermute | solution.py:447
  76.0 4.1 %collective-permute-start.20 = (bf16[32,2560]{1,0:T(8,128)(2,1)S(1)}, bf16[32,2560]{1,0:T(8,128)(2,1)S(1)}, u32[]{:S(2)}, u32[]{:S(2)}) collective-permute-start(bf16[32,2560]{1,0:T(8,128)(2,1)S(1)} %get-tuple-element.58), channel_id=1, source_target_pairs={{0,6},{1,7},{2,4},{3,5},{4,2},{5,3},{6,0},{7,1},{8,14},{9,15},{10,... | collective-permute-start | bytes 491528 | tf_op jit(solution)/shard_map/ppermute | solution.py:447
  80.9 3.9 %collective-permute-start.14 = (bf16[32,2048]{1,0:T(8,128)(2,1)S(1)}, bf16[32,2048]{1,0:T(8,128)(2,1)S(1)}, u32[]{:S(2)}, u32[]{:S(2)}) collective-permute-start(bf16[32,2048]{1,0:T(8,128)(2,1)S(1)} %get-tuple-element.44), channel_id=1, source_target_pairs={{0,6},{1,7},{2,4},{3,5},{4,2},{5,3},{6,0},{7,1},{8,14},{9,15},{10,... | collective-permute-start | bytes 393224 | tf_op jit(solution)/shard_map/ppermute | solution.py:447
  85.1 2.1 %collective-permute-start.23 = (bf16[32,1536]{1,0:T(8,128)(2,1)S(1)}, bf16[32,1536]{1,0:T(8,128)(2,1)S(1)}, u32[]{:S(2)}, u32[]{:S(2)}) collective-permute-start(bf16[32,1536]{1,0:T(8,128)(2,1)S(1)} %get-tuple-element.64), channel_id=1, source_target_pairs={{0,2},{1,3},{2,0},{3,1},{4,6},{5,7},{6,4},{7,5},{8,10},{9,11},{10,... | collective-permute-start | bytes 294920 | tf_op jit(solution)/shard_map/ppermute | solution.py:447
  87.2 4.3 %collective-permute-done.23.refs_7_ = bf16[32,1536]{1,0:T(8,128)(2,1)S(1)} collective-permute-done((bf16[32,1536]{1,0:T(8,128)(2,1)S(1)}, bf16[32,1536]{1,0:T(8,128)(2,1)S(1)}, u32[]{:S(2)}, u32[]{:S(2)}) %collective-permute-start.23) | collective-permute-done | bytes 98336 | tf_op jit(solution)/shard_map/ppermute | solution.py:447
  (41 shorter events, 7.0 us)
Async XLA Ops:
  1.0 7.7 %collective-permute-start.5 = (bf16[528,128]{1,0:T(8,128)(2,1)S(1)}, bf16[528,128]{1,0:T(8,128)(2,1)S(1)}, u32[]{:S(2)}, u32[]{:S(2)}) collective-permute-start(bf16[528,128]{1,0:T(8,128)(2,1)S(1)} %pack.1.own_ref), channel_id=1, source_target_pairs={{0,16},{8,24},{16,0},{24,8},{32,48},{40,56},{48,32},{56,40},{64,80... | collective-permute-start | bytes 405512 | tf_op jit(solution)/shard_map/ppermute | solution.py:375
  4.3 6.9 %collective-permute-start.4 = (bf16[528,128]{1,0:T(8,128)(2,1)S(1)}, bf16[528,128]{1,0:T(8,128)(2,1)S(1)}, u32[]{:S(2)}, u32[]{:S(2)}) collective-permute-start(bf16[528,128]{1,0:T(8,128)(2,1)S(1)} %pack.1.own_ref), channel_id=1, source_target_pairs={{0,24},{8,0},{16,8},{24,16},{32,56},{40,32},{48,40},{56,48},{64,88... | collective-permute-start | bytes 405512 | tf_op jit(solution)/shard_map/ppermute | solution.py:375
  5.3 6.2 %collective-permute-start.3 = (bf16[528,128]{1,0:T(8,128)(2,1)S(1)}, bf16[528,128]{1,0:T(8,128)(2,1)S(1)}, u32[]{:S(2)}, u32[]{:S(2)}) collective-permute-start(bf16[528,128]{1,0:T(8,128)(2,1)S(1)} %pack.1.own_ref), channel_id=1, source_target_pairs={{0,8},{8,16},{16,24},{24,0},{32,40},{40,48},{48,56},{56,32},{64,72... | collective-permute-start | bytes 405512 | tf_op jit(solution)/shard_map/ppermute | solution.py:375
  11.6 18.0 %collective-permute-start.11 = (bf16[792,128]{1,0:T(8,128)(2,1)S(1)}, bf16[792,128]{1,0:T(8,128)(2,1)S(1)}, u32[]{:S(2)}, u32[]{:S(2)}) collective-permute-start(bf16[792,128]{1,0:T(8,128)(2,1)S(1)} %join.3), channel_id=1, source_target_pairs={{0,64},{8,72},{16,80},{24,88},{32,96},{40,104},{48,112},{56,120},{... | collective-permute-start | bytes 608264 | tf_op jit(solution)/shard_map/ppermute | solution.py:375
  13.0 10.9 %collective-permute-start.2 = (bf16[528,128]{1,0:T(8,128)(2,1)S(1)}, bf16[528,128]{1,0:T(8,128)(2,1)S(1)}, u32[]{:S(2)}, u32[]{:S(2)}) collective-permute-start(bf16[528,128]{1,0:T(8,128)(2,1)S(1)} %pack.1.own_ref), channel_id=1, source_target_pairs={{0,64},{8,72},{16,80},{24,88},{32,96},{40,104},{48,112},{56,120},{... | collective-permute-start | bytes 405512 | tf_op jit(solution)/shard_map/ppermute | solution.py:375
  15.2 9.7 %collective-permute-start.1 = (bf16[528,128]{1,0:T(8,128)(2,1)S(1)}, bf16[528,128]{1,0:T(8,128)(2,1)S(1)}, u32[]{:S(2)}, u32[]{:S(2)}) collective-permute-start(bf16[528,128]{1,0:T(8,128)(2,1)S(1)} %pack.1.own_ref), channel_id=1, source_target_pairs={{0,96},{8,104},{16,112},{24,120},{32,0},{40,8},{48,16},{56,24},{64... | collective-permute-start | bytes 405512 | tf_op jit(solution)/shard_map/ppermute | solution.py:375
  16.0 8.9 %collective-permute-start = (bf16[528,128]{1,0:T(8,128)(2,1)S(1)}, bf16[528,128]{1,0:T(8,128)(2,1)S(1)}, u32[]{:S(2)}, u32[]{:S(2)}) collective-permute-start(bf16[528,128]{1,0:T(8,128)(2,1)S(1)} %pack.1.own_ref), channel_id=1, source_target_pairs={{0,32},{8,40},{16,48},{24,56},{32,64},{40,72},{48,80},{56,88},{64,... | collective-permute-start | bytes 405512 | tf_op jit(solution)/shard_map/ppermute | solution.py:375
  18.4 34.2 %collective-permute-start.10 = (bf16[792,128]{1,0:T(8,128)(2,1)S(1)}, bf16[792,128]{1,0:T(8,128)(2,1)S(1)}, u32[]{:S(2)}, u32[]{:S(2)}) collective-permute-start(bf16[792,128]{1,0:T(8,128)(2,1)S(1)} %join.3), channel_id=1, source_target_pairs={{0,96},{8,104},{16,112},{24,120},{32,0},{40,8},{48,16},{56,24},{64... | collective-permute-start | bytes 608264 | tf_op jit(solution)/shard_map/ppermute | solution.py:375
  24.0 28.7 %collective-permute-start.9 = (bf16[792,128]{1,0:T(8,128)(2,1)S(1)}, bf16[792,128]{1,0:T(8,128)(2,1)S(1)}, u32[]{:S(2)}, u32[]{:S(2)}) collective-permute-start(bf16[792,128]{1,0:T(8,128)(2,1)S(1)} %join.3), channel_id=1, source_target_pairs={{0,32},{8,40},{16,48},{24,56},{32,64},{40,72},{48,80},{56,88},{64,... | collective-permute-start | bytes 608264 | tf_op jit(solution)/shard_map/ppermute | solution.py:375
  24.9 27.8 %collective-permute-start.8 = (bf16[792,128]{1,0:T(8,128)(2,1)S(1)}, bf16[792,128]{1,0:T(8,128)(2,1)S(1)}, u32[]{:S(2)}, u32[]{:S(2)}) collective-permute-start(bf16[792,128]{1,0:T(8,128)(2,1)S(1)} %join.2), channel_id=1, source_target_pairs={{0,16},{8,24},{16,0},{24,8},{32,48},{40,56},{48,32},{56,40},{64,80... | collective-permute-start | bytes 608264 | tf_op jit(solution)/shard_map/ppermute | solution.py:375
  28.3 24.3 %collective-permute-start.7 = (bf16[792,128]{1,0:T(8,128)(2,1)S(1)}, bf16[792,128]{1,0:T(8,128)(2,1)S(1)}, u32[]{:S(2)}, u32[]{:S(2)}) collective-permute-start(bf16[792,128]{1,0:T(8,128)(2,1)S(1)} %join.2), channel_id=1, source_target_pairs={{0,24},{8,0},{16,8},{24,16},{32,56},{40,32},{48,40},{56,48},{64,88... | collective-permute-start | bytes 608264 | tf_op jit(solution)/shard_map/ppermute | solution.py:375
  29.6 23.1 %collective-permute-start.6 = (bf16[792,128]{1,0:T(8,128)(2,1)S(1)}, bf16[792,128]{1,0:T(8,128)(2,1)S(1)}, u32[]{:S(2)}, u32[]{:S(2)}) collective-permute-start(bf16[792,128]{1,0:T(8,128)(2,1)S(1)} %join.2), channel_id=1, source_target_pairs={{0,8},{8,16},{16,24},{24,0},{32,40},{40,48},{48,56},{56,32},{64,72... | collective-permute-start | bytes 608264 | tf_op jit(solution)/shard_map/ppermute | solution.py:375
  61.6 3.5 %collective-permute-start.18 = (bf16[128,2560]{1,0:T(8,128)(2,1)S(1)}, bf16[128,2560]{1,0:T(8,128)(2,1)S(1)}, u32[]{:S(2)}, u32[]{:S(2)}) collective-permute-start(bf16[128,2560]{1,0:T(8,128)(2,1)S(1)} %get-tuple-element.54), channel_id=1, source_target_pairs={{0,1},{1,0},{2,3},{3,2},{4,5},{5,4},{6,7},{7,6},{8,9},{9,8},{10,11... | collective-permute-start | bytes 1966088 | tf_op jit(solution)/shard_map/ppermute | solution.py:447
  61.7 5.6 %collective-permute-start.12 = (bf16[128,2048]{1,0:T(8,128)(2,1)S(1)}, bf16[128,2048]{1,0:T(8,128)(2,1)S(1)}, u32[]{:S(2)}, u32[]{:S(2)}) collective-permute-start(bf16[128,2048]{1,0:T(8,128)(2,1)S(1)} %get-tuple-element.40), channel_id=1, source_target_pairs={{0,1},{1,0},{2,3},{3,2},{4,5},{5,4},{6,7},{7,6},{8,9},{9,8},{10,11... | collective-permute-start | bytes 1572872 | tf_op jit(solution)/shard_map/ppermute | solution.py:447
  63.5 4.1 %collective-permute-start.15 = (bf16[128,2048]{1,0:T(8,128)(2,1)S(1)}, bf16[128,2048]{1,0:T(8,128)(2,1)S(1)}, u32[]{:S(2)}, u32[]{:S(2)}) collective-permute-start(bf16[128,2048]{1,0:T(8,128)(2,1)S(1)} %get-tuple-element.47), channel_id=1, source_target_pairs={{0,1},{1,0},{2,3},{3,2},{4,5},{5,4},{6,7},{7,6},{8,9},{9,8},{10,11... | collective-permute-start | bytes 1572872 | tf_op jit(solution)/shard_map/ppermute | solution.py:447
  64.6 7.2 %collective-permute-start.21 = (bf16[128,1536]{1,0:T(8,128)(2,1)S(1)}, bf16[128,1536]{1,0:T(8,128)(2,1)S(1)}, u32[]{:S(2)}, u32[]{:S(2)}) collective-permute-start(bf16[128,1536]{1,0:T(8,128)(2,1)S(1)} %get-tuple-element.60), channel_id=1, source_target_pairs={{0,1},{1,0},{2,3},{3,2},{4,5},{5,4},{6,7},{7,6},{8,9},{9,8},{10,11... | collective-permute-start | bytes 1179656 | tf_op jit(solution)/shard_map/ppermute | solution.py:447
  65.3 10.7 %collective-permute-start.19 = (bf16[64,2560]{1,0:T(8,128)(2,1)S(1)}, bf16[64,2560]{1,0:T(8,128)(2,1)S(1)}, u32[]{:S(2)}, u32[]{:S(2)}) collective-permute-start(bf16[64,2560]{1,0:T(8,128)(2,1)S(1)} %get-tuple-element.56), channel_id=1, source_target_pairs={{0,2},{1,3},{2,0},{3,1},{4,6},{5,7},{6,4},{7,5},{8,10},{9,11},{10,... | collective-permute-start | bytes 983048 | tf_op jit(solution)/shard_map/ppermute | solution.py:447
  67.4 13.4 %collective-permute-start.13 = (bf16[64,2048]{1,0:T(8,128)(2,1)S(1)}, bf16[64,2048]{1,0:T(8,128)(2,1)S(1)}, u32[]{:S(2)}, u32[]{:S(2)}) collective-permute-start(bf16[64,2048]{1,0:T(8,128)(2,1)S(1)} %get-tuple-element.42), channel_id=1, source_target_pairs={{0,2},{1,3},{2,0},{3,1},{4,6},{5,7},{6,4},{7,5},{8,10},{9,11},{10,... | collective-permute-start | bytes 786440 | tf_op jit(solution)/shard_map/ppermute | solution.py:447
  67.8 17.1 %collective-permute-start.16 = (bf16[64,2048]{1,0:T(8,128)(2,1)S(1)}, bf16[64,2048]{1,0:T(8,128)(2,1)S(1)}, u32[]{:S(2)}, u32[]{:S(2)}) collective-permute-start(bf16[64,2048]{1,0:T(8,128)(2,1)S(1)} %get-tuple-element.49), channel_id=1, source_target_pairs={{0,6},{1,7},{2,4},{3,5},{4,2},{5,3},{6,0},{7,1},{8,14},{9,15},{10,... | collective-permute-start | bytes 786440 | tf_op jit(solution)/shard_map/ppermute | solution.py:447
  72.0 13.1 %collective-permute-start.22 = (bf16[64,1536]{1,0:T(8,128)(2,1)S(1)}, bf16[64,1536]{1,0:T(8,128)(2,1)S(1)}, u32[]{:S(2)}, u32[]{:S(2)}) collective-permute-start(bf16[64,1536]{1,0:T(8,128)(2,1)S(1)} %get-tuple-element.62), channel_id=1, source_target_pairs={{0,6},{1,7},{2,4},{3,5},{4,2},{5,3},{6,0},{7,1},{8,14},{9,15},{10,... | collective-permute-start | bytes 589832 | tf_op jit(solution)/shard_map/ppermute | solution.py:447
  76.0 15.4 %collective-permute-start.20 = (bf16[32,2560]{1,0:T(8,128)(2,1)S(1)}, bf16[32,2560]{1,0:T(8,128)(2,1)S(1)}, u32[]{:S(2)}, u32[]{:S(2)}) collective-permute-start(bf16[32,2560]{1,0:T(8,128)(2,1)S(1)} %get-tuple-element.58), channel_id=1, source_target_pairs={{0,6},{1,7},{2,4},{3,5},{4,2},{5,3},{6,0},{7,1},{8,14},{9,15},{10,... | collective-permute-start | bytes 491528 | tf_op jit(solution)/shard_map/ppermute | solution.py:447
  80.9 10.5 %collective-permute-start.14 = (bf16[32,2048]{1,0:T(8,128)(2,1)S(1)}, bf16[32,2048]{1,0:T(8,128)(2,1)S(1)}, u32[]{:S(2)}, u32[]{:S(2)}) collective-permute-start(bf16[32,2048]{1,0:T(8,128)(2,1)S(1)} %get-tuple-element.44), channel_id=1, source_target_pairs={{0,6},{1,7},{2,4},{3,5},{4,2},{5,3},{6,0},{7,1},{8,14},{9,15},{10,... | collective-permute-start | bytes 393224 | tf_op jit(solution)/shard_map/ppermute | solution.py:447
  85.0 6.5 %collective-permute-start.17 = (bf16[32,2048]{1,0:T(8,128)(2,1)S(1)}, bf16[32,2048]{1,0:T(8,128)(2,1)S(1)}, u32[]{:S(2)}, u32[]{:S(2)}) collective-permute-start(bf16[32,2048]{1,0:T(8,128)(2,1)S(1)} %get-tuple-element.51), channel_id=1, source_target_pairs={{0,2},{1,3},{2,0},{3,1},{4,6},{5,7},{6,4},{7,5},{8,10},{9,11},{10,... | collective-permute-start | bytes 393224 | tf_op jit(solution)/shard_map/ppermute | solution.py:447
  85.1 6.4 %collective-permute-start.23 = (bf16[32,1536]{1,0:T(8,128)(2,1)S(1)}, bf16[32,1536]{1,0:T(8,128)(2,1)S(1)}, u32[]{:S(2)}, u32[]{:S(2)}) collective-permute-start(bf16[32,1536]{1,0:T(8,128)(2,1)S(1)} %get-tuple-element.64), channel_id=1, source_target_pairs={{0,2},{1,3},{2,0},{3,1},{4,6},{5,7},{6,4},{7,5},{8,10},{9,11},{10,... | collective-permute-start | bytes 294920 | tf_op jit(solution)/shard_map/ppermute | solution.py:447

commit v8 on v7

--- a/solution.py
+++ b/solution.py
@@ -290,11 +290,17 @@
         send_ref[:, at] = part[rows:]
 
 
-def last_kernel(index_ref, tile_ref, own_ref, f1, f2, f3, f4, f5, f6, m_in, acc_in, w_ref, w_hbm,
+def second_kernel(tile_ref, own_ref, f1, f2, f3, m_in, acc_in, m_ref, acc_ref, kv_ref, peak_ref,
+                  even_ref, odd_ref, list0, list1):
+    rest_of_attention(tile_ref, own_ref, (f1, f2, f3), m_in, acc_in, kv_ref, m_ref, peak_ref,
+                      acc_ref, even_ref, odd_ref, (list0, list1))
+
+
+def last_kernel(index_ref, tile_ref, own_ref, f1, f2, f3, m_in, acc_in, w_ref, w_hbm,
                 keep_ref, send_ref, merged_ref, w_next, acc_ref, kv_ref, m_ref, peak_ref, even_ref,
                 odd_ref, list0, list1, sems):
     fetch_w = fetch_half(1, w_hbm, w_next, sems)
-    rest_of_attention(tile_ref, own_ref, (f1, f2, f3, f4, f5, f6), m_in, acc_in, kv_ref, m_ref,
+    rest_of_attention(tile_ref, own_ref, (f1, f2, f3), m_in, acc_in, kv_ref, m_ref,
                       peak_ref, acc_ref, even_ref, odd_ref, (list0, list1))
     finish(acc_ref, index_ref, merged_ref)
     project(0, merged_ref, w_ref, keep_ref, send_ref)
@@ -420,9 +426,16 @@
     def piece(quarter):
         return [struct((rows, COLUMNS[quarter]), bf16)] * 2
 
-    scratch = walk_scratch(18, 2 * WIDTH, WIDTH)
+    scratch = walk_scratch(9, 2 * WIDTH, WIDTH)
+    second = pl.pallas_call(
+        second_kernel, in_specs=[VMEM] * 7, out_specs=[VMEM] * 2,
+        out_shape=[struct((8, 8, 256), f32), struct((8, 144, 256), f32)],
+        scratch_shapes=scratch[:1] + scratch[2:], compiler_params=params(14), name="second",
+        cost_estimate=estimate(3 * 10 ** 9, 1 << 20),
+    )
+    maxima, acc = second(tiles, own, *fb, maxima, acc)
     last = pl.pallas_call(
-        last_kernel, in_specs=[SMEM] + [VMEM] * 11 + [HBM], out_specs=[VMEM] * 4,
+        last_kernel, in_specs=[SMEM] + [VMEM] * 8 + [HBM], out_specs=[VMEM] * 4,
         out_shape=piece(0) + [struct((2 * rows, 1024), bf16), struct((1024, DOUT // 2), bf16)],
         scratch_shapes=[pltpu.VMEM((2 * WIDTH, 144, 256), f32)] + scratch
         + [pltpu.SemaphoreType.DMA((NW,))],
@@ -447,7 +460,7 @@
         return lax.ppermute(block, "tp", route)
 
     keep, send, merged, weight_b = last(
-        index, tiles, own, *fa, *fb, maxima, acc, weight_a, in_hbm(out_weight)
+        index, tiles, own, *fa, maxima, acc, weight_a, in_hbm(out_weight)
     )
     stays, blocks = [], []
     for q in range(4):

time: 92.6 us -> 86.9 us (0.938)
  waiting for transfers between devices: 20.6 us -> 17.1 us
  starting transfers between devices: 35.5 us -> 32.1 us
  Pallas kernels: 36.1 us -> 37.4 us
    ppermute x12, waiting for transfers between devices: 11.7 us -> 8.18 us  [shifts(): moved.append(lax.ppermute(block, 'ctx', ctx_route(dx * d, dy * d)))]
    ppermute x12, starting transfers between devices: 17.6 us -> 14.2 us  [shifts(): moved.append(lax.ppermute(block, 'ctx', ctx_route(dx * d, dy * d)))]
    pallas_call x1 -> x2, Pallas kernels: 7.41 us -> 8.74 us  [the longest x1 5.18 us: on_device(): last(index, tiles, own, *fa, maxima, acc, weight_a, in_hbm(out_weight))]
  transfers between devices with their start and end apart: 24 -> 24, of which waited for: 8 -> 9; matrix products, arithmetic and copies ran while one was open for 0% -> 0% of each run, Pallas kernels for 27% -> 33%
where the time goes in v8:
time: 86.9 us; the launch traced here: 86.8 us
  Pallas kernels  37.4 us (43%)
  starting transfers between devices  32.1 us (37%)
  waiting for transfers between devices  17.1 us (20%)
    pallas_call x1, Pallas kernels, on_device(): first(in_hbm(queries), in_hbm(out_weight), own, *xs, *ys)  22.3 us
    ppermute x12, starting transfers between devices, move(): return lax.ppermute(block, 'tp', route)  17.9 us
    ppermute x12, starting transfers between devices, shifts(): moved.append(lax.ppermute(block, 'ctx', ctx_route(dx * d, dy * d)))  14.2 us
    ppermute x12, waiting for transfers between devices, move(): return lax.ppermute(block, 'tp', route)  8.94 us
    ppermute x12, waiting for transfers between devices, shifts(): moved.append(lax.ppermute(block, 'ctx', ctx_route(dx * d, dy * d)))  8.18 us
    pallas_call x1, Pallas kernels, on_device(): last(index, tiles, own, *fa, maxima, acc, weight_a, in_hbm(out_weight))  5.18 us
    pallas_call x3, Pallas kernels, rest(): pl.pallas_call(functools.partial(project, quarter), in_specs=[VMEM] * 2,...  3.74 us
    pallas_call x1, Pallas kernels, on_device(): maxima, acc = second(tiles, own, *fb, maxima, acc)  3.55 us
  transfers between devices with their start and end apart: 24, of which 9 were waited for; matrix products, arithmetic and copies ran while one was open for 0% of the time, Pallas kernels for 33%

profile of v8, /device:TPU:6, one launch (start us, length us, event | category | flops | bytes accessed | tf_op | source)
XLA Modules:
  0.0 86.8 jit_solution(3943003391541239970)
XLA Ops:
  0.0 1.0 %pack.1.own_ref = bf16[528,128]{1,0:T(8,128)(2,1)S(1)} custom-call(s32[256]{0:T(256)} %pos_hbm.1, bf16[256,128]{1,0:T(8,128)(2,1)} %k_hbm.1, bf16[256,128]{1,0:T(8,128)(2,1)} %v_hbm.1), custom_call_target="tpu_custom_call" | custom-call | tf_op jit(solution)/shard_map/pack/pallas_call | solution.py:369
  1.0 3.3 %collective-permute-start.5 = (bf16[528,128]{1,0:T(8,128)(2,1)S(1)}, bf16[528,128]{1,0:T(8,128)(2,1)S(1)}, u32[]{:S(2)}, u32[]{:S(2)}) collective-permute-start(bf16[528,128]{1,0:T(8,128)(2,1)S(1)} %pack.1.own_ref), channel_id=1, source_target_pairs={{0,16},{8,24},{16,0},{24,8},{32,48},{40,56},{48,32},{56,40},{64,80... | collective-permute-start | bytes 405512 | tf_op jit(solution)/shard_map/ppermute | solution.py:381
  4.3 1.1 %collective-permute-start.4 = (bf16[528,128]{1,0:T(8,128)(2,1)S(1)}, bf16[528,128]{1,0:T(8,128)(2,1)S(1)}, u32[]{:S(2)}, u32[]{:S(2)}) collective-permute-start(bf16[528,128]{1,0:T(8,128)(2,1)S(1)} %pack.1.own_ref), channel_id=1, source_target_pairs={{0,24},{8,0},{16,8},{24,16},{32,56},{40,32},{48,40},{56,48},{64,88... | collective-permute-start | bytes 405512 | tf_op jit(solution)/shard_map/ppermute | solution.py:381
  5.3 1.0 %collective-permute-start.3 = (bf16[528,128]{1,0:T(8,128)(2,1)S(1)}, bf16[528,128]{1,0:T(8,128)(2,1)S(1)}, u32[]{:S(2)}, u32[]{:S(2)}) collective-permute-start(bf16[528,128]{1,0:T(8,128)(2,1)S(1)} %pack.1.own_ref), channel_id=1, source_target_pairs={{0,8},{8,16},{16,24},{24,0},{32,40},{40,48},{48,56},{56,32},{64,72... | collective-permute-start | bytes 405512 | tf_op jit(solution)/shard_map/ppermute | solution.py:381
  6.3 1.4 %collective-permute-start.2 = (bf16[528,128]{1,0:T(8,128)(2,1)S(1)}, bf16[528,128]{1,0:T(8,128)(2,1)S(1)}, u32[]{:S(2)}, u32[]{:S(2)}) collective-permute-start(bf16[528,128]{1,0:T(8,128)(2,1)S(1)} %pack.1.own_ref), channel_id=1, source_target_pairs={{0,64},{8,72},{16,80},{24,88},{32,96},{40,104},{48,112},{56,120},{... | collective-permute-start | bytes 405512 | tf_op jit(solution)/shard_map/ppermute | solution.py:381
  8.7 2.3 %collective-permute-start = (bf16[528,128]{1,0:T(8,128)(2,1)S(1)}, bf16[528,128]{1,0:T(8,128)(2,1)S(1)}, u32[]{:S(2)}, u32[]{:S(2)}) collective-permute-start(bf16[528,128]{1,0:T(8,128)(2,1)S(1)} %pack.1.own_ref), channel_id=1, source_target_pairs={{0,32},{8,40},{16,48},{24,56},{32,64},{40,72},{48,80},{56,88},{64,... | collective-permute-start | bytes 405512 | tf_op jit(solution)/shard_map/ppermute | solution.py:381
  11.6 1.5 %collective-permute-start.11 = (bf16[792,128]{1,0:T(8,128)(2,1)S(1)}, bf16[792,128]{1,0:T(8,128)(2,1)S(1)}, u32[]{:S(2)}, u32[]{:S(2)}) collective-permute-start(bf16[792,128]{1,0:T(8,128)(2,1)S(1)} %join.3), channel_id=1, source_target_pairs={{0,64},{8,72},{16,80},{24,88},{32,96},{40,104},{48,112},{56,120},{... | collective-permute-start | bytes 608264 | tf_op jit(solution)/shard_map/ppermute | solution.py:381
  13.7 2.6 %collective-permute-start.9 = (bf16[792,128]{1,0:T(8,128)(2,1)S(1)}, bf16[792,128]{1,0:T(8,128)(2,1)S(1)}, u32[]{:S(2)}, u32[]{:S(2)}) collective-permute-start(bf16[792,128]{1,0:T(8,128)(2,1)S(1)} %join.3), channel_id=1, source_target_pairs={{0,32},{8,40},{16,48},{24,56},{32,64},{40,72},{48,80},{56,88},{64,... | collective-permute-start | bytes 608264 | tf_op jit(solution)/shard_map/ppermute | solution.py:381
  16.3 2.6 %collective-permute-done.1.x2.refs_1_ = bf16[528,128]{1,0:T(8,128)(2,1)S(1)} collective-permute-done((bf16[528,128]{1,0:T(8,128)(2,1)S(1)}, bf16[528,128]{1,0:T(8,128)(2,1)S(1)}, u32[]{:S(2)}, u32[]{:S(2)}) %collective-permute-start.1) | collective-permute-done | bytes 135200 | tf_op jit(solution)/shard_map/ppermute | solution.py:381
  19.0 1.0 %collective-permute-start.7 = (bf16[792,128]{1,0:T(8,128)(2,1)S(1)}, bf16[792,128]{1,0:T(8,128)(2,1)S(1)}, u32[]{:S(2)}, u32[]{:S(2)}) collective-permute-start(bf16[792,128]{1,0:T(8,128)(2,1)S(1)} %join.2), channel_id=1, source_target_pairs={{0,24},{8,0},{16,8},{24,16},{32,56},{40,32},{48,40},{56,48},{64,88... | collective-permute-start | bytes 608264 | tf_op jit(solution)/shard_map/ppermute | solution.py:381
  20.0 22.3 %first.1 = (f32[8,8,256]{2,1,0:T(8,128)S(1)}, f32[8,144,256]{2,1,0:T(8,128)S(1)}, bf16[8,256,128]{2,1,0:T(8,128)(2,1)S(1)}, bf16[1024,4096]{1,0:T(8,128)(2,1)S(1)}) custom-call(bf16[256,1024]{1,0:T(8,128)(2,1)} %q_hbm.1, bf16[1024,8192]{1,0:T(8,128)(2,1)} %w_hbm.3, bf16[528,128]{1,0:T(8,128)(2,1)S(1)} %pack.1.own_ref, ...), custom_call_target="tpu_custom_call" | custom-call | flops 4000000000 | bytes 1048576 | tf_op jit(solution)/shard_map/first/pallas_call | solution.py:420
  42.4 3.6 %second.1 = (f32[8,8,256]{2,1,0:T(8,128)S(1)}, f32[8,144,256]{2,1,0:T(8,128)S(1)}) custom-call(bf16[8,256,128]{2,1,0:T(8,128)(2,1)S(1)} %get-tuple-element.37.tile_ref, bf16[528,128]{1,0:T(8,128)(2,1)S(1)} %pack.1.own_ref, bf16[792,128]{1,0:T(8,128)(2,1)S(1)} %collective-permute-done.9.f1, bf16[792,128]{1,0:T(8,128)(2,1)S(1)} %collective-permute-done.10.f2, ...), custom_call_target="tpu_custom_call" | custom-call | flops 3000000000 | bytes 1048576 | tf_op jit(solution)/shard_map/second/pallas_call | solution.py:436
  46.0 3.3 %collective-permute-done.6.f1 = bf16[792,128]{1,0:T(8,128)(2,1)S(1)} collective-permute-done((bf16[792,128]{1,0:T(8,128)(2,1)S(1)}, bf16[792,128]{1,0:T(8,128)(2,1)S(1)}, u32[]{:S(2)}, u32[]{:S(2)}) %collective-permute-start.6) | collective-permute-done | bytes 202784 | tf_op jit(solution)/shard_map/ppermute | solution.py:381
  49.3 5.2 %last.1 = (bf16[128,2048]{1,0:T(8,128)(2,1)S(1)}, bf16[128,2048]{1,0:T(8,128)(2,1)S(1)}, bf16[256,1024]{1,0:T(8,128)(2,1)S(1)}, bf16[1024,4096]{1,0:T(8,128)(2,1)S(1)}) custom-call(s32[1]{0:T(128)} %bitcast.index_ref, bf16[8,256,128]{2,1,0:T(8,128)(2,1)S(1)} %get-tuple-element.37.tile_ref, bf16[528,128]{1,0:T(8,128)(2,1)S(1)} %pack.1.own_ref, ...), custom_call_target="tpu_custom_call" | custom-call | flops 5000000000 | bytes 1048576 | tf_op jit(solution)/shard_map/last/pallas_call | solution.py:462
  54.5 1.5 %shard_map.60 = (bf16[128,2560]{1,0:T(8,128)(2,1)S(1)}, bf16[128,2560]{1,0:T(8,128)(2,1)S(1)}) custom-call(bf16[256,1024]{1,0:T(8,128)(2,1)S(1)} %get-tuple-element.49.merged_ref, bf16[1024,4096]{1,0:T(8,128)(2,1)S(1)} %get-tuple-element.56.w_ref), custom_call_target="tpu_custom_call" | custom-call | flops 1000000000 | bytes 1048576 | tf_op jit(solution)/shard_map/pallas_call | solution.py:446
  56.6 1.2 %shard_map.57 = (bf16[128,2048]{1,0:T(8,128)(2,1)S(1)}, bf16[128,2048]{1,0:T(8,128)(2,1)S(1)}) custom-call(bf16[256,1024]{1,0:T(8,128)(2,1)S(1)} %get-tuple-element.49.merged_ref, bf16[1024,4096]{1,0:T(8,128)(2,1)S(1)} %get-tuple-element.42.w_ref), custom_call_target="tpu_custom_call" | custom-call | flops 1000000000 | bytes 1048576 | tf_op jit(solution)/shard_map/pallas_call | solution.py:446
  58.0 1.0 %shard_map.63 = (bf16[128,1536]{1,0:T(8,128)(2,1)S(1)}, bf16[128,1536]{1,0:T(8,128)(2,1)S(1)}) custom-call(bf16[256,1024]{1,0:T(8,128)(2,1)S(1)} %get-tuple-element.49.merged_ref, bf16[1024,4096]{1,0:T(8,128)(2,1)S(1)} %get-tuple-element.56.w_ref), custom_call_target="tpu_custom_call" | custom-call | flops 1000000000 | bytes 1048576 | tf_op jit(solution)/shard_map/pallas_call | solution.py:446
  59.7 2.0 %collective-permute-start.19 = (bf16[64,2560]{1,0:T(8,128)(2,1)S(1)}, bf16[64,2560]{1,0:T(8,128)(2,1)S(1)}, u32[]{:S(2)}, u32[]{:S(2)}) collective-permute-start(bf16[64,2560]{1,0:T(8,128)(2,1)S(1)} %get-tuple-element.60), channel_id=1, source_target_pairs={{0,2},{1,3},{2,0},{3,1},{4,6},{5,7},{6,4},{7,5},{8,10},{9,11},{10,... | collective-permute-start | bytes 983048 | tf_op jit(solution)/shard_map/ppermute | solution.py:460
  62.1 4.1 %collective-permute-start.16 = (bf16[64,2048]{1,0:T(8,128)(2,1)S(1)}, bf16[64,2048]{1,0:T(8,128)(2,1)S(1)}, u32[]{:S(2)}, u32[]{:S(2)}) collective-permute-start(bf16[64,2048]{1,0:T(8,128)(2,1)S(1)} %get-tuple-element.53), channel_id=1, source_target_pairs={{0,6},{1,7},{2,4},{3,5},{4,2},{5,3},{6,0},{7,1},{8,14},{9,15},{10,... | collective-permute-start | bytes 786440 | tf_op jit(solution)/shard_map/ppermute | solution.py:460
  66.4 3.9 %collective-permute-done.19.got_ref = bf16[64,2560]{1,0:T(8,128)(2,1)S(1)} collective-permute-done((bf16[64,2560]{1,0:T(8,128)(2,1)S(1)}, bf16[64,2560]{1,0:T(8,128)(2,1)S(1)}, u32[]{:S(2)}, u32[]{:S(2)}) %collective-permute-start.19) | collective-permute-done | bytes 327712 | tf_op jit(solution)/shard_map/ppermute | solution.py:460
  70.4 4.1 %collective-permute-start.20 = (bf16[32,2560]{1,0:T(8,128)(2,1)S(1)}, bf16[32,2560]{1,0:T(8,128)(2,1)S(1)}, u32[]{:S(2)}, u32[]{:S(2)}) collective-permute-start(bf16[32,2560]{1,0:T(8,128)(2,1)S(1)} %get-tuple-element.62), channel_id=1, source_target_pairs={{0,6},{1,7},{2,4},{3,5},{4,2},{5,3},{6,0},{7,1},{8,14},{9,15},{10,... | collective-permute-start | bytes 491528 | tf_op jit(solution)/shard_map/ppermute | solution.py:460
  75.3 3.9 %collective-permute-start.14 = (bf16[32,2048]{1,0:T(8,128)(2,1)S(1)}, bf16[32,2048]{1,0:T(8,128)(2,1)S(1)}, u32[]{:S(2)}, u32[]{:S(2)}) collective-permute-start(bf16[32,2048]{1,0:T(8,128)(2,1)S(1)} %get-tuple-element.48), channel_id=1, source_target_pairs={{0,6},{1,7},{2,4},{3,5},{4,2},{5,3},{6,0},{7,1},{8,14},{9,15},{10,... | collective-permute-start | bytes 393224 | tf_op jit(solution)/shard_map/ppermute | solution.py:460
  79.5 2.1 %collective-permute-start.23 = (bf16[32,1536]{1,0:T(8,128)(2,1)S(1)}, bf16[32,1536]{1,0:T(8,128)(2,1)S(1)}, u32[]{:S(2)}, u32[]{:S(2)}) collective-permute-start(bf16[32,1536]{1,0:T(8,128)(2,1)S(1)} %get-tuple-element.68), channel_id=1, source_target_pairs={{0,2},{1,3},{2,0},{3,1},{4,6},{5,7},{6,4},{7,5},{8,10},{9,11},{10,... | collective-permute-start | bytes 294920 | tf_op jit(solution)/shard_map/ppermute | solution.py:460
  81.6 4.3 %collective-permute-done.23.refs_7_ = bf16[32,1536]{1,0:T(8,128)(2,1)S(1)} collective-permute-done((bf16[32,1536]{1,0:T(8,128)(2,1)S(1)}, bf16[32,1536]{1,0:T(8,128)(2,1)S(1)}, u32[]{:S(2)}, u32[]{:S(2)}) %collective-permute-start.23) | collective-permute-done | bytes 98336 | tf_op jit(solution)/shard_map/ppermute | solution.py:460
  (42 shorter events, 6.5 us)
Async XLA Ops:
  1.0 7.7 %collective-permute-start.5 = (bf16[528,128]{1,0:T(8,128)(2,1)S(1)}, bf16[528,128]{1,0:T(8,128)(2,1)S(1)}, u32[]{:S(2)}, u32[]{:S(2)}) collective-permute-start(bf16[528,128]{1,0:T(8,128)(2,1)S(1)} %pack.1.own_ref), channel_id=1, source_target_pairs={{0,16},{8,24},{16,0},{24,8},{32,48},{40,56},{48,32},{56,40},{64,80... | collective-permute-start | bytes 405512 | tf_op jit(solution)/shard_map/ppermute | solution.py:381
  4.3 6.9 %collective-permute-start.4 = (bf16[528,128]{1,0:T(8,128)(2,1)S(1)}, bf16[528,128]{1,0:T(8,128)(2,1)S(1)}, u32[]{:S(2)}, u32[]{:S(2)}) collective-permute-start(bf16[528,128]{1,0:T(8,128)(2,1)S(1)} %pack.1.own_ref), channel_id=1, source_target_pairs={{0,24},{8,0},{16,8},{24,16},{32,56},{40,32},{48,40},{56,48},{64,88... | collective-permute-start | bytes 405512 | tf_op jit(solution)/shard_map/ppermute | solution.py:381
  5.3 6.2 %collective-permute-start.3 = (bf16[528,128]{1,0:T(8,128)(2,1)S(1)}, bf16[528,128]{1,0:T(8,128)(2,1)S(1)}, u32[]{:S(2)}, u32[]{:S(2)}) collective-permute-start(bf16[528,128]{1,0:T(8,128)(2,1)S(1)} %pack.1.own_ref), channel_id=1, source_target_pairs={{0,8},{8,16},{16,24},{24,0},{32,40},{40,48},{48,56},{56,32},{64,72... | collective-permute-start | bytes 405512 | tf_op jit(solution)/shard_map/ppermute | solution.py:381
  6.3 7.4 %collective-permute-start.2 = (bf16[528,128]{1,0:T(8,128)(2,1)S(1)}, bf16[528,128]{1,0:T(8,128)(2,1)S(1)}, u32[]{:S(2)}, u32[]{:S(2)}) collective-permute-start(bf16[528,128]{1,0:T(8,128)(2,1)S(1)} %pack.1.own_ref), channel_id=1, source_target_pairs={{0,64},{8,72},{16,80},{24,88},{32,96},{40,104},{48,112},{56,120},{... | collective-permute-start | bytes 405512 | tf_op jit(solution)/shard_map/ppermute | solution.py:381
  7.7 11.2 %collective-permute-start.1 = (bf16[528,128]{1,0:T(8,128)(2,1)S(1)}, bf16[528,128]{1,0:T(8,128)(2,1)S(1)}, u32[]{:S(2)}, u32[]{:S(2)}) collective-permute-start(bf16[528,128]{1,0:T(8,128)(2,1)S(1)} %pack.1.own_ref), channel_id=1, source_target_pairs={{0,96},{8,104},{16,112},{24,120},{32,0},{40,8},{48,16},{56,24},{64... | collective-permute-start | bytes 405512 | tf_op jit(solution)/shard_map/ppermute | solution.py:381
  8.7 10.2 %collective-permute-start = (bf16[528,128]{1,0:T(8,128)(2,1)S(1)}, bf16[528,128]{1,0:T(8,128)(2,1)S(1)}, u32[]{:S(2)}, u32[]{:S(2)}) collective-permute-start(bf16[528,128]{1,0:T(8,128)(2,1)S(1)} %pack.1.own_ref), channel_id=1, source_target_pairs={{0,32},{8,40},{16,48},{24,56},{32,64},{40,72},{48,80},{56,88},{64,... | collective-permute-start | bytes 405512 | tf_op jit(solution)/shard_map/ppermute | solution.py:381
  11.6 30.7 %collective-permute-start.11 = (bf16[792,128]{1,0:T(8,128)(2,1)S(1)}, bf16[792,128]{1,0:T(8,128)(2,1)S(1)}, u32[]{:S(2)}, u32[]{:S(2)}) collective-permute-start(bf16[792,128]{1,0:T(8,128)(2,1)S(1)} %join.3), channel_id=1, source_target_pairs={{0,64},{8,72},{16,80},{24,88},{32,96},{40,104},{48,112},{56,120},{... | collective-permute-start | bytes 608264 | tf_op jit(solution)/shard_map/ppermute | solution.py:381
  13.0 29.3 %collective-permute-start.10 = (bf16[792,128]{1,0:T(8,128)(2,1)S(1)}, bf16[792,128]{1,0:T(8,128)(2,1)S(1)}, u32[]{:S(2)}, u32[]{:S(2)}) collective-permute-start(bf16[792,128]{1,0:T(8,128)(2,1)S(1)} %join.3), channel_id=1, source_target_pairs={{0,96},{8,104},{16,112},{24,120},{32,0},{40,8},{48,16},{56,24},{64... | collective-permute-start | bytes 608264 | tf_op jit(solution)/shard_map/ppermute | solution.py:381
  13.7 28.6 %collective-permute-start.9 = (bf16[792,128]{1,0:T(8,128)(2,1)S(1)}, bf16[792,128]{1,0:T(8,128)(2,1)S(1)}, u32[]{:S(2)}, u32[]{:S(2)}) collective-permute-start(bf16[792,128]{1,0:T(8,128)(2,1)S(1)} %join.3), channel_id=1, source_target_pairs={{0,32},{8,40},{16,48},{24,56},{32,64},{40,72},{48,80},{56,88},{64,... | collective-permute-start | bytes 608264 | tf_op jit(solution)/shard_map/ppermute | solution.py:381
  18.9 27.1 %collective-permute-start.8 = (bf16[792,128]{1,0:T(8,128)(2,1)S(1)}, bf16[792,128]{1,0:T(8,128)(2,1)S(1)}, u32[]{:S(2)}, u32[]{:S(2)}) collective-permute-start(bf16[792,128]{1,0:T(8,128)(2,1)S(1)} %join.2), channel_id=1, source_target_pairs={{0,16},{8,24},{16,0},{24,8},{32,48},{40,56},{48,32},{56,40},{64,80... | collective-permute-start | bytes 608264 | tf_op jit(solution)/shard_map/ppermute | solution.py:381
  19.0 27.0 %collective-permute-start.7 = (bf16[792,128]{1,0:T(8,128)(2,1)S(1)}, bf16[792,128]{1,0:T(8,128)(2,1)S(1)}, u32[]{:S(2)}, u32[]{:S(2)}) collective-permute-start(bf16[792,128]{1,0:T(8,128)(2,1)S(1)} %join.2), channel_id=1, source_target_pairs={{0,24},{8,0},{16,8},{24,16},{32,56},{40,32},{48,40},{56,48},{64,88... | collective-permute-start | bytes 608264 | tf_op jit(solution)/shard_map/ppermute | solution.py:381
  42.3 7.0 %collective-permute-start.6 = (bf16[792,128]{1,0:T(8,128)(2,1)S(1)}, bf16[792,128]{1,0:T(8,128)(2,1)S(1)}, u32[]{:S(2)}, u32[]{:S(2)}) collective-permute-start(bf16[792,128]{1,0:T(8,128)(2,1)S(1)} %join.2), channel_id=1, source_target_pairs={{0,8},{8,16},{16,24},{24,0},{32,40},{40,48},{48,56},{56,32},{64,72... | collective-permute-start | bytes 608264 | tf_op jit(solution)/shard_map/ppermute | solution.py:381
  56.0 3.5 %collective-permute-start.18 = (bf16[128,2560]{1,0:T(8,128)(2,1)S(1)}, bf16[128,2560]{1,0:T(8,128)(2,1)S(1)}, u32[]{:S(2)}, u32[]{:S(2)}) collective-permute-start(bf16[128,2560]{1,0:T(8,128)(2,1)S(1)} %get-tuple-element.58), channel_id=1, source_target_pairs={{0,1},{1,0},{2,3},{3,2},{4,5},{5,4},{6,7},{7,6},{8,9},{9,8},{10,11... | collective-permute-start | bytes 1966088 | tf_op jit(solution)/shard_map/ppermute | solution.py:460
  56.1 5.6 %collective-permute-start.12 = (bf16[128,2048]{1,0:T(8,128)(2,1)S(1)}, bf16[128,2048]{1,0:T(8,128)(2,1)S(1)}, u32[]{:S(2)}, u32[]{:S(2)}) collective-permute-start(bf16[128,2048]{1,0:T(8,128)(2,1)S(1)} %get-tuple-element.44), channel_id=1, source_target_pairs={{0,1},{1,0},{2,3},{3,2},{4,5},{5,4},{6,7},{7,6},{8,9},{9,8},{10,11... | collective-permute-start | bytes 1572872 | tf_op jit(solution)/shard_map/ppermute | solution.py:460
  57.9 4.1 %collective-permute-start.15 = (bf16[128,2048]{1,0:T(8,128)(2,1)S(1)}, bf16[128,2048]{1,0:T(8,128)(2,1)S(1)}, u32[]{:S(2)}, u32[]{:S(2)}) collective-permute-start(bf16[128,2048]{1,0:T(8,128)(2,1)S(1)} %get-tuple-element.51), channel_id=1, source_target_pairs={{0,1},{1,0},{2,3},{3,2},{4,5},{5,4},{6,7},{7,6},{8,9},{9,8},{10,11... | collective-permute-start | bytes 1572872 | tf_op jit(solution)/shard_map/ppermute | solution.py:460
  59.0 7.2 %collective-permute-start.21 = (bf16[128,1536]{1,0:T(8,128)(2,1)S(1)}, bf16[128,1536]{1,0:T(8,128)(2,1)S(1)}, u32[]{:S(2)}, u32[]{:S(2)}) collective-permute-start(bf16[128,1536]{1,0:T(8,128)(2,1)S(1)} %get-tuple-element.64), channel_id=1, source_target_pairs={{0,1},{1,0},{2,3},{3,2},{4,5},{5,4},{6,7},{7,6},{8,9},{9,8},{10,11... | collective-permute-start | bytes 1179656 | tf_op jit(solution)/shard_map/ppermute | solution.py:460
  59.7 10.7 %collective-permute-start.19 = (bf16[64,2560]{1,0:T(8,128)(2,1)S(1)}, bf16[64,2560]{1,0:T(8,128)(2,1)S(1)}, u32[]{:S(2)}, u32[]{:S(2)}) collective-permute-start(bf16[64,2560]{1,0:T(8,128)(2,1)S(1)} %get-tuple-element.60), channel_id=1, source_target_pairs={{0,2},{1,3},{2,0},{3,1},{4,6},{5,7},{6,4},{7,5},{8,10},{9,11},{10,... | collective-permute-start | bytes 983048 | tf_op jit(solution)/shard_map/ppermute | solution.py:460
  61.8 13.5 %collective-permute-start.13 = (bf16[64,2048]{1,0:T(8,128)(2,1)S(1)}, bf16[64,2048]{1,0:T(8,128)(2,1)S(1)}, u32[]{:S(2)}, u32[]{:S(2)}) collective-permute-start(bf16[64,2048]{1,0:T(8,128)(2,1)S(1)} %get-tuple-element.46), channel_id=1, source_target_pairs={{0,2},{1,3},{2,0},{3,1},{4,6},{5,7},{6,4},{7,5},{8,10},{9,11},{10,... | collective-permute-start | bytes 786440 | tf_op jit(solution)/shard_map/ppermute | solution.py:460
  62.1 17.2 %collective-permute-start.16 = (bf16[64,2048]{1,0:T(8,128)(2,1)S(1)}, bf16[64,2048]{1,0:T(8,128)(2,1)S(1)}, u32[]{:S(2)}, u32[]{:S(2)}) collective-permute-start(bf16[64,2048]{1,0:T(8,128)(2,1)S(1)} %get-tuple-element.53), channel_id=1, source_target_pairs={{0,6},{1,7},{2,4},{3,5},{4,2},{5,3},{6,0},{7,1},{8,14},{9,15},{10,... | collective-permute-start | bytes 786440 | tf_op jit(solution)/shard_map/ppermute | solution.py:460
  66.3 13.1 %collective-permute-start.22 = (bf16[64,1536]{1,0:T(8,128)(2,1)S(1)}, bf16[64,1536]{1,0:T(8,128)(2,1)S(1)}, u32[]{:S(2)}, u32[]{:S(2)}) collective-permute-start(bf16[64,1536]{1,0:T(8,128)(2,1)S(1)} %get-tuple-element.66), channel_id=1, source_target_pairs={{0,6},{1,7},{2,4},{3,5},{4,2},{5,3},{6,0},{7,1},{8,14},{9,15},{10,... | collective-permute-start | bytes 589832 | tf_op jit(solution)/shard_map/ppermute | solution.py:460
  70.4 15.5 %collective-permute-start.20 = (bf16[32,2560]{1,0:T(8,128)(2,1)S(1)}, bf16[32,2560]{1,0:T(8,128)(2,1)S(1)}, u32[]{:S(2)}, u32[]{:S(2)}) collective-permute-start(bf16[32,2560]{1,0:T(8,128)(2,1)S(1)} %get-tuple-element.62), channel_id=1, source_target_pairs={{0,6},{1,7},{2,4},{3,5},{4,2},{5,3},{6,0},{7,1},{8,14},{9,15},{10,... | collective-permute-start | bytes 491528 | tf_op jit(solution)/shard_map/ppermute | solution.py:460
  75.3 10.5 %collective-permute-start.14 = (bf16[32,2048]{1,0:T(8,128)(2,1)S(1)}, bf16[32,2048]{1,0:T(8,128)(2,1)S(1)}, u32[]{:S(2)}, u32[]{:S(2)}) collective-permute-start(bf16[32,2048]{1,0:T(8,128)(2,1)S(1)} %get-tuple-element.48), channel_id=1, source_target_pairs={{0,6},{1,7},{2,4},{3,5},{4,2},{5,3},{6,0},{7,1},{8,14},{9,15},{10,... | collective-permute-start | bytes 393224 | tf_op jit(solution)/shard_map/ppermute | solution.py:460
  79.3 6.5 %collective-permute-start.17 = (bf16[32,2048]{1,0:T(8,128)(2,1)S(1)}, bf16[32,2048]{1,0:T(8,128)(2,1)S(1)}, u32[]{:S(2)}, u32[]{:S(2)}) collective-permute-start(bf16[32,2048]{1,0:T(8,128)(2,1)S(1)} %get-tuple-element.55), channel_id=1, source_target_pairs={{0,2},{1,3},{2,0},{3,1},{4,6},{5,7},{6,4},{7,5},{8,10},{9,11},{10,... | collective-permute-start | bytes 393224 | tf_op jit(solution)/shard_map/ppermute | solution.py:460
  79.5 6.4 %collective-permute-start.23 = (bf16[32,1536]{1,0:T(8,128)(2,1)S(1)}, bf16[32,1536]{1,0:T(8,128)(2,1)S(1)}, u32[]{:S(2)}, u32[]{:S(2)}) collective-permute-start(bf16[32,1536]{1,0:T(8,128)(2,1)S(1)} %get-tuple-element.68), channel_id=1, source_target_pairs={{0,2},{1,3},{2,0},{3,1},{4,6},{5,7},{6,4},{7,5},{8,10},{9,11},{10,... | collective-permute-start | bytes 294920 | tf_op jit(solution)/shard_map/ppermute | solution.py:460
